TPU v7x, 32 devices: a whole 2x2x4 slice. The times are simulated.
32 devices in a mesh: space: 8 (over y, x, core), members: 4 (over z).
Axes of the slice: x: 2, y: 2, z: 4, core: 2. Of those that a mesh axis runs over, the one named last changes fastest.
Arguments:
- ensemble: bfloat16 [128, 65536], P('members', 'space'), may hold values from -6 to 6
- op_blocks: bfloat16 [512, 3, 128, 128], P('space'), may hold values from -0.3125 to 0.3125
- col_index: int32 [512, 2], P('space'), may hold values from 0 to 511, as said below
- weights: float32 [128, 512], P('members', 'space')
- innovations: float32 [2, 65536], P(None, 'space'), may hold values from -6 to 6
- obs_precision: float32 [2, 65536], P(None, 'space'), may hold values from 0.25 to 4
Outputs:
- grad_ens: float32 [128, 65536], P('members', 'space')
- direction: float32 [128, 512], P('members', 'space')
Inputs may be any that keep to these rules, and one draw needn't show every extreme that they name: col_index[r, 0] lies in [r - 32, r - 1] and col_index[r, 1] in [r + 1, r + 32], each clipped to the grid; in every aligned run of 64 block-rows some row reaches back by exactly 32 and some row forward by exactly 32, before clipping.
All inputs are finite; a program needn't handle non-finite values.
Results may differ from a plain program's by a relative error of at most 0.011.
Values may be sent and summed in bfloat16 or wider, within the bound.
No kernel may reach another device: no remote copies, remote signals or barrier semaphores. Data moves between devices by JAX's collectives and lax.ppermute only.
A program may use at most 64 MiB of HBM per device.

v0:
```python
import jax
import jax.numpy as jnp
from jax import lax
from jax.sharding import PartitionSpec as P

MEMBERS = 128


def padded(x, sides, width):
    for axis, dim in sides:
        devices, length = (lax.axis_size(axis), x.shape[dim])
        up = [(i, (i + 1) % devices) for i in range(devices - 1)]
        down = [(j, i) for i, j in up]
        last = lax.slice_in_dim(x, length - width, length, axis=dim)
        leading = lax.slice_in_dim(x, 0, width, axis=dim)
        before = lax.ppermute(last, axis, up)
        after = lax.ppermute(leading, axis, down)
        x = jnp.concatenate([before, x, after], axis=dim)
    return x


def on_device(ensemble, op_blocks, col_index, weights, innovations, obs_precision):
    member_count = ensemble.shape[0]
    blocks = op_blocks.shape[0]
    per_row = op_blocks.shape[1]
    block_size = op_blocks.shape[2]
    offset_rows = lax.axis_index("space") * blocks - blocks
    local_cols = col_index - offset_rows
    own_rows = (jnp.arange(blocks, dtype=jnp.int32) + blocks)[:, None]
    every_col = jnp.concatenate([own_rows, local_cols], axis=1)
    wide_rows = blocks + 2 * blocks

    def widen_halo(flat_values):
        widened = padded(flat_values, (("space", 1),), blocks * block_size)
        return widened.reshape(member_count, wide_rows, block_size)

    def forward(values_in):
        flat_values = values_in.reshape(member_count, blocks * block_size)
        widened = widen_halo(flat_values)
        picked = widened[:, every_col, :]
        return jnp.einsum("rkij,mrkj->mri", op_blocks, picked, preferred_element_type=jnp.float32)

    def adjoint(cotangent):
        contributions = jnp.einsum(
            "rkij,mri->mrkj", op_blocks, cotangent, preferred_element_type=jnp.float32
        )
        spread_rows = jnp.zeros((member_count, wide_rows, block_size), jnp.float32)
        spread_rows = spread_rows.at[:, every_col.reshape(-1), :].add(
            contributions.reshape(member_count, blocks * per_row, block_size)
        )
        outer_rims = jnp.concatenate(
            [spread_rows[:, :blocks], spread_rows[:, blocks + blocks :]], axis=1
        )
        outer_rims = outer_rims.reshape(member_count, 2 * blocks * block_size)
        received = padded(outer_rims, (("space", 1),), blocks * block_size)
        received = received.reshape(member_count, 4 * blocks, block_size)
        own_sums = spread_rows[:, blocks : blocks + blocks]
        own_sums = own_sums.at[:, :blocks].add(received[:, :blocks])
        own_sums = own_sums.at[:, blocks - blocks :].add(received[:, 3 * blocks :])
        return own_sums

    states = ensemble.reshape(member_count, blocks, block_size)
    prop_one = forward(states).astype(jnp.bfloat16)
    prop_two = forward(prop_one).astype(jnp.bfloat16)
    member_scale = (MEMBERS - 1) ** (-0.5)
    weight_col = weights[:, :, None]
    partial_sums = jnp.stack(
        [
            jnp.sum(weight_col * prop_one.astype(jnp.float32), axis=0),
            jnp.sum(weight_col * prop_two.astype(jnp.float32), axis=0),
        ]
    )
    observed = innovations.reshape(2, blocks, block_size)
    precision = obs_precision.reshape(2, blocks, block_size)
    increments = lax.psum(partial_sums, "members") * member_scale
    residual = precision * (increments - observed)
    cot_one = (member_scale * weight_col * residual[0][None]).astype(jnp.bfloat16)
    cot_two = (member_scale * weight_col * residual[1][None]).astype(jnp.bfloat16)
    adjoint_mid = (cot_one.astype(jnp.float32) + adjoint(cot_two)).astype(jnp.bfloat16)
    grad_ens = adjoint(adjoint_mid).reshape(member_count, blocks * block_size)
    products = (
        prop_one.astype(jnp.float32) * residual[0][None]
        + prop_two.astype(jnp.float32) * residual[1][None]
    )
    grad_weights = weights + member_scale * jnp.sum(products, axis=2)
    squares = lax.psum(jnp.sum(grad_weights * grad_weights, axis=1), "space")
    mean_square = squares / (blocks * lax.axis_size("space"))
    direction = grad_weights / jnp.sqrt(mean_square + 1e-06)[:, None]
    return (grad_ens, direction)


def solution(mesh):
    placed = (
        P("members", "space"),
        P("space", None, None, None),
        P("space", None),
        P("members", "space"),
        P(None, "space"),
        P(None, "space"),
    )
    return jax.shard_map(
        on_device,
        mesh=mesh,
        in_specs=placed,
        out_specs=(P("members", "space"), P("members", "space")),
        check_vma=False,
    )
```

profile of v0, /device:TPU:1, one launch (start us, length us, event | category | flops | bytes accessed | tf_op | source)
XLA Modules:
  0.0 225.7 jit_solution(5958671020050633099)
XLA Ops:
  7.2 4.5 %collective-permute-start = (bf16[32,8192]{1,0:T(8,128)(2,1)}, bf16[32,8192]{1,0:T(8,128)(2,1)S(1)}, u32[]{:S(2)}, u32[]{:S(2)}) collective-permute-start(bf16[32,8192]{1,0:T(8,128)(2,1)} %param.22), channel_id=1, source_target_pairs={{0,4},{4,8},{8,12},{12,16},{16,20},{20,24},{24,28},{1,5},{5,9},{9,... | collective-permute-start | bytes 1572872 | tf_op jit(solution)/shard_map/ppermute | solution.py:16
  11.7 1.9 collective-permute-start.1
  13.7 0.7 fusion.36
  14.6 3.5 %collective-permute-done = bf16[32,8192]{1,0:T(8,128)(2,1)S(1)} collective-permute-done((bf16[32,8192]{1,0:T(8,128)(2,1)}, bf16[32,8192]{1,0:T(8,128)(2,1)S(1)}, u32[]{:S(2)}, u32[]{:S(2)}) %collective-permute-start) | collective-permute-done | bytes 524320 | tf_op jit(solution)/shard_map/ppermute | solution.py:16
  18.1 7.2 %collective-permute-done.1 = bf16[32,8192]{1,0:T(8,128)(2,1)S(1)} collective-permute-done((bf16[32,8192]{1,0:T(8,128)(2,1)}, bf16[32,8192]{1,0:T(8,128)(2,1)S(1)}, u32[]{:S(2)}, u32[]{:S(2)}) %collective-permute-start.1) | collective-permute-done | bytes 524320 | tf_op jit(solution)/shard_map/ppermute | solution.py:17
  25.3 1.3 copy_bitcast_fusion.2
  26.6 0.9 gather_fusion
  27.6 5.1 %fusion = bf16[64,32,128]{2,1,0:T(8,128)(2,1)S(1)} fusion(bf16[32,64,3,128]{3,0,2,1:T(8,128)(2,1)S(1)} %bitcast.123, bf16[64,3,128,128]{3,2,1,0:T(8,128)(2,1)} %param.23), kind=kOutput, calls=%fused_computation.17 | convolution fusion | flops 201588736 | bytes 8388608 | tf_op jit(solution)/shard_map/rkij,mrkj->mri/dot_general | solution.py:41
  32.7 1.9 collective-permute-start.3
  34.6 3.6 %collective-permute-start.2 = (bf16[32,8192]{1,0:T(8,128)(2,1)S(1)}, bf16[32,8192]{1,0:T(8,128)(2,1)S(1)}, u32[]{:S(2)}, u32[]{:S(2)}) collective-permute-start(bf16[32,8192]{1,0:T(8,128)(2,1)S(1)} %copy_bitcast_fusion.4), channel_id=1, source_target_pairs={{0,4},{4,8},{8,12},{12,16},{16,20},{20,24},{24,28},{1,5},{5,9},{9,... | collective-permute-start | bytes 1572872 | tf_op jit(solution)/shard_map/ppermute | solution.py:16
  38.6 6.4 %collective-permute-done.3 = bf16[32,8192]{1,0:T(8,128)(2,1)S(1)} collective-permute-done((bf16[32,8192]{1,0:T(8,128)(2,1)S(1)}, bf16[32,8192]{1,0:T(8,128)(2,1)S(1)}, u32[]{:S(2)}, u32[]{:S(2)}) %collective-permute-start.3) | collective-permute-done | bytes 524320 | tf_op jit(solution)/shard_map/ppermute | solution.py:17
  45.2 1.3 pad_maximum_fusion
  46.5 2.3 %gather_fusion.1 = bf16[192,32,128]{2,1,0:T(8,128)(2,1)S(1)} fusion(bf16[32,192,128]{2,0,1:T(8,128)(2,1)} %pad_maximum_fusion, s32[1024]{0:T(1024)S(1)} %pad_clamp_fusion), kind=kCustom, calls=%fused_computation.1 | custom fusion | bytes 3146496 | tf_op jit(solution)/shard_map/gather | solution.py:40
  48.9 5.1 %fusion.4 = (f32[64,128]{1,0:T(8,128)S(1)}, f32[64,128]{1,0:T(8,128)S(1)}, f32[32,64,128]{2,0,1:T(8,128)S(1)}) fusion(f32[32,64]{0,1:T(8,128)S(1)} %copy.44, bf16[64,32,128]{2,1,0:T(8,128)(2,1)S(1)} %fusion, bf16[32,64,3,128]{3,0,2,1:T(8,128)(2,1)S(1)} %bitcast.122, bf16[64,3,128,128]{3,2,1,0:T(8,128)(2,1)} %param.23), kind=kOutput, calls=%fused_computation.21 | convolution fusion | flops 203145216 | bytes 9510912 | tf_op jit(solution)/shard_map/rkij,mrkj->mri/dot_general | solution.py:41
  54.0 0.6 pad_maximum_fusion.1
  54.7 36.1 %all-reduce.2.cloned.1.call-done = f32[2,64,128]{2,1,0:T(8,128)} async-done(((f32[2,64,128]{2,1,0:T(8,128)}), f32[2,64,128]{2,1,0:T(8,128)}) %all-reduce.2.cloned.1.call-update) | async-done | bytes 65552 | tf_op jit(solution)/shard_map/psum | solution.py:75
  90.8 0.9 fusion.22
  91.7 0.4 fusion.6
  92.1 13.8 %psum.15 = f32[32]{0:T(128)S(1)} all-reduce(f32[32]{0:T(128)S(1)} %multiply_reduce_fusion.1), channel_id=1, replica_groups=mesh['space'=8,'members'=4] {'space'}, use_global_device_ids=true, to_apply=%region_7.0 | all-reduce | flops 32 | bytes 256 | tf_op jit(solution)/shard_map/psum | solution.py:86
  105.9 5.7 %fusion.13 = f32[64,32,3,128]{3,1,2,0:T(8,128)} fusion(bf16[64,3,128,128]{3,2,1,0:T(8,128)(2,1)} %param.23, f32[64,128]{1,0:T(8,128)S(1)} %get-tuple-element.99, f32[32,64]{0,1:T(8,128)S(1)} %get-tuple-element.101), kind=kOutput, calls=%fused_computation.36 | convolution fusion | flops 201850880 | bytes 9478144 | tf_op jit(solution)/shard_map/rkij,mri->mrkj/dot_general | solution.py:44
  111.6 0.4 broadcast.210.clone
  112.0 17.3 %scatter_fusion = f32[32,192,128]{2,0,1:T(8,128)S(1)} fusion(f32[32,192,128]{2,0,1:T(8,128)S(1)} %broadcast.210.clone, s32[192]{0:T(256)S(1)} %bitcast.128, f32[192,32,128]{2,1,0:T(8,128)} %bitcast.119), kind=kCustom, calls=%fused_computation.2 | custom fusion | flops 786432 | bytes 9437952 | tf_op jit(solution)/shard_map/scatter-add | solution.py:48
  129.3 0.2 fusion.27
  129.8 1.9 collective-permute-start.4
  131.7 2.6 %collective-permute-start.5 = (f32[32,8192]{1,0:T(8,128)S(1)}, f32[32,8192]{1,0:T(8,128)S(1)}, u32[]{:S(2)}, u32[]{:S(2)}) collective-permute-start(f32[32,8192]{1,0:T(8,128)S(1)} %get-tuple-element.97), channel_id=1, source_target_pairs={{4,0},{8,4},{12,8},{16,12},{20,16},{24,20},{28,24},{5,1},{9,5},{13... | collective-permute-start | bytes 3145736 | tf_op jit(solution)/shard_map/ppermute | solution.py:17
  134.4 9.1 %collective-permute-done.4 = f32[32,8192]{1,0:T(8,128)S(1)} collective-permute-done((f32[32,8192]{1,0:T(8,128)S(1)}, f32[32,8192]{1,0:T(8,128)S(1)}, u32[]{:S(2)}, u32[]{:S(2)}) %collective-permute-start.4) | collective-permute-done | bytes 1048608 | tf_op jit(solution)/shard_map/ppermute | solution.py:16
  143.4 14.6 %collective-permute-done.5 = f32[32,8192]{1,0:T(8,128)S(1)} collective-permute-done((f32[32,8192]{1,0:T(8,128)S(1)}, f32[32,8192]{1,0:T(8,128)S(1)}, u32[]{:S(2)}, u32[]{:S(2)}) %collective-permute-start.5) | collective-permute-done | bytes 1048608 | tf_op jit(solution)/shard_map/ppermute | solution.py:17
  158.0 0.3 maximum_bitcast_fusion
  158.3 0.7 copy.78
  159.1 0.2 fusion.25
  159.3 0.4 slice-done
  159.6 1.3 slice-done.1
  160.9 3.9 %fusion.16 = f32[64,32,3,128]{3,1,2,0:T(8,128)} fusion(bf16[64,3,128,128]{3,2,1,0:T(8,128)(2,1)S(1)} %bitcast.116, f32[32,64,128]{2,1,0:T(8,128)S(1)} %get-tuple-element.89, f32[32,64,128]{2,1,0:T(8,128)S(1)} %get-tuple-element.88, f32[32,192,128]{2,0,1:T(8,128)S(1)} %scatter_fusion, f32[64,128]{1,0:T(8,128)S(1)} %get-tuple-element.98, ...), kind=kOutput, calls=%fused_computation.38 | convolution fusion | flops 203161600 | bytes 12648448 | tf_op jit(solution)/shard_map/rkij,mri->mrkj/dot_general | solution.py:44
  164.8 0.4 broadcast.210
  165.2 17.3 %scatter_fusion.1 = f32[32,192,128]{2,0,1:T(8,128)S(1)} fusion(f32[32,192,128]{2,0,1:T(8,128)S(1)} %broadcast.210, s32[192]{0:T(256)S(1)} %bitcast.129, f32[192,32,128]{2,1,0:T(8,128)} %bitcast.118), kind=kCustom, calls=%fused_computation.3 | custom fusion | flops 786432 | bytes 9437952 | tf_op jit(solution)/shard_map/scatter-add | solution.py:48
  182.5 0.2 fusion.26
  182.6 0.1 copy_bitcast_fusion
  182.8 1.3 copy-done
  184.1 1.5 fusion.28
  185.6 1.9 collective-permute-start.6
  187.5 3.4 %collective-permute-start.7 = (f32[32,8192]{1,0:T(8,128)}, f32[32,8192]{1,0:T(8,128)}, u32[]{:S(2)}, u32[]{:S(2)}) collective-permute-start(f32[32,8192]{1,0:T(8,128)} %get-tuple-element.95), channel_id=1, source_target_pairs={{4,0},{8,4},{12,8},{16,12},{20,16},{24,20},{28,24},{5,1},{9,5},{13... | collective-permute-start | bytes 3145736 | tf_op jit(solution)/shard_map/ppermute | solution.py:17
  190.9 0.7 copy.60
  191.6 8.0 %collective-permute-done.6 = f32[32,8192]{1,0:T(8,128)} collective-permute-done((f32[32,8192]{1,0:T(8,128)}, f32[32,8192]{1,0:T(8,128)}, u32[]{:S(2)}, u32[]{:S(2)}) %collective-permute-start.6) | collective-permute-done | bytes 1048608 | tf_op jit(solution)/shard_map/ppermute | solution.py:16
  199.6 13.6 %collective-permute-done.7 = f32[32,8192]{1,0:T(8,128)} collective-permute-done((f32[32,8192]{1,0:T(8,128)}, f32[32,8192]{1,0:T(8,128)}, u32[]{:S(2)}, u32[]{:S(2)}) %collective-permute-start.7) | collective-permute-done | bytes 1048608 | tf_op jit(solution)/shard_map/ppermute | solution.py:17
  213.2 2.4 %maximum_bitcast_fusion.1 = f32[4,8,256,128]{3,1,2,0:T(8,128)S(1)} fusion(f32[32,8192]{1,0:T(8,128)} %collective-permute-done.7, f32[32,16384]{1,0:T(8,128)} %copy-done, f32[32,8192]{1,0:T(8,128)} %collective-permute-done.6), kind=kLoop, calls=%fused_computation.5 | loop fusion | flops 2097152 | bytes 8388608
  215.6 0.7 copy.79
  216.3 0.2 fusion.24
  216.6 2.2 copy_bitcast_fusion.3
  (36 shorter events, 1.3 us)
Async XLA Ops:
  7.2 83.7 %all-reduce.2.cloned.1.call-start = ((), (), s32[]{:S(2)}) async-start(), calls=%async_computation | async-start | bytes 131072 | tf_op jit(solution)/shard_map/psum | solution.py:75
  7.2 10.9 %collective-permute-start = (bf16[32,8192]{1,0:T(8,128)(2,1)}, bf16[32,8192]{1,0:T(8,128)(2,1)S(1)}, u32[]{:S(2)}, u32[]{:S(2)}) collective-permute-start(bf16[32,8192]{1,0:T(8,128)(2,1)} %param.22), channel_id=1, source_target_pairs={{0,4},{4,8},{8,12},{12,16},{16,20},{20,24},{24,28},{1,5},{5,9},{9,... | collective-permute-start | bytes 1572872 | tf_op jit(solution)/shard_map/ppermute | solution.py:16
  11.7 13.6 %collective-permute-start.1 = (bf16[32,8192]{1,0:T(8,128)(2,1)}, bf16[32,8192]{1,0:T(8,128)(2,1)S(1)}, u32[]{:S(2)}, u32[]{:S(2)}) collective-permute-start(bf16[32,8192]{1,0:T(8,128)(2,1)} %param.22), channel_id=1, source_target_pairs={{4,0},{8,4},{12,8},{16,12},{20,16},{24,20},{28,24},{5,1},{9,5},{13... | collective-permute-start | bytes 1572872 | tf_op jit(solution)/shard_map/ppermute | solution.py:17
  27.5 10.7 %copy-start.4 = (s32[64,2]{0,1:T(2,128)S(1)}, s32[64,2]{0,1:T(2,128)}, u32[]{:S(2)}) copy-start(s32[64,2]{0,1:T(2,128)} %param.24) | copy-start | bytes 1540
  27.5 11.0 %copy-start.3 = (f32[32,64]{1,0:T(8,128)S(1)}, f32[32,64]{1,0:T(8,128)}, u32[]{:S(2)}) copy-start(f32[32,64]{1,0:T(8,128)} %param.25) | copy-start | bytes 24580
  32.7 12.3 %collective-permute-start.3 = (bf16[32,8192]{1,0:T(8,128)(2,1)S(1)}, bf16[32,8192]{1,0:T(8,128)(2,1)S(1)}, u32[]{:S(2)}, u32[]{:S(2)}) collective-permute-start(bf16[32,8192]{1,0:T(8,128)(2,1)S(1)} %copy_bitcast_fusion.4), channel_id=1, source_target_pairs={{4,0},{8,4},{12,8},{16,12},{20,16},{24,20},{28,24},{5,1},{9,5},{13... | collective-permute-start | bytes 1572872 | tf_op jit(solution)/shard_map/ppermute | solution.py:17
  34.6 10.5 %collective-permute-start.2 = (bf16[32,8192]{1,0:T(8,128)(2,1)S(1)}, bf16[32,8192]{1,0:T(8,128)(2,1)S(1)}, u32[]{:S(2)}, u32[]{:S(2)}) collective-permute-start(bf16[32,8192]{1,0:T(8,128)(2,1)S(1)} %copy_bitcast_fusion.4), channel_id=1, source_target_pairs={{0,4},{4,8},{8,12},{12,16},{16,20},{20,24},{24,28},{1,5},{5,9},{9,... | collective-permute-start | bytes 1572872 | tf_op jit(solution)/shard_map/ppermute | solution.py:16
  48.9 42.0 %copy-start.1 = (f32[2,8192]{1,0:T(2,128)S(1)}, f32[2,8192]{1,0:T(2,128)}, u32[]{:S(2)}) copy-start(f32[2,8192]{1,0:T(2,128)} %param.26) | copy-start | bytes 196612
  48.9 42.0 %copy-start.2 = (f32[2,8192]{1,0:T(2,128)S(1)}, f32[2,8192]{1,0:T(2,128)}, u32[]{:S(2)}) copy-start(f32[2,8192]{1,0:T(2,128)} %param.27) | copy-start | bytes 196612
  129.8 13.7 %collective-permute-start.4 = (f32[32,8192]{1,0:T(8,128)S(1)}, f32[32,8192]{1,0:T(8,128)S(1)}, u32[]{:S(2)}, u32[]{:S(2)}) collective-permute-start(f32[32,8192]{1,0:T(8,128)S(1)} %get-tuple-element.96), channel_id=1, source_target_pairs={{0,4},{4,8},{8,12},{12,16},{16,20},{20,24},{24,28},{1,5},{5,9},{9,... | collective-permute-start | bytes 3145736 | tf_op jit(solution)/shard_map/ppermute | solution.py:16
  131.7 26.3 %collective-permute-start.5 = (f32[32,8192]{1,0:T(8,128)S(1)}, f32[32,8192]{1,0:T(8,128)S(1)}, u32[]{:S(2)}, u32[]{:S(2)}) collective-permute-start(f32[32,8192]{1,0:T(8,128)S(1)} %get-tuple-element.97), channel_id=1, source_target_pairs={{4,0},{8,4},{12,8},{16,12},{20,16},{24,20},{28,24},{5,1},{9,5},{13... | collective-permute-start | bytes 3145736 | tf_op jit(solution)/shard_map/ppermute | solution.py:17
  158.0 1.6 slice-start
  158.3 2.6 %slice-start.1 = ((s8[6291456]{0:T(1024)(128)(4,1)}), s8[4194304]{0:T(1024)(128)(4,1)S(1)}, s32[]{:S(2)}) async-start(s8[6291456]{0:T(1024)(128)(4,1)} %bitcast.115), calls=%async_computation.2 | async-start | bytes 8388608
  182.8 1.3 copy-start
  185.6 14.0 %collective-permute-start.6 = (f32[32,8192]{1,0:T(8,128)}, f32[32,8192]{1,0:T(8,128)}, u32[]{:S(2)}, u32[]{:S(2)}) collective-permute-start(f32[32,8192]{1,0:T(8,128)} %get-tuple-element.94), channel_id=1, source_target_pairs={{0,4},{4,8},{8,12},{12,16},{16,20},{20,24},{24,28},{1,5},{5,9},{9,... | collective-permute-start | bytes 3145736 | tf_op jit(solution)/shard_map/ppermute | solution.py:16
  187.5 25.6 %collective-permute-start.7 = (f32[32,8192]{1,0:T(8,128)}, f32[32,8192]{1,0:T(8,128)}, u32[]{:S(2)}, u32[]{:S(2)}) collective-permute-start(f32[32,8192]{1,0:T(8,128)} %get-tuple-element.95), channel_id=1, source_target_pairs={{4,0},{8,4},{12,8},{16,12},{20,16},{24,20},{28,24},{5,1},{9,5},{13... | collective-permute-start | bytes 3145736 | tf_op jit(solution)/shard_map/ppermute | solution.py:17
Sparse Core Ops, SparseCore 0:
  54.8 35.9 all-reduce.1
where the time goes:
time: 227 us; the launch traced here: 226 us
  waiting for transfers between devices  98.4 us (43%)
  other arithmetic  45 us (20%)
  starting transfers between devices  21.9 us (10%)
  matrix products  19.8 us (9%)
  between operations  14.4 us (6%)
  blocking collectives  13.8 us (6%)
  local copies, waits for them, and re-layouts  12.3 us (5%)
    ppermute x4, waiting for transfers between devices, padded(): after = lax.ppermute(leading, axis, down)  41.7 us
    psum x1, waiting for transfers between devices, on_device(): increments = lax.psum(partial_sums, 'members') * member_scale  36.1 us
    scatter-add x2, other arithmetic, adjoint(): spread_rows.at[:, every_col.reshape(-1), :]  34.5 us
    ppermute x4, waiting for transfers between devices, padded(): before = lax.ppermute(last, axis, up)  20.6 us
    psum x1, blocking collectives, on_device(): squares = lax.psum(jnp.sum(grad_weights * grad_weights, axis=1), 'space')  13.8 us
    ppermute x4, starting transfers between devices, padded(): before = lax.ppermute(last, axis, up)  12 us
    dot_general x2, matrix products, forward(): jnp.einsum('rkij,mrkj->mri', op_blocks, picked, preferred_element_type=jn...  10.2 us
    ppermute x4, starting transfers between devices, padded(): after = lax.ppermute(leading, axis, down)  9.86 us
  transfers between devices with their start and end apart: 9, of which 8 were waited for; matrix products, arithmetic and copies ran while one was open for 1% of the time, Pallas kernels for 0%

commit v1 on v0

v1 whole, which is shorter than its diff:
```python
import jax
import jax.numpy as jnp
from jax import lax
from jax.experimental import pallas as pl
from jax.experimental.pallas import tpu as pltpu
from jax.sharding import PartitionSpec as P

MEMBERS = 128
REACH = 32
SCALE = (MEMBERS - 1) ** (-0.5)
F32 = jnp.float32
BF16 = jnp.bfloat16
ROWS_T = (((1,), (1,)), ((), ()))
ROWS_N = (((1,), (0,)), ((), ()))


def dot_t(x, a):
    return lax.dot_general(x, a, ROWS_T, preferred_element_type=F32)


def dot_n(x, a):
    return lax.dot_general(x, a, ROWS_N, preferred_element_type=F32)


def is_even():
    return lax.axis_index("space") % 2 == 0


def base_row(rows):
    return lax.axis_index("space") * rows


def block(ref, start, size):
    return ref[:, pl.ds(pl.multiple_of(start * size, size), size)]


def chunks(total, unroll, body):
    unroll = min(unroll, total)

    def step(i, carry):
        body([i * unroll + u for u in range(unroll)])
        return carry

    lax.fori_loop(0, total // unroll, step, 0)


def inner_pairs(rows):
    return ((2, 0, rows - REACH), (1, REACH, rows - REACH))


def rim_pairs(rows):
    return ((1, 0, REACH), (2, rows - REACH, REACH))


def forward_inner(cols, v, ops, acc):
    rows, _, size, _ = ops.shape
    base = base_row(rows)
    for k, low, count in inner_pairs(rows):

        def some(ids, k=k, low=low):
            outs = []
            for i in ids:
                r = low + i
                c = cols[k - 1, r] - base
                x = jnp.concatenate([block(v, r, size), block(v, c, size)], 1)
                outs.append((r, dot_t(x, jnp.concatenate([ops[r, 0], ops[r, k]], 1))))
            for r, o in outs:
                acc[r] = o

        chunks(count, 16, some)


def fill_wide(wide, v, mate, off, halo):
    length = v.shape[1]
    even = is_even()
    wide[:, halo : halo + length] = v[...]

    @pl.when(even)
    def _():
        wide[:, :halo] = off[...]
        wide[:, halo + length :] = mate[...]

    @pl.when(jnp.logical_not(even))
    def _():
        wide[:, :halo] = mate[...]
        wide[:, halo + length :] = off[...]


def pick(first, last):
    even = is_even()
    return jnp.where(even, last, first), jnp.where(even, first, last)


def forward_rim(cols, acc, v, mate, off, ops, out, wide):
    rows, _, size, _ = ops.shape
    base = base_row(rows)
    fill_wide(wide, v, mate, off, REACH * size)
    for k, low, count in rim_pairs(rows):

        def some(ids, k=k, low=low):
            outs = []
            for i in ids:
                r = low + i
                c = cols[k - 1, r] - base + REACH
                outs.append((r, acc[r] + dot_t(block(wide, c, size), ops[r, k])))
            for r, o in outs:
                out[:, pl.ds(pl.multiple_of(r * size, size), size)] = o.astype(BF16)

        chunks(count, 16, some)


def first_rim(cols, acc, v, mate, off, ops, out, to_mate, to_off, wide):
    forward_rim(cols, acc, v, mate, off, ops, out, wide)
    halo = REACH * ops.shape[2]
    length = out.shape[1]
    even = is_even()

    @pl.when(even)
    def _():
        to_mate[...] = out[:, length - halo :]
        to_off[...] = out[:, :halo]

    @pl.when(jnp.logical_not(even))
    def _():
        to_mate[...] = out[:, :halo]
        to_off[...] = out[:, length - halo :]


def member_sum(v, w, rows, size, store):
    for r in range(rows):
        x = v[:, r * size : (r + 1) * size].astype(F32)
        store(r, jnp.sum(x * w[:, r : r + 1], axis=0, keepdims=True))


def second_inner(cols, v, ops, w, acc, inc):
    forward_inner(cols, v, ops, acc)

    def store(r, s):
        inc[r : r + 1, :] = s

    member_sum(v, w, ops.shape[0], ops.shape[2], store)


def second_rim(cols, acc, v, mate, off, ops, w, inc_one, out, inc, inc_send, wide):
    rows = ops.shape[0]
    forward_rim(cols, acc, v, mate, off, ops, out, wide)
    inc[:rows, :] = inc_one[...]

    def store(r, s):
        inc[rows + r : rows + r + 1, :] = s

    member_sum(out, w, rows, ops.shape[2], store)
    inc_send[...] = inc[...].astype(BF16)


def cot_row(res, r):
    return jnp.broadcast_to(res[pl.ds(r, 1), :], (8, res.shape[1])).astype(BF16)


def residual_rim(inc, innov, prec, ops, cols, w, *rest):
    received = rest[:-4]
    res, to_mate, to_off, rim = rest[-4:]
    rows, _, size, _ = ops.shape
    total = inc[...]
    for other in received:
        total = total + other[...].astype(F32)
    res[...] = prec[...] * (total * SCALE - innov[...])
    res_two = res.at[pl.ds(rows, rows), :]
    start = 0
    for k, low, count in rim_pairs(rows):

        def some(ids, k=k, low=low, start=start):
            outs = [(i, dot_n(cot_row(res_two, low + i), ops[low + i, k])) for i in ids]
            for i, o in outs:
                rim[pl.ds(start + i, 1), :] = o[:1]

        chunks(count, 16, some)
        start += count
    members = w.shape[0]
    first, last = rim[:REACH, :], rim[REACH:, :]
    mate, off = pick(first, last)
    to_mate[:REACH, :] = mate
    to_off[:REACH, :] = off
    mate, off = pick(w[:, :REACH], w[:, rows - REACH :])
    to_mate[REACH : REACH + members, :REACH] = mate
    to_off[REACH : REACH + members, :REACH] = off
    col = cols[...].astype(F32)
    mate, off = pick(col[:1, :REACH], col[1:, rows - REACH :])
    to_mate[REACH : REACH + 1, REACH : 2 * REACH] = mate
    to_off[REACH : REACH + 1, REACH : 2 * REACH] = off


def residual_inner(res, ops, w, one, two, y, gw, squares):
    rows, _, size, _ = ops.shape
    members = w.shape[0]
    res_two = res.at[pl.ds(rows, rows), :]
    start = 0
    for k, low, count in inner_pairs(rows):

        def some(ids, k=k, low=low, start=start):
            outs = []
            for i in ids:
                r = low + i
                o = dot_n(cot_row(res_two, r), jnp.concatenate([ops[r, 0], ops[r, k]], 1))
                outs.append((r, i, o))
            for r, i, o in outs:
                y[pl.ds(r, 1), :] = o[:1, :size] + res[pl.ds(r, 1), :]
                y[pl.ds(rows + start + i, 1), :] = o[:1, size:]

        chunks(count, 16, some)
        start += count
    lanes = lax.broadcasted_iota(jnp.int32, (members, rows), 1)
    grown = jnp.zeros((members, rows), F32)
    for r in range(rows):
        part = slice(r * size, (r + 1) * size)
        prod = one[:, part].astype(F32) * res[r : r + 1, :] + two[:, part].astype(F32) * res[rows + r : rows + r + 1, :]
        grown = jnp.where(lanes == r, jnp.sum(prod, axis=1, keepdims=True), grown)
    grown = w[...] + SCALE * grown
    gw[...] = grown
    squares[...] = jnp.broadcast_to(jnp.sum(grown * grown, axis=1, keepdims=True), squares.shape)


def adjoint_rim(col_s, col_v, w, y, rim, mate, off, ops, mid, own, to_mate, to_off, vals, wp, tgt, wide):
    rows, _, size, _ = ops.shape
    members = w.shape[0]
    base = base_row(rows)
    even = is_even()
    inner = rows - REACH
    vals[:rows, :] = y[:rows, :].astype(BF16)
    vals[rows : rows + REACH, :] = rim[:REACH, :].astype(BF16)
    vals[rows + REACH : 2 * rows, :] = y[rows + inner : rows + 2 * inner, :].astype(BF16)
    vals[2 * rows : 2 * rows + inner, :] = y[rows : rows + inner, :].astype(BF16)
    vals[2 * rows + inner : 3 * rows, :] = rim[REACH:, :].astype(BF16)
    left = jnp.where(even, off[...], mate[...])
    right = jnp.where(even, mate[...], off[...])
    vals[3 * rows : 3 * rows + REACH, :] = left[:REACH, :].astype(BF16)
    vals[3 * rows + REACH :, :] = right[:REACH, :].astype(BF16)
    for k in range(3):
        wp[:, k * rows : (k + 1) * rows] = w[...] * SCALE
    wp[:, 3 * rows : 3 * rows + REACH] = left[REACH : REACH + members, :REACH] * SCALE
    wp[:, 3 * rows + REACH :] = right[REACH : REACH + members, :REACH] * SCALE
    shift = base.astype(F32)
    tgt[:, :rows] = lax.broadcasted_iota(jnp.int32, (8, rows), 1).astype(F32)
    for k in (1, 2):
        tgt[:, k * rows : (k + 1) * rows] = jnp.broadcast_to(col_v[k - 1 : k, :].astype(F32) - shift, (8, rows))
    for start, side in ((3 * rows, left), (3 * rows + REACH, right)):
        tgt[:, start : start + REACH] = jnp.broadcast_to(
            side[REACH : REACH + 1, REACH : 2 * REACH] - shift, (8, REACH)
        )
    weights = wp[...]
    target = tgt[:1, :]
    group = 8
    for g in range(rows // group):
        picked = [jnp.where(target == F32(g * group + c), weights, 0.0).astype(BF16) for c in range(group)]
        part = dot_n(jnp.concatenate(picked, 0), vals[...]).astype(BF16)
        mid[g * group * members : (g + 1) * group * members, :] = part
    wide[...] = jnp.zeros_like(wide)
    for k, low, count in rim_pairs(rows):

        def some(ids, k=k, low=low):
            outs = []
            for i in ids:
                r = low + i
                x = mid[pl.ds(pl.multiple_of(r * members, members), members), :]
                outs.append((col_s[k - 1, r] - base + REACH, dot_n(x, ops[r, k])))
            for c, o in outs:
                wide[c] = wide[c] + o

        chunks(count, 16, some)
    own[...] = wide[REACH : REACH + rows]

    @pl.when(even)
    def _():
        to_mate[...] = wide[REACH + rows :].astype(BF16)
        to_off[...] = wide[:REACH].astype(BF16)

    @pl.when(jnp.logical_not(even))
    def _():
        to_mate[...] = wide[:REACH].astype(BF16)
        to_off[...] = wide[REACH + rows :].astype(BF16)


def adjoint_inner(cols, mid, own, ops, out):
    rows, _, size, _ = ops.shape
    members = own.shape[1]
    base = base_row(rows)
    out[...] = own[...]
    for k, low, count in inner_pairs(rows):

        def some(ids, k=k, low=low):
            outs = []
            for i in ids:
                r = low + i
                x = mid[pl.ds(pl.multiple_of(r * members, members), members), :]
                o = dot_n(x, jnp.concatenate([ops[r, 0], ops[r, k]], 1))
                outs.append((r, o[:, :size]))
                outs.append((cols[k - 1, r] - base, o[:, size:]))
            for c, o in outs:
                out[c] = out[c] + o

        chunks(count, 16, some)


def finish(own, mate, off, out):
    rows, members, size = own.shape
    even = is_even()
    left = jnp.where(even, off[...], mate[...])
    right = jnp.where(even, mate[...], off[...])
    for c in range(rows):
        value = own[c]
        if c < REACH:
            value = value + left[c].astype(F32)
        if c >= rows - REACH:
            value = value + right[c - rows + REACH].astype(F32)
        out[:, c * size : (c + 1) * size] = value


SMEM = pl.BlockSpec(memory_space=pltpu.SMEM)
VMEM = pl.BlockSpec(memory_space=pltpu.VMEM)


def run(body, outs, args, scalars=0, scratch=()):
    return pl.pallas_call(
        body,
        out_shape=[jax.ShapeDtypeStruct(shape, kind) for shape, kind in outs],
        in_specs=[SMEM] * scalars + [VMEM] * (len(args) - scalars),
        out_specs=[VMEM] * len(outs),
        scratch_shapes=list(scratch),
        compiler_params=pltpu.CompilerParams(vmem_limit_bytes=40 * 1024 * 1024),
        name=body.__name__,
    )(*args)


def on_device(ensemble, op_blocks, col_index, weights, innovations, obs_precision):
    members = ensemble.shape[0]
    rows, _, size, _ = op_blocks.shape
    halo = REACH * size
    length = rows * size
    tiles = lax.axis_size("space")
    groups = lax.axis_size("members")
    mates = [(i, i ^ 1) for i in range(tiles)]
    offs = []
    for i in range(1, tiles - 1, 2):
        offs += [(i, i + 1), (i + 1, i)]

    def swap(to_mate, to_off):
        from_off = lax.ppermute(to_off, "space", offs)
        from_mate = lax.ppermute(to_mate, "space", mates)
        return from_mate, from_off

    even = is_even()
    cols = col_index.T
    wide = pltpu.VMEM((members, length + 2 * halo), BF16)
    acc_kind = ((rows, members, size), F32)
    flat_kind = ((members, length), BF16)
    rim_kind = ((members, halo), BF16)

    to_mate = lax.dynamic_slice_in_dim(ensemble, jnp.where(even, length - halo, 0), halo, 1)
    to_off = lax.dynamic_slice_in_dim(ensemble, jnp.where(even, 0, length - halo), halo, 1)
    mate, off = swap(to_mate, to_off)
    (acc,) = run(forward_inner, [acc_kind], (cols, ensemble, op_blocks), 1)
    one, to_mate, to_off = run(
        first_rim, [flat_kind, rim_kind, rim_kind], (cols, acc, ensemble, mate, off, op_blocks), 1, [wide]
    )
    mate, off = swap(to_mate, to_off)
    acc, inc_one = run(second_inner, [acc_kind, ((rows, size), F32)], (cols, one, op_blocks, weights), 1)
    two, inc, inc_send = run(
        second_rim,
        [flat_kind, ((2 * rows, size), F32), ((2 * rows, size), BF16)],
        (cols, acc, one, mate, off, op_blocks, weights, inc_one),
        1,
        [wide],
    )
    received = [
        lax.ppermute(inc_send, "members", [(i, (i + step) % groups) for i in range(groups)])
        for step in range(1, groups)
    ]
    pay_kind = ((REACH + members, size), F32)
    res, to_mate, to_off, rim = run(
        residual_rim,
        [((2 * rows, size), F32), pay_kind, pay_kind, ((2 * REACH, size), F32)],
        (
            inc,
            innovations.reshape(2 * rows, size),
            obs_precision.reshape(2 * rows, size),
            op_blocks,
            cols,
            weights,
            *received,
        ),
    )
    mate, off = swap(to_mate, to_off)
    y, grad_weights, squares = run(
        residual_inner,
        [((3 * rows - 2 * REACH, size), F32), ((members, rows), F32), ((members, size), F32)],
        (res, op_blocks, weights, one, two),
    )
    pairs = 3 * rows + 2 * REACH
    swap_kind = ((REACH, members, size), BF16)
    mid, own, to_mate, to_off = run(
        adjoint_rim,
        [((rows * members, size), BF16), acc_kind, swap_kind, swap_kind],
        (cols, cols, weights, y, rim, mate, off, op_blocks),
        1,
        [
            pltpu.VMEM((pairs, size), BF16),
            pltpu.VMEM((members, pairs), F32),
            pltpu.VMEM((8, pairs), F32),
            pltpu.VMEM((rows + 2 * REACH, members, size), F32),
        ],
    )
    mate, off = swap(to_mate, to_off)
    (own,) = run(adjoint_inner, [acc_kind], (cols, mid, own, op_blocks), 1)
    squares = lax.psum(squares[:, 0], "space")
    mean_square = squares / (rows * tiles)
    direction = grad_weights / jnp.sqrt(mean_square + 1e-06)[:, None]
    (grad_ens,) = run(finish, [((members, length), F32)], (own, mate, off))
    return (grad_ens, direction)


def solution(mesh):
    placed = (
        P("members", "space"),
        P("space", None, None, None),
        P("space", None),
        P("members", "space"),
        P(None, "space"),
        P(None, "space"),
    )
    return jax.shard_map(
        on_device,
        mesh=mesh,
        in_specs=placed,
        out_specs=(P("members", "space"), P("members", "space")),
        check_vma=False,
    )
```

time: 227 us -> 79.4 us (0.35)
  the two profiles are of different devices: /device:TPU:1 before, /device:TPU:3 now
where the time goes in v1:
time: 79.4 us; the launch traced here: 78.9 us
  starting transfers between devices  20.6 us (26%)
  Pallas kernels  17.8 us (22%)
  local copies, waits for them, and re-layouts  14.2 us (18%)
  waiting for transfers between devices  13.6 us (17%)
  blocking collectives  11.3 us (14%)
  between operations  0.88 us (1%)
    pallas_call x9, Pallas kernels, run(): pl.pallas_call(body, out_shape=[jax.ShapeDtypeStruct(shape, kind) for sha...  17.8 us
    ppermute x4, starting transfers between devices, swap(): from_off = lax.ppermute(to_off, 'space', offs)  16.5 us
    unnamed x24, local copies, waits for them, and re-layouts  12.9 us
    psum x1, blocking collectives, on_device(): squares = lax.psum(squares[:, 0], 'space')  11.3 us
    ppermute x4, waiting for transfers between devices, swap(): from_off = lax.ppermute(to_off, 'space', offs)  9.57 us
    ppermute x3, waiting for transfers between devices, on_device(): lax.ppermute(inc_send, 'members', [(i, (i + step) % groups) for i in rang...  3.97 us
    ppermute x3, starting transfers between devices, on_device(): lax.ppermute(inc_send, 'members', [(i, (i + step) % groups) for i in rang...  3.83 us
  transfers between devices with their start and end apart: 11, of which 6 were waited for; matrix products, arithmetic and copies ran while one was open for 1% of the time, Pallas kernels for 11%

profile of v1, /device:TPU:3, one launch (start us, length us, event | category | flops | bytes accessed | tf_op | source)
XLA Modules:
  0.0 78.9 jit_solution(63649371120781073)
XLA Ops:
  0.6 1.1 %constant_dynamic-slice_fusion = (bf16[32,4096]{1,0:T(8,128)(2,1)S(1)}, bf16[32,4096]{1,0:T(8,128)(2,1)S(1)}) fusion(bf16[32,8192]{1,0:T(8,128)(2,1)} %v.3, s32[]{:T(128)S(6)} %select_n.18, s32[]{:T(128)S(6)} %select_n.17), kind=kLoop, calls=%fused_computation.3 | loop fusion | bytes 1048584 | tf_op jit(solution)/shard_map/dynamic_slice | solution.py:359
  1.7 3.7 %collective-permute-start.1 = (bf16[32,4096]{1,0:T(8,128)(2,1)S(1)}, bf16[32,4096]{1,0:T(8,128)(2,1)S(1)}, u32[]{:S(2)}, u32[]{:S(2)}) collective-permute-start(bf16[32,4096]{1,0:T(8,128)(2,1)S(1)} %get-tuple-element.40), channel_id=1, source_target_pairs={{4,8},{8,4},{12,16},{16,12},{20,24},{24,20},{5,9},{9,5},{13,17},{1... | collective-permute-start | bytes 786440 | tf_op jit(solution)/shard_map/ppermute | solution.py:347
  5.4 0.1 collective-permute-start
  5.5 0.0 copy-start
  5.5 2.8 %copy-done = bf16[64,3,128,128]{3,2,1,0:T(8,128)(2,1)S(1)} copy-done((bf16[64,3,128,128]{3,2,1,0:T(8,128)(2,1)S(1)}, bf16[64,3,128,128]{3,2,1,0:T(8,128)(2,1)}, u32[]{:S(2)}) %copy-start) | copy-done | bytes 6291480
  8.3 1.0 %copy-done.4 = bf16[32,8192]{1,0:T(8,128)(2,1)S(1)} copy-done((bf16[32,8192]{1,0:T(8,128)(2,1)S(1)}, bf16[32,8192]{1,0:T(8,128)(2,1)}, u32[]{:S(2)}) %copy-start.4) | copy-done | bytes 524312
  9.3 0.7 copy-done.6
  10.0 2.4 %forward_inner.1.acc = f32[64,32,128]{2,1,0:T(8,128)S(1)} custom-call(s32[2,64]{1,0:T(2,128)S(1)} %bitcast.3, bf16[32,8192]{1,0:T(8,128)(2,1)S(1)} %copy-done.4, bf16[64,3,128,128]{3,2,1,0:T(8,128)(2,1)S(1)} %copy-done), custom_call_target="tpu_custom_call" | custom-call | tf_op jit(solution)/shard_map/forward_inner/pallas_call | solution.py:323
  12.4 0.7 collective-permute-done.1.off
  13.1 0.0 collective-permute-done.mate
  13.1 2.2 %first_rim.1 = (bf16[32,8192]{1,0:T(8,128)(2,1)S(1)}, bf16[32,4096]{1,0:T(8,128)(2,1)S(1)}, bf16[32,4096]{1,0:T(8,128)(2,1)S(1)}) custom-call(s32[2,64]{1,0:T(2,128)S(1)} %bitcast.4, f32[64,32,128]{2,1,0:T(8,128)S(1)} %forward_inner.1.acc, bf16[32,8192]{1,0:T(8,128)(2,1)S(1)} %copy-done.4, bf16[32,4096]{1,0:T(8,128)(2,1)S(1)} %collective-permute-done.mate, ...), custom_call_target="tpu_custom_call" | custom-call | tf_op jit(solution)/shard_map/first_rim/pallas_call | solution.py:323
  15.3 0.1 collective-permute-start.2
  15.4 2.9 %collective-permute-start.3 = (bf16[32,4096]{1,0:T(8,128)(2,1)S(1)}, bf16[32,4096]{1,0:T(8,128)(2,1)S(1)}, u32[]{:S(2)}, u32[]{:S(2)}) collective-permute-start(bf16[32,4096]{1,0:T(8,128)(2,1)S(1)} %get-tuple-element.24), channel_id=1, source_target_pairs={{4,8},{8,4},{12,16},{16,12},{20,24},{24,20},{5,9},{9,5},{13,17},{1... | collective-permute-start | bytes 786440 | tf_op jit(solution)/shard_map/ppermute | solution.py:347
  18.3 0.0 copy-start.8
  18.3 0.0 copy-start.9
  18.3 0.0 copy-start.7
  18.3 2.8 %second_inner.1 = (f32[64,32,128]{2,1,0:T(8,128)S(1)}, f32[64,128]{1,0:T(8,128)S(1)}) custom-call(s32[2,64]{1,0:T(2,128)S(1)} %bitcast.5, bf16[32,8192]{1,0:T(8,128)(2,1)S(1)} %get-tuple-element.21.v.one, bf16[64,3,128,128]{3,2,1,0:T(8,128)(2,1)S(1)} %bitcast.2, f32[32,64]{1,0:T(8,128)S(1)} %copy-done.5), custom_call_target="tpu_custom_call" | custom-call | tf_op jit(solution)/shard_map/second_inner/pallas_call | solution.py:323
  21.1 0.0 collective-permute-done.2.mate
  21.1 4.8 %collective-permute-done.3.off = bf16[32,4096]{1,0:T(8,128)(2,1)S(1)} collective-permute-done((bf16[32,4096]{1,0:T(8,128)(2,1)S(1)}, bf16[32,4096]{1,0:T(8,128)(2,1)S(1)}, u32[]{:S(2)}, u32[]{:S(2)}) %collective-permute-start.3) | collective-permute-done | bytes 262176 | tf_op jit(solution)/shard_map/ppermute | solution.py:347
  25.9 2.6 %second_rim.1 = (bf16[32,8192]{1,0:T(8,128)(2,1)S(1)}, f32[128,128]{1,0:T(8,128)S(1)}, bf16[128,128]{1,0:T(8,128)(2,1)S(1)}) custom-call(s32[2,64]{1,0:T(2,128)S(1)} %bitcast.6, f32[64,32,128]{2,1,0:T(8,128)S(1)} %get-tuple-element.22.acc, bf16[32,8192]{1,0:T(8,128)(2,1)S(1)} %get-tuple-element.21.v.one, bf16[32,4096]{1,0:T(8,128)(2,1)S(1)} %collective-permute-done.2.mate, ...), custom_call_target="tpu_custom_call" | custom-call | tf_op jit(solution)/shard_map/second_rim/pallas_call | solution.py:323
  28.5 3.4 %collective-permute-start.6 = (bf16[128,128]{1,0:T(8,128)(2,1)S(1)}, bf16[128,128]{1,0:T(8,128)(2,1)S(1)}, u32[]{:S(2)}, u32[]{:S(2)}) collective-permute-start(bf16[128,128]{1,0:T(8,128)(2,1)S(1)} %get-tuple-element.27), channel_id=1, source_target_pairs={{0,3},{1,0},{2,1},{3,2},{4,7},{5,4},{6,5},{7,6},{8,11},{9,8},{10,9... | collective-permute-start | bytes 98312 | tf_op jit(solution)/shard_map/ppermute | solution.py:375
  31.9 0.0 collective-permute-start.5
  31.9 0.5 collective-permute-start.4
  32.4 0.1 reshape.11.innov
  32.4 0.1 reshape.12.prec
  32.5 0.4 collective-permute-done.6.rest_2_
  32.9 2.9 %collective-permute-done.5.rest_1_ = bf16[128,128]{1,0:T(8,128)(2,1)S(1)} collective-permute-done((bf16[128,128]{1,0:T(8,128)(2,1)S(1)}, bf16[128,128]{1,0:T(8,128)(2,1)S(1)}, u32[]{:S(2)}, u32[]{:S(2)}) %collective-permute-start.5) | collective-permute-done | bytes 32800 | tf_op jit(solution)/shard_map/ppermute | solution.py:375
  35.8 0.6 collective-permute-done.4.rest_0_
  36.5 2.8 %copy-done.1 = bf16[64,3,128,128]{3,2,1,0:T(8,128)(2,1)S(1)} copy-done((bf16[64,3,128,128]{3,2,1,0:T(8,128)(2,1)S(1)}, bf16[64,3,128,128]{3,2,1,0:T(8,128)(2,1)}, u32[]{:S(2)}) %copy-start.1) | copy-done | bytes 6291480
  39.3 1.1 %residual_rim.1 = (f32[128,128]{1,0:T(8,128)S(1)}, f32[64,128]{1,0:T(8,128)S(1)}, f32[64,128]{1,0:T(8,128)S(1)}, f32[64,128]{1,0:T(8,128)S(1)}) custom-call(f32[128,128]{1,0:T(8,128)S(1)} %get-tuple-element.26.inc, f32[128,128]{1,0:T(8,128)S(1)} %reshape.11.innov, f32[128,128]{1,0:T(8,128)S(1)} %reshape.12.prec, bf16[64,3,128,128]{3,2,1,0:T(8,128)(2,1)S(1)} %copy-done.1, ...), custom_call_target="tpu_custom_call" | custom-call | tf_op jit(solution)/shard_map/residual_rim/pallas_call | solution.py:323
  40.4 0.0 collective-permute-start.7
  40.4 4.9 %collective-permute-start.8 = (f32[64,128]{1,0:T(8,128)S(1)}, f32[64,128]{1,0:T(8,128)S(1)}, u32[]{:S(2)}, u32[]{:S(2)}) collective-permute-start(f32[64,128]{1,0:T(8,128)S(1)} %get-tuple-element.33), channel_id=1, source_target_pairs={{4,8},{8,4},{12,16},{16,12},{20,24},{24,20},{5,9},{9,5},{13,17},{1... | collective-permute-start | bytes 98312 | tf_op jit(solution)/shard_map/ppermute | solution.py:347
  45.3 0.0 copy-start.2
  45.3 2.8 %copy-done.2 = bf16[64,3,128,128]{3,2,1,0:T(8,128)(2,1)S(1)} copy-done((bf16[64,3,128,128]{3,2,1,0:T(8,128)(2,1)S(1)}, bf16[64,3,128,128]{3,2,1,0:T(8,128)(2,1)}, u32[]{:S(2)}) %copy-start.2) | copy-done | bytes 6291480
  48.1 1.4 %residual_inner.1 = (f32[128,128]{1,0:T(8,128)S(1)}, f32[32,64]{1,0:T(8,128)S(1)}, f32[32,128]{1,0:T(8,128)S(1)}) custom-call(f32[128,128]{1,0:T(8,128)S(1)} %get-tuple-element.28.res, bf16[64,3,128,128]{3,2,1,0:T(8,128)(2,1)S(1)} %copy-done.2, f32[32,64]{1,0:T(8,128)S(1)} %copy-done.5, bf16[32,8192]{1,0:T(8,128)(2,1)S(1)} %get-tuple-element.21.v.one, ...), custom_call_target="tpu_custom_call" | custom-call | tf_op jit(solution)/shard_map/residual_inner/pallas_call | solution.py:323
  49.5 0.1 slice_reduce_fusion
  49.6 11.3 %psum.7 = f32[32]{0:T(128)S(1)} all-reduce(f32[32]{0:T(128)S(1)} %slice_reduce_fusion), channel_id=1, replica_groups=mesh['space'=8,'members'=4] {'space'}, use_global_device_ids=true, to_apply=%region_0.1 | all-reduce | flops 32 | bytes 256 | tf_op jit(solution)/shard_map/psum | solution.py:414
  60.9 0.0 collective-permute-done.7.mate
  60.9 0.0 collective-permute-done.8.off
  60.9 2.8 %copy-done.3 = bf16[64,3,128,128]{3,2,1,0:T(8,128)(2,1)S(1)} copy-done((bf16[64,3,128,128]{3,2,1,0:T(8,128)(2,1)S(1)}, bf16[64,3,128,128]{3,2,1,0:T(8,128)(2,1)}, u32[]{:S(2)}) %copy-start.3) | copy-done | bytes 6291480
  63.7 2.3 %adjoint_rim.1 = (bf16[2048,128]{1,0:T(8,128)(2,1)S(1)}, f32[64,32,128]{2,1,0:T(8,128)S(1)}, bf16[32,32,128]{2,1,0:T(8,128)(2,1)S(1)}, bf16[32,32,128]{2,1,0:T(8,128)(2,1)S(1)}) custom-call(s32[2,64]{1,0:T(2,128)S(1)} %bitcast.8, s32[2,64]{1,0:T(2,128)S(1)} %bitcast.9, f32[32,64]{1,0:T(8,128)S(1)} %copy-done.5, f32[128,128]{1,0:T(8,128)S(1)} %get-tuple-element.30.y, ...), custom_call_target="tpu_custom_call" | custom-call | tf_op jit(solution)/shard_map/adjoint_rim/pallas_call | solution.py:323
  66.0 0.1 collective-permute-start.9
  66.1 5.1 %collective-permute-start.10 = (bf16[32,32,128]{2,1,0:T(8,128)(2,1)S(1)}, bf16[32,32,128]{2,1,0:T(8,128)(2,1)S(1)}, u32[]{:S(2)}, u32[]{:S(2)}) collective-permute-start(bf16[32,32,128]{2,1,0:T(8,128)(2,1)S(1)} %get-tuple-element.37), channel_id=1, source_target_pairs={{4,8},{8,4},{12,16},{16,12},{20,24},{24,20},{5,9},{9,5},{13,17},{1... | collective-permute-start | bytes 786440 | tf_op jit(solution)/shard_map/ppermute | solution.py:347
  71.2 0.7 broadcast_divide_fusion
  71.9 1.9 %adjoint_inner.1.own = f32[64,32,128]{2,1,0:T(8,128)S(1)} custom-call(s32[2,64]{1,0:T(2,128)S(1)} %bitcast.10, bf16[2048,128]{1,0:T(8,128)(2,1)S(1)} %get-tuple-element.34.mid, f32[64,32,128]{2,1,0:T(8,128)S(1)} %get-tuple-element.35.own, bf16[64,3,128,128]{3,2,1,0:T(8,128)(2,1)S(1)} %copy-done.3), custom_call_target="tpu_custom_call" | custom-call | tf_op jit(solution)/shard_map/adjoint_inner/pallas_call | solution.py:323
  73.7 0.0 collective-permute-done.9.mate
  73.7 4.1 %collective-permute-done.10.off = bf16[32,32,128]{2,1,0:T(8,128)(2,1)S(1)} collective-permute-done((bf16[32,32,128]{2,1,0:T(8,128)(2,1)S(1)}, bf16[32,32,128]{2,1,0:T(8,128)(2,1)S(1)}, u32[]{:S(2)}, u32[]{:S(2)}) %collective-permute-start.10) | collective-permute-done | bytes 262176 | tf_op jit(solution)/shard_map/ppermute | solution.py:347
  77.8 1.1 %finish.1 = f32[32,8192]{1,0:T(8,128)} custom-call(f32[64,32,128]{2,1,0:T(8,128)S(1)} %adjoint_inner.1.own, bf16[32,32,128]{2,1,0:T(8,128)(2,1)S(1)} %collective-permute-done.9.mate, bf16[32,32,128]{2,1,0:T(8,128)(2,1)S(1)} %collective-permute-done.10.off), custom_call_target="tpu_custom_call" | custom-call | tf_op jit(solution)/shard_map/finish/pallas_call | solution.py:323
  (15 shorter events, 0.0 us)
Async XLA Ops:
  1.7 11.4 %collective-permute-start.1 = (bf16[32,4096]{1,0:T(8,128)(2,1)S(1)}, bf16[32,4096]{1,0:T(8,128)(2,1)S(1)}, u32[]{:S(2)}, u32[]{:S(2)}) collective-permute-start(bf16[32,4096]{1,0:T(8,128)(2,1)S(1)} %get-tuple-element.40), channel_id=1, source_target_pairs={{4,8},{8,4},{12,16},{16,12},{20,24},{24,20},{5,9},{9,5},{13,17},{1... | collective-permute-start | bytes 786440 | tf_op jit(solution)/shard_map/ppermute | solution.py:347
  5.4 7.7 %collective-permute-start = (bf16[32,4096]{1,0:T(8,128)(2,1)S(1)}, bf16[32,4096]{1,0:T(8,128)(2,1)S(1)}, u32[]{:S(2)}, u32[]{:S(2)}) collective-permute-start(bf16[32,4096]{1,0:T(8,128)(2,1)S(1)} %get-tuple-element.41), channel_id=1, source_target_pairs={{0,4},{4,0},{8,12},{12,8},{16,20},{20,16},{24,28},{28,24},{1,5},{5... | collective-permute-start | bytes 786440 | tf_op jit(solution)/shard_map/ppermute | solution.py:348
  5.5 2.8 %copy-start = (bf16[64,3,128,128]{3,2,1,0:T(8,128)(2,1)S(1)}, bf16[64,3,128,128]{3,2,1,0:T(8,128)(2,1)}, u32[]{:S(2)}) copy-start(bf16[64,3,128,128]{3,2,1,0:T(8,128)(2,1)} %ops.15) | copy-start | bytes 18874372
  8.3 1.0 %copy-start.4 = (bf16[32,8192]{1,0:T(8,128)(2,1)S(1)}, bf16[32,8192]{1,0:T(8,128)(2,1)}, u32[]{:S(2)}) copy-start(bf16[32,8192]{1,0:T(8,128)(2,1)} %v.3) | copy-start | bytes 1572868
  9.3 0.7 copy-start.6
  10.0 8.3 %slice-start = ((s8[6291456]{0:T(1024)(128)(4,1)}), s8[4194304]{0:T(1024)(128)(4,1)S(1)}, s32[]{:S(2)}) async-start(s8[6291456]{0:T(1024)(128)(4,1)} %bitcast.1), calls=%async_computation | async-start | bytes 8388608
  10.0 8.3 %copy-start.5 = (f32[32,64]{1,0:T(8,128)S(1)}, f32[32,64]{1,0:T(8,128)}, u32[]{:S(2)}) copy-start(f32[32,64]{1,0:T(8,128)} %w.9) | copy-start | bytes 24580
  12.4 5.9 %slice-start.1 = ((s8[6291456]{0:T(1024)(128)(4,1)}), s8[2097152]{0:T(1024)(128)(4,1)S(1)}, s32[]{:S(2)}) async-start(s8[6291456]{0:T(1024)(128)(4,1)} %bitcast.1), calls=%async_computation.1 | async-start | bytes 4194304
  15.3 5.8 %collective-permute-start.2 = (bf16[32,4096]{1,0:T(8,128)(2,1)S(1)}, bf16[32,4096]{1,0:T(8,128)(2,1)S(1)}, u32[]{:S(2)}, u32[]{:S(2)}) collective-permute-start(bf16[32,4096]{1,0:T(8,128)(2,1)S(1)} %get-tuple-element.23), channel_id=1, source_target_pairs={{0,4},{4,0},{8,12},{12,8},{16,20},{20,16},{24,28},{28,24},{1,5},{5... | collective-permute-start | bytes 786440 | tf_op jit(solution)/shard_map/ppermute | solution.py:348
  15.4 10.5 %collective-permute-start.3 = (bf16[32,4096]{1,0:T(8,128)(2,1)S(1)}, bf16[32,4096]{1,0:T(8,128)(2,1)S(1)}, u32[]{:S(2)}, u32[]{:S(2)}) collective-permute-start(bf16[32,4096]{1,0:T(8,128)(2,1)S(1)} %get-tuple-element.24), channel_id=1, source_target_pairs={{4,8},{8,4},{12,16},{16,12},{20,24},{24,20},{5,9},{9,5},{13,17},{1... | collective-permute-start | bytes 786440 | tf_op jit(solution)/shard_map/ppermute | solution.py:347
  18.3 14.1 %copy-start.8 = (f32[2,8192]{1,0:T(2,128)S(1)}, f32[2,8192]{1,0:T(2,128)}, u32[]{:S(2)}) copy-start(f32[2,8192]{1,0:T(2,128)} %param.10) | copy-start | bytes 196612
  18.3 14.1 %copy-start.9 = (f32[2,8192]{1,0:T(2,128)S(1)}, f32[2,8192]{1,0:T(2,128)}, u32[]{:S(2)}) copy-start(f32[2,8192]{1,0:T(2,128)} %param.11) | copy-start | bytes 196612
  18.3 18.2 %copy-start.7 = (s32[64,2]{0,1:T(2,128)S(1)}, s32[64,2]{0,1:T(2,128)}, u32[]{:S(2)}) copy-start(s32[64,2]{0,1:T(2,128)} %param.8) | copy-start | bytes 1540
  28.5 4.4 %collective-permute-start.6 = (bf16[128,128]{1,0:T(8,128)(2,1)S(1)}, bf16[128,128]{1,0:T(8,128)(2,1)S(1)}, u32[]{:S(2)}, u32[]{:S(2)}) collective-permute-start(bf16[128,128]{1,0:T(8,128)(2,1)S(1)} %get-tuple-element.27), channel_id=1, source_target_pairs={{0,3},{1,0},{2,1},{3,2},{4,7},{5,4},{6,5},{7,6},{8,11},{9,8},{10,9... | collective-permute-start | bytes 98312 | tf_op jit(solution)/shard_map/ppermute | solution.py:375
  31.9 3.9 %collective-permute-start.5 = (bf16[128,128]{1,0:T(8,128)(2,1)S(1)}, bf16[128,128]{1,0:T(8,128)(2,1)S(1)}, u32[]{:S(2)}, u32[]{:S(2)}) collective-permute-start(bf16[128,128]{1,0:T(8,128)(2,1)S(1)} %get-tuple-element.27), channel_id=1, source_target_pairs={{0,2},{1,3},{2,0},{3,1},{4,6},{5,7},{6,4},{7,5},{8,10},{9,11},{10,... | collective-permute-start | bytes 98312 | tf_op jit(solution)/shard_map/ppermute | solution.py:375
  31.9 4.6 %collective-permute-start.4 = (bf16[128,128]{1,0:T(8,128)(2,1)S(1)}, bf16[128,128]{1,0:T(8,128)(2,1)S(1)}, u32[]{:S(2)}, u32[]{:S(2)}) collective-permute-start(bf16[128,128]{1,0:T(8,128)(2,1)S(1)} %get-tuple-element.27), channel_id=1, source_target_pairs={{0,1},{1,2},{2,3},{3,0},{4,5},{5,6},{6,7},{7,4},{8,9},{9,10},{10,1... | collective-permute-start | bytes 98312 | tf_op jit(solution)/shard_map/ppermute | solution.py:375
  36.5 2.8 %copy-start.1 = (bf16[64,3,128,128]{3,2,1,0:T(8,128)(2,1)S(1)}, bf16[64,3,128,128]{3,2,1,0:T(8,128)(2,1)}, u32[]{:S(2)}) copy-start(bf16[64,3,128,128]{3,2,1,0:T(8,128)(2,1)} %ops.15) | copy-start | bytes 18874372
  40.4 20.5 %collective-permute-start.7 = (f32[64,128]{1,0:T(8,128)S(1)}, f32[64,128]{1,0:T(8,128)S(1)}, u32[]{:S(2)}, u32[]{:S(2)}) collective-permute-start(f32[64,128]{1,0:T(8,128)S(1)} %get-tuple-element.32), channel_id=1, source_target_pairs={{0,4},{4,0},{8,12},{12,8},{16,20},{20,16},{24,28},{28,24},{1,5},{5... | collective-permute-start | bytes 98312 | tf_op jit(solution)/shard_map/ppermute | solution.py:348
  40.4 20.5 %collective-permute-start.8 = (f32[64,128]{1,0:T(8,128)S(1)}, f32[64,128]{1,0:T(8,128)S(1)}, u32[]{:S(2)}, u32[]{:S(2)}) collective-permute-start(f32[64,128]{1,0:T(8,128)S(1)} %get-tuple-element.33), channel_id=1, source_target_pairs={{4,8},{8,4},{12,16},{16,12},{20,24},{24,20},{5,9},{9,5},{13,17},{1... | collective-permute-start | bytes 98312 | tf_op jit(solution)/shard_map/ppermute | solution.py:347
  45.3 2.8 %copy-start.2 = (bf16[64,3,128,128]{3,2,1,0:T(8,128)(2,1)S(1)}, bf16[64,3,128,128]{3,2,1,0:T(8,128)(2,1)}, u32[]{:S(2)}) copy-start(bf16[64,3,128,128]{3,2,1,0:T(8,128)(2,1)} %ops.15) | copy-start | bytes 18874372
  60.9 2.8 %copy-start.3 = (bf16[64,3,128,128]{3,2,1,0:T(8,128)(2,1)S(1)}, bf16[64,3,128,128]{3,2,1,0:T(8,128)(2,1)}, u32[]{:S(2)}) copy-start(bf16[64,3,128,128]{3,2,1,0:T(8,128)(2,1)} %ops.15) | copy-start | bytes 18874372
  66.0 7.7 %collective-permute-start.9 = (bf16[32,32,128]{2,1,0:T(8,128)(2,1)S(1)}, bf16[32,32,128]{2,1,0:T(8,128)(2,1)S(1)}, u32[]{:S(2)}, u32[]{:S(2)}) collective-permute-start(bf16[32,32,128]{2,1,0:T(8,128)(2,1)S(1)} %get-tuple-element.36), channel_id=1, source_target_pairs={{0,4},{4,0},{8,12},{12,8},{16,20},{20,16},{24,28},{28,24},{1,5},{5... | collective-permute-start | bytes 786440 | tf_op jit(solution)/shard_map/ppermute | solution.py:348
  66.1 11.7 %collective-permute-start.10 = (bf16[32,32,128]{2,1,0:T(8,128)(2,1)S(1)}, bf16[32,32,128]{2,1,0:T(8,128)(2,1)S(1)}, u32[]{:S(2)}, u32[]{:S(2)}) collective-permute-start(bf16[32,32,128]{2,1,0:T(8,128)(2,1)S(1)} %get-tuple-element.37), channel_id=1, source_target_pairs={{4,8},{8,4},{12,16},{16,12},{20,24},{24,20},{5,9},{9,5},{13,17},{1... | collective-permute-start | bytes 786440 | tf_op jit(solution)/shard_map/ppermute | solution.py:347

commit v2 on v1

--- a/solution.py
+++ b/solution.py
@@ -48,14 +48,45 @@
     return ((2, 0, rows - REACH), (1, REACH, rows - REACH))
 
 
+def split_pairs(pairs, ready):
+    if ready is None:
+        return pairs
+    halves = []
+    for k, low, count in pairs:
+        halves += [(k, low, count // 2), (k, low + count // 2, count // 2)]
+    return halves
+
+
 def rim_pairs(rows):
     return ((1, 0, REACH), (2, rows - REACH, REACH))
 
 
-def forward_inner(cols, v, ops, acc):
+def first_inner(cols, v_far, ops_far, acc, v, ops, v_sem, sems):
+    rows = ops.shape[0]
+    parts = sems.shape[0]
+    step = rows // parts
+    v_copy = pltpu.make_async_copy(v_far, v, v_sem)
+    v_copy.start()
+    copies = []
+    for part in range(parts):
+        where = pl.ds(part * step, step)
+        copies.append(pltpu.make_async_copy(ops_far.at[where], ops.at[where], sems.at[part]))
+        copies[-1].start()
+    v_copy.wait()
+
+    def ready(low, count):
+        for part in range(low // step, (low + count) // step):
+            copies[part].wait()
+
+    forward_inner(cols, v, ops, acc, ready)
+
+
+def forward_inner(cols, v, ops, acc, ready=None):
     rows, _, size, _ = ops.shape
     base = base_row(rows)
-    for k, low, count in inner_pairs(rows):
+    for k, low, count in split_pairs(inner_pairs(rows), ready):
+        if ready is not None:
+            ready(low, count)
 
         def some(ids, k=k, low=low):
             outs = []
@@ -132,8 +163,15 @@
         store(r, jnp.sum(x * w[:, r : r + 1], axis=0, keepdims=True))
 
 
-def second_inner(cols, v, ops, w, acc, inc):
+def second_inner(cols, v, ops, w, innov, prec, acc, inc, innov_rows, prec_rows):
     forward_inner(cols, v, ops, acc)
+    rows, _, size, _ = ops.shape
+    for time in range(2):
+        for r in range(rows):
+            place = slice(time * rows + r, time * rows + r + 1)
+            part = slice(r * size, (r + 1) * size)
+            innov_rows[place, :] = innov[time : time + 1, part]
+            prec_rows[place, :] = prec[time : time + 1, part]
 
     def store(r, s):
         inc[r : r + 1, :] = s
@@ -157,9 +195,22 @@
     return jnp.broadcast_to(res[pl.ds(r, 1), :], (8, res.shape[1])).astype(BF16)
 
 
-def residual_rim(inc, innov, prec, ops, cols, w, *rest):
-    received = rest[:-4]
-    res, to_mate, to_off, rim = rest[-4:]
+def weight_gradient(res, w, one, two):
+    members, rows = w.shape
+    size = res.shape[1]
+    lanes = lax.broadcasted_iota(jnp.int32, (members, rows), 1)
+    grown = jnp.zeros((members, rows), F32)
+    for r in range(rows):
+        part = slice(r * size, (r + 1) * size)
+        prod = one[:, part].astype(F32) * res[r : r + 1, :] + two[:, part].astype(F32) * res[rows + r : rows + r + 1, :]
+        grown = jnp.where(lanes == r, jnp.sum(prod, axis=1, keepdims=True), grown)
+    grown = w[...] + SCALE * grown
+    return grown, jnp.broadcast_to(jnp.sum(grown * grown, axis=1, keepdims=True), (members, size))
+
+
+def residual_rim(inc, innov, prec, ops, cols, w, one, two, *rest):
+    received = rest[:-5]
+    res, to_mate, to_off, rim, gw = rest[-5:]
     rows, _, size, _ = ops.shape
     total = inc[...]
     for other in received:
@@ -177,6 +228,8 @@
         chunks(count, 16, some)
         start += count
     members = w.shape[0]
+    gw[...], squares = weight_gradient(res, w, one, two)
+    to_mate[REACH + members :, :] = squares
     first, last = rim[:REACH, :], rim[REACH:, :]
     mate, off = pick(first, last)
     to_mate[:REACH, :] = mate
@@ -190,9 +243,8 @@
     to_off[REACH : REACH + 1, REACH : 2 * REACH] = off
 
 
-def residual_inner(res, ops, w, one, two, y, gw, squares):
-    rows, _, size, _ = ops.shape
-    members = w.shape[0]
+def residual_inner(res, ops, y):
+    rows, _, size, _ = ops.shape
     res_two = res.at[pl.ds(rows, rows), :]
     start = 0
     for k, low, count in inner_pairs(rows):
@@ -209,15 +261,6 @@
 
         chunks(count, 16, some)
         start += count
-    lanes = lax.broadcasted_iota(jnp.int32, (members, rows), 1)
-    grown = jnp.zeros((members, rows), F32)
-    for r in range(rows):
-        part = slice(r * size, (r + 1) * size)
-        prod = one[:, part].astype(F32) * res[r : r + 1, :] + two[:, part].astype(F32) * res[rows + r : rows + r + 1, :]
-        grown = jnp.where(lanes == r, jnp.sum(prod, axis=1, keepdims=True), grown)
-    grown = w[...] + SCALE * grown
-    gw[...] = grown
-    squares[...] = jnp.broadcast_to(jnp.sum(grown * grown, axis=1, keepdims=True), squares.shape)
 
 
 def adjoint_rim(col_s, col_v, w, y, rim, mate, off, ops, mid, own, to_mate, to_off, vals, wp, tgt, wide):
@@ -231,8 +274,9 @@
     vals[rows + REACH : 2 * rows, :] = y[rows + inner : rows + 2 * inner, :].astype(BF16)
     vals[2 * rows : 2 * rows + inner, :] = y[rows : rows + inner, :].astype(BF16)
     vals[2 * rows + inner : 3 * rows, :] = rim[REACH:, :].astype(BF16)
-    left = jnp.where(even, off[...], mate[...])
-    right = jnp.where(even, mate[...], off[...])
+    near, across = mate[: REACH + members, :], off[...]
+    left = jnp.where(even, across, near)
+    right = jnp.where(even, near, across)
     vals[3 * rows : 3 * rows + REACH, :] = left[:REACH, :].astype(BF16)
     vals[3 * rows + REACH :, :] = right[:REACH, :].astype(BF16)
     for k in range(3):
@@ -301,8 +345,9 @@
         chunks(count, 16, some)
 
 
-def finish(own, mate, off, out):
+def finish(count, own, mate, off, gw, total, out, direction):
     rows, members, size = own.shape
+    direction[...] = gw[...] / jnp.sqrt(total[:, :1] / count[0] + 1e-06)
     even = is_even()
     left = jnp.where(even, off[...], mate[...])
     right = jnp.where(even, mate[...], off[...])
@@ -317,16 +362,18 @@
 
 SMEM = pl.BlockSpec(memory_space=pltpu.SMEM)
 VMEM = pl.BlockSpec(memory_space=pltpu.VMEM)
-
-
-def run(body, outs, args, scalars=0, scratch=()):
+FAR = pl.BlockSpec(memory_space=pltpu.HBM)
+
+
+def run(body, outs, args, scalars=0, scratch=(), far=0, near=True):
+    kind_of = pltpu.VMEM if near else jax.ShapeDtypeStruct
     return pl.pallas_call(
         body,
-        out_shape=[jax.ShapeDtypeStruct(shape, kind) for shape, kind in outs],
-        in_specs=[SMEM] * scalars + [VMEM] * (len(args) - scalars),
+        out_shape=[kind_of(shape, kind) for shape, kind in outs],
+        in_specs=[SMEM] * scalars + [VMEM] * (len(args) - scalars - far) + [FAR] * far,
         out_specs=[VMEM] * len(outs),
         scratch_shapes=list(scratch),
-        compiler_params=pltpu.CompilerParams(vmem_limit_bytes=40 * 1024 * 1024),
+        compiler_params=pltpu.CompilerParams(vmem_limit_bytes=12 * 1024 * 1024),
         name=body.__name__,
     )(*args)
 
@@ -349,6 +396,7 @@
         return from_mate, from_off
 
     even = is_even()
+    far = lambda value: pltpu.with_memory_space_constraint(value, pltpu.HBM)
     cols = col_index.T
     wide = pltpu.VMEM((members, length + 2 * halo), BF16)
     acc_kind = ((rows, members, size), F32)
@@ -358,49 +406,69 @@
     to_mate = lax.dynamic_slice_in_dim(ensemble, jnp.where(even, length - halo, 0), halo, 1)
     to_off = lax.dynamic_slice_in_dim(ensemble, jnp.where(even, 0, length - halo), halo, 1)
     mate, off = swap(to_mate, to_off)
-    (acc,) = run(forward_inner, [acc_kind], (cols, ensemble, op_blocks), 1)
+    acc, ens, ops = run(
+        first_inner,
+        [acc_kind, flat_kind, (op_blocks.shape, BF16)],
+        (cols, far(ensemble), far(op_blocks)),
+        1,
+        [pltpu.SemaphoreType.DMA(()), pltpu.SemaphoreType.DMA((4,))],
+        far=2,
+    )
     one, to_mate, to_off = run(
-        first_rim, [flat_kind, rim_kind, rim_kind], (cols, acc, ensemble, mate, off, op_blocks), 1, [wide]
+        first_rim, [flat_kind, rim_kind, rim_kind], (cols, acc, ens, mate, off, ops), 1, [wide]
     )
     mate, off = swap(to_mate, to_off)
-    acc, inc_one = run(second_inner, [acc_kind, ((rows, size), F32)], (cols, one, op_blocks, weights), 1)
+    row_kind = ((2 * rows, size), F32)
+    acc, inc_one, innov, prec = run(
+        second_inner,
+        [acc_kind, ((rows, size), F32), row_kind, row_kind],
+        (cols, one, ops, weights, innovations, obs_precision),
+        1,
+    )
     two, inc, inc_send = run(
         second_rim,
         [flat_kind, ((2 * rows, size), F32), ((2 * rows, size), BF16)],
-        (cols, acc, one, mate, off, op_blocks, weights, inc_one),
+        (cols, acc, one, mate, off, ops, weights, inc_one),
         1,
         [wide],
     )
     received = [
-        lax.ppermute(inc_send, "members", [(i, (i + step) % groups) for i in range(groups)])
+        lax.ppermute(inc_send, "members", [(i, i ^ step) for i in range(groups)])
         for step in range(1, groups)
     ]
     pay_kind = ((REACH + members, size), F32)
-    res, to_mate, to_off, rim = run(
+    mate_kind = ((REACH + 2 * members, size), F32)
+    res, to_mate, to_off, rim, grad_weights = run(
         residual_rim,
-        [((2 * rows, size), F32), pay_kind, pay_kind, ((2 * REACH, size), F32)],
+        [((2 * rows, size), F32), mate_kind, pay_kind, ((2 * REACH, size), F32), ((members, rows), F32)],
         (
             inc,
-            innovations.reshape(2 * rows, size),
-            obs_precision.reshape(2 * rows, size),
-            op_blocks,
+            innov,
+            prec,
+            ops,
             cols,
             weights,
+            one,
+            two,
             *received,
         ),
     )
+    own_squares = to_mate[REACH + members :]
     mate, off = swap(to_mate, to_off)
-    y, grad_weights, squares = run(
-        residual_inner,
-        [((3 * rows - 2 * REACH, size), F32), ((members, rows), F32), ((members, size), F32)],
-        (res, op_blocks, weights, one, two),
-    )
+    (y,) = run(residual_inner, [((3 * rows - 2 * REACH, size), F32)], (res, ops))
+    total = own_squares + mate[REACH + members :]
+    strides = [2**power for power in range(1, tiles.bit_length() - 1)]
+
+    def partner(value, stride):
+        return lax.ppermute(value, "space", [(i, i ^ stride) for i in range(tiles)])
+
+    total = total + partner(total, strides[0])
     pairs = 3 * rows + 2 * REACH
     swap_kind = ((REACH, members, size), BF16)
     mid, own, to_mate, to_off = run(
         adjoint_rim,
         [((rows * members, size), BF16), acc_kind, swap_kind, swap_kind],
-        (cols, cols, weights, y, rim, mate, off, op_blocks),
+        (cols, cols, weights, y, rim, mate, off, ops),
         1,
         [
             pltpu.VMEM((pairs, size), BF16),
@@ -409,12 +477,18 @@
             pltpu.VMEM((rows + 2 * REACH, members, size), F32),
         ],
     )
+    to_mate, to_off, total = lax.optimization_barrier((to_mate, to_off, total))
     mate, off = swap(to_mate, to_off)
-    (own,) = run(adjoint_inner, [acc_kind], (cols, mid, own, op_blocks), 1)
-    squares = lax.psum(squares[:, 0], "space")
-    mean_square = squares / (rows * tiles)
-    direction = grad_weights / jnp.sqrt(mean_square + 1e-06)[:, None]
-    (grad_ens,) = run(finish, [((members, length), F32)], (own, mate, off))
+    for stride in strides[1:]:
+        total = total + partner(total, stride)
+    (own,) = run(adjoint_inner, [acc_kind], (cols, mid, own, ops), 1)
+    grad_ens, direction = run(
+        finish,
+        [((members, length), F32), ((members, rows), F32)],
+        (jnp.full((1,), rows * tiles, F32), own, mate, off, grad_weights, total),
+        1,
+        near=False,
+    )
     return (grad_ens, direction)
 
 

time: 79.4 us -> 58.6 us (0.74)
  the two profiles are of different devices: /device:TPU:3 before, /device:TPU:1 now
where the time goes in v2:
time: 58.6 us; the launch traced here: 58.2 us
  starting transfers between devices  24.1 us (41%)
  Pallas kernels  20.4 us (35%)
  waiting for transfers between devices  11.1 us (19%)
  local copies, waits for them, and re-layouts  1.75 us (3%)
  between operations  0.83 us (1%)
    pallas_call x9, Pallas kernels, run(): pl.pallas_call(body, out_shape=[kind_of(shape, kind) for shape, kind in o...  20.4 us
    ppermute x4, starting transfers between devices, swap(): from_off = lax.ppermute(to_off, 'space', offs)  16.3 us
    ppermute x4, waiting for transfers between devices, swap(): from_off = lax.ppermute(to_off, 'space', offs)  7.62 us
    ppermute x3, starting transfers between devices, on_device(): lax.ppermute(inc_send, 'members', [(i, i ^ step) for i in range(groups)])  3.74 us
    ppermute x2, starting transfers between devices, partner(): return lax.ppermute(value, 'space', [(i, i ^ stride) for i in range(tiles)])  3.58 us
    ppermute x3, waiting for transfers between devices, on_device(): lax.ppermute(inc_send, 'members', [(i, i ^ step) for i in range(groups)])  3.3 us
  transfers between devices with their start and end apart: 13, of which 6 were waited for; matrix products, arithmetic and copies ran while one was open for 0% of the time, Pallas kernels for 22%

profile of v2, /device:TPU:1, one launch (start us, length us, event | category | flops | bytes accessed | tf_op | source)
XLA Modules:
  0.0 58.2 jit_solution(17950557304028219716)
XLA Ops:
  0.6 1.1 %constant_dynamic-slice_fusion = (bf16[32,4096]{1,0:T(8,128)(2,1)S(1)}, bf16[32,4096]{1,0:T(8,128)(2,1)S(1)}) fusion(bf16[32,8192]{1,0:T(8,128)(2,1)} %v_far.1, s32[]{:T(128)S(6)} %select_n.18, s32[]{:T(128)S(6)} %select_n.17), kind=kLoop, calls=%fused_computation.1 | loop fusion | bytes 1048584 | tf_op jit(solution)/shard_map/dynamic_slice | solution.py:407
  1.7 4.5 %collective-permute-start.1 = (bf16[32,4096]{1,0:T(8,128)(2,1)S(1)}, bf16[32,4096]{1,0:T(8,128)(2,1)S(1)}, u32[]{:S(2)}, u32[]{:S(2)}) collective-permute-start(bf16[32,4096]{1,0:T(8,128)(2,1)S(1)} %get-tuple-element.52), channel_id=1, source_target_pairs={{4,8},{8,4},{12,16},{16,12},{20,24},{24,20},{5,9},{9,5},{13,17},{1... | collective-permute-start | bytes 786440 | tf_op jit(solution)/shard_map/ppermute | solution.py:394
  6.2 0.1 collective-permute-start
  6.3 0.0 copy-start.3
  6.3 0.7 %copy-done.3 = s32[64,2]{0,1:T(2,128)S(1)} copy-done((s32[64,2]{0,1:T(2,128)S(1)}, s32[64,2]{0,1:T(2,128)}, u32[]{:S(2)}) %copy-start.3) | copy-done | bytes 536
  7.0 0.0 copy-start
  7.0 0.0 copy-start.1
  7.0 0.0 copy-start.2
  7.0 4.9 %first_inner.1 = (f32[64,32,128]{2,1,0:T(8,128)S(1)}, bf16[32,8192]{1,0:T(8,128)(2,1)S(1)}, bf16[64,3,128,128]{3,2,1,0:T(8,128)(2,1)S(1)}) custom-call(s32[2,64]{1,0:T(2,128)S(1)} %bitcast.1, bf16[32,8192]{1,0:T(8,128)(2,1)} %v_far.1, bf16[64,3,128,128]{3,2,1,0:T(8,128)(2,1)} %ops_far.1), custom_call_target="tpu_custom_call" | custom-call | tf_op jit(solution)/shard_map/first_inner/pallas_call | solution.py:370
  11.9 0.3 collective-permute-done.1.off
  12.2 0.0 collective-permute-done.mate
  12.2 2.2 %first_rim.1 = (bf16[32,8192]{1,0:T(8,128)(2,1)S(1)}, bf16[32,4096]{1,0:T(8,128)(2,1)S(1)}, bf16[32,4096]{1,0:T(8,128)(2,1)S(1)}) custom-call(s32[2,64]{1,0:T(2,128)S(1)} %bitcast.2, f32[64,32,128]{2,1,0:T(8,128)S(1)} %get-tuple-element.27.acc, bf16[32,8192]{1,0:T(8,128)(2,1)S(1)} %get-tuple-element.28.v, bf16[32,4096]{1,0:T(8,128)(2,1)S(1)} %collective-permute-done.mate, ...), custom_call_target="tpu_custom_call" | custom-call | tf_op jit(solution)/shard_map/first_rim/pallas_call | solution.py:370
  14.4 0.3 collective-permute-start.2
  14.7 5.0 %collective-permute-start.3 = (bf16[32,4096]{1,0:T(8,128)(2,1)S(1)}, bf16[32,4096]{1,0:T(8,128)(2,1)S(1)}, u32[]{:S(2)}, u32[]{:S(2)}) collective-permute-start(bf16[32,4096]{1,0:T(8,128)(2,1)S(1)} %get-tuple-element.33), channel_id=1, source_target_pairs={{4,8},{8,4},{12,16},{16,12},{20,24},{24,20},{5,9},{9,5},{13,17},{1... | collective-permute-start | bytes 786440 | tf_op jit(solution)/shard_map/ppermute | solution.py:394
  19.7 0.0 copy-done
  19.7 0.0 copy-done.1
  19.7 0.0 copy-done.2
  19.7 2.8 %second_inner.1 = (f32[64,32,128]{2,1,0:T(8,128)S(1)}, f32[64,128]{1,0:T(8,128)S(1)}, f32[128,128]{1,0:T(8,128)S(1)}, f32[128,128]{1,0:T(8,128)S(1)}) custom-call(s32[2,64]{1,0:T(2,128)S(1)} %bitcast.3, bf16[32,8192]{1,0:T(8,128)(2,1)S(1)} %get-tuple-element.30.v.one, bf16[64,3,128,128]{3,2,1,0:T(8,128)(2,1)S(1)} %get-tuple-element.29.ops, ...), custom_call_target="tpu_custom_call" | custom-call | tf_op jit(solution)/shard_map/second_inner/pallas_call | solution.py:370
  22.5 0.0 collective-permute-done.2.mate
  22.5 4.0 %collective-permute-done.3.off = bf16[32,4096]{1,0:T(8,128)(2,1)S(1)} collective-permute-done((bf16[32,4096]{1,0:T(8,128)(2,1)S(1)}, bf16[32,4096]{1,0:T(8,128)(2,1)S(1)}, u32[]{:S(2)}, u32[]{:S(2)}) %collective-permute-start.3) | collective-permute-done | bytes 262176 | tf_op jit(solution)/shard_map/ppermute | solution.py:394
  26.5 2.6 %second_rim.1 = (bf16[32,8192]{1,0:T(8,128)(2,1)S(1)}, f32[128,128]{1,0:T(8,128)S(1)}, bf16[128,128]{1,0:T(8,128)(2,1)S(1)}) custom-call(s32[2,64]{1,0:T(2,128)S(1)} %bitcast.4, f32[64,32,128]{2,1,0:T(8,128)S(1)} %get-tuple-element.31.acc, bf16[32,8192]{1,0:T(8,128)(2,1)S(1)} %get-tuple-element.30.v.one, bf16[32,4096]{1,0:T(8,128)(2,1)S(1)} %collective-permute-done.2.mate, ...), custom_call_target="tpu_custom_call" | custom-call | tf_op jit(solution)/shard_map/second_rim/pallas_call | solution.py:370
  29.1 3.4 %collective-permute-start.6 = (bf16[128,128]{1,0:T(8,128)(2,1)S(1)}, bf16[128,128]{1,0:T(8,128)(2,1)S(1)}, u32[]{:S(2)}, u32[]{:S(2)}) collective-permute-start(bf16[128,128]{1,0:T(8,128)(2,1)S(1)} %get-tuple-element.39), channel_id=1, source_target_pairs={{0,3},{1,2},{2,1},{3,0},{4,7},{5,6},{6,5},{7,4},{8,11},{9,10},{10,... | collective-permute-start | bytes 98312 | tf_op jit(solution)/shard_map/ppermute | solution.py:436
  32.5 0.0 collective-permute-start.5
  32.5 0.4 collective-permute-start.4
  32.9 0.9 %collective-permute-done.6.rest_2_ = bf16[128,128]{1,0:T(8,128)(2,1)S(1)} collective-permute-done((bf16[128,128]{1,0:T(8,128)(2,1)S(1)}, bf16[128,128]{1,0:T(8,128)(2,1)S(1)}, u32[]{:S(2)}, u32[]{:S(2)}) %collective-permute-start.6) | collective-permute-done | bytes 32800 | tf_op jit(solution)/shard_map/ppermute | solution.py:436
  33.8 2.4 %collective-permute-done.5.rest_1_ = bf16[128,128]{1,0:T(8,128)(2,1)S(1)} collective-permute-done((bf16[128,128]{1,0:T(8,128)(2,1)S(1)}, bf16[128,128]{1,0:T(8,128)(2,1)S(1)}, u32[]{:S(2)}, u32[]{:S(2)}) %collective-permute-start.5) | collective-permute-done | bytes 32800 | tf_op jit(solution)/shard_map/ppermute | solution.py:436
  36.2 0.0 collective-permute-done.4.rest_0_
  36.2 1.5 %residual_rim.1 = (f32[128,128]{1,0:T(8,128)S(1)}, f32[96,128]{1,0:T(8,128)S(1)}, f32[64,128]{1,0:T(8,128)S(1)}, f32[64,128]{1,0:T(8,128)S(1)}, f32[32,64]{1,0:T(8,128)S(1)}) custom-call(f32[128,128]{1,0:T(8,128)S(1)} %get-tuple-element.35.inc, f32[128,128]{1,0:T(8,128)S(1)} %get-tuple-element.36.innov, f32[128,128]{1,0:T(8,128)S(1)} %get-tuple-element.37.prec, ...), custom_call_target="tpu_custom_call" | custom-call | tf_op jit(solution)/shard_map/residual_rim/pallas_call | solution.py:370
  37.7 0.1 collective-permute-start.7
  37.7 3.7 %collective-permute-start.8 = (f32[64,128]{1,0:T(8,128)S(1)}, f32[64,128]{1,0:T(8,128)S(1)}, u32[]{:S(2)}, u32[]{:S(2)}) collective-permute-start(f32[64,128]{1,0:T(8,128)S(1)} %get-tuple-element.43), channel_id=1, source_target_pairs={{4,8},{8,4},{12,16},{16,12},{20,24},{24,20},{5,9},{9,5},{13,17},{1... | collective-permute-start | bytes 98312 | tf_op jit(solution)/shard_map/ppermute | solution.py:394
  41.5 0.0 collective-permute-done.7.mate
  41.5 2.7 %collective-permute-start.9 = (f32[32,128]{1,0:T(8,128)S(1)}, f32[32,128]{1,0:T(8,128)S(1)}, u32[]{:S(2)}, u32[]{:S(2)}) collective-permute-start(f32[32,128]{1,0:T(8,128)S(1)} %slice_add_fusion), channel_id=1, source_target_pairs={{0,8},{4,12},{8,0},{12,4},{16,24},{20,28},{24,16},{28,20},{1,9},{5... | collective-permute-start | bytes 49160 | tf_op jit(solution)/shard_map/ppermute | solution.py:463
  44.2 1.0 %residual_inner.1.y = f32[128,128]{1,0:T(8,128)S(1)} custom-call(f32[128,128]{1,0:T(8,128)S(1)} %get-tuple-element.40.res, bf16[64,3,128,128]{3,2,1,0:T(8,128)(2,1)S(1)} %get-tuple-element.29.ops), custom_call_target="tpu_custom_call" | custom-call | tf_op jit(solution)/shard_map/residual_inner/pallas_call | solution.py:370
  45.2 0.0 collective-permute-done.8.off
  45.2 2.3 %adjoint_rim.1 = (bf16[2048,128]{1,0:T(8,128)(2,1)S(1)}, f32[64,32,128]{2,1,0:T(8,128)S(1)}, bf16[32,32,128]{2,1,0:T(8,128)(2,1)S(1)}, bf16[32,32,128]{2,1,0:T(8,128)(2,1)S(1)}) custom-call(s32[2,64]{1,0:T(2,128)S(1)} %bitcast.6, s32[2,64]{1,0:T(2,128)S(1)} %bitcast.7, f32[32,64]{1,0:T(8,128)S(1)} %copy-done, f32[128,128]{1,0:T(8,128)S(1)} %residual_inner.1.y, ...), custom_call_target="tpu_custom_call" | custom-call | tf_op jit(solution)/shard_map/adjoint_rim/pallas_call | solution.py:370
  47.5 0.0 collective-permute-done.9
  47.5 0.1 collective-permute-start.10
  47.6 3.1 %collective-permute-start.11 = (bf16[32,32,128]{2,1,0:T(8,128)(2,1)S(1)}, bf16[32,32,128]{2,1,0:T(8,128)(2,1)S(1)}, u32[]{:S(2)}, u32[]{:S(2)}) collective-permute-start(bf16[32,32,128]{2,1,0:T(8,128)(2,1)S(1)} %get-tuple-element.49), channel_id=1, source_target_pairs={{4,8},{8,4},{12,16},{16,12},{20,24},{24,20},{5,9},{9,5},{13,17},{1... | collective-permute-start | bytes 786440 | tf_op jit(solution)/shard_map/ppermute | solution.py:394
  50.7 0.9 %collective-permute-start.12 = (f32[32,128]{1,0:T(8,128)S(1)}, f32[32,128]{1,0:T(8,128)S(1)}, u32[]{:S(2)}, u32[]{:S(2)}) collective-permute-start(f32[32,128]{1,0:T(8,128)S(1)} %add.17), channel_id=1, source_target_pairs={{0,16},{4,20},{8,24},{12,28},{16,0},{20,4},{24,8},{28,12},{1,17},{... | collective-permute-start | bytes 49160 | tf_op jit(solution)/shard_map/ppermute | solution.py:463
  51.6 1.9 %adjoint_inner.1.own = f32[64,32,128]{2,1,0:T(8,128)S(1)} custom-call(s32[2,64]{1,0:T(2,128)S(1)} %bitcast.8, bf16[2048,128]{1,0:T(8,128)(2,1)S(1)} %get-tuple-element.44.mid, f32[64,32,128]{2,1,0:T(8,128)S(1)} %get-tuple-element.45.own, bf16[64,3,128,128]{3,2,1,0:T(8,128)(2,1)S(1)} %get-tuple-element.29.ops), custom_call_target="tpu_custom_call" | custom-call | tf_op jit(solution)/shard_map/adjoint_inner/pallas_call | solution.py:370
  53.5 0.2 collective-permute-done.12
  53.6 0.0 collective-permute-done.10.mate
  53.6 3.4 %collective-permute-done.11.off = bf16[32,32,128]{2,1,0:T(8,128)(2,1)S(1)} collective-permute-done((bf16[32,32,128]{2,1,0:T(8,128)(2,1)S(1)}, bf16[32,32,128]{2,1,0:T(8,128)(2,1)S(1)}, u32[]{:S(2)}, u32[]{:S(2)}) %collective-permute-start.11) | collective-permute-done | bytes 262176 | tf_op jit(solution)/shard_map/ppermute | solution.py:394
  57.0 1.2 %finish.1 = (f32[32,8192]{1,0:T(8,128)}, f32[32,64]{1,0:T(8,128)}) custom-call(f32[1]{0:T(128)} %constant.20.clone.1.count, f32[64,32,128]{2,1,0:T(8,128)S(1)} %adjoint_inner.1.own, bf16[32,32,128]{2,1,0:T(8,128)(2,1)S(1)} %collective-permute-done.10.mate, bf16[32,32,128]{2,1,0:T(8,128)(2,1)S(1)} %collective-permute-done.11.off, ...), custom_call_target="tpu_custom_call" | custom-call | tf_op jit(solution)/shard_map/finish/pallas_call | solution.py:370
  (3 shorter events, 0.0 us)
Async XLA Ops:
  1.7 10.5 %collective-permute-start.1 = (bf16[32,4096]{1,0:T(8,128)(2,1)S(1)}, bf16[32,4096]{1,0:T(8,128)(2,1)S(1)}, u32[]{:S(2)}, u32[]{:S(2)}) collective-permute-start(bf16[32,4096]{1,0:T(8,128)(2,1)S(1)} %get-tuple-element.52), channel_id=1, source_target_pairs={{4,8},{8,4},{12,16},{16,12},{20,24},{24,20},{5,9},{9,5},{13,17},{1... | collective-permute-start | bytes 786440 | tf_op jit(solution)/shard_map/ppermute | solution.py:394
  6.2 6.0 %collective-permute-start = (bf16[32,4096]{1,0:T(8,128)(2,1)S(1)}, bf16[32,4096]{1,0:T(8,128)(2,1)S(1)}, u32[]{:S(2)}, u32[]{:S(2)}) collective-permute-start(bf16[32,4096]{1,0:T(8,128)(2,1)S(1)} %get-tuple-element.53), channel_id=1, source_target_pairs={{0,4},{4,0},{8,12},{12,8},{16,20},{20,16},{24,28},{28,24},{1,5},{5... | collective-permute-start | bytes 786440 | tf_op jit(solution)/shard_map/ppermute | solution.py:395
  6.3 0.7 %copy-start.3 = (s32[64,2]{0,1:T(2,128)S(1)}, s32[64,2]{0,1:T(2,128)}, u32[]{:S(2)}) copy-start(s32[64,2]{0,1:T(2,128)} %param.8) | copy-start | bytes 1540
  7.0 12.7 %copy-start = (f32[32,64]{1,0:T(8,128)S(1)}, f32[32,64]{1,0:T(8,128)}, u32[]{:S(2)}) copy-start(f32[32,64]{1,0:T(8,128)} %w.7) | copy-start | bytes 24580
  7.0 12.7 %copy-start.1 = (f32[2,8192]{1,0:T(2,128)S(1)}, f32[2,8192]{1,0:T(2,128)}, u32[]{:S(2)}) copy-start(f32[2,8192]{1,0:T(2,128)} %innov.1) | copy-start | bytes 196612
  7.0 12.7 %copy-start.2 = (f32[2,8192]{1,0:T(2,128)S(1)}, f32[2,8192]{1,0:T(2,128)}, u32[]{:S(2)}) copy-start(f32[2,8192]{1,0:T(2,128)} %prec.1) | copy-start | bytes 196612
  14.4 8.1 %collective-permute-start.2 = (bf16[32,4096]{1,0:T(8,128)(2,1)S(1)}, bf16[32,4096]{1,0:T(8,128)(2,1)S(1)}, u32[]{:S(2)}, u32[]{:S(2)}) collective-permute-start(bf16[32,4096]{1,0:T(8,128)(2,1)S(1)} %get-tuple-element.32), channel_id=1, source_target_pairs={{0,4},{4,0},{8,12},{12,8},{16,20},{20,16},{24,28},{28,24},{1,5},{5... | collective-permute-start | bytes 786440 | tf_op jit(solution)/shard_map/ppermute | solution.py:395
  14.7 11.8 %collective-permute-start.3 = (bf16[32,4096]{1,0:T(8,128)(2,1)S(1)}, bf16[32,4096]{1,0:T(8,128)(2,1)S(1)}, u32[]{:S(2)}, u32[]{:S(2)}) collective-permute-start(bf16[32,4096]{1,0:T(8,128)(2,1)S(1)} %get-tuple-element.33), channel_id=1, source_target_pairs={{4,8},{8,4},{12,16},{16,12},{20,24},{24,20},{5,9},{9,5},{13,17},{1... | collective-permute-start | bytes 786440 | tf_op jit(solution)/shard_map/ppermute | solution.py:394
  29.1 4.7 %collective-permute-start.6 = (bf16[128,128]{1,0:T(8,128)(2,1)S(1)}, bf16[128,128]{1,0:T(8,128)(2,1)S(1)}, u32[]{:S(2)}, u32[]{:S(2)}) collective-permute-start(bf16[128,128]{1,0:T(8,128)(2,1)S(1)} %get-tuple-element.39), channel_id=1, source_target_pairs={{0,3},{1,2},{2,1},{3,0},{4,7},{5,6},{6,5},{7,4},{8,11},{9,10},{10,... | collective-permute-start | bytes 98312 | tf_op jit(solution)/shard_map/ppermute | solution.py:436
  32.5 3.7 %collective-permute-start.5 = (bf16[128,128]{1,0:T(8,128)(2,1)S(1)}, bf16[128,128]{1,0:T(8,128)(2,1)S(1)}, u32[]{:S(2)}, u32[]{:S(2)}) collective-permute-start(bf16[128,128]{1,0:T(8,128)(2,1)S(1)} %get-tuple-element.39), channel_id=1, source_target_pairs={{0,2},{1,3},{2,0},{3,1},{4,6},{5,7},{6,4},{7,5},{8,10},{9,11},{10,... | collective-permute-start | bytes 98312 | tf_op jit(solution)/shard_map/ppermute | solution.py:436
  32.5 3.7 %collective-permute-start.4 = (bf16[128,128]{1,0:T(8,128)(2,1)S(1)}, bf16[128,128]{1,0:T(8,128)(2,1)S(1)}, u32[]{:S(2)}, u32[]{:S(2)}) collective-permute-start(bf16[128,128]{1,0:T(8,128)(2,1)S(1)} %get-tuple-element.39), channel_id=1, source_target_pairs={{0,1},{1,0},{2,3},{3,2},{4,5},{5,4},{6,7},{7,6},{8,9},{9,8},{10,11... | collective-permute-start | bytes 98312 | tf_op jit(solution)/shard_map/ppermute | solution.py:436
  37.7 3.8 %collective-permute-start.7 = (f32[96,128]{1,0:T(8,128)S(1)}, f32[96,128]{1,0:T(8,128)S(1)}, u32[]{:S(2)}, u32[]{:S(2)}) collective-permute-start(f32[96,128]{1,0:T(8,128)S(1)} %get-tuple-element.42), channel_id=1, source_target_pairs={{0,4},{4,0},{8,12},{12,8},{16,20},{20,16},{24,28},{28,24},{1,5},{5... | collective-permute-start | bytes 147464 | tf_op jit(solution)/shard_map/ppermute | solution.py:395
  37.7 7.4 %collective-permute-start.8 = (f32[64,128]{1,0:T(8,128)S(1)}, f32[64,128]{1,0:T(8,128)S(1)}, u32[]{:S(2)}, u32[]{:S(2)}) collective-permute-start(f32[64,128]{1,0:T(8,128)S(1)} %get-tuple-element.43), channel_id=1, source_target_pairs={{4,8},{8,4},{12,16},{16,12},{20,24},{24,20},{5,9},{9,5},{13,17},{1... | collective-permute-start | bytes 98312 | tf_op jit(solution)/shard_map/ppermute | solution.py:394
  41.5 6.0 %collective-permute-start.9 = (f32[32,128]{1,0:T(8,128)S(1)}, f32[32,128]{1,0:T(8,128)S(1)}, u32[]{:S(2)}, u32[]{:S(2)}) collective-permute-start(f32[32,128]{1,0:T(8,128)S(1)} %slice_add_fusion), channel_id=1, source_target_pairs={{0,8},{4,12},{8,0},{12,4},{16,24},{20,28},{24,16},{28,20},{1,9},{5... | collective-permute-start | bytes 49160 | tf_op jit(solution)/shard_map/ppermute | solution.py:463
  47.5 6.1 %collective-permute-start.10 = (bf16[32,32,128]{2,1,0:T(8,128)(2,1)S(1)}, bf16[32,32,128]{2,1,0:T(8,128)(2,1)S(1)}, u32[]{:S(2)}, u32[]{:S(2)}) collective-permute-start(bf16[32,32,128]{2,1,0:T(8,128)(2,1)S(1)} %get-tuple-element.48), channel_id=1, source_target_pairs={{0,4},{4,0},{8,12},{12,8},{16,20},{20,16},{24,28},{28,24},{1,5},{5... | collective-permute-start | bytes 786440 | tf_op jit(solution)/shard_map/ppermute | solution.py:395
  47.6 9.4 %collective-permute-start.11 = (bf16[32,32,128]{2,1,0:T(8,128)(2,1)S(1)}, bf16[32,32,128]{2,1,0:T(8,128)(2,1)S(1)}, u32[]{:S(2)}, u32[]{:S(2)}) collective-permute-start(bf16[32,32,128]{2,1,0:T(8,128)(2,1)S(1)} %get-tuple-element.49), channel_id=1, source_target_pairs={{4,8},{8,4},{12,16},{16,12},{20,24},{24,20},{5,9},{9,5},{13,17},{1... | collective-permute-start | bytes 786440 | tf_op jit(solution)/shard_map/ppermute | solution.py:394
  50.7 3.0 %collective-permute-start.12 = (f32[32,128]{1,0:T(8,128)S(1)}, f32[32,128]{1,0:T(8,128)S(1)}, u32[]{:S(2)}, u32[]{:S(2)}) collective-permute-start(f32[32,128]{1,0:T(8,128)S(1)} %add.17), channel_id=1, source_target_pairs={{0,16},{4,20},{8,24},{12,28},{16,0},{20,4},{24,8},{28,12},{1,17},{... | collective-permute-start | bytes 49160 | tf_op jit(solution)/shard_map/ppermute | solution.py:463

commit v3 on v0

v3 whole, which is shorter than its diff:
```python
import jax
import jax.numpy as jnp
from jax import lax
from jax.experimental import pallas as pl
from jax.experimental.pallas import tpu as pltpu
from jax.sharding import PartitionSpec as P

MEMBERS = 128
REACH = 32
SCALE = (MEMBERS - 1) ** (-0.5)
F32 = jnp.float32
BF16 = jnp.bfloat16
I32 = jnp.int32
UNROLL = 16


def dot_t(x, a):
    return lax.dot_general(x, a, (((1,), (1,)), ((), ())), preferred_element_type=F32)


def dot_n(x, a):
    return lax.dot_general(x, a, (((1,), (0,)), ((), ())), preferred_element_type=F32)


class Sides:
    def __init__(self, rows):
        place = lax.axis_index("space")
        self.even = place % 2 == 0
        self.base = place * rows
        self.flip = jnp.where(self.even, 0, 3 * REACH)
        self.off_row = jnp.where(self.even, 0, REACH)
        self.mate_row = REACH - self.off_row
        self.off_k = jnp.where(self.even, 1, 2)
        self.mate_k = 3 - self.off_k

    def place(self, col):
        return (col - self.base + REACH) ^ self.flip

    def pick(self, first, last):
        return jnp.where(self.even, first, last), jnp.where(self.even, last, first)


def lanes(ref, index, size):
    return ref.at[:, pl.ds(pl.multiple_of(index * size, size), size)]


def chunks(total, body):
    def step(i, carry):
        body([i * UNROLL + u for u in range(UNROLL)])
        return carry

    lax.fori_loop(0, total // UNROLL, step, 0)


def load(ens, off, mate, sems):
    size = ens.shape[1] // (2 * REACH)
    sides = Sides(2 * REACH)
    width = REACH * size
    copies = []
    for n, (row, out) in enumerate(((sides.off_row, off), (sides.mate_row, mate))):
        source = ens.at[:, pl.ds(pl.multiple_of(row * size, size), width)]
        copies.append(pltpu.make_async_copy(source, out, sems.at[n]))
        copies[-1].start()
    for copy in copies:
        copy.wait()


def inner(cols, wide, ops, acc, sides, ready=None):
    size = ops.shape[2]
    for row, k, q in ((sides.off_row, sides.mate_k, 0), (sides.mate_row, sides.off_k, REACH)):
        for half in range(2):
            low = half * REACH // 2
            if ready is not None:
                ready((q + low) // (REACH // 2))

            def some(ids, row=row, k=k, q=q, low=low):
                outs = []
                for i in ids:
                    r = row + low + i
                    e = sides.place(cols[k - 1, r])
                    x = [lanes(wide, REACH + q + low + i, size)[...], lanes(wide, e, size)[...]]
                    outs.append((q + low + i, dot_t(jnp.concatenate(x, 1), jnp.concatenate([ops[r, 0], ops[r, k]], 1))))
                for place, o in outs:
                    acc[place] = o

            chunks(REACH // 2, some)


def first_inner(cols, off, mate, ops_far, acc, wide, ops, sems):
    rows, _, size, _ = ops.shape
    sides = Sides(rows)
    step = REACH // 2
    copies = []
    for part in range(2 * REACH // step):
        start = (sides.off_row if part * step < REACH else sides.mate_row) + part * step % REACH
        where = pl.ds(start, step)
        copies.append(pltpu.make_async_copy(ops_far.at[where], ops.at[where], sems.at[part]))
        copies[-1].start()
    wide[:, REACH * size : 2 * REACH * size] = off[...]
    wide[:, 2 * REACH * size : 3 * REACH * size] = mate[...]
    inner(cols, wide, ops, acc, sides, lambda part: copies[part].wait())


def rim(cols, acc, wide, ops, sides, near, store):
    size = ops.shape[2]
    row, k, q = (sides.mate_row, sides.mate_k, REACH) if near else (sides.off_row, sides.off_k, 0)

    def some(ids):
        outs = []
        for i in ids:
            e = sides.place(cols[k - 1, row + i])
            outs.append((i, acc[q + i] + dot_t(lanes(wide, e, size)[...], ops[row + i, k])))
        for i, o in outs:
            store(i, o.astype(BF16))

    chunks(REACH, some)


def first_mate(cols, acc, wide_in, halo, ops, wide, out, send):
    size = ops.shape[2]
    wide[:, 3 * REACH * size :] = halo[...]

    def store(i, o):
        lanes(out, 2 * REACH + i, size)[...] = o
        lanes(send, i, size)[...] = o

    rim(cols, acc, wide, ops, Sides(ops.shape[0]), True, store)


def first_off(cols, acc, wide_in, out_in, halo, ops, wide, out, send):
    size = ops.shape[2]
    wide[:, : REACH * size] = halo[...]

    def store(i, o):
        lanes(out, REACH + i, size)[...] = o
        lanes(send, i, size)[...] = o

    rim(cols, acc, wide, ops, Sides(ops.shape[0]), False, store)


def turned(sides, w):
    swapped = jnp.concatenate([w[:, REACH:], w[:, :REACH]], 1)
    return jnp.where(sides.even, w, swapped)


def member_sums(value, start, w, first, count, size, store):
    for i in range(count):
        x = value[:, (start + i) * size : (start + i + 1) * size].astype(F32)
        store(i, jnp.sum(x * w[:, first + i : first + i + 1], axis=0, keepdims=True))


def second_inner(cols, wide, ops, w, innov, prec, acc, inc, innov_rows, prec_rows, w_turned):
    rows, _, size, _ = ops.shape
    sides = Sides(rows)
    inner(cols, wide, ops, acc, sides)
    weights = turned(sides, w[...])
    w_turned[...] = weights
    for q in range(rows):
        r = q + (sides.off_row if q < REACH else sides.mate_row - REACH)
        for time in range(2):
            place = slice(time * rows + q, time * rows + q + 1)
            innov_rows[place, :] = lanes(innov, r, size)[time : time + 1, :]
            prec_rows[place, :] = lanes(prec, r, size)[time : time + 1, :]

    def store(i, s):
        inc[i : i + 1, :] = s

    member_sums(wide, REACH, weights, 0, rows, size, store)


def second_mate(cols, acc, wide_in, halo, ops, w, wide, out, inc):
    size = ops.shape[2]
    wide[:, 3 * REACH * size :] = halo[...]

    def store(i, o):
        lanes(out, i, size)[...] = o

    rim(cols, acc, wide, ops, Sides(ops.shape[0]), True, store)

    def keep(i, s):
        inc[i : i + 1, :] = s

    member_sums(out, 0, w, REACH, REACH, size, keep)


def second_off(cols, acc, wide_in, halo, ops, w, inc_one, inc_mate, wide, out, inc, send):
    rows, _, size, _ = ops.shape
    wide[:, : REACH * size] = halo[...]

    def store(i, o):
        lanes(out, i, size)[...] = o

    rim(cols, acc, wide, ops, Sides(rows), False, store)

    def keep(i, s):
        inc[rows + i : rows + i + 1, :] = s

    member_sums(out, 0, w, 0, REACH, size, keep)
    inc[:rows, :] = inc_one[...]
    inc[rows + REACH :, :] = inc_mate[...]
    send[...] = inc[...].astype(BF16)


def cot_row(res, place):
    return jnp.broadcast_to(res[pl.ds(place, 1), :], (8, res.shape[1])).astype(BF16)


def rim_rows(res, ops, sides, near, out):
    rows = ops.shape[0]
    row, k, q = (sides.mate_row, sides.mate_k, REACH) if near else (sides.off_row, sides.off_k, 0)

    def some(ids):
        outs = [(i, dot_n(cot_row(res, rows + q + i), ops[row + i, k])) for i in ids]
        for i, o in outs:
            out[pl.ds(i, 1), :] = o[:1]

    chunks(REACH, some)


def side_facts(cols, w, sides, near, out):
    members = w.shape[0]
    first, last = (REACH, 2 * REACH) if near else (0, REACH)
    out[REACH : REACH + members, :REACH] = w[:, first:last]
    off, mate = sides.pick(cols[:1, :REACH], cols[1:, REACH:])
    out[REACH : REACH + 1, REACH : 2 * REACH] = (mate if near else off).astype(F32)


def residual_rim(cols, inc, innov, prec, ops, w, one, two_off, two_mate, *rest):
    received = rest[:-4]
    res, send_off, send_mate, gw = rest[-4:]
    rows, _, size, _ = ops.shape
    members = w.shape[0]
    sides = Sides(rows)
    total = inc[...]
    for other in received:
        total = total + other[...].astype(F32)
    res[...] = prec[...] * (total * SCALE - innov[...])
    for near, send in ((False, send_off), (True, send_mate)):
        rim_rows(res, ops, sides, near, send)
        side_facts(cols, w, sides, near, send)
    index = lax.broadcasted_iota(I32, (members, rows), 1)
    grown = jnp.zeros((members, rows), F32)
    for q in range(rows):
        two, place = (two_off, q) if q < REACH else (two_mate, q - REACH)
        prod = one[:, (REACH + q) * size : (REACH + q + 1) * size].astype(F32) * res[q : q + 1, :]
        prod = prod + two[:, place * size : (place + 1) * size].astype(F32) * res[rows + q : rows + q + 1, :]
        grown = jnp.where(index == q, jnp.sum(prod, axis=1, keepdims=True), grown)
    grown = w[...] + SCALE * grown
    gw[...] = grown
    send_mate[REACH + members :, :] = jnp.broadcast_to(jnp.sum(grown * grown, axis=1, keepdims=True), (members, size))


def residual_inner(res, ops, y):
    rows, _, size, _ = ops.shape
    sides = Sides(rows)
    for row, k, q in ((sides.off_row, sides.mate_k, 0), (sides.mate_row, sides.off_k, REACH)):

        def some(ids, row=row, k=k, q=q):
            outs = []
            for i in ids:
                r = row + i
                o = dot_n(cot_row(res, rows + q + i), jnp.concatenate([ops[r, 0], ops[r, k]], 1))
                outs.append((q + i, o))
            for place, o in outs:
                y[pl.ds(place, 1), :] = o[:1, :size] + res[pl.ds(place, 1), :]
                y[pl.ds(rows + place, 1), :] = o[:1, size:]

        chunks(REACH, some)


def middle(weights, target, vals, q, mid):
    members = weights.shape[0]
    group = 8
    for g in range(REACH // group):
        place = REACH + q + g * group
        picked = [jnp.where(target == place + c, weights, 0.0).astype(BF16) for c in range(group)]
        mid[g * group * members : (g + 1) * group * members, :] = dot_n(jnp.concatenate(picked, 0), vals).astype(BF16)


def adjoint_side(cols, mid, ops, sides, near, sums):
    members = mid.shape[0] // REACH
    row, k, low = (sides.mate_row, sides.mate_k, 2 * REACH) if near else (sides.off_row, sides.off_k, 0)
    sums[...] = jnp.zeros_like(sums)

    def some(ids):
        outs = []
        for i in ids:
            x = mid[pl.ds(pl.multiple_of(i * members, members), members), :]
            outs.append((sides.place(cols[k - 1, row + i]) - low, dot_n(x, ops[row + i, k])))
        for place, o in outs:
            sums[place] = sums[place] + o

    chunks(REACH, some)


def adjoint_off(cols, col_rows, w, y, own_off, own_mate, off, mate, ops, mid, sums, send, vals, wp, tgt):
    rows, _, size, _ = ops.shape
    members = w.shape[0]
    sides = Sides(rows)
    vals[:rows, :] = y[:rows, :].astype(BF16)
    vals[2 * rows : 3 * rows, :] = y[rows:, :].astype(BF16)
    for n, part in enumerate((own_off, own_mate)):
        vals[rows + n * REACH : rows + (n + 1) * REACH, :] = part[:REACH, :].astype(BF16)
    for k in range(3):
        wp[:, k * rows : (k + 1) * rows] = w[...] * SCALE
    col = col_rows[...]
    rim_off, rim_mate = sides.pick(col[:1, :REACH], col[1:, REACH:])
    inner_off, inner_mate = sides.pick(col[1:, :REACH], col[:1, REACH:])
    tgt[:, :rows] = lax.broadcasted_iota(I32, (1, rows), 1) + REACH
    for n, part in enumerate((rim_off, rim_mate, inner_off, inner_mate)):
        tgt[:, rows + n * REACH : rows + (n + 1) * REACH] = sides.place(part)
    for n, part in enumerate((off, mate)):
        where = slice(3 * rows + n * REACH, 3 * rows + (n + 1) * REACH)
        vals[where, :] = part[:REACH, :].astype(BF16)
        wp[:, where] = part[REACH : REACH + members, :REACH] * SCALE
        tgt[:, where] = sides.place(part[REACH : REACH + 1, REACH : 2 * REACH].astype(I32))
    middle(wp[...], tgt[...], vals[...], 0, mid)
    adjoint_side(cols, mid, ops, sides, False, sums)
    send[...] = sums[:REACH].astype(BF16)


def adjoint_mate(cols, wp, tgt, vals, ops, mid, sums, send):
    sides = Sides(ops.shape[0])
    middle(wp[...], tgt[...], vals[...], REACH, mid)
    adjoint_side(cols, mid, ops, sides, True, sums)
    send[...] = sums[REACH:].astype(BF16)


def adjoint_inner(cols, mid_off, mid_mate, sums_off, sums_mate, ops, out):
    rows, _, size, _ = ops.shape
    members = sums_off.shape[1]
    sides = Sides(rows)
    out[:REACH] = sums_off[REACH:]
    out[REACH:] = sums_mate[:REACH]
    for row, k, q, mid in ((sides.off_row, sides.mate_k, 0, mid_off), (sides.mate_row, sides.off_k, REACH, mid_mate)):

        def some(ids, row=row, k=k, q=q, mid=mid):
            outs = []
            for i in ids:
                r = row + i
                x = mid[pl.ds(pl.multiple_of(i * members, members), members), :]
                o = dot_n(x, jnp.concatenate([ops[r, 0], ops[r, k]], 1))
                outs.append((q + i, o[:, :size]))
                outs.append((sides.place(cols[k - 1, r]) - REACH, o[:, size:]))
            for place, o in outs:
                out[place] = out[place] + o

        chunks(REACH, some)


def finish(count, own, off, mate, gw, total, out, direction):
    rows, members, size = own.shape
    sides = Sides(rows)
    weights = gw[...] / jnp.sqrt(total[:, :1] / count[0] + 1e-06)
    direction[...] = turned(sides, weights)
    for row, q, halo in ((sides.off_row, 0, off), (sides.mate_row, REACH, mate)):
        for i in range(REACH):
            lanes(out, row + i, size)[...] = own[q + i] + halo[i].astype(F32)


SMEM = pl.BlockSpec(memory_space=pltpu.SMEM)
VMEM = pl.BlockSpec(memory_space=pltpu.VMEM)
FAR = pl.BlockSpec(memory_space=pltpu.HBM)


def run(body, outs, args, scalars=0, scratch=(), far=0, alias=None, near=True):
    kind_of = pltpu.VMEM if near else jax.ShapeDtypeStruct
    return pl.pallas_call(
        body,
        out_shape=[kind_of(shape, kind) for shape, kind in outs],
        in_specs=[SMEM] * scalars + [VMEM] * (len(args) - scalars - far) + [FAR] * far,
        out_specs=[VMEM] * len(outs),
        scratch_shapes=list(scratch),
        input_output_aliases=alias or {},
        compiler_params=pltpu.CompilerParams(vmem_limit_bytes=12 * 1024 * 1024),
        name=body.__name__,
    )(*args)


def on_device(ensemble, op_blocks, col_index, weights, innovations, obs_precision):
    members = ensemble.shape[0]
    rows, per_row, size, _ = op_blocks.shape
    assert rows == 2 * REACH and per_row == 3
    length = rows * size
    halo = REACH * size
    tiles = lax.axis_size("space")
    groups = lax.axis_size("members")
    mates = [(i, i ^ 1) for i in range(tiles)]
    offs = []
    for i in range(1, tiles - 1, 2):
        offs += [(i, i + 1), (i + 1, i)]
    sem = pltpu.SemaphoreType.DMA

    def far(value):
        return pltpu.with_memory_space_constraint(value, pltpu.HBM)

    def to_mate(value):
        return lax.ppermute(value, "space", mates)

    def to_off(value):
        return lax.ppermute(value, "space", offs)

    def partner(value, stride):
        return lax.ppermute(value, "space", [(i, i ^ stride) for i in range(tiles)])

    cols = col_index.T
    acc_kind = ((rows, members, size), F32)
    wide_kind = ((members, length + 2 * halo), BF16)
    side_kind = ((members, halo), BF16)
    part_kind = ((REACH, size), F32)
    row_kind = ((2 * rows, size), F32)

    off, mate = run(load, [side_kind, side_kind], (far(ensemble),), 0, [sem((2,))], far=1)
    from_off, from_mate = to_off(off), to_mate(mate)
    acc, wide, ops = run(
        first_inner,
        [acc_kind, wide_kind, (op_blocks.shape, BF16)],
        (cols, off, mate, far(op_blocks)),
        1,
        [sem((4,))],
        far=1,
    )
    wide, one, send = run(
        first_mate, [wide_kind, wide_kind, side_kind], (cols, acc, wide, from_mate, ops), 1, alias={2: 0}
    )
    from_mate = to_mate(send)
    wide, one, send = run(
        first_off,
        [wide_kind, wide_kind, side_kind],
        (cols, acc, wide, one, from_off, ops),
        1,
        alias={2: 0, 3: 1},
    )
    from_off = to_off(send)
    acc, inc_one, innov, prec, w = run(
        second_inner,
        [acc_kind, ((rows, size), F32), row_kind, row_kind, ((members, rows), F32)],
        (cols, one, ops, weights, innovations, obs_precision),
        1,
    )
    one, two_mate, inc_mate = run(
        second_mate, [wide_kind, side_kind, part_kind], (cols, acc, one, from_mate, ops, w), 1, alias={2: 0}
    )
    one, two_off, inc, send = run(
        second_off,
        [wide_kind, side_kind, row_kind, (row_kind[0], BF16)],
        (cols, acc, one, from_off, ops, w, inc_one, inc_mate),
        1,
        alias={2: 0},
    )
    received = [lax.ppermute(send, "members", [(i, i ^ step) for i in range(groups)]) for step in range(1, groups)]
    res, own_off, own_mate, grad_weights = run(
        residual_rim,
        [row_kind, ((REACH + members, size), F32), ((REACH + 2 * members, size), F32), ((members, rows), F32)],
        (cols, inc, innov, prec, ops, w, one, two_off, two_mate, *received),
    )
    from_off, from_mate = to_off(own_off), to_mate(own_mate)
    (y,) = run(residual_inner, [row_kind], (res, ops))
    total = own_mate[REACH + members :] + from_mate[REACH + members :]
    strides = [2**power for power in range(1, tiles.bit_length() - 1)]
    total = total + partner(total, strides[0])
    pairs = 3 * rows + 2 * REACH
    mid_kind = ((REACH * members, size), BF16)
    sums_kind = ((2 * REACH, members, size), F32)
    send_kind = ((REACH, members, size), BF16)
    mid_off, sums_off, send, vals, wp, tgt = run(
        adjoint_off,
        [mid_kind, sums_kind, send_kind, ((pairs, size), BF16), ((members, pairs), F32), ((1, pairs), I32)],
        (cols, cols, w, y, own_off, own_mate, from_off, from_mate, ops),
        1,
    )
    from_off = to_off(send)
    mid_mate, sums_mate, send = run(
        adjoint_mate, [mid_kind, sums_kind, send_kind], (cols, wp, tgt, vals, ops), 1
    )
    send, total = lax.optimization_barrier((send, total))
    for stride in strides[1:]:
        total = total + partner(total, stride)
    from_mate = to_mate(send)
    (own,) = run(adjoint_inner, [acc_kind], (cols, mid_off, mid_mate, sums_off, sums_mate, ops), 1)
    grad_ens, direction = run(
        finish,
        [((members, length), F32), ((members, rows), F32)],
        (jnp.full((1,), rows * tiles, F32), own, from_off, from_mate, grad_weights, total),
        1,
        near=False,
    )
    return (grad_ens, direction)


def solution(mesh):
    placed = (
        P("members", "space"),
        P("space", None, None, None),
        P("space", None),
        P("members", "space"),
        P(None, "space"),
        P(None, "space"),
    )
    return jax.shard_map(
        on_device,
        mesh=mesh,
        in_specs=placed,
        out_specs=(P("members", "space"), P("members", "space")),
        check_vma=False,
    )
```

time: 227 us -> 55.4 us (0.24)
  waiting for transfers between devices: 98.4 us -> 6.57 us
  other arithmetic: 45 us -> 0.02 us
  Pallas kernels: 0 us -> 21.5 us
  matrix products: 19.8 us -> 0 us
  blocking collectives: 13.8 us -> 0 us
  between operations: 14.4 us -> 0.87 us
  local copies, waits for them, and re-layouts: 12.3 us -> 0.7 us
  starting transfers between devices: 21.9 us -> 25.4 us
    ppermute x8 -> x13, waiting for transfers between devices: 62.3 us -> 6.57 us  [the longest x3 3.3 us: on_device(): lax.ppermute(send, 'members', [(i, i ^ step) for i in range(groups)])]
    psum x1 -> x0, waiting for transfers between devices: 36.1 us -> none  [on_device(): increments = lax.psum(partial_sums, 'members') * member_scale]
    scatter-add x2 -> x0, other arithmetic: 34.5 us -> none  [adjoint(): spread_rows.at[:, every_col.reshape(-1), :]]
    pallas_call x0 -> x13, Pallas kernels: none -> 21.5 us  [run(): pl.pallas_call(body, out_shape=[kind_of(shape, kind) for shape, kind in o...]
    dot_general x4 -> x0, matrix products: 19.8 us -> none  [the longest x2 10.2 us: forward(): jnp.einsum('rkij,mrkj->mri', op_blocks, picked, preferred_element_type=jn...]
    psum x1 -> x0, blocking collectives: 13.8 us -> none  [on_device(): squares = lax.psum(jnp.sum(grad_weights * grad_weights, axis=1), 'space')]
    unnamed x18 -> x10, local copies, waits for them, and re-layouts: 5.28 us -> 0.7 us
    reshape x4 -> x0, other arithmetic: 3.81 us -> none  [the longest x1 2.22 us: on_device(): grad_ens = adjoint(adjoint_mid).reshape(member_count, blocks * block_size)]
  transfers between devices with their start and end apart: 9 -> 13, of which waited for: 8 -> 4; matrix products, arithmetic and copies ran while one was open for 1% -> 0% of each run, Pallas kernels for 0% -> 29%
where the time goes in v3:
time: 55.4 us; the launch traced here: 55 us
  starting transfers between devices  25.4 us (46%)
  Pallas kernels  21.5 us (39%)
  waiting for transfers between devices  6.57 us (12%)
  between operations  0.87 us (2%)
  local copies, waits for them, and re-layouts  0.7 us (1%)
    pallas_call x13, Pallas kernels, run(): pl.pallas_call(body, out_shape=[kind_of(shape, kind) for shape, kind in o...  21.5 us
    ppermute x4, starting transfers between devices, to_off(): return lax.ppermute(value, 'space', offs)  14.6 us
    ppermute x3, starting transfers between devices, on_device(): lax.ppermute(send, 'members', [(i, i ^ step) for i in range(groups)])  5.33 us
    ppermute x2, starting transfers between devices, partner(): return lax.ppermute(value, 'space', [(i, i ^ stride) for i in range(tiles)])  5.16 us
    ppermute x3, waiting for transfers between devices, on_device(): lax.ppermute(send, 'members', [(i, i ^ step) for i in range(groups)])  3.3 us
    ppermute x4, waiting for transfers between devices, to_off(): return lax.ppermute(value, 'space', offs)  3.25 us
  transfers between devices with their start and end apart: 13, of which 4 were waited for; matrix products, arithmetic and copies ran while one was open for 0% of the time, Pallas kernels for 29%

profile of v3, /device:TPU:1, one launch (start us, length us, event | category | flops | bytes accessed | tf_op | source)
XLA Modules:
  0.0 55.0 jit_solution(9063224989753763098)
XLA Ops:
  0.6 1.1 %load.1 = (bf16[32,4096]{1,0:T(8,128)(2,1)S(1)}, bf16[32,4096]{1,0:T(8,128)(2,1)S(1)}) custom-call(bf16[32,8192]{1,0:T(8,128)(2,1)} %ens.1), custom_call_target="tpu_custom_call" | custom-call | tf_op jit(solution)/shard_map/load/pallas_call | solution.py:368
  1.7 0.1 collective-permute-start
  1.8 4.5 %collective-permute-start.1 = (bf16[32,4096]{1,0:T(8,128)(2,1)S(1)}, bf16[32,4096]{1,0:T(8,128)(2,1)S(1)}, u32[]{:S(2)}, u32[]{:S(2)}) collective-permute-start(bf16[32,4096]{1,0:T(8,128)(2,1)S(1)} %get-tuple-element.39.off), channel_id=1, source_target_pairs={{4,8},{8,4},{12,16},{16,12},{20,24},{24,20},{5,9},{9,5},{13,17},{1... | collective-permute-start | bytes 786440 | tf_op jit(solution)/shard_map/ppermute | solution.py:401
  6.3 0.0 copy-start
  6.3 0.7 %copy-done = s32[64,2]{0,1:T(2,128)S(1)} copy-done((s32[64,2]{0,1:T(2,128)S(1)}, s32[64,2]{0,1:T(2,128)}, u32[]{:S(2)}) %copy-start) | copy-done | bytes 536
  7.0 3.9 %first_inner.1 = (f32[64,32,128]{2,1,0:T(8,128)S(1)}, bf16[32,16384]{1,0:T(8,128)(2,1)S(1)}, bf16[64,3,128,128]{3,2,1,0:T(8,128)(2,1)S(1)}) custom-call(s32[2,64]{1,0:T(2,128)S(1)} %bitcast.1, bf16[32,4096]{1,0:T(8,128)(2,1)S(1)} %get-tuple-element.39.off, bf16[32,4096]{1,0:T(8,128)(2,1)S(1)} %get-tuple-element.40.mate, bf16[64,3,128,128]{3,2,1,0:T(8,128)(2,1)} %ops_far.1), custom_call_target="tpu_custom_call" | custom-call | tf_op jit(solution)/shard_map/first_inner/pallas_call | solution.py:368
  10.9 0.0 collective-permute-done.halo
  10.9 1.3 %first_mate.1 = (bf16[32,16384]{1,0:T(8,128)(2,1)S(1)}, bf16[32,16384]{1,0:T(8,128)(2,1)S(1)}, bf16[32,4096]{1,0:T(8,128)(2,1)S(1)}) custom-call(s32[2,64]{1,0:T(2,128)S(1)} %bitcast.2, f32[64,32,128]{2,1,0:T(8,128)S(1)} %get-tuple-element.41.acc, bf16[32,16384]{1,0:T(8,128)(2,1)S(1)} %get-tuple-element.42.wide_in, ...), custom_call_target="tpu_custom_call", output_to_operand_aliasing={{0}: (2, {})} | custom-call | tf_op jit(solution)/shard_map/first_mate/pallas_call | solution.py:368
  12.3 0.0 copy-start.2
  12.3 0.0 copy-start.3
  12.3 0.0 copy-start.4
  12.3 0.1 collective-permute-start.2
  12.4 0.0 collective-permute-done.1.halo
  12.4 1.3 %first_off.1 = (bf16[32,16384]{1,0:T(8,128)(2,1)S(1)}, bf16[32,16384]{1,0:T(8,128)(2,1)S(1)}, bf16[32,4096]{1,0:T(8,128)(2,1)S(1)}) custom-call(s32[2,64]{1,0:T(2,128)S(1)} %bitcast.3, f32[64,32,128]{2,1,0:T(8,128)S(1)} %get-tuple-element.41.acc, bf16[32,16384]{1,0:T(8,128)(2,1)S(1)} %get-tuple-element.44.wide_in, ...), custom_call_target="tpu_custom_call", output_to_operand_aliasing={{0}: (2, {}), {1}: (3, {})} | custom-call | tf_op jit(solution)/shard_map/first_off/pallas_call | solution.py:368
  13.7 3.5 %collective-permute-start.3 = (bf16[32,4096]{1,0:T(8,128)(2,1)S(1)}, bf16[32,4096]{1,0:T(8,128)(2,1)S(1)}, u32[]{:S(2)}, u32[]{:S(2)}) collective-permute-start(bf16[32,4096]{1,0:T(8,128)(2,1)S(1)} %get-tuple-element.51), channel_id=1, source_target_pairs={{4,8},{8,4},{12,16},{16,12},{20,24},{24,20},{5,9},{9,5},{13,17},{1... | collective-permute-start | bytes 786440 | tf_op jit(solution)/shard_map/ppermute | solution.py:401
  17.2 0.0 copy-done.1
  17.2 0.0 copy-done.2
  17.3 0.0 copy-done.3
  17.3 0.0 copy-done.4
  17.3 2.1 %second_inner.1 = (f32[64,32,128]{2,1,0:T(8,128)S(1)}, f32[64,128]{1,0:T(8,128)S(1)}, f32[128,128]{1,0:T(8,128)S(1)}, f32[128,128]{1,0:T(8,128)S(1)}, f32[32,64]{1,0:T(8,128)S(1)}) custom-call(s32[2,64]{1,0:T(2,128)S(1)} %bitcast.4, bf16[32,16384]{1,0:T(8,128)(2,1)S(1)} %get-tuple-element.46.wide.wide_in, ...), custom_call_target="tpu_custom_call" | custom-call | tf_op jit(solution)/shard_map/second_inner/pallas_call | solution.py:368
  19.4 0.0 collective-permute-done.2.halo
  19.4 1.6 %second_mate.1 = (bf16[32,16384]{1,0:T(8,128)(2,1)S(1)}, bf16[32,4096]{1,0:T(8,128)(2,1)S(1)}, f32[32,128]{1,0:T(8,128)S(1)}) custom-call(s32[2,64]{1,0:T(2,128)S(1)} %bitcast.5, f32[64,32,128]{2,1,0:T(8,128)S(1)} %get-tuple-element.48.acc, bf16[32,16384]{1,0:T(8,128)(2,1)S(1)} %get-tuple-element.46.wide.wide_in, ...), custom_call_target="tpu_custom_call", output_to_operand_aliasing={{0}: (2, {})} | custom-call | tf_op jit(solution)/shard_map/second_mate/pallas_call | solution.py:368
  21.0 1.5 %collective-permute-done.3.halo = bf16[32,4096]{1,0:T(8,128)(2,1)S(1)} collective-permute-done((bf16[32,4096]{1,0:T(8,128)(2,1)S(1)}, bf16[32,4096]{1,0:T(8,128)(2,1)S(1)}, u32[]{:S(2)}, u32[]{:S(2)}) %collective-permute-start.3) | collective-permute-done | bytes 262176 | tf_op jit(solution)/shard_map/ppermute | solution.py:401
  22.5 1.6 %second_off.1 = (bf16[32,16384]{1,0:T(8,128)(2,1)S(1)}, bf16[32,4096]{1,0:T(8,128)(2,1)S(1)}, f32[128,128]{1,0:T(8,128)S(1)}, bf16[128,128]{1,0:T(8,128)(2,1)S(1)}) custom-call(s32[2,64]{1,0:T(2,128)S(1)} %bitcast.6, f32[64,32,128]{2,1,0:T(8,128)S(1)} %get-tuple-element.48.acc, ...), custom_call_target="tpu_custom_call", output_to_operand_aliasing={{0}: (2, {})} | custom-call | tf_op jit(solution)/shard_map/second_off/pallas_call | solution.py:368
  24.1 5.0 %collective-permute-start.6 = (bf16[128,128]{1,0:T(8,128)(2,1)S(1)}, bf16[128,128]{1,0:T(8,128)(2,1)S(1)}, u32[]{:S(2)}, u32[]{:S(2)}) collective-permute-start(bf16[128,128]{1,0:T(8,128)(2,1)S(1)} %get-tuple-element.60), channel_id=1, source_target_pairs={{0,3},{1,2},{2,1},{3,0},{4,7},{5,6},{6,5},{7,4},{8,11},{9,10},{10,... | collective-permute-start | bytes 98312 | tf_op jit(solution)/shard_map/ppermute | solution.py:451
  29.1 0.0 collective-permute-start.5
  29.1 0.4 collective-permute-start.4
  29.4 0.9 %collective-permute-done.6.rest_2_ = bf16[128,128]{1,0:T(8,128)(2,1)S(1)} collective-permute-done((bf16[128,128]{1,0:T(8,128)(2,1)S(1)}, bf16[128,128]{1,0:T(8,128)(2,1)S(1)}, u32[]{:S(2)}, u32[]{:S(2)}) %collective-permute-start.6) | collective-permute-done | bytes 32800 | tf_op jit(solution)/shard_map/ppermute | solution.py:451
  30.4 2.4 %collective-permute-done.5.rest_1_ = bf16[128,128]{1,0:T(8,128)(2,1)S(1)} collective-permute-done((bf16[128,128]{1,0:T(8,128)(2,1)S(1)}, bf16[128,128]{1,0:T(8,128)(2,1)S(1)}, u32[]{:S(2)}, u32[]{:S(2)}) %collective-permute-start.5) | collective-permute-done | bytes 32800 | tf_op jit(solution)/shard_map/ppermute | solution.py:451
  32.7 0.0 collective-permute-done.4.rest_0_
  32.7 1.5 %residual_rim.1 = (f32[128,128]{1,0:T(8,128)S(1)}, f32[64,128]{1,0:T(8,128)S(1)}, f32[96,128]{1,0:T(8,128)S(1)}, f32[32,64]{1,0:T(8,128)S(1)}) custom-call(s32[2,64]{1,0:T(2,128)S(1)} %bitcast.7, f32[128,128]{1,0:T(8,128)S(1)} %get-tuple-element.54.inc, f32[128,128]{1,0:T(8,128)S(1)} %get-tuple-element.55.innov, f32[128,128]{1,0:T(8,128)S(1)} %get-tuple-element.56.prec, ...), custom_call_target="tpu_custom_call" | custom-call | tf_op jit(solution)/shard_map/residual_rim/pallas_call | solution.py:368
  34.2 0.0 collective-permute-start.8
  34.3 4.8 %collective-permute-start.7 = (f32[64,128]{1,0:T(8,128)S(1)}, f32[64,128]{1,0:T(8,128)S(1)}, u32[]{:S(2)}, u32[]{:S(2)}) collective-permute-start(f32[64,128]{1,0:T(8,128)S(1)} %get-tuple-element.62.own_off), channel_id=1, source_target_pairs={{4,8},{8,4},{12,16},{16,12},{20,24},{24,20},{5,9},{9,5},{13,17},{1... | collective-permute-start | bytes 98312 | tf_op jit(solution)/shard_map/ppermute | solution.py:401
  39.0 0.0 collective-permute-done.8.mate
  39.1 2.8 %collective-permute-start.10 = (f32[32,128]{1,0:T(8,128)S(1)}, f32[32,128]{1,0:T(8,128)S(1)}, u32[]{:S(2)}, u32[]{:S(2)}) collective-permute-start(f32[32,128]{1,0:T(8,128)S(1)} %slice_add_fusion), channel_id=1, source_target_pairs={{0,8},{4,12},{8,0},{12,4},{16,24},{20,28},{24,16},{28,20},{1,9},{5... | collective-permute-start | bytes 49160 | tf_op jit(solution)/shard_map/ppermute | solution.py:404
  41.9 1.0 %residual_inner.1.y = f32[128,128]{1,0:T(8,128)S(1)} custom-call(f32[128,128]{1,0:T(8,128)S(1)} %get-tuple-element.61.res, bf16[64,3,128,128]{3,2,1,0:T(8,128)(2,1)S(1)} %get-tuple-element.43.ops), custom_call_target="tpu_custom_call" | custom-call | tf_op jit(solution)/shard_map/residual_inner/pallas_call | solution.py:368
  42.9 0.0 collective-permute-done.7.off
  42.9 1.5 %adjoint_off.1 = (bf16[1024,128]{1,0:T(8,128)(2,1)S(1)}, f32[64,32,128]{2,1,0:T(8,128)S(1)}, bf16[32,32,128]{2,1,0:T(8,128)(2,1)S(1)}, bf16[256,128]{1,0:T(8,128...) custom-call(s32[2,64]{1,0:T(2,128)S(1)} %bitcast.8, s32[2,64]{1,0:T(2,128)S(1)} %bitcast.9, ...), custom_call_target="tpu_custom_call" | custom-call | tf_op jit(solution)/shard_map/adjoint_off/pallas_call | solution.py:368
  44.4 1.9 %collective-permute-start.9 = (bf16[32,32,128]{2,1,0:T(8,128)(2,1)S(1)}, bf16[32,32,128]{2,1,0:T(8,128)(2,1)S(1)}, u32[]{:S(2)}, u32[]{:S(2)}) collective-permute-start(bf16[32,32,128]{2,1,0:T(8,128)(2,1)S(1)} %get-tuple-element.71), channel_id=1, source_target_pairs={{4,8},{8,4},{12,16},{16,12},{20,24},{24,20},{5,9},{9,5},{13,17},{1... | collective-permute-start | bytes 786440 | tf_op jit(solution)/shard_map/ppermute | solution.py:401
  46.4 1.4 %adjoint_mate.1 = (bf16[1024,128]{1,0:T(8,128)(2,1)S(1)}, f32[64,32,128]{2,1,0:T(8,128)S(1)}, bf16[32,32,128]{2,1,0:T(8,128)(2,1)S(1)}) custom-call(s32[2,64]{1,0:T(2,128)S(1)} %bitcast.10, f32[32,256]{1,0:T(8,128)S(1)} %get-tuple-element.65.wp, s32[1,256]{1,0:T(1,128)S(1)} %get-tuple-element.66.tgt, bf16[256,128]{1,0:T(8,128)(2,1)S(1)} %get-tuple-element.67.vals, ...), custom_call_target="tpu_custom_call" | custom-call | tf_op jit(solution)/shard_map/adjoint_mate/pallas_call | solution.py:368
  47.8 0.0 collective-permute-done.10
  47.8 0.1 collective-permute-start.11
  47.9 2.3 %collective-permute-start.12 = (f32[32,128]{1,0:T(8,128)S(1)}, f32[32,128]{1,0:T(8,128)S(1)}, u32[]{:S(2)}, u32[]{:S(2)}) collective-permute-start(f32[32,128]{1,0:T(8,128)S(1)} %add.10), channel_id=1, source_target_pairs={{0,16},{4,20},{8,24},{12,28},{16,0},{20,4},{24,8},{28,12},{1,17},{... | collective-permute-start | bytes 49160 | tf_op jit(solution)/shard_map/ppermute | solution.py:404
  50.2 1.9 %adjoint_inner.1.own = f32[64,32,128]{2,1,0:T(8,128)S(1)} custom-call(s32[2,64]{1,0:T(2,128)S(1)} %bitcast.11, bf16[1024,128]{1,0:T(8,128)(2,1)S(1)} %get-tuple-element.64.mid_off, bf16[1024,128]{1,0:T(8,128)(2,1)S(1)} %get-tuple-element.68.mid_mate, f32[64,32,128]{2,1,0:T(8,128)S(1)} %get-tuple-element.69.sums_off, ...), custom_call_target="tpu_custom_call" | custom-call | tf_op jit(solution)/shard_map/adjoint_inner/pallas_call | solution.py:368
  52.1 0.0 collective-permute-done.12
  52.1 1.7 %collective-permute-done.9.off = bf16[32,32,128]{2,1,0:T(8,128)(2,1)S(1)} collective-permute-done((bf16[32,32,128]{2,1,0:T(8,128)(2,1)S(1)}, bf16[32,32,128]{2,1,0:T(8,128)(2,1)S(1)}, u32[]{:S(2)}, u32[]{:S(2)}) %collective-permute-start.9) | collective-permute-done | bytes 262176 | tf_op jit(solution)/shard_map/ppermute | solution.py:401
  53.9 0.0 collective-permute-done.11.mate
  53.9 1.2 %finish.1 = (f32[32,8192]{1,0:T(8,128)}, f32[32,64]{1,0:T(8,128)}) custom-call(f32[1]{0:T(128)} %constant.0.clone.1.count, f32[64,32,128]{2,1,0:T(8,128)S(1)} %adjoint_inner.1.own, bf16[32,32,128]{2,1,0:T(8,128)(2,1)S(1)} %collective-permute-done.9.off, bf16[32,32,128]{2,1,0:T(8,128)(2,1)S(1)} %collective-permute-done.11.mate, ...), custom_call_target="tpu_custom_call" | custom-call | tf_op jit(solution)/shard_map/finish/pallas_call | solution.py:368
  (4 shorter events, 0.0 us)
Async XLA Ops:
  1.7 9.2 %collective-permute-start = (bf16[32,4096]{1,0:T(8,128)(2,1)S(1)}, bf16[32,4096]{1,0:T(8,128)(2,1)S(1)}, u32[]{:S(2)}, u32[]{:S(2)}) collective-permute-start(bf16[32,4096]{1,0:T(8,128)(2,1)S(1)} %get-tuple-element.40.mate), channel_id=1, source_target_pairs={{0,4},{4,0},{8,12},{12,8},{16,20},{20,16},{24,28},{28,24},{1,5},{5... | collective-permute-start | bytes 786440 | tf_op jit(solution)/shard_map/ppermute | solution.py:398
  1.8 10.6 %collective-permute-start.1 = (bf16[32,4096]{1,0:T(8,128)(2,1)S(1)}, bf16[32,4096]{1,0:T(8,128)(2,1)S(1)}, u32[]{:S(2)}, u32[]{:S(2)}) collective-permute-start(bf16[32,4096]{1,0:T(8,128)(2,1)S(1)} %get-tuple-element.39.off), channel_id=1, source_target_pairs={{4,8},{8,4},{12,16},{16,12},{20,24},{24,20},{5,9},{9,5},{13,17},{1... | collective-permute-start | bytes 786440 | tf_op jit(solution)/shard_map/ppermute | solution.py:401
  6.3 0.7 %copy-start = (s32[64,2]{0,1:T(2,128)S(1)}, s32[64,2]{0,1:T(2,128)}, u32[]{:S(2)}) copy-start(s32[64,2]{0,1:T(2,128)} %param.8) | copy-start | bytes 1540
  12.2 5.0 %copy-start.1 = (s32[64,2]{0,1:T(2,128)S(1)}, s32[64,2]{0,1:T(2,128)}, u32[]{:S(2)}) copy-start(s32[64,2]{0,1:T(2,128)} %param.8) | copy-start | bytes 1540
  12.3 5.0 %copy-start.2 = (f32[2,8192]{1,0:T(2,128)S(1)}, f32[2,8192]{1,0:T(2,128)}, u32[]{:S(2)}) copy-start(f32[2,8192]{1,0:T(2,128)} %innov.1) | copy-start | bytes 196612
  12.3 5.0 %copy-start.3 = (f32[2,8192]{1,0:T(2,128)S(1)}, f32[2,8192]{1,0:T(2,128)}, u32[]{:S(2)}) copy-start(f32[2,8192]{1,0:T(2,128)} %prec.1) | copy-start | bytes 196612
  12.3 5.0 %copy-start.4 = (f32[32,64]{1,0:T(8,128)S(1)}, f32[32,64]{1,0:T(8,128)}, u32[]{:S(2)}) copy-start(f32[32,64]{1,0:T(8,128)} %w.1) | copy-start | bytes 24580
  12.3 7.1 %collective-permute-start.2 = (bf16[32,4096]{1,0:T(8,128)(2,1)S(1)}, bf16[32,4096]{1,0:T(8,128)(2,1)S(1)}, u32[]{:S(2)}, u32[]{:S(2)}) collective-permute-start(bf16[32,4096]{1,0:T(8,128)(2,1)S(1)} %get-tuple-element.49), channel_id=1, source_target_pairs={{0,4},{4,0},{8,12},{12,8},{16,20},{20,16},{24,28},{28,24},{1,5},{5... | collective-permute-start | bytes 786440 | tf_op jit(solution)/shard_map/ppermute | solution.py:398
  13.7 8.8 %collective-permute-start.3 = (bf16[32,4096]{1,0:T(8,128)(2,1)S(1)}, bf16[32,4096]{1,0:T(8,128)(2,1)S(1)}, u32[]{:S(2)}, u32[]{:S(2)}) collective-permute-start(bf16[32,4096]{1,0:T(8,128)(2,1)S(1)} %get-tuple-element.51), channel_id=1, source_target_pairs={{4,8},{8,4},{12,16},{16,12},{20,24},{24,20},{5,9},{9,5},{13,17},{1... | collective-permute-start | bytes 786440 | tf_op jit(solution)/shard_map/ppermute | solution.py:401
  24.1 6.3 %collective-permute-start.6 = (bf16[128,128]{1,0:T(8,128)(2,1)S(1)}, bf16[128,128]{1,0:T(8,128)(2,1)S(1)}, u32[]{:S(2)}, u32[]{:S(2)}) collective-permute-start(bf16[128,128]{1,0:T(8,128)(2,1)S(1)} %get-tuple-element.60), channel_id=1, source_target_pairs={{0,3},{1,2},{2,1},{3,0},{4,7},{5,6},{6,5},{7,4},{8,11},{9,10},{10,... | collective-permute-start | bytes 98312 | tf_op jit(solution)/shard_map/ppermute | solution.py:451
  29.1 3.7 %collective-permute-start.5 = (bf16[128,128]{1,0:T(8,128)(2,1)S(1)}, bf16[128,128]{1,0:T(8,128)(2,1)S(1)}, u32[]{:S(2)}, u32[]{:S(2)}) collective-permute-start(bf16[128,128]{1,0:T(8,128)(2,1)S(1)} %get-tuple-element.60), channel_id=1, source_target_pairs={{0,2},{1,3},{2,0},{3,1},{4,6},{5,7},{6,4},{7,5},{8,10},{9,11},{10,... | collective-permute-start | bytes 98312 | tf_op jit(solution)/shard_map/ppermute | solution.py:451
  29.1 3.7 %collective-permute-start.4 = (bf16[128,128]{1,0:T(8,128)(2,1)S(1)}, bf16[128,128]{1,0:T(8,128)(2,1)S(1)}, u32[]{:S(2)}, u32[]{:S(2)}) collective-permute-start(bf16[128,128]{1,0:T(8,128)(2,1)S(1)} %get-tuple-element.60), channel_id=1, source_target_pairs={{0,1},{1,0},{2,3},{3,2},{4,5},{5,4},{6,7},{7,6},{8,9},{9,8},{10,11... | collective-permute-start | bytes 98312 | tf_op jit(solution)/shard_map/ppermute | solution.py:451
  34.2 4.8 %collective-permute-start.8 = (f32[96,128]{1,0:T(8,128)S(1)}, f32[96,128]{1,0:T(8,128)S(1)}, u32[]{:S(2)}, u32[]{:S(2)}) collective-permute-start(f32[96,128]{1,0:T(8,128)S(1)} %get-tuple-element.63.own_mate), channel_id=1, source_target_pairs={{0,4},{4,0},{8,12},{12,8},{16,20},{20,16},{24,28},{28,24},{1,5},{5... | collective-permute-start | bytes 147464 | tf_op jit(solution)/shard_map/ppermute | solution.py:398
  34.3 8.6 %collective-permute-start.7 = (f32[64,128]{1,0:T(8,128)S(1)}, f32[64,128]{1,0:T(8,128)S(1)}, u32[]{:S(2)}, u32[]{:S(2)}) collective-permute-start(f32[64,128]{1,0:T(8,128)S(1)} %get-tuple-element.62.own_off), channel_id=1, source_target_pairs={{4,8},{8,4},{12,16},{16,12},{20,24},{24,20},{5,9},{9,5},{13,17},{1... | collective-permute-start | bytes 98312 | tf_op jit(solution)/shard_map/ppermute | solution.py:401
  39.1 8.7 %collective-permute-start.10 = (f32[32,128]{1,0:T(8,128)S(1)}, f32[32,128]{1,0:T(8,128)S(1)}, u32[]{:S(2)}, u32[]{:S(2)}) collective-permute-start(f32[32,128]{1,0:T(8,128)S(1)} %slice_add_fusion), channel_id=1, source_target_pairs={{0,8},{4,12},{8,0},{12,4},{16,24},{20,28},{24,16},{28,20},{1,9},{5... | collective-permute-start | bytes 49160 | tf_op jit(solution)/shard_map/ppermute | solution.py:404
  44.4 9.4 %collective-permute-start.9 = (bf16[32,32,128]{2,1,0:T(8,128)(2,1)S(1)}, bf16[32,32,128]{2,1,0:T(8,128)(2,1)S(1)}, u32[]{:S(2)}, u32[]{:S(2)}) collective-permute-start(bf16[32,32,128]{2,1,0:T(8,128)(2,1)S(1)} %get-tuple-element.71), channel_id=1, source_target_pairs={{4,8},{8,4},{12,16},{16,12},{20,24},{24,20},{5,9},{9,5},{13,17},{1... | collective-permute-start | bytes 786440 | tf_op jit(solution)/shard_map/ppermute | solution.py:401
  47.8 6.1 %collective-permute-start.11 = (bf16[32,32,128]{2,1,0:T(8,128)(2,1)S(1)}, bf16[32,32,128]{2,1,0:T(8,128)(2,1)S(1)}, u32[]{:S(2)}, u32[]{:S(2)}) collective-permute-start(bf16[32,32,128]{2,1,0:T(8,128)(2,1)S(1)} %get-tuple-element.73), channel_id=1, source_target_pairs={{0,4},{4,0},{8,12},{12,8},{16,20},{20,16},{24,28},{28,24},{1,5},{5... | collective-permute-start | bytes 786440 | tf_op jit(solution)/shard_map/ppermute | solution.py:398
  47.9 4.2 %collective-permute-start.12 = (f32[32,128]{1,0:T(8,128)S(1)}, f32[32,128]{1,0:T(8,128)S(1)}, u32[]{:S(2)}, u32[]{:S(2)}) collective-permute-start(f32[32,128]{1,0:T(8,128)S(1)} %add.10), channel_id=1, source_target_pairs={{0,16},{4,20},{8,24},{12,28},{16,0},{20,4},{24,8},{28,12},{1,17},{... | collective-permute-start | bytes 49160 | tf_op jit(solution)/shard_map/ppermute | solution.py:404

commit v4 on v3

--- a/solution.py
+++ b/solution.py
@@ -1,3 +1,5 @@
+import functools
+
 import jax
 import jax.numpy as jnp
 from jax import lax
@@ -11,7 +13,7 @@
 F32 = jnp.float32
 BF16 = jnp.bfloat16
 I32 = jnp.int32
-UNROLL = 16
+UNROLL = 32
 
 
 def dot_t(x, a):
@@ -41,15 +43,20 @@
 
 
 def lanes(ref, index, size):
-    return ref.at[:, pl.ds(pl.multiple_of(index * size, size), size)]
+    return ref.at[:, pl.ds(index * size if isinstance(index, int) else pl.multiple_of(index * size, size), size)]
 
 
 def chunks(total, body):
+    unroll = min(total, UNROLL)
+
     def step(i, carry):
-        body([i * UNROLL + u for u in range(UNROLL)])
+        body([i * unroll + u for u in range(unroll)])
         return carry
 
-    lax.fori_loop(0, total // UNROLL, step, 0)
+    if total == unroll:
+        body(list(range(total)))
+    else:
+        lax.fori_loop(0, total // unroll, step, 0)
 
 
 def load(ens, off, mate, sems):
@@ -68,10 +75,10 @@
 def inner(cols, wide, ops, acc, sides, ready=None):
     size = ops.shape[2]
     for row, k, q in ((sides.off_row, sides.mate_k, 0), (sides.mate_row, sides.off_k, REACH)):
-        for half in range(2):
-            low = half * REACH // 2
+        step = REACH if ready is None else REACH // 2
+        for low in range(0, REACH, step):
             if ready is not None:
-                ready((q + low) // (REACH // 2))
+                ready((q + low) // step)
 
             def some(ids, row=row, k=k, q=q, low=low):
                 outs = []
@@ -83,10 +90,10 @@
                 for place, o in outs:
                     acc[place] = o
 
-            chunks(REACH // 2, some)
-
-
-def first_inner(cols, off, mate, ops_far, acc, wide, ops, sems):
+            chunks(step, some)
+
+
+def first_inner(cols_in, off, mate, ops_far, acc, wide, ops, cols, sems):
     rows, _, size, _ = ops.shape
     sides = Sides(rows)
     step = REACH // 2
@@ -96,6 +103,9 @@
         where = pl.ds(start, step)
         copies.append(pltpu.make_async_copy(ops_far.at[where], ops.at[where], sems.at[part]))
         copies[-1].start()
+    for k in range(cols.shape[0]):
+        for r in range(rows):
+            cols[k, r] = cols_in[k, r]
     wide[:, REACH * size : 2 * REACH * size] = off[...]
     wide[:, 2 * REACH * size : 3 * REACH * size] = mate[...]
     inner(cols, wide, ops, acc, sides, lambda part: copies[part].wait())
@@ -348,10 +358,10 @@
         chunks(REACH, some)
 
 
-def finish(count, own, off, mate, gw, total, out, direction):
+def finish(own, off, mate, gw, total, out, direction, *, count):
     rows, members, size = own.shape
     sides = Sides(rows)
-    weights = gw[...] / jnp.sqrt(total[:, :1] / count[0] + 1e-06)
+    weights = gw[...] / jnp.sqrt(total[:, :1] / count + 1e-06)
     direction[...] = turned(sides, weights)
     for row, q, halo in ((sides.off_row, 0, off), (sides.mate_row, REACH, mate)):
         for i in range(REACH):
@@ -363,13 +373,18 @@
 FAR = pl.BlockSpec(memory_space=pltpu.HBM)
 
 
-def run(body, outs, args, scalars=0, scratch=(), far=0, alias=None, near=True):
+def run(body, outs, args, scalars=0, scratch=(), far=0, alias=None, near=True, table=None, **fixed):
     kind_of = pltpu.VMEM if near else jax.ShapeDtypeStruct
+    shapes = [kind_of(shape, kind) for shape, kind in outs]
+    places = [VMEM] * len(outs)
+    if table is not None:
+        shapes.append(pltpu.SMEM(table, I32))
+        places.append(SMEM)
     return pl.pallas_call(
-        body,
-        out_shape=[kind_of(shape, kind) for shape, kind in outs],
+        functools.partial(body, **fixed) if fixed else body,
+        out_shape=shapes,
         in_specs=[SMEM] * scalars + [VMEM] * (len(args) - scalars - far) + [FAR] * far,
-        out_specs=[VMEM] * len(outs),
+        out_specs=places,
         scratch_shapes=list(scratch),
         input_output_aliases=alias or {},
         compiler_params=pltpu.CompilerParams(vmem_limit_bytes=12 * 1024 * 1024),
@@ -412,22 +427,23 @@
 
     off, mate = run(load, [side_kind, side_kind], (far(ensemble),), 0, [sem((2,))], far=1)
     from_off, from_mate = to_off(off), to_mate(mate)
-    acc, wide, ops = run(
+    acc, wide, ops, table = run(
         first_inner,
         [acc_kind, wide_kind, (op_blocks.shape, BF16)],
         (cols, off, mate, far(op_blocks)),
         1,
         [sem((4,))],
         far=1,
+        table=cols.shape,
     )
     wide, one, send = run(
-        first_mate, [wide_kind, wide_kind, side_kind], (cols, acc, wide, from_mate, ops), 1, alias={2: 0}
+        first_mate, [wide_kind, wide_kind, side_kind], (table, acc, wide, from_mate, ops), 1, alias={2: 0}
     )
     from_mate = to_mate(send)
     wide, one, send = run(
         first_off,
         [wide_kind, wide_kind, side_kind],
-        (cols, acc, wide, one, from_off, ops),
+        (table, acc, wide, one, from_off, ops),
         1,
         alias={2: 0, 3: 1},
     )
@@ -435,16 +451,16 @@
     acc, inc_one, innov, prec, w = run(
         second_inner,
         [acc_kind, ((rows, size), F32), row_kind, row_kind, ((members, rows), F32)],
-        (cols, one, ops, weights, innovations, obs_precision),
+        (table, one, ops, weights, innovations, obs_precision),
         1,
     )
     one, two_mate, inc_mate = run(
-        second_mate, [wide_kind, side_kind, part_kind], (cols, acc, one, from_mate, ops, w), 1, alias={2: 0}
+        second_mate, [wide_kind, side_kind, part_kind], (table, acc, one, from_mate, ops, w), 1, alias={2: 0}
     )
     one, two_off, inc, send = run(
         second_off,
         [wide_kind, side_kind, row_kind, (row_kind[0], BF16)],
-        (cols, acc, one, from_off, ops, w, inc_one, inc_mate),
+        (table, acc, one, from_off, ops, w, inc_one, inc_mate),
         1,
         alias={2: 0},
     )
@@ -466,24 +482,24 @@
     mid_off, sums_off, send, vals, wp, tgt = run(
         adjoint_off,
         [mid_kind, sums_kind, send_kind, ((pairs, size), BF16), ((members, pairs), F32), ((1, pairs), I32)],
-        (cols, cols, w, y, own_off, own_mate, from_off, from_mate, ops),
+        (table, cols, w, y, own_off, own_mate, from_off, from_mate, ops),
         1,
     )
     from_off = to_off(send)
     mid_mate, sums_mate, send = run(
-        adjoint_mate, [mid_kind, sums_kind, send_kind], (cols, wp, tgt, vals, ops), 1
+        adjoint_mate, [mid_kind, sums_kind, send_kind], (table, wp, tgt, vals, ops), 1
     )
     send, total = lax.optimization_barrier((send, total))
     for stride in strides[1:]:
         total = total + partner(total, stride)
     from_mate = to_mate(send)
-    (own,) = run(adjoint_inner, [acc_kind], (cols, mid_off, mid_mate, sums_off, sums_mate, ops), 1)
+    (own,) = run(adjoint_inner, [acc_kind], (table, mid_off, mid_mate, sums_off, sums_mate, ops), 1)
     grad_ens, direction = run(
         finish,
         [((members, length), F32), ((members, rows), F32)],
-        (jnp.full((1,), rows * tiles, F32), own, from_off, from_mate, grad_weights, total),
-        1,
+        (own, from_off, from_mate, grad_weights, total),
         near=False,
+        count=rows * tiles,
     )
     return (grad_ens, direction)
 

time: 55.4 us -> 52 us (0.939)
  Pallas kernels: 21.5 us -> 14.2 us
  waiting for transfers between devices: 6.57 us -> 10.2 us
    pallas_call x13, Pallas kernels: 21.5 us -> 14.2 us  [run(): pl.pallas_call(functools.partial(body, **fixed) if fixed else body, out_s...]
    ppermute x4, waiting for transfers between devices: 3.25 us -> 6.7 us  [to_off(): return lax.ppermute(value, 'space', offs)]
    ppermute x4, starting transfers between devices: 14.6 us -> 14.1 us  [to_off(): return lax.ppermute(value, 'space', offs)]
  transfers between devices with their start and end apart: 13 -> 13, of which waited for: 4 -> 6; matrix products, arithmetic and copies ran while one was open for 0% -> 0% of each run, Pallas kernels for 29% -> 21%
where the time goes in v4:
time: 52 us; the launch traced here: 51.2 us
  starting transfers between devices  25.2 us (48%)
  Pallas kernels  14.2 us (27%)
  waiting for transfers between devices  10.2 us (20%)
  between operations  0.84 us (2%)
  local copies, waits for them, and re-layouts  0.69 us (1%)
    pallas_call x13, Pallas kernels, run(): pl.pallas_call(functools.partial(body, **fixed) if fixed else body, out_s...  14.2 us
    ppermute x4, starting transfers between devices, to_off(): return lax.ppermute(value, 'space', offs)  14.1 us
    ppermute x4, waiting for transfers between devices, to_off(): return lax.ppermute(value, 'space', offs)  6.7 us
    ppermute x2, starting transfers between devices, partner(): return lax.ppermute(value, 'space', [(i, i ^ stride) for i in range(tiles)])  5.54 us
    ppermute x3, starting transfers between devices, on_device(): lax.ppermute(send, 'members', [(i, i ^ step) for i in range(groups)])  5.28 us
    ppermute x3, waiting for transfers between devices, on_device(): lax.ppermute(send, 'members', [(i, i ^ step) for i in range(groups)])  3.3 us
  transfers between devices with their start and end apart: 13, of which 6 were waited for; matrix products, arithmetic and copies ran while one was open for 0% of the time, Pallas kernels for 21%

profile of v4, /device:TPU:1, one launch (start us, length us, event | category | flops | bytes accessed | tf_op | source)
XLA Modules:
  0.0 51.2 jit_solution(5671740638105932300)
XLA Ops:
  0.6 1.1 %load.1 = (bf16[32,4096]{1,0:T(8,128)(2,1)S(1)}, bf16[32,4096]{1,0:T(8,128)(2,1)S(1)}) custom-call(bf16[32,8192]{1,0:T(8,128)(2,1)} %ens.1), custom_call_target="tpu_custom_call" | custom-call | tf_op jit(solution)/shard_map/load/pallas_call | solution.py:383
  1.7 0.1 collective-permute-start
  1.8 4.5 %collective-permute-start.1 = (bf16[32,4096]{1,0:T(8,128)(2,1)S(1)}, bf16[32,4096]{1,0:T(8,128)(2,1)S(1)}, u32[]{:S(2)}, u32[]{:S(2)}) collective-permute-start(bf16[32,4096]{1,0:T(8,128)(2,1)S(1)} %get-tuple-element.40.off), channel_id=1, source_target_pairs={{4,8},{8,4},{12,16},{16,12},{20,24},{24,20},{5,9},{9,5},{13,17},{1... | collective-permute-start | bytes 786440 | tf_op jit(solution)/shard_map/ppermute | solution.py:416
  6.3 0.0 copy-start.3
  6.3 0.7 %copy-done.3 = s32[64,2]{0,1:T(2,128)S(1)} copy-done((s32[64,2]{0,1:T(2,128)S(1)}, s32[64,2]{0,1:T(2,128)}, u32[]{:S(2)}) %copy-start.3) | copy-done | bytes 536
  7.0 3.9 %first_inner.1 = (f32[64,32,128]{2,1,0:T(8,128)S(1)}, bf16[32,16384]{1,0:T(8,128)(2,1)S(1)}, bf16[64,3,128,128]{3,2,1,0:T(8,128)(2,1)S(1)}, s32[2,64]{1,0:T(2,128)S(4)}) custom-call(s32[2,64]{1,0:T(2,128)S(1)} %bitcast.1, bf16[32,4096]{1,0:T(8,128)(2,1)S(1)} %get-tuple-element.40.off, bf16[32,4096]{1,0:T(8,128)(2,1)S(1)} %get-tuple-element.41.mate, ...), custom_call_target="tpu_custom_call" | custom-call | tf_op jit(solution)/shard_map/first_inner/pallas_call | solution.py:383
  10.9 0.0 collective-permute-done.halo
  10.9 0.7 %first_mate.1 = (bf16[32,16384]{1,0:T(8,128)(2,1)S(1)}, bf16[32,16384]{1,0:T(8,128)(2,1)S(1)}, bf16[32,4096]{1,0:T(8,128)(2,1)S(1)}) custom-call(s32[2,64]{1,0:T(2,128)S(4)} %get-tuple-element.42.cols, f32[64,32,128]{2,1,0:T(8,128)S(1)} %get-tuple-element.43.acc, bf16[32,16384]{1,0:T(8,128)(2,1)S(1)} %get-tuple-element.44.wide_in, ...), custom_call_target="tpu_custom_call", output_to_operand_aliasing={{0}: (2, {})} | custom-call | tf_op jit(solution)/shard_map/first_mate/pallas_call | solution.py:383
  11.6 0.0 copy-start
  11.6 0.0 copy-start.1
  11.6 0.0 copy-start.2
  11.6 0.1 collective-permute-start.2
  11.7 0.6 %collective-permute-done.1.halo = bf16[32,4096]{1,0:T(8,128)(2,1)S(1)} collective-permute-done((bf16[32,4096]{1,0:T(8,128)(2,1)S(1)}, bf16[32,4096]{1,0:T(8,128)(2,1)S(1)}, u32[]{:S(2)}, u32[]{:S(2)}) %collective-permute-start.1) | collective-permute-done | bytes 262176 | tf_op jit(solution)/shard_map/ppermute | solution.py:416
  12.3 0.7 %first_off.1 = (bf16[32,16384]{1,0:T(8,128)(2,1)S(1)}, bf16[32,16384]{1,0:T(8,128)(2,1)S(1)}, bf16[32,4096]{1,0:T(8,128)(2,1)S(1)}) custom-call(s32[2,64]{1,0:T(2,128)S(4)} %get-tuple-element.42.cols, f32[64,32,128]{2,1,0:T(8,128)S(1)} %get-tuple-element.43.acc, ...), custom_call_target="tpu_custom_call", output_to_operand_aliasing={{0}: (2, {}), {1}: (3, {})} | custom-call | tf_op jit(solution)/shard_map/first_off/pallas_call | solution.py:383
  12.9 2.9 %collective-permute-start.3 = (bf16[32,4096]{1,0:T(8,128)(2,1)S(1)}, bf16[32,4096]{1,0:T(8,128)(2,1)S(1)}, u32[]{:S(2)}, u32[]{:S(2)}) collective-permute-start(bf16[32,4096]{1,0:T(8,128)(2,1)S(1)} %get-tuple-element.53), channel_id=1, source_target_pairs={{4,8},{8,4},{12,16},{16,12},{20,24},{24,20},{5,9},{9,5},{13,17},{1... | collective-permute-start | bytes 786440 | tf_op jit(solution)/shard_map/ppermute | solution.py:416
  15.9 0.0 copy-done
  15.9 0.0 copy-done.1
  15.9 0.0 copy-done.2
  15.9 1.6 %second_inner.1 = (f32[64,32,128]{2,1,0:T(8,128)S(1)}, f32[64,128]{1,0:T(8,128)S(1)}, f32[128,128]{1,0:T(8,128)S(1)}, f32[128,128]{1,0:T(8,128)S(1)}, f32[32,64]{1,0:T(8,128)S(1)}) custom-call(s32[2,64]{1,0:T(2,128)S(4)} %get-tuple-element.42.cols, bf16[32,16384]{1,0:T(8,128)(2,1)S(1)} %get-tuple-element.48.wide.wide_in, ...), custom_call_target="tpu_custom_call" | custom-call | tf_op jit(solution)/shard_map/second_inner/pallas_call | solution.py:383
  17.5 0.0 collective-permute-done.2.halo
  17.5 0.8 %second_mate.1 = (bf16[32,16384]{1,0:T(8,128)(2,1)S(1)}, bf16[32,4096]{1,0:T(8,128)(2,1)S(1)}, f32[32,128]{1,0:T(8,128)S(1)}) custom-call(s32[2,64]{1,0:T(2,128)S(4)} %get-tuple-element.42.cols, f32[64,32,128]{2,1,0:T(8,128)S(1)} %get-tuple-element.50.acc, bf16[32,16384]{1,0:T(8,128)(2,1)S(1)} %get-tuple-element.48.wide.wide_in, ...), custom_call_target="tpu_custom_call", output_to_operand_aliasing={{0}: (2, {})} | custom-call | tf_op jit(solution)/shard_map/second_mate/pallas_call | solution.py:383
  18.2 3.6 %collective-permute-done.3.halo = bf16[32,4096]{1,0:T(8,128)(2,1)S(1)} collective-permute-done((bf16[32,4096]{1,0:T(8,128)(2,1)S(1)}, bf16[32,4096]{1,0:T(8,128)(2,1)S(1)}, u32[]{:S(2)}, u32[]{:S(2)}) %collective-permute-start.3) | collective-permute-done | bytes 262176 | tf_op jit(solution)/shard_map/ppermute | solution.py:416
  21.9 0.7 %second_off.1 = (bf16[32,16384]{1,0:T(8,128)(2,1)S(1)}, bf16[32,4096]{1,0:T(8,128)(2,1)S(1)}, f32[128,128]{1,0:T(8,128)S(1)}, bf16[128,128]{1,0:T(8,128)(2,1)S(1)}) custom-call(s32[2,64]{1,0:T(2,128)S(4)} %get-tuple-element.42.cols, f32[64,32,128]{2,1,0:T(8,128)S(1)} %get-tuple-element.50.acc, ...), custom_call_target="tpu_custom_call", output_to_operand_aliasing={{0}: (2, {})} | custom-call | tf_op jit(solution)/shard_map/second_off/pallas_call | solution.py:383
  22.6 4.9 %collective-permute-start.6 = (bf16[128,128]{1,0:T(8,128)(2,1)S(1)}, bf16[128,128]{1,0:T(8,128)(2,1)S(1)}, u32[]{:S(2)}, u32[]{:S(2)}) collective-permute-start(bf16[128,128]{1,0:T(8,128)(2,1)S(1)} %get-tuple-element.62), channel_id=1, source_target_pairs={{0,3},{1,2},{2,1},{3,0},{4,7},{5,6},{6,5},{7,4},{8,11},{9,10},{10,... | collective-permute-start | bytes 98312 | tf_op jit(solution)/shard_map/ppermute | solution.py:467
  27.5 0.0 collective-permute-start.5
  27.5 0.4 collective-permute-start.4
  27.9 0.9 %collective-permute-done.6.rest_2_ = bf16[128,128]{1,0:T(8,128)(2,1)S(1)} collective-permute-done((bf16[128,128]{1,0:T(8,128)(2,1)S(1)}, bf16[128,128]{1,0:T(8,128)(2,1)S(1)}, u32[]{:S(2)}, u32[]{:S(2)}) %collective-permute-start.6) | collective-permute-done | bytes 32800 | tf_op jit(solution)/shard_map/ppermute | solution.py:467
  28.8 2.4 %collective-permute-done.5.rest_1_ = bf16[128,128]{1,0:T(8,128)(2,1)S(1)} collective-permute-done((bf16[128,128]{1,0:T(8,128)(2,1)S(1)}, bf16[128,128]{1,0:T(8,128)(2,1)S(1)}, u32[]{:S(2)}, u32[]{:S(2)}) %collective-permute-start.5) | collective-permute-done | bytes 32800 | tf_op jit(solution)/shard_map/ppermute | solution.py:467
  31.2 0.0 collective-permute-done.4.rest_0_
  31.2 0.7 %residual_rim.1 = (f32[128,128]{1,0:T(8,128)S(1)}, f32[64,128]{1,0:T(8,128)S(1)}, f32[96,128]{1,0:T(8,128)S(1)}, f32[32,64]{1,0:T(8,128)S(1)}) custom-call(s32[2,64]{1,0:T(2,128)S(1)} %bitcast.2, f32[128,128]{1,0:T(8,128)S(1)} %get-tuple-element.56.inc, f32[128,128]{1,0:T(8,128)S(1)} %get-tuple-element.57.innov, f32[128,128]{1,0:T(8,128)S(1)} %get-tuple-element.58.prec, ...), custom_call_target="tpu_custom_call" | custom-call | tf_op jit(solution)/shard_map/residual_rim/pallas_call | solution.py:383
  31.9 0.0 collective-permute-start.8
  31.9 4.8 %collective-permute-start.7 = (f32[64,128]{1,0:T(8,128)S(1)}, f32[64,128]{1,0:T(8,128)S(1)}, u32[]{:S(2)}, u32[]{:S(2)}) collective-permute-start(f32[64,128]{1,0:T(8,128)S(1)} %get-tuple-element.64.own_off), channel_id=1, source_target_pairs={{4,8},{8,4},{12,16},{16,12},{20,24},{24,20},{5,9},{9,5},{13,17},{1... | collective-permute-start | bytes 98312 | tf_op jit(solution)/shard_map/ppermute | solution.py:416
  36.7 0.0 collective-permute-done.8.mate
  36.7 2.8 %collective-permute-start.10 = (f32[32,128]{1,0:T(8,128)S(1)}, f32[32,128]{1,0:T(8,128)S(1)}, u32[]{:S(2)}, u32[]{:S(2)}) collective-permute-start(f32[32,128]{1,0:T(8,128)S(1)} %slice_add_fusion), channel_id=1, source_target_pairs={{0,8},{4,12},{8,0},{12,4},{16,24},{20,28},{24,16},{28,20},{1,9},{5... | collective-permute-start | bytes 49160 | tf_op jit(solution)/shard_map/ppermute | solution.py:419
  39.6 0.7 %residual_inner.1.y = f32[128,128]{1,0:T(8,128)S(1)} custom-call(f32[128,128]{1,0:T(8,128)S(1)} %get-tuple-element.63.res, bf16[64,3,128,128]{3,2,1,0:T(8,128)(2,1)S(1)} %get-tuple-element.45.ops), custom_call_target="tpu_custom_call" | custom-call | tf_op jit(solution)/shard_map/residual_inner/pallas_call | solution.py:383
  40.2 0.0 collective-permute-done.7.off
  40.2 0.0 copy-done.4
  40.2 0.8 %adjoint_off.1 = (bf16[1024,128]{1,0:T(8,128)(2,1)S(1)}, f32[64,32,128]{2,1,0:T(8,128)S(1)}, bf16[32,32,128]{2,1,0:T(8,128)(2,1)S(1)}, bf16[256,128]{1,0:T(8,128...) custom-call(s32[2,64]{1,0:T(2,128)S(4)} %get-tuple-element.42.cols, s32[2,64]{1,0:T(2,128)S(1)} %bitcast.3, ...), custom_call_target="tpu_custom_call" | custom-call | tf_op jit(solution)/shard_map/adjoint_off/pallas_call | solution.py:383
  41.0 1.9 %collective-permute-start.9 = (bf16[32,32,128]{2,1,0:T(8,128)(2,1)S(1)}, bf16[32,32,128]{2,1,0:T(8,128)(2,1)S(1)}, u32[]{:S(2)}, u32[]{:S(2)}) collective-permute-start(bf16[32,32,128]{2,1,0:T(8,128)(2,1)S(1)} %get-tuple-element.73), channel_id=1, source_target_pairs={{4,8},{8,4},{12,16},{16,12},{20,24},{24,20},{5,9},{9,5},{13,17},{1... | collective-permute-start | bytes 786440 | tf_op jit(solution)/shard_map/ppermute | solution.py:416
  42.9 0.6 %adjoint_mate.1 = (bf16[1024,128]{1,0:T(8,128)(2,1)S(1)}, f32[64,32,128]{2,1,0:T(8,128)S(1)}, bf16[32,32,128]{2,1,0:T(8,128)(2,1)S(1)}) custom-call(s32[2,64]{1,0:T(2,128)S(4)} %get-tuple-element.42.cols, f32[32,256]{1,0:T(8,128)S(1)} %get-tuple-element.67.wp, s32[1,256]{1,0:T(1,128)S(1)} %get-tuple-element.68.tgt, ...), custom_call_target="tpu_custom_call" | custom-call | tf_op jit(solution)/shard_map/adjoint_mate/pallas_call | solution.py:383
  43.6 0.0 collective-permute-done.10
  43.6 0.1 collective-permute-start.11
  43.7 2.7 %collective-permute-start.12 = (f32[32,128]{1,0:T(8,128)S(1)}, f32[32,128]{1,0:T(8,128)S(1)}, u32[]{:S(2)}, u32[]{:S(2)}) collective-permute-start(f32[32,128]{1,0:T(8,128)S(1)} %add.10), channel_id=1, source_target_pairs={{0,16},{4,20},{8,24},{12,28},{16,0},{20,4},{24,8},{28,12},{1,17},{... | collective-permute-start | bytes 49160 | tf_op jit(solution)/shard_map/ppermute | solution.py:419
  46.4 0.9 %adjoint_inner.1.own = f32[64,32,128]{2,1,0:T(8,128)S(1)} custom-call(s32[2,64]{1,0:T(2,128)S(4)} %get-tuple-element.42.cols, bf16[1024,128]{1,0:T(8,128)(2,1)S(1)} %get-tuple-element.66.mid_off, bf16[1024,128]{1,0:T(8,128)(2,1)S(1)} %get-tuple-element.70.mid_mate, f32[64,32,128]{2,1,0:T(8,128)S(1)} %get-tuple-element.71.sums_off, ...), custom_call_target="tpu_custom_call" | custom-call | tf_op jit(solution)/shard_map/adjoint_inner/pallas_call | solution.py:383
  47.3 0.2 collective-permute-done.12
  47.5 2.5 %collective-permute-done.9.off = bf16[32,32,128]{2,1,0:T(8,128)(2,1)S(1)} collective-permute-done((bf16[32,32,128]{2,1,0:T(8,128)(2,1)S(1)}, bf16[32,32,128]{2,1,0:T(8,128)(2,1)S(1)}, u32[]{:S(2)}, u32[]{:S(2)}) %collective-permute-start.9) | collective-permute-done | bytes 262176 | tf_op jit(solution)/shard_map/ppermute | solution.py:416
  50.0 0.0 collective-permute-done.11.mate
  50.0 1.2 %finish.1 = (f32[32,8192]{1,0:T(8,128)}, f32[32,64]{1,0:T(8,128)}) custom-call(f32[64,32,128]{2,1,0:T(8,128)S(1)} %adjoint_inner.1.own, bf16[32,32,128]{2,1,0:T(8,128)(2,1)S(1)} %collective-permute-done.9.off, bf16[32,32,128]{2,1,0:T(8,128)(2,1)S(1)} %collective-permute-done.11.mate, f32[32,64]{1,0:T(8,128)S(1)} %get-tuple-element.76.gw, ...), custom_call_target="tpu_custom_call" | custom-call | tf_op jit(solution)/shard_map/finish/pallas_call | solution.py:383
  (4 shorter events, 0.0 us)
Async XLA Ops:
  1.7 9.2 %collective-permute-start = (bf16[32,4096]{1,0:T(8,128)(2,1)S(1)}, bf16[32,4096]{1,0:T(8,128)(2,1)S(1)}, u32[]{:S(2)}, u32[]{:S(2)}) collective-permute-start(bf16[32,4096]{1,0:T(8,128)(2,1)S(1)} %get-tuple-element.41.mate), channel_id=1, source_target_pairs={{0,4},{4,0},{8,12},{12,8},{16,20},{20,16},{24,28},{28,24},{1,5},{5... | collective-permute-start | bytes 786440 | tf_op jit(solution)/shard_map/ppermute | solution.py:413
  1.8 10.4 %collective-permute-start.1 = (bf16[32,4096]{1,0:T(8,128)(2,1)S(1)}, bf16[32,4096]{1,0:T(8,128)(2,1)S(1)}, u32[]{:S(2)}, u32[]{:S(2)}) collective-permute-start(bf16[32,4096]{1,0:T(8,128)(2,1)S(1)} %get-tuple-element.40.off), channel_id=1, source_target_pairs={{4,8},{8,4},{12,16},{16,12},{20,24},{24,20},{5,9},{9,5},{13,17},{1... | collective-permute-start | bytes 786440 | tf_op jit(solution)/shard_map/ppermute | solution.py:416
  6.3 0.7 %copy-start.3 = (s32[64,2]{0,1:T(2,128)S(1)}, s32[64,2]{0,1:T(2,128)}, u32[]{:S(2)}) copy-start(s32[64,2]{0,1:T(2,128)} %param.8) | copy-start | bytes 1540
  11.6 4.3 %copy-start = (f32[2,8192]{1,0:T(2,128)S(1)}, f32[2,8192]{1,0:T(2,128)}, u32[]{:S(2)}) copy-start(f32[2,8192]{1,0:T(2,128)} %innov.1) | copy-start | bytes 196612
  11.6 4.3 %copy-start.1 = (f32[2,8192]{1,0:T(2,128)S(1)}, f32[2,8192]{1,0:T(2,128)}, u32[]{:S(2)}) copy-start(f32[2,8192]{1,0:T(2,128)} %prec.1) | copy-start | bytes 196612
  11.6 4.3 %copy-start.2 = (f32[32,64]{1,0:T(8,128)S(1)}, f32[32,64]{1,0:T(8,128)}, u32[]{:S(2)}) copy-start(f32[32,64]{1,0:T(8,128)} %w.1) | copy-start | bytes 24580
  11.6 5.9 %collective-permute-start.2 = (bf16[32,4096]{1,0:T(8,128)(2,1)S(1)}, bf16[32,4096]{1,0:T(8,128)(2,1)S(1)}, u32[]{:S(2)}, u32[]{:S(2)}) collective-permute-start(bf16[32,4096]{1,0:T(8,128)(2,1)S(1)} %get-tuple-element.51), channel_id=1, source_target_pairs={{0,4},{4,0},{8,12},{12,8},{16,20},{20,16},{24,28},{28,24},{1,5},{5... | collective-permute-start | bytes 786440 | tf_op jit(solution)/shard_map/ppermute | solution.py:413
  12.9 8.9 %collective-permute-start.3 = (bf16[32,4096]{1,0:T(8,128)(2,1)S(1)}, bf16[32,4096]{1,0:T(8,128)(2,1)S(1)}, u32[]{:S(2)}, u32[]{:S(2)}) collective-permute-start(bf16[32,4096]{1,0:T(8,128)(2,1)S(1)} %get-tuple-element.53), channel_id=1, source_target_pairs={{4,8},{8,4},{12,16},{16,12},{20,24},{24,20},{5,9},{9,5},{13,17},{1... | collective-permute-start | bytes 786440 | tf_op jit(solution)/shard_map/ppermute | solution.py:416
  22.6 6.2 %collective-permute-start.6 = (bf16[128,128]{1,0:T(8,128)(2,1)S(1)}, bf16[128,128]{1,0:T(8,128)(2,1)S(1)}, u32[]{:S(2)}, u32[]{:S(2)}) collective-permute-start(bf16[128,128]{1,0:T(8,128)(2,1)S(1)} %get-tuple-element.62), channel_id=1, source_target_pairs={{0,3},{1,2},{2,1},{3,0},{4,7},{5,6},{6,5},{7,4},{8,11},{9,10},{10,... | collective-permute-start | bytes 98312 | tf_op jit(solution)/shard_map/ppermute | solution.py:467
  27.5 3.7 %collective-permute-start.5 = (bf16[128,128]{1,0:T(8,128)(2,1)S(1)}, bf16[128,128]{1,0:T(8,128)(2,1)S(1)}, u32[]{:S(2)}, u32[]{:S(2)}) collective-permute-start(bf16[128,128]{1,0:T(8,128)(2,1)S(1)} %get-tuple-element.62), channel_id=1, source_target_pairs={{0,2},{1,3},{2,0},{3,1},{4,6},{5,7},{6,4},{7,5},{8,10},{9,11},{10,... | collective-permute-start | bytes 98312 | tf_op jit(solution)/shard_map/ppermute | solution.py:467
  27.5 3.7 %collective-permute-start.4 = (bf16[128,128]{1,0:T(8,128)(2,1)S(1)}, bf16[128,128]{1,0:T(8,128)(2,1)S(1)}, u32[]{:S(2)}, u32[]{:S(2)}) collective-permute-start(bf16[128,128]{1,0:T(8,128)(2,1)S(1)} %get-tuple-element.62), channel_id=1, source_target_pairs={{0,1},{1,0},{2,3},{3,2},{4,5},{5,4},{6,7},{7,6},{8,9},{9,8},{10,11... | collective-permute-start | bytes 98312 | tf_op jit(solution)/shard_map/ppermute | solution.py:467
  31.2 9.0 %copy-start.4 = (s32[64,2]{0,1:T(2,128)S(1)}, s32[64,2]{0,1:T(2,128)}, u32[]{:S(2)}) copy-start(s32[64,2]{0,1:T(2,128)} %param.8) | copy-start | bytes 1540
  31.9 4.8 %collective-permute-start.8 = (f32[96,128]{1,0:T(8,128)S(1)}, f32[96,128]{1,0:T(8,128)S(1)}, u32[]{:S(2)}, u32[]{:S(2)}) collective-permute-start(f32[96,128]{1,0:T(8,128)S(1)} %get-tuple-element.65.own_mate), channel_id=1, source_target_pairs={{0,4},{4,0},{8,12},{12,8},{16,20},{20,16},{24,28},{28,24},{1,5},{5... | collective-permute-start | bytes 147464 | tf_op jit(solution)/shard_map/ppermute | solution.py:413
  31.9 8.3 %collective-permute-start.7 = (f32[64,128]{1,0:T(8,128)S(1)}, f32[64,128]{1,0:T(8,128)S(1)}, u32[]{:S(2)}, u32[]{:S(2)}) collective-permute-start(f32[64,128]{1,0:T(8,128)S(1)} %get-tuple-element.64.own_off), channel_id=1, source_target_pairs={{4,8},{8,4},{12,16},{16,12},{20,24},{24,20},{5,9},{9,5},{13,17},{1... | collective-permute-start | bytes 98312 | tf_op jit(solution)/shard_map/ppermute | solution.py:416
  36.7 6.9 %collective-permute-start.10 = (f32[32,128]{1,0:T(8,128)S(1)}, f32[32,128]{1,0:T(8,128)S(1)}, u32[]{:S(2)}, u32[]{:S(2)}) collective-permute-start(f32[32,128]{1,0:T(8,128)S(1)} %slice_add_fusion), channel_id=1, source_target_pairs={{0,8},{4,12},{8,0},{12,4},{16,24},{20,28},{24,16},{28,20},{1,9},{5... | collective-permute-start | bytes 49160 | tf_op jit(solution)/shard_map/ppermute | solution.py:419
  41.0 9.0 %collective-permute-start.9 = (bf16[32,32,128]{2,1,0:T(8,128)(2,1)S(1)}, bf16[32,32,128]{2,1,0:T(8,128)(2,1)S(1)}, u32[]{:S(2)}, u32[]{:S(2)}) collective-permute-start(bf16[32,32,128]{2,1,0:T(8,128)(2,1)S(1)} %get-tuple-element.73), channel_id=1, source_target_pairs={{4,8},{8,4},{12,16},{16,12},{20,24},{24,20},{5,9},{9,5},{13,17},{1... | collective-permute-start | bytes 786440 | tf_op jit(solution)/shard_map/ppermute | solution.py:416
  43.6 6.4 %collective-permute-start.11 = (bf16[32,32,128]{2,1,0:T(8,128)(2,1)S(1)}, bf16[32,32,128]{2,1,0:T(8,128)(2,1)S(1)}, u32[]{:S(2)}, u32[]{:S(2)}) collective-permute-start(bf16[32,32,128]{2,1,0:T(8,128)(2,1)S(1)} %get-tuple-element.75), channel_id=1, source_target_pairs={{0,4},{4,0},{8,12},{12,8},{16,20},{20,16},{24,28},{28,24},{1,5},{5... | collective-permute-start | bytes 786440 | tf_op jit(solution)/shard_map/ppermute | solution.py:413
  43.7 3.8 %collective-permute-start.12 = (f32[32,128]{1,0:T(8,128)S(1)}, f32[32,128]{1,0:T(8,128)S(1)}, u32[]{:S(2)}, u32[]{:S(2)}) collective-permute-start(f32[32,128]{1,0:T(8,128)S(1)} %add.10), channel_id=1, source_target_pairs={{0,16},{4,20},{8,24},{12,28},{16,0},{20,4},{24,8},{28,12},{1,17},{... | collective-permute-start | bytes 49160 | tf_op jit(solution)/shard_map/ppermute | solution.py:419

commit v5 on v4

--- a/solution.py
+++ b/solution.py
@@ -59,17 +59,36 @@
         lax.fori_loop(0, total // unroll, step, 0)
 
 
-def load(ens, off, mate, sems):
+def split_terms(value):
+    high = value.astype(BF16)
+    return high, (value - high.astype(F32)).astype(BF16)
+
+
+def as_column(row):
+    count = row.shape[1]
+    shape = (count, count)
+    on = lax.broadcasted_iota(I32, shape, 0) == lax.broadcasted_iota(I32, shape, 1)
+    return jnp.sum(jnp.where(on, jnp.broadcast_to(row.astype(F32), shape), 0.0), axis=1, keepdims=True)
+
+
+def load(ens, w_far, cols_far, off, mate, w, cols, sems):
     size = ens.shape[1] // (2 * REACH)
     sides = Sides(2 * REACH)
     width = REACH * size
     copies = []
-    for n, (row, out) in enumerate(((sides.off_row, off), (sides.mate_row, mate))):
+    for n, (row, out) in enumerate(((sides.off_row, off.at[:, :width]), (sides.mate_row, mate))):
         source = ens.at[:, pl.ds(pl.multiple_of(row * size, size), width)]
         copies.append(pltpu.make_async_copy(source, out, sems.at[n]))
-        copies[-1].start()
+    copies.append(pltpu.make_async_copy(w_far, w, sems.at[2]))
+    copies.append(pltpu.make_async_copy(cols_far, cols, sems.at[3]))
     for copy in copies:
+        copy.start()
+    for copy in reversed(copies):
         copy.wait()
+    high, low = split_terms(sides.pick(w[:, :REACH], w[:, REACH:])[0])
+    col = sides.pick(cols[:1, :REACH], cols[1:, REACH:])[0]
+    spread = [jnp.broadcast_to(part.astype(F32), high.shape).astype(BF16) for part in (col >> 8, col & 255)]
+    off[:, width:] = jnp.concatenate([high, low] + spread, 1)
 
 
 def inner(cols, wide, ops, acc, sides, ready=None):
@@ -106,7 +125,7 @@
     for k in range(cols.shape[0]):
         for r in range(rows):
             cols[k, r] = cols_in[k, r]
-    wide[:, REACH * size : 2 * REACH * size] = off[...]
+    wide[:, REACH * size : 2 * REACH * size] = off[:, : REACH * size]
     wide[:, 2 * REACH * size : 3 * REACH * size] = mate[...]
     inner(cols, wide, ops, acc, sides, lambda part: copies[part].wait())
 
@@ -128,6 +147,7 @@
 
 def first_mate(cols, acc, wide_in, halo, ops, wide, out, send):
     size = ops.shape[2]
+    out[:, : REACH * size] = jnp.zeros_like(halo)
     wide[:, 3 * REACH * size :] = halo[...]
 
     def store(i, o):
@@ -137,15 +157,27 @@
     rim(cols, acc, wide, ops, Sides(ops.shape[0]), True, store)
 
 
-def first_off(cols, acc, wide_in, out_in, halo, ops, wide, out, send):
+def first_off(cols, acc, wide_in, out_in, halo, ops, wide, out, send, slot):
     size = ops.shape[2]
-    wide[:, : REACH * size] = halo[...]
+    width = REACH * size
+    sides = Sides(ops.shape[0])
+    wide[:, :width] = halo[:, :width]
+    facts = halo[:, width:].astype(F32)
+    weights = facts[:, :REACH] + facts[:, REACH : 2 * REACH]
+    col = as_column(facts[:1, 2 * REACH : 3 * REACH] * 256.0 + facts[:1, 3 * REACH : 4 * REACH]).astype(I32)
+    place = sides.place(col) - REACH
+    place = jnp.where((place >= 0) & (place < REACH), place, -1)
+    slot[...] = jnp.broadcast_to(place, slot.shape)
 
     def store(i, o):
         lanes(out, REACH + i, size)[...] = o
-        lanes(send, i, size)[...] = o
-
-    rim(cols, acc, wide, ops, Sides(ops.shape[0]), False, store)
+
+    rim(cols, acc, wide, ops, sides, False, store)
+    for p in range(REACH):
+        at = slot[p, 0]
+        x = lanes(out, REACH + jnp.maximum(at, 0), size)[...].astype(F32)
+        part = jnp.sum(x * weights[:, p : p + 1], axis=0, keepdims=True)
+        send[p : p + 1, :] = jnp.where(at >= 0, part, 0.0)
 
 
 def turned(sides, w):
@@ -159,7 +191,7 @@
         store(i, jnp.sum(x * w[:, first + i : first + i + 1], axis=0, keepdims=True))
 
 
-def second_inner(cols, wide, ops, w, innov, prec, acc, inc, innov_rows, prec_rows, w_turned):
+def second_inner(cols, wide, ops, w, innov, prec, acc, inc, innov_rows, prec_rows, w_turned, two_off, inc_off):
     rows, _, size, _ = ops.shape
     sides = Sides(rows)
     inner(cols, wide, ops, acc, sides)
@@ -177,6 +209,16 @@
 
     member_sums(wide, REACH, weights, 0, rows, size, store)
 
+    def keep_row(i, o):
+        lanes(two_off, i, size)[...] = o
+
+    rim(cols, acc, wide, ops, sides, False, keep_row)
+
+    def keep(i, s):
+        inc_off[i : i + 1, :] = s
+
+    member_sums(two_off, 0, weights, 0, REACH, size, keep)
+
 
 def second_mate(cols, acc, wide_in, halo, ops, w, wide, out, inc):
     size = ops.shape[2]
@@ -193,21 +235,17 @@
     member_sums(out, 0, w, REACH, REACH, size, keep)
 
 
-def second_off(cols, acc, wide_in, halo, ops, w, inc_one, inc_mate, wide, out, inc, send):
-    rows, _, size, _ = ops.shape
-    wide[:, : REACH * size] = halo[...]
-
-    def store(i, o):
-        lanes(out, i, size)[...] = o
-
-    rim(cols, acc, wide, ops, Sides(rows), False, store)
-
-    def keep(i, s):
-        inc[rows + i : rows + i + 1, :] = s
-
-    member_sums(out, 0, w, 0, REACH, size, keep)
+def second_off(halo, ops, inc_one, inc_off, inc_mate, inc, send):
+    rows, _, size, _ = ops.shape
+    sides = Sides(rows)
     inc[:rows, :] = inc_one[...]
     inc[rows + REACH :, :] = inc_mate[...]
+    parts = []
+    for i in range(REACH):
+        row = jnp.broadcast_to(halo[i : i + 1, :], (8, size)).astype(BF16)
+        parts.append(dot_t(row, ops[sides.off_row + i, sides.off_k]))
+    for i, part in enumerate(parts):
+        inc[rows + i : rows + i + 1, :] = inc_off[i : i + 1, :] + part[:1]
     send[...] = inc[...].astype(BF16)
 
 
@@ -257,7 +295,7 @@
         grown = jnp.where(index == q, jnp.sum(prod, axis=1, keepdims=True), grown)
     grown = w[...] + SCALE * grown
     gw[...] = grown
-    send_mate[REACH + members :, :] = jnp.broadcast_to(jnp.sum(grown * grown, axis=1, keepdims=True), (members, size))
+    send_off[REACH : REACH + members, 2 * REACH : 3 * REACH] = grown[:, :REACH]
 
 
 def residual_inner(res, ops, y):
@@ -303,7 +341,7 @@
     chunks(REACH, some)
 
 
-def adjoint_off(cols, col_rows, w, y, own_off, own_mate, off, mate, ops, mid, sums, send, vals, wp, tgt):
+def adjoint_off(cols, col_rows, w, y, own_off, own_mate, off, mate, ops, one, gw, slot, mid, sums, send, vals, wp, tgt, squares):
     rows, _, size, _ = ops.shape
     members = w.shape[0]
     sides = Sides(rows)
@@ -326,7 +364,22 @@
         tgt[:, where] = sides.place(part[REACH : REACH + 1, REACH : 2 * REACH].astype(I32))
     middle(wp[...], tgt[...], vals[...], 0, mid)
     adjoint_side(cols, mid, ops, sides, False, sums)
-    send[...] = sums[:REACH].astype(BF16)
+    send[:REACH] = sums[:REACH].astype(BF16)
+    index = lax.broadcasted_iota(I32, (members, REACH), 1)
+    drawn = jnp.zeros((members, REACH), F32)
+    for p in range(REACH):
+        at = slot[p, 0]
+        x = lanes(one, REACH + jnp.maximum(at, 0), size)[...].astype(F32) * off[p : p + 1, :]
+        part = jnp.where(at >= 0, jnp.sum(x, axis=1, keepdims=True), 0.0)
+        drawn = jnp.where(index == p, part, drawn)
+    drawn = drawn * SCALE
+    high, low = split_terms(drawn)
+    send[REACH] = jnp.concatenate([high, low, jnp.zeros((members, size - 2 * REACH), BF16)], 1)
+    theirs = off[REACH : REACH + members, 2 * REACH : 3 * REACH]
+    grown = gw[...]
+    total = jnp.sum(grown * grown, axis=1, keepdims=True)
+    total = total + jnp.sum((2.0 * theirs + drawn) * drawn, axis=1, keepdims=True)
+    squares[...] = jnp.broadcast_to(total, squares.shape)
 
 
 def adjoint_mate(cols, wp, tgt, vals, ops, mid, sums, send):
@@ -361,8 +414,11 @@
 def finish(own, off, mate, gw, total, out, direction, *, count):
     rows, members, size = own.shape
     sides = Sides(rows)
-    weights = gw[...] / jnp.sqrt(total[:, :1] / count + 1e-06)
-    direction[...] = turned(sides, weights)
+    drawn = off[REACH].astype(F32)
+    grown = gw[...]
+    drawn = drawn[:, :REACH] + drawn[:, REACH : 2 * REACH]
+    grown = jnp.concatenate([grown[:, :REACH] + drawn, grown[:, REACH:]], 1)
+    direction[...] = turned(sides, grown / jnp.sqrt(total[:, :1] / count + 1e-06))
     for row, q, halo in ((sides.off_row, 0, off), (sides.mate_row, REACH, mate)):
         for i in range(REACH):
             lanes(out, row + i, size)[...] = own[q + i] + halo[i].astype(F32)
@@ -425,7 +481,14 @@
     part_kind = ((REACH, size), F32)
     row_kind = ((2 * rows, size), F32)
 
-    off, mate = run(load, [side_kind, side_kind], (far(ensemble),), 0, [sem((2,))], far=1)
+    off, mate = run(
+        load,
+        [((members, halo + 4 * REACH), BF16), side_kind],
+        (far(ensemble), far(weights), far(cols)),
+        0,
+        [pltpu.VMEM((members, rows), F32), pltpu.VMEM(cols.shape, I32), sem((4,))],
+        far=3,
+    )
     from_off, from_mate = to_off(off), to_mate(mate)
     acc, wide, ops, table = run(
         first_inner,
@@ -440,59 +503,62 @@
         first_mate, [wide_kind, wide_kind, side_kind], (table, acc, wide, from_mate, ops), 1, alias={2: 0}
     )
     from_mate = to_mate(send)
-    wide, one, send = run(
+    wide, one, send, slot = run(
         first_off,
-        [wide_kind, wide_kind, side_kind],
+        [wide_kind, wide_kind, part_kind, ((REACH, size), I32)],
         (table, acc, wide, one, from_off, ops),
         1,
         alias={2: 0, 3: 1},
     )
     from_off = to_off(send)
-    acc, inc_one, innov, prec, w = run(
+    acc, inc_one, innov, prec, w, two_off, inc_off = run(
         second_inner,
-        [acc_kind, ((rows, size), F32), row_kind, row_kind, ((members, rows), F32)],
+        [acc_kind, ((rows, size), F32), row_kind, row_kind, ((members, rows), F32), side_kind, part_kind],
         (table, one, ops, weights, innovations, obs_precision),
         1,
     )
     one, two_mate, inc_mate = run(
         second_mate, [wide_kind, side_kind, part_kind], (table, acc, one, from_mate, ops, w), 1, alias={2: 0}
     )
-    one, two_off, inc, send = run(
-        second_off,
-        [wide_kind, side_kind, row_kind, (row_kind[0], BF16)],
-        (table, acc, one, from_off, ops, w, inc_one, inc_mate),
-        1,
-        alias={2: 0},
-    )
+    inc, send = run(second_off, [row_kind, (row_kind[0], BF16)], (from_off, ops, inc_one, inc_off, inc_mate))
     received = [lax.ppermute(send, "members", [(i, i ^ step) for i in range(groups)]) for step in range(1, groups)]
+    pay_kind = ((REACH + members, size), F32)
     res, own_off, own_mate, grad_weights = run(
         residual_rim,
-        [row_kind, ((REACH + members, size), F32), ((REACH + 2 * members, size), F32), ((members, rows), F32)],
+        [row_kind, pay_kind, pay_kind, ((members, rows), F32)],
         (cols, inc, innov, prec, ops, w, one, two_off, two_mate, *received),
     )
     from_off, from_mate = to_off(own_off), to_mate(own_mate)
     (y,) = run(residual_inner, [row_kind], (res, ops))
-    total = own_mate[REACH + members :] + from_mate[REACH + members :]
-    strides = [2**power for power in range(1, tiles.bit_length() - 1)]
-    total = total + partner(total, strides[0])
     pairs = 3 * rows + 2 * REACH
     mid_kind = ((REACH * members, size), BF16)
     sums_kind = ((2 * REACH, members, size), F32)
     send_kind = ((REACH, members, size), BF16)
-    mid_off, sums_off, send, vals, wp, tgt = run(
+    mid_off, sums_off, send, vals, wp, tgt, total = run(
         adjoint_off,
-        [mid_kind, sums_kind, send_kind, ((pairs, size), BF16), ((members, pairs), F32), ((1, pairs), I32)],
-        (table, cols, w, y, own_off, own_mate, from_off, from_mate, ops),
+        [
+            mid_kind,
+            sums_kind,
+            ((REACH + 1, members, size), BF16),
+            ((pairs, size), BF16),
+            ((members, pairs), F32),
+            ((1, pairs), I32),
+            ((members, size), F32),
+        ],
+        (table, cols, w, y, own_off, own_mate, from_off, from_mate, ops, one, grad_weights, slot),
         1,
     )
     from_off = to_off(send)
+    total = total + partner(total, 1)
     mid_mate, sums_mate, send = run(
         adjoint_mate, [mid_kind, sums_kind, send_kind], (table, wp, tgt, vals, ops), 1
     )
     send, total = lax.optimization_barrier((send, total))
-    for stride in strides[1:]:
+    from_mate = to_mate(send)
+    stride = 2
+    while stride < tiles:
         total = total + partner(total, stride)
-    from_mate = to_mate(send)
+        stride *= 2
     (own,) = run(adjoint_inner, [acc_kind], (table, mid_off, mid_mate, sums_off, sums_mate, ops), 1)
     grad_ens, direction = run(
         finish,

time: 52 us -> 52.1 us (level)
  Pallas kernels: 14.2 us -> 15.1 us
  starting transfers between devices: 25.2 us -> 24.3 us
    ppermute x2 -> x3, waiting for transfers between devices: 0.21 us -> 5.73 us  [partner(): return lax.ppermute(value, 'space', [(i, i ^ stride) for i in range(tiles)])]
    ppermute x4, waiting for transfers between devices: 6.7 us -> 1.57 us  [to_off(): return lax.ppermute(value, 'space', offs)]
    ppermute x4, starting transfers between devices: 14.1 us -> 17.2 us  [to_off(): return lax.ppermute(value, 'space', offs)]
    ppermute x2 -> x3, starting transfers between devices: 5.54 us -> 2.64 us  [partner(): return lax.ppermute(value, 'space', [(i, i ^ stride) for i in range(tiles)])]
    ppermute x3, starting transfers between devices: 5.28 us -> 4.15 us  [on_device(): lax.ppermute(send, 'members', [(i, i ^ step) for i in range(groups)])]
    pallas_call x13, Pallas kernels: 14.2 us -> 15.1 us  [run(): pl.pallas_call(functools.partial(body, **fixed) if fixed else body, out_s...]
  transfers between devices with their start and end apart: 13 -> 14, of which waited for: 6 -> 6; matrix products, arithmetic and copies ran while one was open for 0% -> 0% of each run, Pallas kernels for 21% -> 20%
where the time goes in v5:
time: 52.1 us; the launch traced here: 51.6 us
  starting transfers between devices  24.3 us (47%)
  Pallas kernels  15.1 us (29%)
  waiting for transfers between devices  10.6 us (20%)
  between operations  0.87 us (2%)
  local copies, waits for them, and re-layouts  0.7 us (1%)
    ppermute x4, starting transfers between devices, to_off(): return lax.ppermute(value, 'space', offs)  17.2 us
    pallas_call x13, Pallas kernels, run(): pl.pallas_call(functools.partial(body, **fixed) if fixed else body, out_s...  15.1 us
    ppermute x3, waiting for transfers between devices, partner(): return lax.ppermute(value, 'space', [(i, i ^ stride) for i in range(tiles)])  5.73 us
    ppermute x3, starting transfers between devices, on_device(): lax.ppermute(send, 'members', [(i, i ^ step) for i in range(groups)])  4.15 us
    ppermute x3, waiting for transfers between devices, on_device(): lax.ppermute(send, 'members', [(i, i ^ step) for i in range(groups)])  3.31 us
    ppermute x3, starting transfers between devices, partner(): return lax.ppermute(value, 'space', [(i, i ^ stride) for i in range(tiles)])  2.64 us
    ppermute x4, waiting for transfers between devices, to_off(): return lax.ppermute(value, 'space', offs)  1.57 us
  transfers between devices with their start and end apart: 14, of which 6 were waited for; matrix products, arithmetic and copies ran while one was open for 0% of the time, Pallas kernels for 20%

profile of v5, /device:TPU:1, one launch (start us, length us, event | category | flops | bytes accessed | tf_op | source)
XLA Modules:
  0.0 51.6 jit_solution(15273081385417946548)
XLA Ops:
  0.6 1.2 %load.1 = (bf16[32,4224]{1,0:T(8,128)(2,1)S(1)}, bf16[32,4096]{1,0:T(8,128)(2,1)S(1)}) custom-call(bf16[32,8192]{1,0:T(8,128)(2,1)} %ens.1, f32[32,64]{1,0:T(8,128)} %w.1, s32[2,64]{1,0:T(2,128)} %bitcast.1), custom_call_target="tpu_custom_call" | custom-call | tf_op jit(solution)/shard_map/load/pallas_call | solution.py:439
  1.9 0.1 collective-permute-start
  2.0 4.5 %collective-permute-start.1 = (bf16[32,4224]{1,0:T(8,128)(2,1)S(1)}, bf16[32,4224]{1,0:T(8,128)(2,1)S(1)}, u32[]{:S(2)}, u32[]{:S(2)}) collective-permute-start(bf16[32,4224]{1,0:T(8,128)(2,1)S(1)} %get-tuple-element.42.off), channel_id=1, source_target_pairs={{4,8},{8,4},{12,16},{16,12},{20,24},{24,20},{5,9},{9,5},{13,17},{1... | collective-permute-start | bytes 811016 | tf_op jit(solution)/shard_map/ppermute | solution.py:472
  6.5 0.0 copy-start.3
  6.5 0.7 %copy-done.3 = s32[64,2]{0,1:T(2,128)S(1)} copy-done((s32[64,2]{0,1:T(2,128)S(1)}, s32[64,2]{0,1:T(2,128)}, u32[]{:S(2)}) %copy-start.3) | copy-done | bytes 536
  7.1 3.9 %first_inner.1 = (f32[64,32,128]{2,1,0:T(8,128)S(1)}, bf16[32,16384]{1,0:T(8,128)(2,1)S(1)}, bf16[64,3,128,128]{3,2,1,0:T(8,128)(2,1)S(1)}, s32[2,64]{1,0:T(2,128)S(4)}) custom-call(s32[2,64]{1,0:T(2,128)S(1)} %bitcast.2, bf16[32,4224]{1,0:T(8,128)(2,1)S(1)} %get-tuple-element.42.off, bf16[32,4096]{1,0:T(8,128)(2,1)S(1)} %get-tuple-element.43.mate, ...), custom_call_target="tpu_custom_call" | custom-call | tf_op jit(solution)/shard_map/first_inner/pallas_call | solution.py:439
  11.1 0.0 collective-permute-done.halo
  11.1 0.7 %first_mate.1 = (bf16[32,16384]{1,0:T(8,128)(2,1)S(1)}, bf16[32,16384]{1,0:T(8,128)(2,1)S(1)}, bf16[32,4096]{1,0:T(8,128)(2,1)S(1)}) custom-call(s32[2,64]{1,0:T(2,128)S(4)} %get-tuple-element.44.cols, f32[64,32,128]{2,1,0:T(8,128)S(1)} %get-tuple-element.45.acc, bf16[32,16384]{1,0:T(8,128)(2,1)S(1)} %get-tuple-element.46.wide_in, ...), custom_call_target="tpu_custom_call", output_to_operand_aliasing={{0}: (2, {})} | custom-call | tf_op jit(solution)/shard_map/first_mate/pallas_call | solution.py:439
  11.8 0.0 copy-start.1
  11.8 0.0 copy-start.2
  11.8 0.1 collective-permute-start.3
  11.9 0.7 %collective-permute-done.1.halo = bf16[32,4224]{1,0:T(8,128)(2,1)S(1)} collective-permute-done((bf16[32,4224]{1,0:T(8,128)(2,1)S(1)}, bf16[32,4224]{1,0:T(8,128)(2,1)S(1)}, u32[]{:S(2)}, u32[]{:S(2)}) %collective-permute-start.1) | collective-permute-done | bytes 270368 | tf_op jit(solution)/shard_map/ppermute | solution.py:472
  12.6 0.8 %first_off.1 = (bf16[32,16384]{1,0:T(8,128)(2,1)S(1)}, bf16[32,16384]{1,0:T(8,128)(2,1)S(1)}, f32[32,128]{1,0:T(8,128)S(1)}, s32[32,128]{1,0:T(8,128)S(1)}) custom-call(s32[2,64]{1,0:T(2,128)S(4)} %get-tuple-element.44.cols, f32[64,32,128]{2,1,0:T(8,128)S(1)} %get-tuple-element.45.acc, ...), custom_call_target="tpu_custom_call", output_to_operand_aliasing={{0}: (2, {}), {1}: (3, {})} | custom-call | tf_op jit(solution)/shard_map/first_off/pallas_call | solution.py:439
  13.4 2.8 %collective-permute-start.2 = (f32[32,128]{1,0:T(8,128)S(1)}, f32[32,128]{1,0:T(8,128)S(1)}, u32[]{:S(2)}, u32[]{:S(2)}) collective-permute-start(f32[32,128]{1,0:T(8,128)S(1)} %get-tuple-element.52), channel_id=1, source_target_pairs={{4,8},{8,4},{12,16},{16,12},{20,24},{24,20},{5,9},{9,5},{13,17},{1... | collective-permute-start | bytes 49160 | tf_op jit(solution)/shard_map/ppermute | solution.py:472
  16.2 0.0 copy-done
  16.2 0.0 copy-done.1
  16.2 2.2 %second_inner.1 = (f32[64,32,128]{2,1,0:T(8,128)S(1)}, f32[64,128]{1,0:T(8,128)S(1)}, f32[128,128]{1,0:T(8,128)S(1)}, f32[128,128]{1,0:T(8,128)S(1)}, f32[32,64]...) custom-call(s32[2,64]{1,0:T(2,128)S(4)} %get-tuple-element.44.cols, ...), custom_call_target="tpu_custom_call" | custom-call | tf_op jit(solution)/shard_map/second_inner/pallas_call | solution.py:439
  18.4 0.0 collective-permute-done.3.halo
  18.4 0.0 copy-start.4
  18.4 0.7 %second_mate.1 = (bf16[32,16384]{1,0:T(8,128)(2,1)S(1)}, bf16[32,4096]{1,0:T(8,128)(2,1)S(1)}, f32[32,128]{1,0:T(8,128)S(1)}) custom-call(s32[2,64]{1,0:T(2,128)S(4)} %get-tuple-element.44.cols, f32[64,32,128]{2,1,0:T(8,128)S(1)} %get-tuple-element.55.acc, bf16[32,16384]{1,0:T(8,128)(2,1)S(1)} %get-tuple-element.50.wide.wide_in, ...), custom_call_target="tpu_custom_call", output_to_operand_aliasing={{0}: (2, {})} | custom-call | tf_op jit(solution)/shard_map/second_mate/pallas_call | solution.py:439
  19.2 0.0 collective-permute-done.2.halo
  19.2 0.7 %second_off.1 = (f32[128,128]{1,0:T(8,128)S(1)}, bf16[128,128]{1,0:T(8,128)(2,1)S(1)}) custom-call(f32[32,128]{1,0:T(8,128)S(1)} %collective-permute-done.2.halo, bf16[64,3,128,128]{3,2,1,0:T(8,128)(2,1)S(1)} %get-tuple-element.47.ops, f32[64,128]{1,0:T(8,128)S(1)} %get-tuple-element.53.inc_one, f32[32,128]{1,0:T(8,128)S(1)} %get-tuple-element.54.inc_off, ...), custom_call_target="tpu_custom_call" | custom-call | tf_op jit(solution)/shard_map/second_off/pallas_call | solution.py:439
  19.8 3.8 %collective-permute-start.6 = (bf16[128,128]{1,0:T(8,128)(2,1)S(1)}, bf16[128,128]{1,0:T(8,128)(2,1)S(1)}, u32[]{:S(2)}, u32[]{:S(2)}) collective-permute-start(bf16[128,128]{1,0:T(8,128)(2,1)S(1)} %get-tuple-element.64), channel_id=1, source_target_pairs={{0,3},{1,2},{2,1},{3,0},{4,7},{5,6},{6,5},{7,4},{8,11},{9,10},{10,... | collective-permute-start | bytes 98312 | tf_op jit(solution)/shard_map/ppermute | solution.py:524
  23.6 0.0 collective-permute-start.5
  23.6 0.3 collective-permute-start.4
  24.0 0.9 %collective-permute-done.6.rest_2_ = bf16[128,128]{1,0:T(8,128)(2,1)S(1)} collective-permute-done((bf16[128,128]{1,0:T(8,128)(2,1)S(1)}, bf16[128,128]{1,0:T(8,128)(2,1)S(1)}, u32[]{:S(2)}, u32[]{:S(2)}) %collective-permute-start.6) | collective-permute-done | bytes 32800 | tf_op jit(solution)/shard_map/ppermute | solution.py:524
  24.9 2.4 %collective-permute-done.5.rest_1_ = bf16[128,128]{1,0:T(8,128)(2,1)S(1)} collective-permute-done((bf16[128,128]{1,0:T(8,128)(2,1)S(1)}, bf16[128,128]{1,0:T(8,128)(2,1)S(1)}, u32[]{:S(2)}, u32[]{:S(2)}) %collective-permute-start.5) | collective-permute-done | bytes 32800 | tf_op jit(solution)/shard_map/ppermute | solution.py:524
  27.3 0.0 collective-permute-done.4.rest_0_
  27.3 0.7 %residual_rim.1 = (f32[128,128]{1,0:T(8,128)S(1)}, f32[64,128]{1,0:T(8,128)S(1)}, f32[64,128]{1,0:T(8,128)S(1)}, f32[32,64]{1,0:T(8,128)S(1)}) custom-call(s32[2,64]{1,0:T(2,128)S(1)} %bitcast.3, f32[128,128]{1,0:T(8,128)S(1)} %get-tuple-element.58.inc, f32[128,128]{1,0:T(8,128)S(1)} %get-tuple-element.59.innov, f32[128,128]{1,0:T(8,128)S(1)} %get-tuple-element.60.prec, ...), custom_call_target="tpu_custom_call" | custom-call | tf_op jit(solution)/shard_map/residual_rim/pallas_call | solution.py:439
  28.0 5.1 %collective-permute-start.7 = (f32[64,128]{1,0:T(8,128)S(1)}, f32[64,128]{1,0:T(8,128)S(1)}, u32[]{:S(2)}, u32[]{:S(2)}) collective-permute-start(f32[64,128]{1,0:T(8,128)S(1)} %get-tuple-element.66.own_off), channel_id=1, source_target_pairs={{4,8},{8,4},{12,16},{16,12},{20,24},{24,20},{5,9},{9,5},{13,17},{1... | collective-permute-start | bytes 98312 | tf_op jit(solution)/shard_map/ppermute | solution.py:472
  33.1 0.1 collective-permute-start.8
  33.2 0.7 %residual_inner.1.y = f32[128,128]{1,0:T(8,128)S(1)} custom-call(f32[128,128]{1,0:T(8,128)S(1)} %get-tuple-element.65.res, bf16[64,3,128,128]{3,2,1,0:T(8,128)(2,1)S(1)} %get-tuple-element.47.ops), custom_call_target="tpu_custom_call" | custom-call | tf_op jit(solution)/shard_map/residual_inner/pallas_call | solution.py:439
  33.9 0.8 %collective-permute-done.7.off = f32[64,128]{1,0:T(8,128)S(1)} collective-permute-done((f32[64,128]{1,0:T(8,128)S(1)}, f32[64,128]{1,0:T(8,128)S(1)}, u32[]{:S(2)}, u32[]{:S(2)}) %collective-permute-start.7) | collective-permute-done | bytes 32800 | tf_op jit(solution)/shard_map/ppermute | solution.py:472
  34.7 0.0 collective-permute-done.8.mate
  34.7 0.8 %adjoint_off.1 = (bf16[1024,128]{1,0:T(8,128)(2,1)S(1)}, f32[64,32,128]{2,1,0:T(8,128)S(1)}, bf16[33,32,128]{2,1,0:T(8,128)(2,1)S(1)}, bf16[256,128]{1,0:T(8,128...) custom-call(s32[2,64]{1,0:T(2,128)S(4)} %get-tuple-element.44.cols, ...), custom_call_target="tpu_custom_call" | custom-call | tf_op jit(solution)/shard_map/adjoint_off/pallas_call | solution.py:439
  35.5 0.1 collective-permute-start.10
  35.6 4.9 %collective-permute-start.9 = (bf16[33,32,128]{2,1,0:T(8,128)(2,1)S(1)}, bf16[33,32,128]{2,1,0:T(8,128)(2,1)S(1)}, u32[]{:S(2)}, u32[]{:S(2)}) collective-permute-start(bf16[33,32,128]{2,1,0:T(8,128)(2,1)S(1)} %get-tuple-element.77), channel_id=1, source_target_pairs={{4,8},{8,4},{12,16},{16,12},{20,24},{24,20},{5,9},{9,5},{13,17},{1... | collective-permute-start | bytes 811016 | tf_op jit(solution)/shard_map/ppermute | solution.py:472
  40.5 0.7 %adjoint_mate.1 = (bf16[1024,128]{1,0:T(8,128)(2,1)S(1)}, f32[64,32,128]{2,1,0:T(8,128)S(1)}, bf16[32,32,128]{2,1,0:T(8,128)(2,1)S(1)}) custom-call(s32[2,64]{1,0:T(2,128)S(4)} %get-tuple-element.44.cols, f32[32,256]{1,0:T(8,128)S(1)} %get-tuple-element.71.wp, s32[1,256]{1,0:T(1,128)S(1)} %get-tuple-element.72.tgt, ...), custom_call_target="tpu_custom_call" | custom-call | tf_op jit(solution)/shard_map/adjoint_mate/pallas_call | solution.py:439
  41.1 0.0 collective-permute-done.10
  41.2 0.1 collective-permute-start.11
  41.3 2.3 %collective-permute-start.12 = (f32[32,128]{1,0:T(8,128)S(1)}, f32[32,128]{1,0:T(8,128)S(1)}, u32[]{:S(2)}, u32[]{:S(2)}) collective-permute-start(f32[32,128]{1,0:T(8,128)S(1)} %add.9), channel_id=1, source_target_pairs={{0,8},{4,12},{8,0},{12,4},{16,24},{20,28},{24,16},{28,20},{1,9},{5... | collective-permute-start | bytes 49160 | tf_op jit(solution)/shard_map/ppermute | solution.py:475
  43.6 4.3 %collective-permute-done.12 = f32[32,128]{1,0:T(8,128)S(1)} collective-permute-done((f32[32,128]{1,0:T(8,128)S(1)}, f32[32,128]{1,0:T(8,128)S(1)}, u32[]{:S(2)}, u32[]{:S(2)}) %collective-permute-start.12) | collective-permute-done | bytes 16416 | tf_op jit(solution)/shard_map/ppermute | solution.py:475
  47.9 0.2 collective-permute-start.13
  48.1 0.9 %adjoint_inner.1.own = f32[64,32,128]{2,1,0:T(8,128)S(1)} custom-call(s32[2,64]{1,0:T(2,128)S(4)} %get-tuple-element.44.cols, bf16[1024,128]{1,0:T(8,128)(2,1)S(1)} %get-tuple-element.70.mid_off, bf16[1024,128]{1,0:T(8,128)(2,1)S(1)} %get-tuple-element.74.mid_mate, f32[64,32,128]{2,1,0:T(8,128)S(1)} %get-tuple-element.75.sums_off, ...), custom_call_target="tpu_custom_call" | custom-call | tf_op jit(solution)/shard_map/adjoint_inner/pallas_call | solution.py:439
  49.0 1.5 %collective-permute-done.13 = f32[32,128]{1,0:T(8,128)S(1)} collective-permute-done((f32[32,128]{1,0:T(8,128)S(1)}, f32[32,128]{1,0:T(8,128)S(1)}, u32[]{:S(2)}, u32[]{:S(2)}) %collective-permute-start.13) | collective-permute-done | bytes 16416 | tf_op jit(solution)/shard_map/ppermute | solution.py:475
  50.5 0.0 collective-permute-done.9.off
  50.5 0.0 collective-permute-done.11.mate
  50.5 1.2 %finish.1 = (f32[32,8192]{1,0:T(8,128)}, f32[32,64]{1,0:T(8,128)}) custom-call(f32[64,32,128]{2,1,0:T(8,128)S(1)} %adjoint_inner.1.own, bf16[33,32,128]{2,1,0:T(8,128)(2,1)S(1)} %collective-permute-done.9.off, bf16[32,32,128]{2,1,0:T(8,128)(2,1)S(1)} %collective-permute-done.11.mate, f32[32,64]{1,0:T(8,128)S(1)} %get-tuple-element.68.gw, ...), custom_call_target="tpu_custom_call" | custom-call | tf_op jit(solution)/shard_map/finish/pallas_call | solution.py:439
  (6 shorter events, 0.0 us)
Async XLA Ops:
  1.9 9.2 %collective-permute-start = (bf16[32,4096]{1,0:T(8,128)(2,1)S(1)}, bf16[32,4096]{1,0:T(8,128)(2,1)S(1)}, u32[]{:S(2)}, u32[]{:S(2)}) collective-permute-start(bf16[32,4096]{1,0:T(8,128)(2,1)S(1)} %get-tuple-element.43.mate), channel_id=1, source_target_pairs={{0,4},{4,0},{8,12},{12,8},{16,20},{20,16},{24,28},{28,24},{1,5},{5... | collective-permute-start | bytes 786440 | tf_op jit(solution)/shard_map/ppermute | solution.py:469
  2.0 10.6 %collective-permute-start.1 = (bf16[32,4224]{1,0:T(8,128)(2,1)S(1)}, bf16[32,4224]{1,0:T(8,128)(2,1)S(1)}, u32[]{:S(2)}, u32[]{:S(2)}) collective-permute-start(bf16[32,4224]{1,0:T(8,128)(2,1)S(1)} %get-tuple-element.42.off), channel_id=1, source_target_pairs={{4,8},{8,4},{12,16},{16,12},{20,24},{24,20},{5,9},{9,5},{13,17},{1... | collective-permute-start | bytes 811016 | tf_op jit(solution)/shard_map/ppermute | solution.py:472
  6.5 0.7 %copy-start.3 = (s32[64,2]{0,1:T(2,128)S(1)}, s32[64,2]{0,1:T(2,128)}, u32[]{:S(2)}) copy-start(s32[64,2]{0,1:T(2,128)} %param.8) | copy-start | bytes 1540
  11.7 4.4 %copy-start = (f32[2,8192]{1,0:T(2,128)S(1)}, f32[2,8192]{1,0:T(2,128)}, u32[]{:S(2)}) copy-start(f32[2,8192]{1,0:T(2,128)} %innov.1) | copy-start | bytes 196612
  11.8 4.4 %copy-start.1 = (f32[2,8192]{1,0:T(2,128)S(1)}, f32[2,8192]{1,0:T(2,128)}, u32[]{:S(2)}) copy-start(f32[2,8192]{1,0:T(2,128)} %prec.1) | copy-start | bytes 196612
  11.8 4.4 %copy-start.2 = (f32[32,64]{1,0:T(8,128)S(1)}, f32[32,64]{1,0:T(8,128)}, u32[]{:S(2)}) copy-start(f32[32,64]{1,0:T(8,128)} %w.1) | copy-start | bytes 24580
  11.8 6.6 %collective-permute-start.3 = (bf16[32,4096]{1,0:T(8,128)(2,1)S(1)}, bf16[32,4096]{1,0:T(8,128)(2,1)S(1)}, u32[]{:S(2)}, u32[]{:S(2)}) collective-permute-start(bf16[32,4096]{1,0:T(8,128)(2,1)S(1)} %get-tuple-element.56), channel_id=1, source_target_pairs={{0,4},{4,0},{8,12},{12,8},{16,20},{20,16},{24,28},{28,24},{1,5},{5... | collective-permute-start | bytes 786440 | tf_op jit(solution)/shard_map/ppermute | solution.py:469
  13.4 5.8 %collective-permute-start.2 = (f32[32,128]{1,0:T(8,128)S(1)}, f32[32,128]{1,0:T(8,128)S(1)}, u32[]{:S(2)}, u32[]{:S(2)}) collective-permute-start(f32[32,128]{1,0:T(8,128)S(1)} %get-tuple-element.52), channel_id=1, source_target_pairs={{4,8},{8,4},{12,16},{16,12},{20,24},{24,20},{5,9},{9,5},{13,17},{1... | collective-permute-start | bytes 49160 | tf_op jit(solution)/shard_map/ppermute | solution.py:472
  18.4 8.9 %copy-start.4 = (s32[64,2]{0,1:T(2,128)S(1)}, s32[64,2]{0,1:T(2,128)}, u32[]{:S(2)}) copy-start(s32[64,2]{0,1:T(2,128)} %param.8) | copy-start | bytes 1540
  19.8 5.1 %collective-permute-start.6 = (bf16[128,128]{1,0:T(8,128)(2,1)S(1)}, bf16[128,128]{1,0:T(8,128)(2,1)S(1)}, u32[]{:S(2)}, u32[]{:S(2)}) collective-permute-start(bf16[128,128]{1,0:T(8,128)(2,1)S(1)} %get-tuple-element.64), channel_id=1, source_target_pairs={{0,3},{1,2},{2,1},{3,0},{4,7},{5,6},{6,5},{7,4},{8,11},{9,10},{10,... | collective-permute-start | bytes 98312 | tf_op jit(solution)/shard_map/ppermute | solution.py:524
  23.6 3.7 %collective-permute-start.5 = (bf16[128,128]{1,0:T(8,128)(2,1)S(1)}, bf16[128,128]{1,0:T(8,128)(2,1)S(1)}, u32[]{:S(2)}, u32[]{:S(2)}) collective-permute-start(bf16[128,128]{1,0:T(8,128)(2,1)S(1)} %get-tuple-element.64), channel_id=1, source_target_pairs={{0,2},{1,3},{2,0},{3,1},{4,6},{5,7},{6,4},{7,5},{8,10},{9,11},{10,... | collective-permute-start | bytes 98312 | tf_op jit(solution)/shard_map/ppermute | solution.py:524
  23.6 3.7 %collective-permute-start.4 = (bf16[128,128]{1,0:T(8,128)(2,1)S(1)}, bf16[128,128]{1,0:T(8,128)(2,1)S(1)}, u32[]{:S(2)}, u32[]{:S(2)}) collective-permute-start(bf16[128,128]{1,0:T(8,128)(2,1)S(1)} %get-tuple-element.64), channel_id=1, source_target_pairs={{0,1},{1,0},{2,3},{3,2},{4,5},{5,4},{6,7},{7,6},{8,9},{9,8},{10,11... | collective-permute-start | bytes 98312 | tf_op jit(solution)/shard_map/ppermute | solution.py:524
  28.0 6.7 %collective-permute-start.7 = (f32[64,128]{1,0:T(8,128)S(1)}, f32[64,128]{1,0:T(8,128)S(1)}, u32[]{:S(2)}, u32[]{:S(2)}) collective-permute-start(f32[64,128]{1,0:T(8,128)S(1)} %get-tuple-element.66.own_off), channel_id=1, source_target_pairs={{4,8},{8,4},{12,16},{16,12},{20,24},{24,20},{5,9},{9,5},{13,17},{1... | collective-permute-start | bytes 98312 | tf_op jit(solution)/shard_map/ppermute | solution.py:472
  33.1 1.6 %collective-permute-start.8 = (f32[64,128]{1,0:T(8,128)S(1)}, f32[64,128]{1,0:T(8,128)S(1)}, u32[]{:S(2)}, u32[]{:S(2)}) collective-permute-start(f32[64,128]{1,0:T(8,128)S(1)} %get-tuple-element.67.own_mate), channel_id=1, source_target_pairs={{0,4},{4,0},{8,12},{12,8},{16,20},{20,16},{24,28},{28,24},{1,5},{5... | collective-permute-start | bytes 98312 | tf_op jit(solution)/shard_map/ppermute | solution.py:469
  35.5 5.6 %collective-permute-start.10 = (f32[32,128]{1,0:T(8,128)S(1)}, f32[32,128]{1,0:T(8,128)S(1)}, u32[]{:S(2)}, u32[]{:S(2)}) collective-permute-start(f32[32,128]{1,0:T(8,128)S(1)} %get-tuple-element.79), channel_id=1, source_target_pairs={{0,4},{4,0},{8,12},{12,8},{16,20},{20,16},{24,28},{28,24},{1,5},{5... | collective-permute-start | bytes 49160 | tf_op jit(solution)/shard_map/ppermute | solution.py:475
  35.6 14.9 %collective-permute-start.9 = (bf16[33,32,128]{2,1,0:T(8,128)(2,1)S(1)}, bf16[33,32,128]{2,1,0:T(8,128)(2,1)S(1)}, u32[]{:S(2)}, u32[]{:S(2)}) collective-permute-start(bf16[33,32,128]{2,1,0:T(8,128)(2,1)S(1)} %get-tuple-element.77), channel_id=1, source_target_pairs={{4,8},{8,4},{12,16},{16,12},{20,24},{24,20},{5,9},{9,5},{13,17},{1... | collective-permute-start | bytes 811016 | tf_op jit(solution)/shard_map/ppermute | solution.py:472
  41.2 9.3 %collective-permute-start.11 = (bf16[32,32,128]{2,1,0:T(8,128)(2,1)S(1)}, bf16[32,32,128]{2,1,0:T(8,128)(2,1)S(1)}, u32[]{:S(2)}, u32[]{:S(2)}) collective-permute-start(bf16[32,32,128]{2,1,0:T(8,128)(2,1)S(1)} %get-tuple-element.80), channel_id=1, source_target_pairs={{0,4},{4,0},{8,12},{12,8},{16,20},{20,16},{24,28},{28,24},{1,5},{5... | collective-permute-start | bytes 786440 | tf_op jit(solution)/shard_map/ppermute | solution.py:469
  41.3 6.6 %collective-permute-start.12 = (f32[32,128]{1,0:T(8,128)S(1)}, f32[32,128]{1,0:T(8,128)S(1)}, u32[]{:S(2)}, u32[]{:S(2)}) collective-permute-start(f32[32,128]{1,0:T(8,128)S(1)} %add.9), channel_id=1, source_target_pairs={{0,8},{4,12},{8,0},{12,4},{16,24},{20,28},{24,16},{28,20},{1,9},{5... | collective-permute-start | bytes 49160 | tf_op jit(solution)/shard_map/ppermute | solution.py:475
  47.9 2.6 %collective-permute-start.13 = (f32[32,128]{1,0:T(8,128)S(1)}, f32[32,128]{1,0:T(8,128)S(1)}, u32[]{:S(2)}, u32[]{:S(2)}) collective-permute-start(f32[32,128]{1,0:T(8,128)S(1)} %add.10), channel_id=1, source_target_pairs={{0,16},{4,20},{8,24},{12,28},{16,0},{20,4},{24,8},{28,12},{1,17},{... | collective-permute-start | bytes 49160 | tf_op jit(solution)/shard_map/ppermute | solution.py:475

commit v6 on v5

--- a/solution.py
+++ b/solution.py
@@ -411,17 +411,21 @@
         chunks(REACH, some)
 
 
-def finish(own, off, mate, gw, total, out, direction, *, count):
-    rows, members, size = own.shape
-    sides = Sides(rows)
-    drawn = off[REACH].astype(F32)
-    grown = gw[...]
-    drawn = drawn[:, :REACH] + drawn[:, REACH : 2 * REACH]
-    grown = jnp.concatenate([grown[:, :REACH] + drawn, grown[:, REACH:]], 1)
-    direction[...] = turned(sides, grown / jnp.sqrt(total[:, :1] / count + 1e-06))
+def finish(own, off, mate, out):
+    size = own.shape[2]
+    sides = Sides(own.shape[0])
     for row, q, halo in ((sides.off_row, 0, off), (sides.mate_row, REACH, mate)):
         for i in range(REACH):
             lanes(out, row + i, size)[...] = own[q + i] + halo[i].astype(F32)
+
+
+def normalize(off, gw, total, mate_total, direction, *, count):
+    drawn = off[REACH].astype(F32)
+    drawn = drawn[:, :REACH] + drawn[:, REACH : 2 * REACH]
+    grown = gw[...]
+    grown = jnp.concatenate([grown[:, :REACH] + drawn, grown[:, REACH:]], 1)
+    mean = (total[:, :1] + mate_total[:, :1]) / count
+    direction[...] = turned(Sides(2 * REACH), grown / jnp.sqrt(mean + 1e-06))
 
 
 SMEM = pl.BlockSpec(memory_space=pltpu.SMEM)
@@ -549,21 +553,25 @@
         1,
     )
     from_off = to_off(send)
-    total = total + partner(total, 1)
+    total = total + partner(total, 2)
     mid_mate, sums_mate, send = run(
         adjoint_mate, [mid_kind, sums_kind, send_kind], (table, wp, tgt, vals, ops), 1
     )
     send, total = lax.optimization_barrier((send, total))
     from_mate = to_mate(send)
-    stride = 2
+    stride = 4
     while stride < tiles:
         total = total + partner(total, stride)
         stride *= 2
     (own,) = run(adjoint_inner, [acc_kind], (table, mid_off, mid_mate, sums_off, sums_mate, ops), 1)
-    grad_ens, direction = run(
-        finish,
-        [((members, length), F32), ((members, rows), F32)],
-        (own, from_off, from_mate, grad_weights, total),
+    total, own = lax.optimization_barrier((total, own))
+    mate_total = to_mate(total)
+    (grad_ens,) = run(finish, [((members, length), F32)], (own, from_off, from_mate), near=False)
+    grad_ens, grad_weights = lax.optimization_barrier((grad_ens, grad_weights))
+    (direction,) = run(
+        normalize,
+        [((members, rows), F32)],
+        (from_off, grad_weights, total, mate_total),
         near=False,
         count=rows * tiles,
     )

time: 52.1 us -> 50.3 us (0.965)
  waiting for transfers between devices: 10.6 us -> 6.87 us
  starting transfers between devices: 24.3 us -> 25.9 us
  Pallas kernels: 15.1 us -> 15.8 us
    ppermute x3 -> x2, waiting for transfers between devices: 5.73 us -> 0.24 us  [partner(): return lax.ppermute(value, 'space', [(i, i ^ stride) for i in range(tiles)])]
    ppermute x3 -> x2, starting transfers between devices: 2.64 us -> 5.91 us  [partner(): return lax.ppermute(value, 'space', [(i, i ^ stride) for i in range(tiles)])]
    ppermute x4, starting transfers between devices: 17.2 us -> 14.2 us  [to_off(): return lax.ppermute(value, 'space', offs)]
    ppermute x4, waiting for transfers between devices: 1.57 us -> 3.31 us  [to_off(): return lax.ppermute(value, 'space', offs)]
    ppermute x4 -> x5, starting transfers between devices: 0.34 us -> 1.63 us  [to_mate(): return lax.ppermute(value, 'space', mates)]
    pallas_call x13 -> x14, Pallas kernels: 15.1 us -> 15.8 us  [run(): pl.pallas_call(functools.partial(body, **fixed) if fixed else body, out_s...]
  transfers between devices with their start and end apart: 14 -> 14, of which waited for: 6 -> 6; matrix products, arithmetic and copies ran while one was open for 0% -> 0% of each run, Pallas kernels for 20% -> 23%
where the time goes in v6:
time: 50.3 us; the launch traced here: 50.1 us
  starting transfers between devices  25.9 us (51%)
  Pallas kernels  15.8 us (31%)
  waiting for transfers between devices  6.87 us (14%)
  between operations  0.85 us (2%)
  local copies, waits for them, and re-layouts  0.7 us (1%)
    pallas_call x14, Pallas kernels, run(): pl.pallas_call(functools.partial(body, **fixed) if fixed else body, out_s...  15.8 us
    ppermute x4, starting transfers between devices, to_off(): return lax.ppermute(value, 'space', offs)  14.2 us
    ppermute x2, starting transfers between devices, partner(): return lax.ppermute(value, 'space', [(i, i ^ stride) for i in range(tiles)])  5.91 us
    ppermute x3, starting transfers between devices, on_device(): lax.ppermute(send, 'members', [(i, i ^ step) for i in range(groups)])  4.15 us
    ppermute x3, waiting for transfers between devices, on_device(): lax.ppermute(send, 'members', [(i, i ^ step) for i in range(groups)])  3.31 us
    ppermute x4, waiting for transfers between devices, to_off(): return lax.ppermute(value, 'space', offs)  3.31 us
    ppermute x5, starting transfers between devices, to_mate(): return lax.ppermute(value, 'space', mates)  1.63 us
  transfers between devices with their start and end apart: 14, of which 6 were waited for; matrix products, arithmetic and copies ran while one was open for 0% of the time, Pallas kernels for 23%

profile of v6, /device:TPU:1, one launch (start us, length us, event | category | flops | bytes accessed | tf_op | source)
XLA Modules:
  0.0 50.1 jit_solution(7531704641949409810)
XLA Ops:
  0.6 1.2 %load.1 = (bf16[32,4224]{1,0:T(8,128)(2,1)S(1)}, bf16[32,4096]{1,0:T(8,128)(2,1)S(1)}) custom-call(bf16[32,8192]{1,0:T(8,128)(2,1)} %ens.1, f32[32,64]{1,0:T(8,128)} %w.1, s32[2,64]{1,0:T(2,128)} %bitcast.1), custom_call_target="tpu_custom_call" | custom-call | tf_op jit(solution)/shard_map/load/pallas_call | solution.py:443
  1.9 0.1 collective-permute-start
  2.0 4.5 %collective-permute-start.1 = (bf16[32,4224]{1,0:T(8,128)(2,1)S(1)}, bf16[32,4224]{1,0:T(8,128)(2,1)S(1)}, u32[]{:S(2)}, u32[]{:S(2)}) collective-permute-start(bf16[32,4224]{1,0:T(8,128)(2,1)S(1)} %get-tuple-element.46.off), channel_id=1, source_target_pairs={{4,8},{8,4},{12,16},{16,12},{20,24},{24,20},{5,9},{9,5},{13,17},{1... | collective-permute-start | bytes 811016 | tf_op jit(solution)/shard_map/ppermute | solution.py:476
  6.5 0.0 copy-start.3
  6.5 0.7 %copy-done.3 = s32[64,2]{0,1:T(2,128)S(1)} copy-done((s32[64,2]{0,1:T(2,128)S(1)}, s32[64,2]{0,1:T(2,128)}, u32[]{:S(2)}) %copy-start.3) | copy-done | bytes 536
  7.1 3.9 %first_inner.1 = (f32[64,32,128]{2,1,0:T(8,128)S(1)}, bf16[32,16384]{1,0:T(8,128)(2,1)S(1)}, bf16[64,3,128,128]{3,2,1,0:T(8,128)(2,1)S(1)}, s32[2,64]{1,0:T(2,128)S(4)}) custom-call(s32[2,64]{1,0:T(2,128)S(1)} %bitcast.2, bf16[32,4224]{1,0:T(8,128)(2,1)S(1)} %get-tuple-element.46.off, bf16[32,4096]{1,0:T(8,128)(2,1)S(1)} %get-tuple-element.47.mate, ...), custom_call_target="tpu_custom_call" | custom-call | tf_op jit(solution)/shard_map/first_inner/pallas_call | solution.py:443
  11.1 0.0 collective-permute-done.halo
  11.1 0.7 %first_mate.1 = (bf16[32,16384]{1,0:T(8,128)(2,1)S(1)}, bf16[32,16384]{1,0:T(8,128)(2,1)S(1)}, bf16[32,4096]{1,0:T(8,128)(2,1)S(1)}) custom-call(s32[2,64]{1,0:T(2,128)S(4)} %get-tuple-element.48.cols, f32[64,32,128]{2,1,0:T(8,128)S(1)} %get-tuple-element.49.acc, bf16[32,16384]{1,0:T(8,128)(2,1)S(1)} %get-tuple-element.50.wide_in, ...), custom_call_target="tpu_custom_call", output_to_operand_aliasing={{0}: (2, {})} | custom-call | tf_op jit(solution)/shard_map/first_mate/pallas_call | solution.py:443
  11.8 0.0 copy-start.1
  11.8 0.0 copy-start.2
  11.8 0.1 collective-permute-start.3
  11.9 0.7 %collective-permute-done.1.halo = bf16[32,4224]{1,0:T(8,128)(2,1)S(1)} collective-permute-done((bf16[32,4224]{1,0:T(8,128)(2,1)S(1)}, bf16[32,4224]{1,0:T(8,128)(2,1)S(1)}, u32[]{:S(2)}, u32[]{:S(2)}) %collective-permute-start.1) | collective-permute-done | bytes 270368 | tf_op jit(solution)/shard_map/ppermute | solution.py:476
  12.6 0.8 %first_off.1 = (bf16[32,16384]{1,0:T(8,128)(2,1)S(1)}, bf16[32,16384]{1,0:T(8,128)(2,1)S(1)}, f32[32,128]{1,0:T(8,128)S(1)}, s32[32,128]{1,0:T(8,128)S(1)}) custom-call(s32[2,64]{1,0:T(2,128)S(4)} %get-tuple-element.48.cols, f32[64,32,128]{2,1,0:T(8,128)S(1)} %get-tuple-element.49.acc, ...), custom_call_target="tpu_custom_call", output_to_operand_aliasing={{0}: (2, {}), {1}: (3, {})} | custom-call | tf_op jit(solution)/shard_map/first_off/pallas_call | solution.py:443
  13.4 2.8 %collective-permute-start.2 = (f32[32,128]{1,0:T(8,128)S(1)}, f32[32,128]{1,0:T(8,128)S(1)}, u32[]{:S(2)}, u32[]{:S(2)}) collective-permute-start(f32[32,128]{1,0:T(8,128)S(1)} %get-tuple-element.56), channel_id=1, source_target_pairs={{4,8},{8,4},{12,16},{16,12},{20,24},{24,20},{5,9},{9,5},{13,17},{1... | collective-permute-start | bytes 49160 | tf_op jit(solution)/shard_map/ppermute | solution.py:476
  16.2 2.2 %second_inner.1 = (f32[64,32,128]{2,1,0:T(8,128)S(1)}, f32[64,128]{1,0:T(8,128)S(1)}, f32[128,128]{1,0:T(8,128)S(1)}, f32[128,128]{1,0:T(8,128)S(1)}, f32[32,64]...) custom-call(s32[2,64]{1,0:T(2,128)S(4)} %get-tuple-element.48.cols, ...), custom_call_target="tpu_custom_call" | custom-call | tf_op jit(solution)/shard_map/second_inner/pallas_call | solution.py:443
  18.4 0.0 collective-permute-done.3.halo
  18.4 0.0 copy-start.4
  18.4 0.7 %second_mate.1 = (bf16[32,16384]{1,0:T(8,128)(2,1)S(1)}, bf16[32,4096]{1,0:T(8,128)(2,1)S(1)}, f32[32,128]{1,0:T(8,128)S(1)}) custom-call(s32[2,64]{1,0:T(2,128)S(4)} %get-tuple-element.48.cols, f32[64,32,128]{2,1,0:T(8,128)S(1)} %get-tuple-element.59.acc, bf16[32,16384]{1,0:T(8,128)(2,1)S(1)} %get-tuple-element.54.wide.wide_in, ...), custom_call_target="tpu_custom_call", output_to_operand_aliasing={{0}: (2, {})} | custom-call | tf_op jit(solution)/shard_map/second_mate/pallas_call | solution.py:443
  19.2 0.0 collective-permute-done.2.halo
  19.2 0.7 %second_off.1 = (f32[128,128]{1,0:T(8,128)S(1)}, bf16[128,128]{1,0:T(8,128)(2,1)S(1)}) custom-call(f32[32,128]{1,0:T(8,128)S(1)} %collective-permute-done.2.halo, bf16[64,3,128,128]{3,2,1,0:T(8,128)(2,1)S(1)} %get-tuple-element.51.ops, f32[64,128]{1,0:T(8,128)S(1)} %get-tuple-element.57.inc_one, f32[32,128]{1,0:T(8,128)S(1)} %get-tuple-element.58.inc_off, ...), custom_call_target="tpu_custom_call" | custom-call | tf_op jit(solution)/shard_map/second_off/pallas_call | solution.py:443
  19.8 3.8 %collective-permute-start.6 = (bf16[128,128]{1,0:T(8,128)(2,1)S(1)}, bf16[128,128]{1,0:T(8,128)(2,1)S(1)}, u32[]{:S(2)}, u32[]{:S(2)}) collective-permute-start(bf16[128,128]{1,0:T(8,128)(2,1)S(1)} %get-tuple-element.68), channel_id=1, source_target_pairs={{0,3},{1,2},{2,1},{3,0},{4,7},{5,6},{6,5},{7,4},{8,11},{9,10},{10,... | collective-permute-start | bytes 98312 | tf_op jit(solution)/shard_map/ppermute | solution.py:528
  23.6 0.0 collective-permute-start.5
  23.7 0.3 collective-permute-start.4
  24.0 0.9 %collective-permute-done.6.rest_2_ = bf16[128,128]{1,0:T(8,128)(2,1)S(1)} collective-permute-done((bf16[128,128]{1,0:T(8,128)(2,1)S(1)}, bf16[128,128]{1,0:T(8,128)(2,1)S(1)}, u32[]{:S(2)}, u32[]{:S(2)}) %collective-permute-start.6) | collective-permute-done | bytes 32800 | tf_op jit(solution)/shard_map/ppermute | solution.py:528
  24.9 2.4 %collective-permute-done.5.rest_1_ = bf16[128,128]{1,0:T(8,128)(2,1)S(1)} collective-permute-done((bf16[128,128]{1,0:T(8,128)(2,1)S(1)}, bf16[128,128]{1,0:T(8,128)(2,1)S(1)}, u32[]{:S(2)}, u32[]{:S(2)}) %collective-permute-start.5) | collective-permute-done | bytes 32800 | tf_op jit(solution)/shard_map/ppermute | solution.py:528
  27.3 0.0 collective-permute-done.4.rest_0_
  27.3 0.0 copy-done.4
  27.3 0.7 %residual_rim.1 = (f32[128,128]{1,0:T(8,128)S(1)}, f32[64,128]{1,0:T(8,128)S(1)}, f32[64,128]{1,0:T(8,128)S(1)}, f32[32,64]{1,0:T(8,128)S(1)}) custom-call(s32[2,64]{1,0:T(2,128)S(1)} %bitcast.3, f32[128,128]{1,0:T(8,128)S(1)} %get-tuple-element.62.inc, f32[128,128]{1,0:T(8,128)S(1)} %get-tuple-element.63.innov, f32[128,128]{1,0:T(8,128)S(1)} %get-tuple-element.64.prec, ...), custom_call_target="tpu_custom_call" | custom-call | tf_op jit(solution)/shard_map/residual_rim/pallas_call | solution.py:443
  28.0 5.1 %collective-permute-start.7 = (f32[64,128]{1,0:T(8,128)S(1)}, f32[64,128]{1,0:T(8,128)S(1)}, u32[]{:S(2)}, u32[]{:S(2)}) collective-permute-start(f32[64,128]{1,0:T(8,128)S(1)} %get-tuple-element.70.own_off), channel_id=1, source_target_pairs={{4,8},{8,4},{12,16},{16,12},{20,24},{24,20},{5,9},{9,5},{13,17},{1... | collective-permute-start | bytes 98312 | tf_op jit(solution)/shard_map/ppermute | solution.py:476
  33.1 0.1 collective-permute-start.8
  33.2 0.7 %residual_inner.1.y = f32[128,128]{1,0:T(8,128)S(1)} custom-call(f32[128,128]{1,0:T(8,128)S(1)} %get-tuple-element.69.res, bf16[64,3,128,128]{3,2,1,0:T(8,128)(2,1)S(1)} %get-tuple-element.51.ops), custom_call_target="tpu_custom_call" | custom-call | tf_op jit(solution)/shard_map/residual_inner/pallas_call | solution.py:443
  33.9 0.8 %collective-permute-done.7.off = f32[64,128]{1,0:T(8,128)S(1)} collective-permute-done((f32[64,128]{1,0:T(8,128)S(1)}, f32[64,128]{1,0:T(8,128)S(1)}, u32[]{:S(2)}, u32[]{:S(2)}) %collective-permute-start.7) | collective-permute-done | bytes 32800 | tf_op jit(solution)/shard_map/ppermute | solution.py:476
  34.7 0.0 collective-permute-done.8.mate
  34.7 0.8 %adjoint_off.1 = (bf16[1024,128]{1,0:T(8,128)(2,1)S(1)}, f32[64,32,128]{2,1,0:T(8,128)S(1)}, bf16[33,32,128]{2,1,0:T(8,128)(2,1)S(1)}, bf16[256,128]{1,0:T(8,128...) custom-call(s32[2,64]{1,0:T(2,128)S(4)} %get-tuple-element.48.cols, ...), custom_call_target="tpu_custom_call" | custom-call | tf_op jit(solution)/shard_map/adjoint_off/pallas_call | solution.py:443
  35.5 2.7 %collective-permute-start.9 = (f32[32,128]{1,0:T(8,128)S(1)}, f32[32,128]{1,0:T(8,128)S(1)}, u32[]{:S(2)}, u32[]{:S(2)}) collective-permute-start(f32[32,128]{1,0:T(8,128)S(1)} %get-tuple-element.78), channel_id=1, source_target_pairs={{0,8},{4,12},{8,0},{12,4},{16,24},{20,28},{24,16},{28,20},{1,9},{5... | collective-permute-start | bytes 49160 | tf_op jit(solution)/shard_map/ppermute | solution.py:479
  38.2 1.9 %collective-permute-start.11 = (bf16[33,32,128]{2,1,0:T(8,128)(2,1)S(1)}, bf16[33,32,128]{2,1,0:T(8,128)(2,1)S(1)}, u32[]{:S(2)}, u32[]{:S(2)}) collective-permute-start(bf16[33,32,128]{2,1,0:T(8,128)(2,1)S(1)} %get-tuple-element.85), channel_id=1, source_target_pairs={{4,8},{8,4},{12,16},{16,12},{20,24},{24,20},{5,9},{9,5},{13,17},{1... | collective-permute-start | bytes 811016 | tf_op jit(solution)/shard_map/ppermute | solution.py:476
  40.1 0.7 %adjoint_mate.1 = (bf16[1024,128]{1,0:T(8,128)(2,1)S(1)}, f32[64,32,128]{2,1,0:T(8,128)S(1)}, bf16[32,32,128]{2,1,0:T(8,128)(2,1)S(1)}) custom-call(s32[2,64]{1,0:T(2,128)S(4)} %get-tuple-element.48.cols, f32[32,256]{1,0:T(8,128)S(1)} %get-tuple-element.74.wp, s32[1,256]{1,0:T(1,128)S(1)} %get-tuple-element.75.tgt, ...), custom_call_target="tpu_custom_call" | custom-call | tf_op jit(solution)/shard_map/adjoint_mate/pallas_call | solution.py:443
  40.8 0.0 collective-permute-done.9
  40.8 0.1 collective-permute-start.12
  40.9 3.2 %collective-permute-start.10 = (f32[32,128]{1,0:T(8,128)S(1)}, f32[32,128]{1,0:T(8,128)S(1)}, u32[]{:S(2)}, u32[]{:S(2)}) collective-permute-start(f32[32,128]{1,0:T(8,128)S(1)} %add.6), channel_id=1, source_target_pairs={{0,16},{4,20},{8,24},{12,28},{16,0},{20,4},{24,8},{28,12},{1,17},{... | collective-permute-start | bytes 49160 | tf_op jit(solution)/shard_map/ppermute | solution.py:479
  44.1 0.9 %adjoint_inner.1.own = f32[64,32,128]{2,1,0:T(8,128)S(1)} custom-call(s32[2,64]{1,0:T(2,128)S(4)} %get-tuple-element.48.cols, bf16[1024,128]{1,0:T(8,128)(2,1)S(1)} %get-tuple-element.80.mid_off, bf16[1024,128]{1,0:T(8,128)(2,1)S(1)} %get-tuple-element.81.mid_mate, f32[64,32,128]{2,1,0:T(8,128)S(1)} %get-tuple-element.82.sums_off, ...), custom_call_target="tpu_custom_call" | custom-call | tf_op jit(solution)/shard_map/adjoint_inner/pallas_call | solution.py:443
  45.0 0.2 collective-permute-done.10
  45.2 1.3 %collective-permute-start.13 = (f32[32,128]{1,0:T(8,128)S(1)}, f32[32,128]{1,0:T(8,128)S(1)}, u32[]{:S(2)}, u32[]{:S(2)}) collective-permute-start(f32[32,128]{1,0:T(8,128)S(1)} %add.7.total), channel_id=1, source_target_pairs={{0,4},{4,0},{8,12},{12,8},{16,20},{20,16},{24,28},{28,24},{1,5},{5... | collective-permute-start | bytes 49160 | tf_op jit(solution)/shard_map/ppermute | solution.py:473
  46.5 1.7 %collective-permute-done.11.off = bf16[33,32,128]{2,1,0:T(8,128)(2,1)S(1)} collective-permute-done((bf16[33,32,128]{2,1,0:T(8,128)(2,1)S(1)}, bf16[33,32,128]{2,1,0:T(8,128)(2,1)S(1)}, u32[]{:S(2)}, u32[]{:S(2)}) %collective-permute-start.11) | collective-permute-done | bytes 270368 | tf_op jit(solution)/shard_map/ppermute | solution.py:476
  48.3 0.0 collective-permute-done.12.mate
  48.3 1.1 %finish.1 = f32[32,8192]{1,0:T(8,128)} custom-call(f32[64,32,128]{2,1,0:T(8,128)S(1)} %adjoint_inner.1.own, bf16[33,32,128]{2,1,0:T(8,128)(2,1)S(1)} %collective-permute-done.11.off, bf16[32,32,128]{2,1,0:T(8,128)(2,1)S(1)} %collective-permute-done.12.mate), custom_call_target="tpu_custom_call" | custom-call | tf_op jit(solution)/shard_map/finish/pallas_call | solution.py:443
  49.3 0.0 collective-permute-done.13.mate_total
  49.4 0.8 %normalize.1 = f32[32,64]{1,0:T(8,128)} custom-call(bf16[33,32,128]{2,1,0:T(8,128)(2,1)S(1)} %collective-permute-done.11.off, f32[32,64]{1,0:T(8,128)S(1)} %get-tuple-element.88.gw, f32[32,128]{1,0:T(8,128)S(1)} %add.7.total, f32[32,128]{1,0:T(8,128)S(1)} %collective-permute-done.13.mate_total), custom_call_target="tpu_custom_call" | custom-call | tf_op jit(solution)/shard_map/normalize/pallas_call | solution.py:443
  (6 shorter events, 0.0 us)
Async XLA Ops:
  1.9 9.2 %collective-permute-start = (bf16[32,4096]{1,0:T(8,128)(2,1)S(1)}, bf16[32,4096]{1,0:T(8,128)(2,1)S(1)}, u32[]{:S(2)}, u32[]{:S(2)}) collective-permute-start(bf16[32,4096]{1,0:T(8,128)(2,1)S(1)} %get-tuple-element.47.mate), channel_id=1, source_target_pairs={{0,4},{4,0},{8,12},{12,8},{16,20},{20,16},{24,28},{28,24},{1,5},{5... | collective-permute-start | bytes 786440 | tf_op jit(solution)/shard_map/ppermute | solution.py:473
  2.0 10.6 %collective-permute-start.1 = (bf16[32,4224]{1,0:T(8,128)(2,1)S(1)}, bf16[32,4224]{1,0:T(8,128)(2,1)S(1)}, u32[]{:S(2)}, u32[]{:S(2)}) collective-permute-start(bf16[32,4224]{1,0:T(8,128)(2,1)S(1)} %get-tuple-element.46.off), channel_id=1, source_target_pairs={{4,8},{8,4},{12,16},{16,12},{20,24},{24,20},{5,9},{9,5},{13,17},{1... | collective-permute-start | bytes 811016 | tf_op jit(solution)/shard_map/ppermute | solution.py:476
  6.5 0.7 %copy-start.3 = (s32[64,2]{0,1:T(2,128)S(1)}, s32[64,2]{0,1:T(2,128)}, u32[]{:S(2)}) copy-start(s32[64,2]{0,1:T(2,128)} %param.8) | copy-start | bytes 1540
  11.7 4.4 %copy-start = (f32[2,8192]{1,0:T(2,128)S(1)}, f32[2,8192]{1,0:T(2,128)}, u32[]{:S(2)}) copy-start(f32[2,8192]{1,0:T(2,128)} %innov.1) | copy-start | bytes 196612
  11.8 4.4 %copy-start.1 = (f32[2,8192]{1,0:T(2,128)S(1)}, f32[2,8192]{1,0:T(2,128)}, u32[]{:S(2)}) copy-start(f32[2,8192]{1,0:T(2,128)} %prec.1) | copy-start | bytes 196612
  11.8 4.4 %copy-start.2 = (f32[32,64]{1,0:T(8,128)S(1)}, f32[32,64]{1,0:T(8,128)}, u32[]{:S(2)}) copy-start(f32[32,64]{1,0:T(8,128)} %w.1) | copy-start | bytes 24580
  11.8 6.6 %collective-permute-start.3 = (bf16[32,4096]{1,0:T(8,128)(2,1)S(1)}, bf16[32,4096]{1,0:T(8,128)(2,1)S(1)}, u32[]{:S(2)}, u32[]{:S(2)}) collective-permute-start(bf16[32,4096]{1,0:T(8,128)(2,1)S(1)} %get-tuple-element.60), channel_id=1, source_target_pairs={{0,4},{4,0},{8,12},{12,8},{16,20},{20,16},{24,28},{28,24},{1,5},{5... | collective-permute-start | bytes 786440 | tf_op jit(solution)/shard_map/ppermute | solution.py:473
  13.4 5.8 %collective-permute-start.2 = (f32[32,128]{1,0:T(8,128)S(1)}, f32[32,128]{1,0:T(8,128)S(1)}, u32[]{:S(2)}, u32[]{:S(2)}) collective-permute-start(f32[32,128]{1,0:T(8,128)S(1)} %get-tuple-element.56), channel_id=1, source_target_pairs={{4,8},{8,4},{12,16},{16,12},{20,24},{24,20},{5,9},{9,5},{13,17},{1... | collective-permute-start | bytes 49160 | tf_op jit(solution)/shard_map/ppermute | solution.py:476
  18.4 8.9 %copy-start.4 = (s32[64,2]{0,1:T(2,128)S(1)}, s32[64,2]{0,1:T(2,128)}, u32[]{:S(2)}) copy-start(s32[64,2]{0,1:T(2,128)} %param.8) | copy-start | bytes 1540
  19.8 5.1 %collective-permute-start.6 = (bf16[128,128]{1,0:T(8,128)(2,1)S(1)}, bf16[128,128]{1,0:T(8,128)(2,1)S(1)}, u32[]{:S(2)}, u32[]{:S(2)}) collective-permute-start(bf16[128,128]{1,0:T(8,128)(2,1)S(1)} %get-tuple-element.68), channel_id=1, source_target_pairs={{0,3},{1,2},{2,1},{3,0},{4,7},{5,6},{6,5},{7,4},{8,11},{9,10},{10,... | collective-permute-start | bytes 98312 | tf_op jit(solution)/shard_map/ppermute | solution.py:528
  23.6 3.7 %collective-permute-start.5 = (bf16[128,128]{1,0:T(8,128)(2,1)S(1)}, bf16[128,128]{1,0:T(8,128)(2,1)S(1)}, u32[]{:S(2)}, u32[]{:S(2)}) collective-permute-start(bf16[128,128]{1,0:T(8,128)(2,1)S(1)} %get-tuple-element.68), channel_id=1, source_target_pairs={{0,2},{1,3},{2,0},{3,1},{4,6},{5,7},{6,4},{7,5},{8,10},{9,11},{10,... | collective-permute-start | bytes 98312 | tf_op jit(solution)/shard_map/ppermute | solution.py:528
  23.7 3.7 %collective-permute-start.4 = (bf16[128,128]{1,0:T(8,128)(2,1)S(1)}, bf16[128,128]{1,0:T(8,128)(2,1)S(1)}, u32[]{:S(2)}, u32[]{:S(2)}) collective-permute-start(bf16[128,128]{1,0:T(8,128)(2,1)S(1)} %get-tuple-element.68), channel_id=1, source_target_pairs={{0,1},{1,0},{2,3},{3,2},{4,5},{5,4},{6,7},{7,6},{8,9},{9,8},{10,11... | collective-permute-start | bytes 98312 | tf_op jit(solution)/shard_map/ppermute | solution.py:528
  28.0 6.7 %collective-permute-start.7 = (f32[64,128]{1,0:T(8,128)S(1)}, f32[64,128]{1,0:T(8,128)S(1)}, u32[]{:S(2)}, u32[]{:S(2)}) collective-permute-start(f32[64,128]{1,0:T(8,128)S(1)} %get-tuple-element.70.own_off), channel_id=1, source_target_pairs={{4,8},{8,4},{12,16},{16,12},{20,24},{24,20},{5,9},{9,5},{13,17},{1... | collective-permute-start | bytes 98312 | tf_op jit(solution)/shard_map/ppermute | solution.py:476
  33.1 1.6 %collective-permute-start.8 = (f32[64,128]{1,0:T(8,128)S(1)}, f32[64,128]{1,0:T(8,128)S(1)}, u32[]{:S(2)}, u32[]{:S(2)}) collective-permute-start(f32[64,128]{1,0:T(8,128)S(1)} %get-tuple-element.71.own_mate), channel_id=1, source_target_pairs={{0,4},{4,0},{8,12},{12,8},{16,20},{20,16},{24,28},{28,24},{1,5},{5... | collective-permute-start | bytes 98312 | tf_op jit(solution)/shard_map/ppermute | solution.py:473
  35.5 5.2 %collective-permute-start.9 = (f32[32,128]{1,0:T(8,128)S(1)}, f32[32,128]{1,0:T(8,128)S(1)}, u32[]{:S(2)}, u32[]{:S(2)}) collective-permute-start(f32[32,128]{1,0:T(8,128)S(1)} %get-tuple-element.78), channel_id=1, source_target_pairs={{0,8},{4,12},{8,0},{12,4},{16,24},{20,28},{24,16},{28,20},{1,9},{5... | collective-permute-start | bytes 49160 | tf_op jit(solution)/shard_map/ppermute | solution.py:479
  38.2 10.1 %collective-permute-start.11 = (bf16[33,32,128]{2,1,0:T(8,128)(2,1)S(1)}, bf16[33,32,128]{2,1,0:T(8,128)(2,1)S(1)}, u32[]{:S(2)}, u32[]{:S(2)}) collective-permute-start(bf16[33,32,128]{2,1,0:T(8,128)(2,1)S(1)} %get-tuple-element.85), channel_id=1, source_target_pairs={{4,8},{8,4},{12,16},{16,12},{20,24},{24,20},{5,9},{9,5},{13,17},{1... | collective-permute-start | bytes 811016 | tf_op jit(solution)/shard_map/ppermute | solution.py:476
  40.8 7.5 %collective-permute-start.12 = (bf16[32,32,128]{2,1,0:T(8,128)(2,1)S(1)}, bf16[32,32,128]{2,1,0:T(8,128)(2,1)S(1)}, u32[]{:S(2)}, u32[]{:S(2)}) collective-permute-start(bf16[32,32,128]{2,1,0:T(8,128)(2,1)S(1)} %get-tuple-element.86), channel_id=1, source_target_pairs={{0,4},{4,0},{8,12},{12,8},{16,20},{20,16},{24,28},{28,24},{1,5},{5... | collective-permute-start | bytes 786440 | tf_op jit(solution)/shard_map/ppermute | solution.py:473
  40.9 4.4 %collective-permute-start.10 = (f32[32,128]{1,0:T(8,128)S(1)}, f32[32,128]{1,0:T(8,128)S(1)}, u32[]{:S(2)}, u32[]{:S(2)}) collective-permute-start(f32[32,128]{1,0:T(8,128)S(1)} %add.6), channel_id=1, source_target_pairs={{0,16},{4,20},{8,24},{12,28},{16,0},{20,4},{24,8},{28,12},{1,17},{... | collective-permute-start | bytes 49160 | tf_op jit(solution)/shard_map/ppermute | solution.py:479
  45.2 4.1 %collective-permute-start.13 = (f32[32,128]{1,0:T(8,128)S(1)}, f32[32,128]{1,0:T(8,128)S(1)}, u32[]{:S(2)}, u32[]{:S(2)}) collective-permute-start(f32[32,128]{1,0:T(8,128)S(1)} %add.7.total), channel_id=1, source_target_pairs={{0,4},{4,0},{8,12},{12,8},{16,20},{20,16},{24,28},{28,24},{1,5},{5... | collective-permute-start | bytes 49160 | tf_op jit(solution)/shard_map/ppermute | solution.py:473

commit v7 on v5

--- a/solution.py
+++ b/solution.py
@@ -83,12 +83,14 @@
     copies.append(pltpu.make_async_copy(cols_far, cols, sems.at[3]))
     for copy in copies:
         copy.start()
-    for copy in reversed(copies):
-        copy.wait()
+    copies[3].wait()
+    copies[2].wait()
     high, low = split_terms(sides.pick(w[:, :REACH], w[:, REACH:])[0])
     col = sides.pick(cols[:1, :REACH], cols[1:, REACH:])[0]
     spread = [jnp.broadcast_to(part.astype(F32), high.shape).astype(BF16) for part in (col >> 8, col & 255)]
     off[:, width:] = jnp.concatenate([high, low] + spread, 1)
+    copies[1].wait()
+    copies[0].wait()
 
 
 def inner(cols, wide, ops, acc, sides, ready=None):
@@ -157,15 +159,17 @@
     rim(cols, acc, wide, ops, Sides(ops.shape[0]), True, store)
 
 
-def first_off(cols, acc, wide_in, out_in, halo, ops, wide, out, send, slot):
+def first_off(cols, acc, wide_in, out_in, halo, ops, wide, out, send, slot, near_w, near_at, sums):
     size = ops.shape[2]
     width = REACH * size
     sides = Sides(ops.shape[0])
     wide[:, :width] = halo[:, :width]
     facts = halo[:, width:].astype(F32)
     weights = facts[:, :REACH] + facts[:, REACH : 2 * REACH]
-    col = as_column(facts[:1, 2 * REACH : 3 * REACH] * 256.0 + facts[:1, 3 * REACH : 4 * REACH]).astype(I32)
-    place = sides.place(col) - REACH
+    col = facts[:1, 2 * REACH : 3 * REACH] * 256.0 + facts[:1, 3 * REACH : 4 * REACH]
+    near_w[...] = weights
+    near_at[...] = sides.place(col.astype(I32))
+    place = sides.place(as_column(col).astype(I32)) - REACH
     place = jnp.where((place >= 0) & (place < REACH), place, -1)
     slot[...] = jnp.broadcast_to(place, slot.shape)
 
@@ -177,7 +181,8 @@
         at = slot[p, 0]
         x = lanes(out, REACH + jnp.maximum(at, 0), size)[...].astype(F32)
         part = jnp.sum(x * weights[:, p : p + 1], axis=0, keepdims=True)
-        send[p : p + 1, :] = jnp.where(at >= 0, part, 0.0)
+        sums[p : p + 1, :] = jnp.where(at >= 0, part, 0.0)
+    send[...] = sums[...].astype(BF16)
 
 
 def turned(sides, w):
@@ -242,7 +247,7 @@
     inc[rows + REACH :, :] = inc_mate[...]
     parts = []
     for i in range(REACH):
-        row = jnp.broadcast_to(halo[i : i + 1, :], (8, size)).astype(BF16)
+        row = jnp.broadcast_to(halo[i : i + 1, :].astype(F32), (8, size)).astype(BF16)
         parts.append(dot_t(row, ops[sides.off_row + i, sides.off_k]))
     for i, part in enumerate(parts):
         inc[rows + i : rows + i + 1, :] = inc_off[i : i + 1, :] + part[:1]
@@ -265,17 +270,9 @@
     chunks(REACH, some)
 
 
-def side_facts(cols, w, sides, near, out):
-    members = w.shape[0]
-    first, last = (REACH, 2 * REACH) if near else (0, REACH)
-    out[REACH : REACH + members, :REACH] = w[:, first:last]
-    off, mate = sides.pick(cols[:1, :REACH], cols[1:, REACH:])
-    out[REACH : REACH + 1, REACH : 2 * REACH] = (mate if near else off).astype(F32)
-
-
 def residual_rim(cols, inc, innov, prec, ops, w, one, two_off, two_mate, *rest):
-    received = rest[:-4]
-    res, send_off, send_mate, gw = rest[-4:]
+    received = rest[:-5]
+    res, rim_off, send_off, send_mate, gw = rest[-5:]
     rows, _, size, _ = ops.shape
     members = w.shape[0]
     sides = Sides(rows)
@@ -283,9 +280,11 @@
     for other in received:
         total = total + other[...].astype(F32)
     res[...] = prec[...] * (total * SCALE - innov[...])
-    for near, send in ((False, send_off), (True, send_mate)):
-        rim_rows(res, ops, sides, near, send)
-        side_facts(cols, w, sides, near, send)
+    rim_rows(res, ops, sides, False, rim_off)
+    rim_rows(res, ops, sides, True, send_mate)
+    send_off[:REACH, :] = rim_off[...].astype(BF16)
+    send_mate[REACH:, :REACH] = w[:, REACH:]
+    send_mate[REACH : REACH + 1, REACH : 2 * REACH] = sides.pick(cols[:1, :REACH], cols[1:, REACH:])[1].astype(F32)
     index = lax.broadcasted_iota(I32, (members, rows), 1)
     grown = jnp.zeros((members, rows), F32)
     for q in range(rows):
@@ -295,7 +294,8 @@
         grown = jnp.where(index == q, jnp.sum(prod, axis=1, keepdims=True), grown)
     grown = w[...] + SCALE * grown
     gw[...] = grown
-    send_off[REACH : REACH + members, 2 * REACH : 3 * REACH] = grown[:, :REACH]
+    high, low = split_terms(grown[:, :REACH])
+    send_off[REACH:, :] = jnp.concatenate([high, low, jnp.zeros((members, size - 2 * REACH), BF16)], 1)
 
 
 def residual_inner(res, ops, y):
@@ -341,7 +341,7 @@
     chunks(REACH, some)
 
 
-def adjoint_off(cols, col_rows, w, y, own_off, own_mate, off, mate, ops, one, gw, slot, mid, sums, send, vals, wp, tgt, squares):
+def adjoint_off(cols, col_rows, w, y, own_off, own_mate, off, mate, near_w, near_at, ops, one, gw, slot, mid, sums, send, vals, wp, tgt, squares):
     rows, _, size, _ = ops.shape
     members = w.shape[0]
     sides = Sides(rows)
@@ -357,11 +357,14 @@
     tgt[:, :rows] = lax.broadcasted_iota(I32, (1, rows), 1) + REACH
     for n, part in enumerate((rim_off, rim_mate, inner_off, inner_mate)):
         tgt[:, rows + n * REACH : rows + (n + 1) * REACH] = sides.place(part)
-    for n, part in enumerate((off, mate)):
-        where = slice(3 * rows + n * REACH, 3 * rows + (n + 1) * REACH)
-        vals[where, :] = part[:REACH, :].astype(BF16)
-        wp[:, where] = part[REACH : REACH + members, :REACH] * SCALE
-        tgt[:, where] = sides.place(part[REACH : REACH + 1, REACH : 2 * REACH].astype(I32))
+    where = slice(3 * rows, 3 * rows + REACH)
+    vals[where, :] = off[:REACH, :]
+    wp[:, where] = near_w[...] * SCALE
+    tgt[:, where] = near_at[...]
+    where = slice(3 * rows + REACH, 3 * rows + 2 * REACH)
+    vals[where, :] = mate[:REACH, :].astype(BF16)
+    wp[:, where] = mate[REACH:, :REACH] * SCALE
+    tgt[:, where] = sides.place(mate[REACH : REACH + 1, REACH : 2 * REACH].astype(I32))
     middle(wp[...], tgt[...], vals[...], 0, mid)
     adjoint_side(cols, mid, ops, sides, False, sums)
     send[:REACH] = sums[:REACH].astype(BF16)
@@ -369,13 +372,13 @@
     drawn = jnp.zeros((members, REACH), F32)
     for p in range(REACH):
         at = slot[p, 0]
-        x = lanes(one, REACH + jnp.maximum(at, 0), size)[...].astype(F32) * off[p : p + 1, :]
+        x = lanes(one, REACH + jnp.maximum(at, 0), size)[...].astype(F32) * off[p : p + 1, :].astype(F32)
         part = jnp.where(at >= 0, jnp.sum(x, axis=1, keepdims=True), 0.0)
         drawn = jnp.where(index == p, part, drawn)
     drawn = drawn * SCALE
     high, low = split_terms(drawn)
     send[REACH] = jnp.concatenate([high, low, jnp.zeros((members, size - 2 * REACH), BF16)], 1)
-    theirs = off[REACH : REACH + members, 2 * REACH : 3 * REACH]
+    theirs = off[REACH:, :REACH].astype(F32) + off[REACH:, REACH : 2 * REACH].astype(F32)
     grown = gw[...]
     total = jnp.sum(grown * grown, axis=1, keepdims=True)
     total = total + jnp.sum((2.0 * theirs + drawn) * drawn, axis=1, keepdims=True)
@@ -411,14 +414,15 @@
         chunks(REACH, some)
 
 
-def finish(own, off, mate, gw, total, out, direction, *, count):
-    rows, members, size = own.shape
-    sides = Sides(rows)
+def finish(own, off, mate, gw, total, mate_total, out, direction, *, count):
+    size = own.shape[2]
+    sides = Sides(own.shape[0])
     drawn = off[REACH].astype(F32)
+    drawn = drawn[:, :REACH] + drawn[:, REACH : 2 * REACH]
     grown = gw[...]
-    drawn = drawn[:, :REACH] + drawn[:, REACH : 2 * REACH]
     grown = jnp.concatenate([grown[:, :REACH] + drawn, grown[:, REACH:]], 1)
-    direction[...] = turned(sides, grown / jnp.sqrt(total[:, :1] / count + 1e-06))
+    mean = (total[:, :1] + mate_total[:, :1]) / count
+    direction[...] = turned(sides, grown / jnp.sqrt(mean + 1e-06))
     for row, q, halo in ((sides.off_row, 0, off), (sides.mate_row, REACH, mate)):
         for i in range(REACH):
             lanes(out, row + i, size)[...] = own[q + i] + halo[i].astype(F32)
@@ -503,11 +507,19 @@
         first_mate, [wide_kind, wide_kind, side_kind], (table, acc, wide, from_mate, ops), 1, alias={2: 0}
     )
     from_mate = to_mate(send)
-    wide, one, send, slot = run(
+    wide, one, send, slot, near_w, near_at = run(
         first_off,
-        [wide_kind, wide_kind, part_kind, ((REACH, size), I32)],
+        [
+            wide_kind,
+            wide_kind,
+            ((REACH, size), BF16),
+            ((REACH, size), I32),
+            ((members, REACH), F32),
+            ((1, REACH), I32),
+        ],
         (table, acc, wide, one, from_off, ops),
         1,
+        [pltpu.VMEM((REACH, size), F32)],
         alias={2: 0, 3: 1},
     )
     from_off = to_off(send)
@@ -523,9 +535,9 @@
     inc, send = run(second_off, [row_kind, (row_kind[0], BF16)], (from_off, ops, inc_one, inc_off, inc_mate))
     received = [lax.ppermute(send, "members", [(i, i ^ step) for i in range(groups)]) for step in range(1, groups)]
     pay_kind = ((REACH + members, size), F32)
-    res, own_off, own_mate, grad_weights = run(
+    res, rim_off, own_off, own_mate, grad_weights = run(
         residual_rim,
-        [row_kind, pay_kind, pay_kind, ((members, rows), F32)],
+        [row_kind, part_kind, (pay_kind[0], BF16), pay_kind, ((members, rows), F32)],
         (cols, inc, innov, prec, ops, w, one, two_off, two_mate, *received),
     )
     from_off, from_mate = to_off(own_off), to_mate(own_mate)
@@ -545,25 +557,27 @@
             ((1, pairs), I32),
             ((members, size), F32),
         ],
-        (table, cols, w, y, own_off, own_mate, from_off, from_mate, ops, one, grad_weights, slot),
+        (table, cols, w, y, rim_off, own_mate, from_off, from_mate, near_w, near_at, ops, one, grad_weights, slot),
         1,
     )
     from_off = to_off(send)
-    total = total + partner(total, 1)
+    total = total + partner(total, 2)
     mid_mate, sums_mate, send = run(
         adjoint_mate, [mid_kind, sums_kind, send_kind], (table, wp, tgt, vals, ops), 1
     )
     send, total = lax.optimization_barrier((send, total))
     from_mate = to_mate(send)
-    stride = 2
+    stride = 4
     while stride < tiles:
         total = total + partner(total, stride)
         stride *= 2
     (own,) = run(adjoint_inner, [acc_kind], (table, mid_off, mid_mate, sums_off, sums_mate, ops), 1)
+    total, own = lax.optimization_barrier((total, own))
+    mate_total = to_mate(total)
     grad_ens, direction = run(
         finish,
         [((members, length), F32), ((members, rows), F32)],
-        (own, from_off, from_mate, grad_weights, total),
+        (own, from_off, from_mate, grad_weights, total, mate_total),
         near=False,
         count=rows * tiles,
     )

time: 52.1 us -> 49.7 us (0.954)
  waiting for transfers between devices: 10.6 us -> 7.01 us
  starting transfers between devices: 24.3 us -> 25.9 us
    ppermute x3 -> x2, waiting for transfers between devices: 5.73 us -> 0.23 us  [partner(): return lax.ppermute(value, 'space', [(i, i ^ stride) for i in range(tiles)])]
    ppermute x3 -> x2, starting transfers between devices: 2.64 us -> 5.58 us  [partner(): return lax.ppermute(value, 'space', [(i, i ^ stride) for i in range(tiles)])]
    ppermute x4, starting transfers between devices: 17.2 us -> 14.6 us  [to_off(): return lax.ppermute(value, 'space', offs)]
    ppermute x4 -> x5, starting transfers between devices: 0.34 us -> 1.61 us  [to_mate(): return lax.ppermute(value, 'space', mates)]
    ppermute x4, waiting for transfers between devices: 1.57 us -> 2.61 us  [to_off(): return lax.ppermute(value, 'space', offs)]
    ppermute x4 -> x5, waiting for transfers between devices: 0.01 us -> 0.85 us  [to_mate(): return lax.ppermute(value, 'space', mates)]
  transfers between devices with their start and end apart: 14 -> 14, of which waited for: 6 -> 7; matrix products, arithmetic and copies ran while one was open for 0% -> 0% of each run, Pallas kernels for 20% -> 21%
where the time goes in v7:
time: 49.7 us; the launch traced here: 49.5 us
  starting transfers between devices  25.9 us (52%)
  Pallas kernels  15 us (30%)
  waiting for transfers between devices  7.01 us (14%)
  between operations  0.85 us (2%)
  local copies, waits for them, and re-layouts  0.7 us (1%)
    pallas_call x13, Pallas kernels, run(): pl.pallas_call(functools.partial(body, **fixed) if fixed else body, out_s...  15 us
    ppermute x4, starting transfers between devices, to_off(): return lax.ppermute(value, 'space', offs)  14.6 us
    ppermute x2, starting transfers between devices, partner(): return lax.ppermute(value, 'space', [(i, i ^ stride) for i in range(tiles)])  5.58 us
    ppermute x3, starting transfers between devices, on_device(): lax.ppermute(send, 'members', [(i, i ^ step) for i in range(groups)])  4.07 us
    ppermute x3, waiting for transfers between devices, on_device(): lax.ppermute(send, 'members', [(i, i ^ step) for i in range(groups)])  3.31 us
    ppermute x4, waiting for transfers between devices, to_off(): return lax.ppermute(value, 'space', offs)  2.61 us
    ppermute x5, starting transfers between devices, to_mate(): return lax.ppermute(value, 'space', mates)  1.61 us
  transfers between devices with their start and end apart: 14, of which 7 were waited for; matrix products, arithmetic and copies ran while one was open for 0% of the time, Pallas kernels for 21%

profile of v7, /device:TPU:1, one launch (start us, length us, event | category | flops | bytes accessed | tf_op | source)
XLA Modules:
  0.0 49.5 jit_solution(899565572333165659)
XLA Ops:
  0.6 1.2 %load.1 = (bf16[32,4224]{1,0:T(8,128)(2,1)S(1)}, bf16[32,4096]{1,0:T(8,128)(2,1)S(1)}) custom-call(bf16[32,8192]{1,0:T(8,128)(2,1)} %ens.1, f32[32,64]{1,0:T(8,128)} %w.1, s32[2,64]{1,0:T(2,128)} %bitcast.1), custom_call_target="tpu_custom_call" | custom-call | tf_op jit(solution)/shard_map/load/pallas_call | solution.py:443
  1.8 0.1 collective-permute-start
  1.9 4.5 %collective-permute-start.1 = (bf16[32,4224]{1,0:T(8,128)(2,1)S(1)}, bf16[32,4224]{1,0:T(8,128)(2,1)S(1)}, u32[]{:S(2)}, u32[]{:S(2)}) collective-permute-start(bf16[32,4224]{1,0:T(8,128)(2,1)S(1)} %get-tuple-element.47.off), channel_id=1, source_target_pairs={{4,8},{8,4},{12,16},{16,12},{20,24},{24,20},{5,9},{9,5},{13,17},{1... | collective-permute-start | bytes 811016 | tf_op jit(solution)/shard_map/ppermute | solution.py:476
  6.4 0.0 copy-start.3
  6.4 0.7 %copy-done.3 = s32[64,2]{0,1:T(2,128)S(1)} copy-done((s32[64,2]{0,1:T(2,128)S(1)}, s32[64,2]{0,1:T(2,128)}, u32[]{:S(2)}) %copy-start.3) | copy-done | bytes 536
  7.1 3.9 %first_inner.1 = (f32[64,32,128]{2,1,0:T(8,128)S(1)}, bf16[32,16384]{1,0:T(8,128)(2,1)S(1)}, bf16[64,3,128,128]{3,2,1,0:T(8,128)(2,1)S(1)}, s32[2,64]{1,0:T(2,128)S(4)}) custom-call(s32[2,64]{1,0:T(2,128)S(1)} %bitcast.2, bf16[32,4224]{1,0:T(8,128)(2,1)S(1)} %get-tuple-element.47.off, bf16[32,4096]{1,0:T(8,128)(2,1)S(1)} %get-tuple-element.48.mate, ...), custom_call_target="tpu_custom_call" | custom-call | tf_op jit(solution)/shard_map/first_inner/pallas_call | solution.py:443
  11.0 0.0 collective-permute-done.halo
  11.0 0.7 %first_mate.1 = (bf16[32,16384]{1,0:T(8,128)(2,1)S(1)}, bf16[32,16384]{1,0:T(8,128)(2,1)S(1)}, bf16[32,4096]{1,0:T(8,128)(2,1)S(1)}) custom-call(s32[2,64]{1,0:T(2,128)S(4)} %get-tuple-element.49.cols, f32[64,32,128]{2,1,0:T(8,128)S(1)} %get-tuple-element.50.acc, bf16[32,16384]{1,0:T(8,128)(2,1)S(1)} %get-tuple-element.51.wide_in, ...), custom_call_target="tpu_custom_call", output_to_operand_aliasing={{0}: (2, {})} | custom-call | tf_op jit(solution)/shard_map/first_mate/pallas_call | solution.py:443
  11.7 0.0 copy-start.1
  11.7 0.0 copy-start.2
  11.7 0.1 collective-permute-start.3
  11.8 0.7 %collective-permute-done.1.halo = bf16[32,4224]{1,0:T(8,128)(2,1)S(1)} collective-permute-done((bf16[32,4224]{1,0:T(8,128)(2,1)S(1)}, bf16[32,4224]{1,0:T(8,128)(2,1)S(1)}, u32[]{:S(2)}, u32[]{:S(2)}) %collective-permute-start.1) | collective-permute-done | bytes 270368 | tf_op jit(solution)/shard_map/ppermute | solution.py:476
  12.5 0.8 %first_off.1 = (bf16[32,16384]{1,0:T(8,128)(2,1)S(1)}, bf16[32,16384]{1,0:T(8,128)(2,1)S(1)}, bf16[32,128]{1,0:T(8,128)(2,1)S(1)}, s32[32,128]{1,0:T(8,128)S(1)}...) custom-call(s32[2,64]{1,0:T(2,128)S(4)} %get-tuple-element.49.cols, ...), custom_call_target="tpu_custom_call", output_to_operand_aliasing={{0}: (2, {}), {1}: (3, {})} | custom-call | tf_op jit(solution)/shard_map/first_off/pallas_call | solution.py:443
  13.3 2.8 %collective-permute-start.2 = (bf16[32,128]{1,0:T(8,128)(2,1)S(1)}, bf16[32,128]{1,0:T(8,128)(2,1)S(1)}, u32[]{:S(2)}, u32[]{:S(2)}) collective-permute-start(bf16[32,128]{1,0:T(8,128)(2,1)S(1)} %get-tuple-element.57), channel_id=1, source_target_pairs={{4,8},{8,4},{12,16},{16,12},{20,24},{24,20},{5,9},{9,5},{13,17},{1... | collective-permute-start | bytes 24584 | tf_op jit(solution)/shard_map/ppermute | solution.py:476
  16.1 0.0 copy-done
  16.1 2.2 %second_inner.1 = (f32[64,32,128]{2,1,0:T(8,128)S(1)}, f32[64,128]{1,0:T(8,128)S(1)}, f32[128,128]{1,0:T(8,128)S(1)}, f32[128,128]{1,0:T(8,128)S(1)}, f32[32,64]...) custom-call(s32[2,64]{1,0:T(2,128)S(4)} %get-tuple-element.49.cols, ...), custom_call_target="tpu_custom_call" | custom-call | tf_op jit(solution)/shard_map/second_inner/pallas_call | solution.py:443
  18.3 0.0 collective-permute-done.3.halo
  18.3 0.0 copy-start.4
  18.4 0.7 %second_mate.1 = (bf16[32,16384]{1,0:T(8,128)(2,1)S(1)}, bf16[32,4096]{1,0:T(8,128)(2,1)S(1)}, f32[32,128]{1,0:T(8,128)S(1)}) custom-call(s32[2,64]{1,0:T(2,128)S(4)} %get-tuple-element.49.cols, f32[64,32,128]{2,1,0:T(8,128)S(1)} %get-tuple-element.60.acc, bf16[32,16384]{1,0:T(8,128)(2,1)S(1)} %get-tuple-element.55.wide.wide_in, ...), custom_call_target="tpu_custom_call", output_to_operand_aliasing={{0}: (2, {})} | custom-call | tf_op jit(solution)/shard_map/second_mate/pallas_call | solution.py:443
  19.1 0.0 collective-permute-done.2.halo
  19.1 0.7 %second_off.1 = (f32[128,128]{1,0:T(8,128)S(1)}, bf16[128,128]{1,0:T(8,128)(2,1)S(1)}) custom-call(bf16[32,128]{1,0:T(8,128)(2,1)S(1)} %collective-permute-done.2.halo, bf16[64,3,128,128]{3,2,1,0:T(8,128)(2,1)S(1)} %get-tuple-element.52.ops, f32[64,128]{1,0:T(8,128)S(1)} %get-tuple-element.58.inc_one, f32[32,128]{1,0:T(8,128)S(1)} %get-tuple-element.59.inc_off, ...), custom_call_target="tpu_custom_call" | custom-call | tf_op jit(solution)/shard_map/second_off/pallas_call | solution.py:443
  19.8 3.7 %collective-permute-start.6 = (bf16[128,128]{1,0:T(8,128)(2,1)S(1)}, bf16[128,128]{1,0:T(8,128)(2,1)S(1)}, u32[]{:S(2)}, u32[]{:S(2)}) collective-permute-start(bf16[128,128]{1,0:T(8,128)(2,1)S(1)} %get-tuple-element.69), channel_id=1, source_target_pairs={{0,3},{1,2},{2,1},{3,0},{4,7},{5,6},{6,5},{7,4},{8,11},{9,10},{10,... | collective-permute-start | bytes 98312 | tf_op jit(solution)/shard_map/ppermute | solution.py:536
  23.5 0.0 collective-permute-start.5
  23.5 0.3 collective-permute-start.4
  23.9 0.9 %collective-permute-done.6.rest_2_ = bf16[128,128]{1,0:T(8,128)(2,1)S(1)} collective-permute-done((bf16[128,128]{1,0:T(8,128)(2,1)S(1)}, bf16[128,128]{1,0:T(8,128)(2,1)S(1)}, u32[]{:S(2)}, u32[]{:S(2)}) %collective-permute-start.6) | collective-permute-done | bytes 32800 | tf_op jit(solution)/shard_map/ppermute | solution.py:536
  24.8 2.4 %collective-permute-done.5.rest_1_ = bf16[128,128]{1,0:T(8,128)(2,1)S(1)} collective-permute-done((bf16[128,128]{1,0:T(8,128)(2,1)S(1)}, bf16[128,128]{1,0:T(8,128)(2,1)S(1)}, u32[]{:S(2)}, u32[]{:S(2)}) %collective-permute-start.5) | collective-permute-done | bytes 32800 | tf_op jit(solution)/shard_map/ppermute | solution.py:536
  27.2 0.0 collective-permute-done.4.rest_0_
  27.2 0.0 copy-done.4
  27.2 0.7 %residual_rim.1 = (f32[128,128]{1,0:T(8,128)S(1)}, f32[32,128]{1,0:T(8,128)S(1)}, bf16[64,128]{1,0:T(8,128)(2,1)S(1)}, f32[64,128]{1,0:T(8,128)S(1)}, f32[32,64]{1,0:T(8,128)S(1)}) custom-call(s32[2,64]{1,0:T(2,128)S(1)} %bitcast.3, f32[128,128]{1,0:T(8,128)S(1)} %get-tuple-element.63.inc, f32[128,128]{1,0:T(8,128)S(1)} %get-tuple-element.64.innov, ...), custom_call_target="tpu_custom_call" | custom-call | tf_op jit(solution)/shard_map/residual_rim/pallas_call | solution.py:443
  27.9 0.0 collective-permute-start.8
  27.9 5.5 %collective-permute-start.7 = (bf16[64,128]{1,0:T(8,128)(2,1)S(1)}, bf16[64,128]{1,0:T(8,128)(2,1)S(1)}, u32[]{:S(2)}, u32[]{:S(2)}) collective-permute-start(bf16[64,128]{1,0:T(8,128)(2,1)S(1)} %get-tuple-element.73), channel_id=1, source_target_pairs={{4,8},{8,4},{12,16},{16,12},{20,24},{24,20},{5,9},{9,5},{13,17},{1... | collective-permute-start | bytes 49160 | tf_op jit(solution)/shard_map/ppermute | solution.py:476
  33.4 0.7 %residual_inner.1.y = f32[128,128]{1,0:T(8,128)S(1)} custom-call(f32[128,128]{1,0:T(8,128)S(1)} %get-tuple-element.70.res, bf16[64,3,128,128]{3,2,1,0:T(8,128)(2,1)S(1)} %get-tuple-element.52.ops), custom_call_target="tpu_custom_call" | custom-call | tf_op jit(solution)/shard_map/residual_inner/pallas_call | solution.py:443
  34.1 0.7 %collective-permute-done.7.off = bf16[64,128]{1,0:T(8,128)(2,1)S(1)} collective-permute-done((bf16[64,128]{1,0:T(8,128)(2,1)S(1)}, bf16[64,128]{1,0:T(8,128)(2,1)S(1)}, u32[]{:S(2)}, u32[]{:S(2)}) %collective-permute-start.7) | collective-permute-done | bytes 16416 | tf_op jit(solution)/shard_map/ppermute | solution.py:476
  34.8 0.0 collective-permute-done.8.mate
  34.8 0.8 %adjoint_off.1 = (bf16[1024,128]{1,0:T(8,128)(2,1)S(1)}, f32[64,32,128]{2,1,0:T(8,128)S(1)}, bf16[33,32,128]{2,1,0:T(8,128)(2,1)S(1)}, bf16[256,128]{1,0:T(8,128...) custom-call(s32[2,64]{1,0:T(2,128)S(4)} %get-tuple-element.49.cols, ...), custom_call_target="tpu_custom_call" | custom-call | tf_op jit(solution)/shard_map/adjoint_off/pallas_call | solution.py:443
  35.6 2.4 %collective-permute-start.9 = (f32[32,128]{1,0:T(8,128)S(1)}, f32[32,128]{1,0:T(8,128)S(1)}, u32[]{:S(2)}, u32[]{:S(2)}) collective-permute-start(f32[32,128]{1,0:T(8,128)S(1)} %get-tuple-element.82), channel_id=1, source_target_pairs={{0,8},{4,12},{8,0},{12,4},{16,24},{20,28},{24,16},{28,20},{1,9},{5... | collective-permute-start | bytes 49160 | tf_op jit(solution)/shard_map/ppermute | solution.py:479
  38.1 1.9 %collective-permute-start.11 = (bf16[33,32,128]{2,1,0:T(8,128)(2,1)S(1)}, bf16[33,32,128]{2,1,0:T(8,128)(2,1)S(1)}, u32[]{:S(2)}, u32[]{:S(2)}) collective-permute-start(bf16[33,32,128]{2,1,0:T(8,128)(2,1)S(1)} %get-tuple-element.89), channel_id=1, source_target_pairs={{4,8},{8,4},{12,16},{16,12},{20,24},{24,20},{5,9},{9,5},{13,17},{1... | collective-permute-start | bytes 811016 | tf_op jit(solution)/shard_map/ppermute | solution.py:476
  40.0 0.7 %adjoint_mate.1 = (bf16[1024,128]{1,0:T(8,128)(2,1)S(1)}, f32[64,32,128]{2,1,0:T(8,128)S(1)}, bf16[32,32,128]{2,1,0:T(8,128)(2,1)S(1)}) custom-call(s32[2,64]{1,0:T(2,128)S(4)} %get-tuple-element.49.cols, f32[32,256]{1,0:T(8,128)S(1)} %get-tuple-element.78.wp, s32[1,256]{1,0:T(1,128)S(1)} %get-tuple-element.79.tgt, ...), custom_call_target="tpu_custom_call" | custom-call | tf_op jit(solution)/shard_map/adjoint_mate/pallas_call | solution.py:443
  40.7 0.0 collective-permute-done.9
  40.7 0.1 collective-permute-start.12
  40.8 3.1 %collective-permute-start.10 = (f32[32,128]{1,0:T(8,128)S(1)}, f32[32,128]{1,0:T(8,128)S(1)}, u32[]{:S(2)}, u32[]{:S(2)}) collective-permute-start(f32[32,128]{1,0:T(8,128)S(1)} %add.6), channel_id=1, source_target_pairs={{0,16},{4,20},{8,24},{12,28},{16,0},{20,4},{24,8},{28,12},{1,17},{... | collective-permute-start | bytes 49160 | tf_op jit(solution)/shard_map/ppermute | solution.py:479
  43.9 0.9 %adjoint_inner.1.own = f32[64,32,128]{2,1,0:T(8,128)S(1)} custom-call(s32[2,64]{1,0:T(2,128)S(4)} %get-tuple-element.49.cols, bf16[1024,128]{1,0:T(8,128)(2,1)S(1)} %get-tuple-element.84.mid_off, bf16[1024,128]{1,0:T(8,128)(2,1)S(1)} %get-tuple-element.85.mid_mate, f32[64,32,128]{2,1,0:T(8,128)S(1)} %get-tuple-element.86.sums_off, ...), custom_call_target="tpu_custom_call" | custom-call | tf_op jit(solution)/shard_map/adjoint_inner/pallas_call | solution.py:443
  44.8 0.2 collective-permute-done.10
  45.0 1.3 %collective-permute-start.13 = (f32[32,128]{1,0:T(8,128)S(1)}, f32[32,128]{1,0:T(8,128)S(1)}, u32[]{:S(2)}, u32[]{:S(2)}) collective-permute-start(f32[32,128]{1,0:T(8,128)S(1)} %add.7.total), channel_id=1, source_target_pairs={{0,4},{4,0},{8,12},{12,8},{16,20},{20,16},{24,28},{28,24},{1,5},{5... | collective-permute-start | bytes 49160 | tf_op jit(solution)/shard_map/ppermute | solution.py:473
  46.3 0.8 %collective-permute-done.13.mate_total = f32[32,128]{1,0:T(8,128)S(1)} collective-permute-done((f32[32,128]{1,0:T(8,128)S(1)}, f32[32,128]{1,0:T(8,128)S(1)}, u32[]{:S(2)}, u32[]{:S(2)}) %collective-permute-start.13) | collective-permute-done | bytes 16416 | tf_op jit(solution)/shard_map/ppermute | solution.py:473
  47.2 1.1 %collective-permute-done.11.off = bf16[33,32,128]{2,1,0:T(8,128)(2,1)S(1)} collective-permute-done((bf16[33,32,128]{2,1,0:T(8,128)(2,1)S(1)}, bf16[33,32,128]{2,1,0:T(8,128)(2,1)S(1)}, u32[]{:S(2)}, u32[]{:S(2)}) %collective-permute-start.11) | collective-permute-done | bytes 270368 | tf_op jit(solution)/shard_map/ppermute | solution.py:476
  48.3 0.0 collective-permute-done.12.mate
  48.3 1.2 %finish.1 = (f32[32,8192]{1,0:T(8,128)}, f32[32,64]{1,0:T(8,128)}) custom-call(f32[64,32,128]{2,1,0:T(8,128)S(1)} %adjoint_inner.1.own, bf16[33,32,128]{2,1,0:T(8,128)(2,1)S(1)} %collective-permute-done.11.off, bf16[32,32,128]{2,1,0:T(8,128)(2,1)S(1)} %collective-permute-done.12.mate, f32[32,64]{1,0:T(8,128)S(1)} %get-tuple-element.76.gw, ...), custom_call_target="tpu_custom_call" | custom-call | tf_op jit(solution)/shard_map/finish/pallas_call | solution.py:443
  (5 shorter events, 0.0 us)
Async XLA Ops:
  1.8 9.2 %collective-permute-start = (bf16[32,4096]{1,0:T(8,128)(2,1)S(1)}, bf16[32,4096]{1,0:T(8,128)(2,1)S(1)}, u32[]{:S(2)}, u32[]{:S(2)}) collective-permute-start(bf16[32,4096]{1,0:T(8,128)(2,1)S(1)} %get-tuple-element.48.mate), channel_id=1, source_target_pairs={{0,4},{4,0},{8,12},{12,8},{16,20},{20,16},{24,28},{28,24},{1,5},{5... | collective-permute-start | bytes 786440 | tf_op jit(solution)/shard_map/ppermute | solution.py:473
  1.9 10.6 %collective-permute-start.1 = (bf16[32,4224]{1,0:T(8,128)(2,1)S(1)}, bf16[32,4224]{1,0:T(8,128)(2,1)S(1)}, u32[]{:S(2)}, u32[]{:S(2)}) collective-permute-start(bf16[32,4224]{1,0:T(8,128)(2,1)S(1)} %get-tuple-element.47.off), channel_id=1, source_target_pairs={{4,8},{8,4},{12,16},{16,12},{20,24},{24,20},{5,9},{9,5},{13,17},{1... | collective-permute-start | bytes 811016 | tf_op jit(solution)/shard_map/ppermute | solution.py:476
  6.4 0.7 %copy-start.3 = (s32[64,2]{0,1:T(2,128)S(1)}, s32[64,2]{0,1:T(2,128)}, u32[]{:S(2)}) copy-start(s32[64,2]{0,1:T(2,128)} %param.8) | copy-start | bytes 1540
  11.7 4.4 %copy-start = (f32[2,8192]{1,0:T(2,128)S(1)}, f32[2,8192]{1,0:T(2,128)}, u32[]{:S(2)}) copy-start(f32[2,8192]{1,0:T(2,128)} %innov.1) | copy-start | bytes 196612
  11.7 4.4 %copy-start.1 = (f32[2,8192]{1,0:T(2,128)S(1)}, f32[2,8192]{1,0:T(2,128)}, u32[]{:S(2)}) copy-start(f32[2,8192]{1,0:T(2,128)} %prec.1) | copy-start | bytes 196612
  11.7 4.4 %copy-start.2 = (f32[32,64]{1,0:T(8,128)S(1)}, f32[32,64]{1,0:T(8,128)}, u32[]{:S(2)}) copy-start(f32[32,64]{1,0:T(8,128)} %w.1) | copy-start | bytes 24580
  11.7 6.6 %collective-permute-start.3 = (bf16[32,4096]{1,0:T(8,128)(2,1)S(1)}, bf16[32,4096]{1,0:T(8,128)(2,1)S(1)}, u32[]{:S(2)}, u32[]{:S(2)}) collective-permute-start(bf16[32,4096]{1,0:T(8,128)(2,1)S(1)} %get-tuple-element.61), channel_id=1, source_target_pairs={{0,4},{4,0},{8,12},{12,8},{16,20},{20,16},{24,28},{28,24},{1,5},{5... | collective-permute-start | bytes 786440 | tf_op jit(solution)/shard_map/ppermute | solution.py:473
  13.3 5.8 %collective-permute-start.2 = (bf16[32,128]{1,0:T(8,128)(2,1)S(1)}, bf16[32,128]{1,0:T(8,128)(2,1)S(1)}, u32[]{:S(2)}, u32[]{:S(2)}) collective-permute-start(bf16[32,128]{1,0:T(8,128)(2,1)S(1)} %get-tuple-element.57), channel_id=1, source_target_pairs={{4,8},{8,4},{12,16},{16,12},{20,24},{24,20},{5,9},{9,5},{13,17},{1... | collective-permute-start | bytes 24584 | tf_op jit(solution)/shard_map/ppermute | solution.py:476
  18.3 8.8 %copy-start.4 = (s32[64,2]{0,1:T(2,128)S(1)}, s32[64,2]{0,1:T(2,128)}, u32[]{:S(2)}) copy-start(s32[64,2]{0,1:T(2,128)} %param.8) | copy-start | bytes 1540
  19.8 5.0 %collective-permute-start.6 = (bf16[128,128]{1,0:T(8,128)(2,1)S(1)}, bf16[128,128]{1,0:T(8,128)(2,1)S(1)}, u32[]{:S(2)}, u32[]{:S(2)}) collective-permute-start(bf16[128,128]{1,0:T(8,128)(2,1)S(1)} %get-tuple-element.69), channel_id=1, source_target_pairs={{0,3},{1,2},{2,1},{3,0},{4,7},{5,6},{6,5},{7,4},{8,11},{9,10},{10,... | collective-permute-start | bytes 98312 | tf_op jit(solution)/shard_map/ppermute | solution.py:536
  23.5 3.7 %collective-permute-start.5 = (bf16[128,128]{1,0:T(8,128)(2,1)S(1)}, bf16[128,128]{1,0:T(8,128)(2,1)S(1)}, u32[]{:S(2)}, u32[]{:S(2)}) collective-permute-start(bf16[128,128]{1,0:T(8,128)(2,1)S(1)} %get-tuple-element.69), channel_id=1, source_target_pairs={{0,2},{1,3},{2,0},{3,1},{4,6},{5,7},{6,4},{7,5},{8,10},{9,11},{10,... | collective-permute-start | bytes 98312 | tf_op jit(solution)/shard_map/ppermute | solution.py:536
  23.5 3.7 %collective-permute-start.4 = (bf16[128,128]{1,0:T(8,128)(2,1)S(1)}, bf16[128,128]{1,0:T(8,128)(2,1)S(1)}, u32[]{:S(2)}, u32[]{:S(2)}) collective-permute-start(bf16[128,128]{1,0:T(8,128)(2,1)S(1)} %get-tuple-element.69), channel_id=1, source_target_pairs={{0,1},{1,0},{2,3},{3,2},{4,5},{5,4},{6,7},{7,6},{8,9},{9,8},{10,11... | collective-permute-start | bytes 98312 | tf_op jit(solution)/shard_map/ppermute | solution.py:536
  27.9 7.0 %collective-permute-start.8 = (f32[64,128]{1,0:T(8,128)S(1)}, f32[64,128]{1,0:T(8,128)S(1)}, u32[]{:S(2)}, u32[]{:S(2)}) collective-permute-start(f32[64,128]{1,0:T(8,128)S(1)} %get-tuple-element.72.own_mate), channel_id=1, source_target_pairs={{0,4},{4,0},{8,12},{12,8},{16,20},{20,16},{24,28},{28,24},{1,5},{5... | collective-permute-start | bytes 98312 | tf_op jit(solution)/shard_map/ppermute | solution.py:473
  27.9 6.9 %collective-permute-start.7 = (bf16[64,128]{1,0:T(8,128)(2,1)S(1)}, bf16[64,128]{1,0:T(8,128)(2,1)S(1)}, u32[]{:S(2)}, u32[]{:S(2)}) collective-permute-start(bf16[64,128]{1,0:T(8,128)(2,1)S(1)} %get-tuple-element.73), channel_id=1, source_target_pairs={{4,8},{8,4},{12,16},{16,12},{20,24},{24,20},{5,9},{9,5},{13,17},{1... | collective-permute-start | bytes 49160 | tf_op jit(solution)/shard_map/ppermute | solution.py:476
  35.6 5.0 %collective-permute-start.9 = (f32[32,128]{1,0:T(8,128)S(1)}, f32[32,128]{1,0:T(8,128)S(1)}, u32[]{:S(2)}, u32[]{:S(2)}) collective-permute-start(f32[32,128]{1,0:T(8,128)S(1)} %get-tuple-element.82), channel_id=1, source_target_pairs={{0,8},{4,12},{8,0},{12,4},{16,24},{20,28},{24,16},{28,20},{1,9},{5... | collective-permute-start | bytes 49160 | tf_op jit(solution)/shard_map/ppermute | solution.py:479
  38.1 10.2 %collective-permute-start.11 = (bf16[33,32,128]{2,1,0:T(8,128)(2,1)S(1)}, bf16[33,32,128]{2,1,0:T(8,128)(2,1)S(1)}, u32[]{:S(2)}, u32[]{:S(2)}) collective-permute-start(bf16[33,32,128]{2,1,0:T(8,128)(2,1)S(1)} %get-tuple-element.89), channel_id=1, source_target_pairs={{4,8},{8,4},{12,16},{16,12},{20,24},{24,20},{5,9},{9,5},{13,17},{1... | collective-permute-start | bytes 811016 | tf_op jit(solution)/shard_map/ppermute | solution.py:476
  40.7 7.6 %collective-permute-start.12 = (bf16[32,32,128]{2,1,0:T(8,128)(2,1)S(1)}, bf16[32,32,128]{2,1,0:T(8,128)(2,1)S(1)}, u32[]{:S(2)}, u32[]{:S(2)}) collective-permute-start(bf16[32,32,128]{2,1,0:T(8,128)(2,1)S(1)} %get-tuple-element.90), channel_id=1, source_target_pairs={{0,4},{4,0},{8,12},{12,8},{16,20},{20,16},{24,28},{28,24},{1,5},{5... | collective-permute-start | bytes 786440 | tf_op jit(solution)/shard_map/ppermute | solution.py:473
  40.8 4.3 %collective-permute-start.10 = (f32[32,128]{1,0:T(8,128)S(1)}, f32[32,128]{1,0:T(8,128)S(1)}, u32[]{:S(2)}, u32[]{:S(2)}) collective-permute-start(f32[32,128]{1,0:T(8,128)S(1)} %add.6), channel_id=1, source_target_pairs={{0,16},{4,20},{8,24},{12,28},{16,0},{20,4},{24,8},{28,12},{1,17},{... | collective-permute-start | bytes 49160 | tf_op jit(solution)/shard_map/ppermute | solution.py:479
  45.0 2.1 %collective-permute-start.13 = (f32[32,128]{1,0:T(8,128)S(1)}, f32[32,128]{1,0:T(8,128)S(1)}, u32[]{:S(2)}, u32[]{:S(2)}) collective-permute-start(f32[32,128]{1,0:T(8,128)S(1)} %add.7.total), channel_id=1, source_target_pairs={{0,4},{4,0},{8,12},{12,8},{16,20},{20,16},{24,28},{28,24},{1,5},{5... | collective-permute-start | bytes 49160 | tf_op jit(solution)/shard_map/ppermute | solution.py:473

commit v8 on v7

--- a/solution.py
+++ b/solution.py
@@ -14,6 +14,7 @@
 BF16 = jnp.bfloat16
 I32 = jnp.int32
 UNROLL = 32
+HOPS = 5
 
 
 def dot_t(x, a):
@@ -196,7 +197,30 @@
         store(i, jnp.sum(x * w[:, first + i : first + i + 1], axis=0, keepdims=True))
 
 
-def second_inner(cols, wide, ops, w, innov, prec, acc, inc, innov_rows, prec_rows, w_turned, two_off, inc_off):
+def rim_and_inner(col, sides):
+    rim_off, rim_mate = sides.pick(col[:1, :REACH], col[1:, REACH:])
+    inner_off, inner_mate = sides.pick(col[1:, :REACH], col[:1, REACH:])
+    return [sides.place(part) for part in (rim_off, rim_mate, inner_off, inner_mate)]
+
+
+def hop_rows(cols, col_rows, near_at, sides, shape):
+    rim_off, _, inner_off, inner_mate = rim_and_inner(col_rows, sides)
+    own = lax.broadcasted_iota(I32, (1, REACH), 1) + REACH
+    blank = jnp.full((1, 3 * REACH), -1, I32)
+    targets = (jnp.concatenate([own, rim_off, inner_off, inner_mate], 1), jnp.concatenate([near_at, blank], 1))
+    found = [jnp.full(target.shape, -1, I32) for target in targets]
+    for i in range(REACH):
+        hop = sides.place(cols[sides.off_k - 1, sides.off_row + i])
+        hop = jnp.where(hop < REACH, hop, -1)
+        found = [jnp.where(target == REACH + i, hop, old) for target, old in zip(targets, found)]
+    row = lax.broadcasted_iota(I32, shape, 0)
+    first, second = [jnp.broadcast_to(part, shape) for part in found]
+    return jnp.where(row == 0, first, jnp.where(row == 1, second, -1)).astype(F32).astype(BF16)
+
+
+def second_inner(
+    cols, wide, ops, w, innov, prec, col_rows, near_at, acc, inc, innov_rows, prec_rows, w_turned, two_off, inc_off, hops
+):
     rows, _, size, _ = ops.shape
     sides = Sides(rows)
     inner(cols, wide, ops, acc, sides)
@@ -223,6 +247,7 @@
         inc_off[i : i + 1, :] = s
 
     member_sums(two_off, 0, weights, 0, REACH, size, keep)
+    hops[...] = hop_rows(cols, col_rows[...], near_at[...], sides, hops.shape)
 
 
 def second_mate(cols, acc, wide_in, halo, ops, w, wide, out, inc):
@@ -270,7 +295,7 @@
     chunks(REACH, some)
 
 
-def residual_rim(cols, inc, innov, prec, ops, w, one, two_off, two_mate, *rest):
+def residual_rim(cols, inc, innov, prec, ops, w, one, two_off, two_mate, hops, *rest):
     received = rest[:-5]
     res, rim_off, send_off, send_mate, gw = rest[-5:]
     rows, _, size, _ = ops.shape
@@ -294,8 +319,9 @@
         grown = jnp.where(index == q, jnp.sum(prod, axis=1, keepdims=True), grown)
     grown = w[...] + SCALE * grown
     gw[...] = grown
-    high, low = split_terms(grown[:, :REACH])
-    send_off[REACH:, :] = jnp.concatenate([high, low, jnp.zeros((members, size - 2 * REACH), BF16)], 1)
+    terms = split_terms(grown[:, :REACH]) + split_terms(w[:, REACH:])
+    send_off[REACH : REACH + members, :] = jnp.concatenate(terms, 1)
+    send_off[REACH + members :, :] = hops[...]
 
 
 def residual_inner(res, ops, y):
@@ -341,33 +367,32 @@
     chunks(REACH, some)
 
 
-def adjoint_off(cols, col_rows, w, y, own_off, own_mate, off, mate, near_w, near_at, ops, one, gw, slot, mid, sums, send, vals, wp, tgt, squares):
+def adjoint_off(
+    cols, col_rows, w, y, own_off, own_mate, off, mate, near_w, near_at, ops, one, gw, slot, send, vals, wp, tgt, squares, hop
+):
     rows, _, size, _ = ops.shape
     members = w.shape[0]
     sides = Sides(rows)
-    vals[:rows, :] = y[:rows, :].astype(BF16)
-    vals[2 * rows : 3 * rows, :] = y[rows:, :].astype(BF16)
-    for n, part in enumerate((own_off, own_mate)):
-        vals[rows + n * REACH : rows + (n + 1) * REACH, :] = part[:REACH, :].astype(BF16)
-    for k in range(3):
-        wp[:, k * rows : (k + 1) * rows] = w[...] * SCALE
-    col = col_rows[...]
-    rim_off, rim_mate = sides.pick(col[:1, :REACH], col[1:, REACH:])
-    inner_off, inner_mate = sides.pick(col[1:, :REACH], col[:1, REACH:])
-    tgt[:, :rows] = lax.broadcasted_iota(I32, (1, rows), 1) + REACH
-    for n, part in enumerate((rim_off, rim_mate, inner_off, inner_mate)):
-        tgt[:, rows + n * REACH : rows + (n + 1) * REACH] = sides.place(part)
-    where = slice(3 * rows, 3 * rows + REACH)
-    vals[where, :] = off[:REACH, :]
-    wp[:, where] = near_w[...] * SCALE
-    tgt[:, where] = near_at[...]
-    where = slice(3 * rows + REACH, 3 * rows + 2 * REACH)
-    vals[where, :] = mate[:REACH, :].astype(BF16)
-    wp[:, where] = mate[REACH:, :REACH] * SCALE
-    tgt[:, where] = sides.place(mate[REACH : REACH + 1, REACH : 2 * REACH].astype(I32))
-    middle(wp[...], tgt[...], vals[...], 0, mid)
-    adjoint_side(cols, mid, ops, sides, False, sums)
-    send[:REACH] = sums[:REACH].astype(BF16)
+
+    def point(k, row, i):
+        return sides.place(cols[k - 1, row + i]) - REACH
+
+    groups = (
+        (y, 0, lambda i: i),
+        (own_off, 0, lambda i: point(sides.off_k, sides.off_row, i)),
+        (y, rows, lambda i: point(sides.mate_k, sides.off_row, i)),
+        (y, rows + REACH, lambda i: point(sides.off_k, sides.mate_row, i)),
+        (off, 0, lambda i: slot[i, 0]),
+    )
+    for n, (source, start, at) in enumerate(groups):
+        outs = []
+        for i in range(REACH):
+            row = jnp.broadcast_to(source[start + i : start + i + 1, :].astype(F32), (8, size)).astype(BF16)
+            place = jnp.clip(at(i), 0, REACH - 1)
+            outs.append(dot_n(row, ops[sides.off_row + place, sides.off_k]))
+        for i, o in enumerate(outs):
+            hop[n * REACH + i : n * REACH + i + 1, :] = o[:1]
+    send[: HOPS * REACH, :] = hop[...].astype(BF16)
     index = lax.broadcasted_iota(I32, (members, REACH), 1)
     drawn = jnp.zeros((members, REACH), F32)
     for p in range(REACH):
@@ -377,34 +402,53 @@
         drawn = jnp.where(index == p, part, drawn)
     drawn = drawn * SCALE
     high, low = split_terms(drawn)
-    send[REACH] = jnp.concatenate([high, low, jnp.zeros((members, size - 2 * REACH), BF16)], 1)
-    theirs = off[REACH:, :REACH].astype(F32) + off[REACH:, REACH : 2 * REACH].astype(F32)
+    send[HOPS * REACH :, :] = jnp.concatenate([high, low, jnp.zeros((members, size - 2 * REACH), BF16)], 1)
+    theirs = off[REACH : REACH + members, : 2 * REACH].astype(F32)
+    theirs = theirs[:, :REACH] + theirs[:, REACH:]
     grown = gw[...]
     total = jnp.sum(grown * grown, axis=1, keepdims=True)
     total = total + jnp.sum((2.0 * theirs + drawn) * drawn, axis=1, keepdims=True)
     squares[...] = jnp.broadcast_to(total, squares.shape)
-
-
-def adjoint_mate(cols, wp, tgt, vals, ops, mid, sums, send):
-    sides = Sides(ops.shape[0])
-    middle(wp[...], tgt[...], vals[...], REACH, mid)
-    adjoint_side(cols, mid, ops, sides, True, sums)
+    vals[:rows, :] = y[:rows, :].astype(BF16)
+    vals[2 * rows : 3 * rows, :] = y[rows:, :].astype(BF16)
+    for n, part in enumerate((own_off, own_mate)):
+        vals[rows + n * REACH : rows + (n + 1) * REACH, :] = part[:REACH, :].astype(BF16)
+    for k in range(3):
+        wp[:, k * rows : (k + 1) * rows] = w[...] * SCALE
+    tgt[:, :rows] = lax.broadcasted_iota(I32, (1, rows), 1) + REACH
+    for n, part in enumerate(rim_and_inner(col_rows[...], sides)):
+        tgt[:, rows + n * REACH : rows + (n + 1) * REACH] = part
+    where = slice(3 * rows, 3 * rows + REACH)
+    vals[where, :] = off[:REACH, :]
+    wp[:, where] = near_w[...] * SCALE
+    tgt[:, where] = near_at[...]
+    where = slice(3 * rows + REACH, 3 * rows + 2 * REACH)
+    vals[where, :] = mate[:REACH, :].astype(BF16)
+    wp[:, where] = mate[REACH:, :REACH] * SCALE
+    tgt[:, where] = sides.place(mate[REACH : REACH + 1, REACH : 2 * REACH].astype(I32))
+
+
+def adjoint_mate(cols, mid, ops, sums, send):
+    adjoint_side(cols, mid, ops, Sides(ops.shape[0]), True, sums)
     send[...] = sums[REACH:].astype(BF16)
 
 
-def adjoint_inner(cols, mid_off, mid_mate, sums_off, sums_mate, ops, out):
+def adjoint_inner(cols, wp, tgt, vals, ops, w, near, near_w, out, spread, mid_mate, mid_off, sums_off):
     rows, _, size, _ = ops.shape
-    members = sums_off.shape[1]
-    sides = Sides(rows)
+    members = w.shape[0]
+    sides = Sides(rows)
+    middle(wp[...], tgt[...], vals[...], 0, mid_off)
+    middle(wp[...], tgt[...], vals[...], REACH, mid_mate)
+    adjoint_side(cols, mid_off, ops, sides, False, sums_off)
     out[:REACH] = sums_off[REACH:]
-    out[REACH:] = sums_mate[:REACH]
+    out[REACH:] = jnp.zeros((REACH, members, size), F32)
     for row, k, q, mid in ((sides.off_row, sides.mate_k, 0, mid_off), (sides.mate_row, sides.off_k, REACH, mid_mate)):
 
         def some(ids, row=row, k=k, q=q, mid=mid):
             outs = []
             for i in ids:
                 r = row + i
-                x = mid[pl.ds(pl.multiple_of(i * members, members), members), :]
+                x = mid[pl.ds(i * members if isinstance(i, int) else pl.multiple_of(i * members, members), members), :]
                 o = dot_n(x, jnp.concatenate([ops[r, 0], ops[r, k]], 1))
                 outs.append((q + i, o[:, :size]))
                 outs.append((sides.place(cols[k - 1, r]) - REACH, o[:, size:]))
@@ -412,20 +456,36 @@
                 out[place] = out[place] + o
 
         chunks(REACH, some)
-
-
-def finish(own, off, mate, gw, total, mate_total, out, direction, *, count):
-    size = own.shape[2]
-    sides = Sides(own.shape[0])
-    drawn = off[REACH].astype(F32)
+    terms = near[REACH : REACH + members, 2 * REACH :].astype(F32)
+    far_w = terms[:, :REACH] + terms[:, REACH:]
+    near_rows = near_w[...]
+    blank = jnp.zeros((members, (8 - HOPS) * REACH), F32)
+    weights = jnp.concatenate([near_rows, near_rows, near_rows, far_w, w[:, :REACH], blank], 1) * SCALE
+    hops = near[REACH + members :, :].astype(F32)
+    target = jnp.concatenate([hops[:1, :], hops[1:2, :]], 1)
+    for c in range(REACH):
+        spread[c * members : (c + 1) * members, :] = jnp.where(target == float(c), weights, 0.0).astype(BF16)
+
+
+def finish(own, sums_mate, off, mate, spread, gw, total, mate_total, out, direction, vectors, *, count):
+    rows, members, size = own.shape
+    sides = Sides(rows)
+    vectors[: HOPS * REACH, :] = off[: HOPS * REACH, :]
+    vectors[HOPS * REACH :, :] = jnp.zeros(((8 - HOPS) * REACH, size), BF16)
+    for i in range(REACH):
+        lanes(out, sides.mate_row + i, size)[...] = own[REACH + i] + (sums_mate[i] + mate[i].astype(F32))
+    group = 8
+    for g in range(REACH // group):
+        halo = dot_n(spread[g * group * members : (g + 1) * group * members, :], vectors[...])
+        for c in range(group):
+            i = g * group + c
+            lanes(out, sides.off_row + i, size)[...] = own[i] + halo[c * members : (c + 1) * members, :]
+    drawn = off[HOPS * REACH :, :].astype(F32)
     drawn = drawn[:, :REACH] + drawn[:, REACH : 2 * REACH]
     grown = gw[...]
     grown = jnp.concatenate([grown[:, :REACH] + drawn, grown[:, REACH:]], 1)
     mean = (total[:, :1] + mate_total[:, :1]) / count
     direction[...] = turned(sides, grown / jnp.sqrt(mean + 1e-06))
-    for row, q, halo in ((sides.off_row, 0, off), (sides.mate_row, REACH, mate)):
-        for i in range(REACH):
-            lanes(out, row + i, size)[...] = own[q + i] + halo[i].astype(F32)
 
 
 SMEM = pl.BlockSpec(memory_space=pltpu.SMEM)
@@ -523,10 +583,19 @@
         alias={2: 0, 3: 1},
     )
     from_off = to_off(send)
-    acc, inc_one, innov, prec, w, two_off, inc_off = run(
+    acc, inc_one, innov, prec, w, two_off, inc_off, hops = run(
         second_inner,
-        [acc_kind, ((rows, size), F32), row_kind, row_kind, ((members, rows), F32), side_kind, part_kind],
-        (table, one, ops, weights, innovations, obs_precision),
+        [
+            acc_kind,
+            ((rows, size), F32),
+            row_kind,
+            row_kind,
+            ((members, rows), F32),
+            side_kind,
+            part_kind,
+            ((16, size), BF16),
+        ],
+        (table, one, ops, weights, innovations, obs_precision, cols, near_at),
         1,
     )
     one, two_mate, inc_mate = run(
@@ -537,8 +606,8 @@
     pay_kind = ((REACH + members, size), F32)
     res, rim_off, own_off, own_mate, grad_weights = run(
         residual_rim,
-        [row_kind, part_kind, (pay_kind[0], BF16), pay_kind, ((members, rows), F32)],
-        (cols, inc, innov, prec, ops, w, one, two_off, two_mate, *received),
+        [row_kind, part_kind, ((REACH + members + 16, size), BF16), pay_kind, ((members, rows), F32)],
+        (cols, inc, innov, prec, ops, w, one, two_off, two_mate, hops, *received),
     )
     from_off, from_mate = to_off(own_off), to_mate(own_mate)
     (y,) = run(residual_inner, [row_kind], (res, ops))
@@ -546,12 +615,10 @@
     mid_kind = ((REACH * members, size), BF16)
     sums_kind = ((2 * REACH, members, size), F32)
     send_kind = ((REACH, members, size), BF16)
-    mid_off, sums_off, send, vals, wp, tgt, total = run(
+    send, vals, wp, tgt, total = run(
         adjoint_off,
         [
-            mid_kind,
-            sums_kind,
-            ((REACH + 1, members, size), BF16),
+            ((HOPS * REACH + members, size), BF16),
             ((pairs, size), BF16),
             ((members, pairs), F32),
             ((1, pairs), I32),
@@ -559,25 +626,32 @@
         ],
         (table, cols, w, y, rim_off, own_mate, from_off, from_mate, near_w, near_at, ops, one, grad_weights, slot),
         1,
-    )
+        [pltpu.VMEM((HOPS * REACH, size), F32)],
+    )
+    near = from_off
     from_off = to_off(send)
     total = total + partner(total, 2)
-    mid_mate, sums_mate, send = run(
-        adjoint_mate, [mid_kind, sums_kind, send_kind], (table, wp, tgt, vals, ops), 1
-    )
-    send, total = lax.optimization_barrier((send, total))
-    from_mate = to_mate(send)
+    own, spread, mid_mate = run(
+        adjoint_inner,
+        [acc_kind, ((REACH * members, 8 * REACH), BF16), mid_kind],
+        (table, wp, tgt, vals, ops, w, near, near_w),
+        1,
+        [pltpu.VMEM(*mid_kind), pltpu.VMEM(*sums_kind)],
+    )
+    mid_mate, from_off, total = lax.optimization_barrier((mid_mate, from_off, total))
     stride = 4
     while stride < tiles:
         total = total + partner(total, stride)
         stride *= 2
-    (own,) = run(adjoint_inner, [acc_kind], (table, mid_off, mid_mate, sums_off, sums_mate, ops), 1)
-    total, own = lax.optimization_barrier((total, own))
+    sums_mate, send = run(adjoint_mate, [sums_kind, send_kind], (table, mid_mate, ops), 1)
+    from_mate = to_mate(send)
     mate_total = to_mate(total)
     grad_ens, direction = run(
         finish,
         [((members, length), F32), ((members, rows), F32)],
-        (own, from_off, from_mate, grad_weights, total, mate_total),
+        (own, sums_mate, from_off, from_mate, spread, grad_weights, total, mate_total),
+        0,
+        [pltpu.VMEM((8 * REACH, size), BF16)],
         near=False,
         count=rows * tiles,
     )

time: 49.7 us -> 52.6 us (1.058)
  Pallas kernels: 15 us -> 16.6 us
  starting transfers between devices: 25.9 us -> 27.1 us
    ppermute x4, starting transfers between devices: 14.6 us -> 16.4 us  [to_off(): return lax.ppermute(value, 'space', offs)]
    pallas_call x13, Pallas kernels: 15 us -> 16.6 us  [run(): pl.pallas_call(functools.partial(body, **fixed) if fixed else body, out_s...]
    ppermute x4, waiting for transfers between devices: 2.61 us -> 1.5 us  [to_off(): return lax.ppermute(value, 'space', offs)]
    ppermute x2, waiting for transfers between devices: 0.23 us -> 1.15 us  [partner(): return lax.ppermute(value, 'space', [(i, i ^ stride) for i in range(tiles)])]
    ppermute x2, starting transfers between devices: 5.58 us -> 4.75 us  [partner(): return lax.ppermute(value, 'space', [(i, i ^ stride) for i in range(tiles)])]
  transfers between devices with their start and end apart: 14 -> 14, of which waited for: 7 -> 6; matrix products, arithmetic and copies ran while one was open for 0% -> 0% of each run, Pallas kernels for 21% -> 21%
where the time goes in v8:
time: 52.6 us; the launch traced here: 52 us
  starting transfers between devices  27.1 us (52%)
  Pallas kernels  16.6 us (32%)
  waiting for transfers between devices  6.82 us (13%)
  between operations  0.86 us (2%)
  local copies, waits for them, and re-layouts  0.7 us (1%)
    pallas_call x13, Pallas kernels, run(): pl.pallas_call(functools.partial(body, **fixed) if fixed else body, out_s...  16.6 us
    ppermute x4, starting transfers between devices, to_off(): return lax.ppermute(value, 'space', offs)  16.4 us
    ppermute x2, starting transfers between devices, partner(): return lax.ppermute(value, 'space', [(i, i ^ stride) for i in range(tiles)])  4.75 us
    ppermute x3, starting transfers between devices, on_device(): lax.ppermute(send, 'members', [(i, i ^ step) for i in range(groups)])  4.05 us
    ppermute x3, waiting for transfers between devices, on_device(): lax.ppermute(send, 'members', [(i, i ^ step) for i in range(groups)])  3.31 us
    ppermute x5, starting transfers between devices, to_mate(): return lax.ppermute(value, 'space', mates)  1.89 us
    ppermute x4, waiting for transfers between devices, to_off(): return lax.ppermute(value, 'space', offs)  1.5 us
    ppermute x2, waiting for transfers between devices, partner(): return lax.ppermute(value, 'space', [(i, i ^ stride) for i in range(tiles)])  1.15 us
  transfers between devices with their start and end apart: 14, of which 6 were waited for; matrix products, arithmetic and copies ran while one was open for 0% of the time, Pallas kernels for 21%

profile of v8, /device:TPU:1, one launch (start us, length us, event | category | flops | bytes accessed | tf_op | source)
XLA Modules:
  0.0 52.0 jit_solution(5984578935346251924)
XLA Ops:
  0.6 1.2 %load.1 = (bf16[32,4224]{1,0:T(8,128)(2,1)S(1)}, bf16[32,4096]{1,0:T(8,128)(2,1)S(1)}) custom-call(bf16[32,8192]{1,0:T(8,128)(2,1)} %ens.1, f32[32,64]{1,0:T(8,128)} %w.1, s32[2,64]{1,0:T(2,128)} %bitcast.1), custom_call_target="tpu_custom_call" | custom-call | tf_op jit(solution)/shard_map/load/pallas_call | solution.py:503
  1.8 0.1 collective-permute-start
  1.9 4.5 %collective-permute-start.1 = (bf16[32,4224]{1,0:T(8,128)(2,1)S(1)}, bf16[32,4224]{1,0:T(8,128)(2,1)S(1)}, u32[]{:S(2)}, u32[]{:S(2)}) collective-permute-start(bf16[32,4224]{1,0:T(8,128)(2,1)S(1)} %get-tuple-element.47.off), channel_id=1, source_target_pairs={{4,8},{8,4},{12,16},{16,12},{20,24},{24,20},{5,9},{9,5},{13,17},{1... | collective-permute-start | bytes 811016 | tf_op jit(solution)/shard_map/ppermute | solution.py:536
  6.4 0.0 copy-start.3
  6.4 0.7 %copy-done.3 = s32[64,2]{0,1:T(2,128)S(1)} copy-done((s32[64,2]{0,1:T(2,128)S(1)}, s32[64,2]{0,1:T(2,128)}, u32[]{:S(2)}) %copy-start.3) | copy-done | bytes 536
  7.1 3.9 %first_inner.1 = (f32[64,32,128]{2,1,0:T(8,128)S(1)}, bf16[32,16384]{1,0:T(8,128)(2,1)S(1)}, bf16[64,3,128,128]{3,2,1,0:T(8,128)(2,1)S(1)}, s32[2,64]{1,0:T(2,128)S(4)}) custom-call(s32[2,64]{1,0:T(2,128)S(1)} %bitcast.2, bf16[32,4224]{1,0:T(8,128)(2,1)S(1)} %get-tuple-element.47.off, bf16[32,4096]{1,0:T(8,128)(2,1)S(1)} %get-tuple-element.48.mate, ...), custom_call_target="tpu_custom_call" | custom-call | tf_op jit(solution)/shard_map/first_inner/pallas_call | solution.py:503
  11.0 0.0 collective-permute-done.halo
  11.0 0.7 %first_mate.1 = (bf16[32,16384]{1,0:T(8,128)(2,1)S(1)}, bf16[32,16384]{1,0:T(8,128)(2,1)S(1)}, bf16[32,4096]{1,0:T(8,128)(2,1)S(1)}) custom-call(s32[2,64]{1,0:T(2,128)S(4)} %get-tuple-element.49.cols, f32[64,32,128]{2,1,0:T(8,128)S(1)} %get-tuple-element.50.acc, bf16[32,16384]{1,0:T(8,128)(2,1)S(1)} %get-tuple-element.51.wide_in, ...), custom_call_target="tpu_custom_call", output_to_operand_aliasing={{0}: (2, {})} | custom-call | tf_op jit(solution)/shard_map/first_mate/pallas_call | solution.py:503
  11.7 0.0 copy-start.1
  11.7 0.0 copy-start.2
  11.7 0.0 copy-start.4
  11.7 0.1 collective-permute-start.3
  11.8 0.7 %collective-permute-done.1.halo = bf16[32,4224]{1,0:T(8,128)(2,1)S(1)} collective-permute-done((bf16[32,4224]{1,0:T(8,128)(2,1)S(1)}, bf16[32,4224]{1,0:T(8,128)(2,1)S(1)}, u32[]{:S(2)}, u32[]{:S(2)}) %collective-permute-start.1) | collective-permute-done | bytes 270368 | tf_op jit(solution)/shard_map/ppermute | solution.py:536
  12.5 0.8 %first_off.1 = (bf16[32,16384]{1,0:T(8,128)(2,1)S(1)}, bf16[32,16384]{1,0:T(8,128)(2,1)S(1)}, bf16[32,128]{1,0:T(8,128)(2,1)S(1)}, s32[32,128]{1,0:T(8,128)S(1)}...) custom-call(s32[2,64]{1,0:T(2,128)S(4)} %get-tuple-element.49.cols, ...), custom_call_target="tpu_custom_call", output_to_operand_aliasing={{0}: (2, {}), {1}: (3, {})} | custom-call | tf_op jit(solution)/shard_map/first_off/pallas_call | solution.py:503
  13.3 2.8 %collective-permute-start.2 = (bf16[32,128]{1,0:T(8,128)(2,1)S(1)}, bf16[32,128]{1,0:T(8,128)(2,1)S(1)}, u32[]{:S(2)}, u32[]{:S(2)}) collective-permute-start(bf16[32,128]{1,0:T(8,128)(2,1)S(1)} %get-tuple-element.58), channel_id=1, source_target_pairs={{4,8},{8,4},{12,16},{16,12},{20,24},{24,20},{5,9},{9,5},{13,17},{1... | collective-permute-start | bytes 24584 | tf_op jit(solution)/shard_map/ppermute | solution.py:536
  16.1 0.0 copy-done
  16.1 0.0 copy-done.1
  16.1 2.2 %second_inner.1 = (f32[64,32,128]{2,1,0:T(8,128)S(1)}, f32[64,128]{1,0:T(8,128)S(1)}, f32[128,128]{1,0:T(8,128)S(1)}, f32[128,128]{1,0:T(8,128)S(1)}, f32[32,64]...) custom-call(s32[2,64]{1,0:T(2,128)S(4)} %get-tuple-element.49.cols, ...), custom_call_target="tpu_custom_call" | custom-call | tf_op jit(solution)/shard_map/second_inner/pallas_call | solution.py:503
  18.4 0.0 collective-permute-done.3.halo
  18.4 0.7 %second_mate.1 = (bf16[32,16384]{1,0:T(8,128)(2,1)S(1)}, bf16[32,4096]{1,0:T(8,128)(2,1)S(1)}, f32[32,128]{1,0:T(8,128)S(1)}) custom-call(s32[2,64]{1,0:T(2,128)S(4)} %get-tuple-element.49.cols, f32[64,32,128]{2,1,0:T(8,128)S(1)} %get-tuple-element.61.acc, bf16[32,16384]{1,0:T(8,128)(2,1)S(1)} %get-tuple-element.55.wide.wide_in, ...), custom_call_target="tpu_custom_call", output_to_operand_aliasing={{0}: (2, {})} | custom-call | tf_op jit(solution)/shard_map/second_mate/pallas_call | solution.py:503
  19.1 0.0 collective-permute-done.2.halo
  19.2 0.7 %second_off.1 = (f32[128,128]{1,0:T(8,128)S(1)}, bf16[128,128]{1,0:T(8,128)(2,1)S(1)}) custom-call(bf16[32,128]{1,0:T(8,128)(2,1)S(1)} %collective-permute-done.2.halo, bf16[64,3,128,128]{3,2,1,0:T(8,128)(2,1)S(1)} %get-tuple-element.52.ops, f32[64,128]{1,0:T(8,128)S(1)} %get-tuple-element.59.inc_one, f32[32,128]{1,0:T(8,128)S(1)} %get-tuple-element.60.inc_off, ...), custom_call_target="tpu_custom_call" | custom-call | tf_op jit(solution)/shard_map/second_off/pallas_call | solution.py:503
  19.8 3.7 %collective-permute-start.6 = (bf16[128,128]{1,0:T(8,128)(2,1)S(1)}, bf16[128,128]{1,0:T(8,128)(2,1)S(1)}, u32[]{:S(2)}, u32[]{:S(2)}) collective-permute-start(bf16[128,128]{1,0:T(8,128)(2,1)S(1)} %get-tuple-element.71), channel_id=1, source_target_pairs={{0,3},{1,2},{2,1},{3,0},{4,7},{5,6},{6,5},{7,4},{8,11},{9,10},{10,... | collective-permute-start | bytes 98312 | tf_op jit(solution)/shard_map/ppermute | solution.py:605
  23.5 0.0 collective-permute-start.5
  23.5 0.3 collective-permute-start.4
  23.9 0.9 %collective-permute-done.6.rest_2_ = bf16[128,128]{1,0:T(8,128)(2,1)S(1)} collective-permute-done((bf16[128,128]{1,0:T(8,128)(2,1)S(1)}, bf16[128,128]{1,0:T(8,128)(2,1)S(1)}, u32[]{:S(2)}, u32[]{:S(2)}) %collective-permute-start.6) | collective-permute-done | bytes 32800 | tf_op jit(solution)/shard_map/ppermute | solution.py:605
  24.8 2.4 %collective-permute-done.5.rest_1_ = bf16[128,128]{1,0:T(8,128)(2,1)S(1)} collective-permute-done((bf16[128,128]{1,0:T(8,128)(2,1)S(1)}, bf16[128,128]{1,0:T(8,128)(2,1)S(1)}, u32[]{:S(2)}, u32[]{:S(2)}) %collective-permute-start.5) | collective-permute-done | bytes 32800 | tf_op jit(solution)/shard_map/ppermute | solution.py:605
  27.2 0.0 collective-permute-done.4.rest_0_
  27.2 0.7 %residual_rim.1 = (f32[128,128]{1,0:T(8,128)S(1)}, f32[32,128]{1,0:T(8,128)S(1)}, bf16[80,128]{1,0:T(8,128)(2,1)S(1)}, f32[64,128]{1,0:T(8,128)S(1)}, f32[32,64]{1,0:T(8,128)S(1)}) custom-call(s32[2,64]{1,0:T(2,128)S(1)} %bitcast.4, f32[128,128]{1,0:T(8,128)S(1)} %get-tuple-element.64.inc, f32[128,128]{1,0:T(8,128)S(1)} %get-tuple-element.65.innov, ...), custom_call_target="tpu_custom_call" | custom-call | tf_op jit(solution)/shard_map/residual_rim/pallas_call | solution.py:503
  27.9 0.0 collective-permute-start.8
  28.0 5.5 %collective-permute-start.7 = (bf16[80,128]{1,0:T(8,128)(2,1)S(1)}, bf16[80,128]{1,0:T(8,128)(2,1)S(1)}, u32[]{:S(2)}, u32[]{:S(2)}) collective-permute-start(bf16[80,128]{1,0:T(8,128)(2,1)S(1)} %get-tuple-element.75), channel_id=1, source_target_pairs={{4,8},{8,4},{12,16},{16,12},{20,24},{24,20},{5,9},{9,5},{13,17},{1... | collective-permute-start | bytes 61448 | tf_op jit(solution)/shard_map/ppermute | solution.py:536
  33.5 0.7 %residual_inner.1.y = f32[128,128]{1,0:T(8,128)S(1)} custom-call(f32[128,128]{1,0:T(8,128)S(1)} %get-tuple-element.72.res, bf16[64,3,128,128]{3,2,1,0:T(8,128)(2,1)S(1)} %get-tuple-element.52.ops), custom_call_target="tpu_custom_call" | custom-call | tf_op jit(solution)/shard_map/residual_inner/pallas_call | solution.py:503
  34.1 0.8 %collective-permute-done.7.off.near = bf16[80,128]{1,0:T(8,128)(2,1)S(1)} collective-permute-done((bf16[80,128]{1,0:T(8,128)(2,1)S(1)}, bf16[80,128]{1,0:T(8,128)(2,1)S(1)}, u32[]{:S(2)}, u32[]{:S(2)}) %collective-permute-start.7) | collective-permute-done | bytes 20512 | tf_op jit(solution)/shard_map/ppermute | solution.py:536
  34.9 0.0 collective-permute-done.8.mate
  34.9 1.6 %adjoint_off.1 = (bf16[192,128]{1,0:T(8,128)(2,1)S(1)}, bf16[256,128]{1,0:T(8,128)(2,1)S(1)}, f32[32,256]{1,0:T(8,128)S(1)}, s32[1,256]{1,0:T(1,128)S(1)}, f32[32,128]{1,0:T(8,128)S(1)}) custom-call(s32[2,64]{1,0:T(2,128)S(4)} %get-tuple-element.49.cols, s32[2,64]{1,0:T(2,128)S(1)} %bitcast.5, f32[32,64]{1,0:T(8,128)S(1)} %get-tuple-element.57.w, ...), custom_call_target="tpu_custom_call" | custom-call | tf_op jit(solution)/shard_map/adjoint_off/pallas_call | solution.py:503
  36.5 3.6 %collective-permute-start.9 = (bf16[192,128]{1,0:T(8,128)(2,1)S(1)}, bf16[192,128]{1,0:T(8,128)(2,1)S(1)}, u32[]{:S(2)}, u32[]{:S(2)}) collective-permute-start(bf16[192,128]{1,0:T(8,128)(2,1)S(1)} %get-tuple-element.84), channel_id=1, source_target_pairs={{4,8},{8,4},{12,16},{16,12},{20,24},{24,20},{5,9},{9,5},{13,17},{1... | collective-permute-start | bytes 147464 | tf_op jit(solution)/shard_map/ppermute | solution.py:536
  40.1 3.2 %collective-permute-start.10 = (f32[32,128]{1,0:T(8,128)S(1)}, f32[32,128]{1,0:T(8,128)S(1)}, u32[]{:S(2)}, u32[]{:S(2)}) collective-permute-start(f32[32,128]{1,0:T(8,128)S(1)} %get-tuple-element.85), channel_id=1, source_target_pairs={{0,8},{4,12},{8,0},{12,4},{16,24},{20,28},{24,16},{28,20},{1,9},{5... | collective-permute-start | bytes 49160 | tf_op jit(solution)/shard_map/ppermute | solution.py:539
  43.4 1.7 %adjoint_inner.1 = (f32[64,32,128]{2,1,0:T(8,128)S(1)}, bf16[1024,256]{1,0:T(8,128)(2,1)S(1)}, bf16[1024,128]{1,0:T(8,128)(2,1)S(1)}) custom-call(s32[2,64]{1,0:T(2,128)S(4)} %get-tuple-element.49.cols, f32[32,256]{1,0:T(8,128)S(1)} %get-tuple-element.79.wp, s32[1,256]{1,0:T(1,128)S(1)} %get-tuple-element.80.tgt, ...), custom_call_target="tpu_custom_call" | custom-call | tf_op jit(solution)/shard_map/adjoint_inner/pallas_call | solution.py:503
  45.1 0.0 collective-permute-done.10
  45.1 0.0 collective-permute-done.9.off
  45.1 0.4 adjoint_mate.1
  45.6 0.1 collective-permute-start.11
  45.6 1.5 %collective-permute-start.12 = (f32[32,128]{1,0:T(8,128)S(1)}, f32[32,128]{1,0:T(8,128)S(1)}, u32[]{:S(2)}, u32[]{:S(2)}) collective-permute-start(f32[32,128]{1,0:T(8,128)S(1)} %add.6), channel_id=1, source_target_pairs={{0,16},{4,20},{8,24},{12,28},{16,0},{20,4},{24,8},{28,12},{1,17},{... | collective-permute-start | bytes 49160 | tf_op jit(solution)/shard_map/ppermute | solution.py:539
  47.2 1.1 %collective-permute-done.12 = f32[32,128]{1,0:T(8,128)S(1)} collective-permute-done((f32[32,128]{1,0:T(8,128)S(1)}, f32[32,128]{1,0:T(8,128)S(1)}, u32[]{:S(2)}, u32[]{:S(2)}) %collective-permute-start.12) | collective-permute-done | bytes 16416 | tf_op jit(solution)/shard_map/ppermute | solution.py:539
  48.3 1.6 %collective-permute-start.13 = (f32[32,128]{1,0:T(8,128)S(1)}, f32[32,128]{1,0:T(8,128)S(1)}, u32[]{:S(2)}, u32[]{:S(2)}) collective-permute-start(f32[32,128]{1,0:T(8,128)S(1)} %add.7.total), channel_id=1, source_target_pairs={{0,4},{4,0},{8,12},{12,8},{16,20},{20,16},{24,28},{28,24},{1,5},{5... | collective-permute-start | bytes 49160 | tf_op jit(solution)/shard_map/ppermute | solution.py:533
  49.9 0.8 %collective-permute-done.13.mate_total = f32[32,128]{1,0:T(8,128)S(1)} collective-permute-done((f32[32,128]{1,0:T(8,128)S(1)}, f32[32,128]{1,0:T(8,128)S(1)}, u32[]{:S(2)}, u32[]{:S(2)}) %collective-permute-start.13) | collective-permute-done | bytes 16416 | tf_op jit(solution)/shard_map/ppermute | solution.py:533
  50.7 0.0 collective-permute-done.11.mate
  50.7 1.3 %finish.1 = (f32[32,8192]{1,0:T(8,128)}, f32[32,64]{1,0:T(8,128)}) custom-call(f32[64,32,128]{2,1,0:T(8,128)S(1)} %get-tuple-element.82.own, f32[64,32,128]{2,1,0:T(8,128)S(1)} %get-tuple-element.87.sums_mate, bf16[192,128]{1,0:T(8,128)(2,1)S(1)} %collective-permute-done.9.off, bf16[32,32,128]{2,1,0:T(8,128)(2,1)S(1)} %collective-permute-done.11.mate, ...), custom_call_target="tpu_custom_call" | custom-call | tf_op jit(solution)/shard_map/finish/pallas_call | solution.py:503
  (5 shorter events, 0.0 us)
Async XLA Ops:
  1.8 9.2 %collective-permute-start = (bf16[32,4096]{1,0:T(8,128)(2,1)S(1)}, bf16[32,4096]{1,0:T(8,128)(2,1)S(1)}, u32[]{:S(2)}, u32[]{:S(2)}) collective-permute-start(bf16[32,4096]{1,0:T(8,128)(2,1)S(1)} %get-tuple-element.48.mate), channel_id=1, source_target_pairs={{0,4},{4,0},{8,12},{12,8},{16,20},{20,16},{24,28},{28,24},{1,5},{5... | collective-permute-start | bytes 786440 | tf_op jit(solution)/shard_map/ppermute | solution.py:533
  1.9 10.6 %collective-permute-start.1 = (bf16[32,4224]{1,0:T(8,128)(2,1)S(1)}, bf16[32,4224]{1,0:T(8,128)(2,1)S(1)}, u32[]{:S(2)}, u32[]{:S(2)}) collective-permute-start(bf16[32,4224]{1,0:T(8,128)(2,1)S(1)} %get-tuple-element.47.off), channel_id=1, source_target_pairs={{4,8},{8,4},{12,16},{16,12},{20,24},{24,20},{5,9},{9,5},{13,17},{1... | collective-permute-start | bytes 811016 | tf_op jit(solution)/shard_map/ppermute | solution.py:536
  6.4 0.7 %copy-start.3 = (s32[64,2]{0,1:T(2,128)S(1)}, s32[64,2]{0,1:T(2,128)}, u32[]{:S(2)}) copy-start(s32[64,2]{0,1:T(2,128)} %param.8) | copy-start | bytes 1540
  11.7 4.4 %copy-start = (f32[2,8192]{1,0:T(2,128)S(1)}, f32[2,8192]{1,0:T(2,128)}, u32[]{:S(2)}) copy-start(f32[2,8192]{1,0:T(2,128)} %innov.1) | copy-start | bytes 196612
  11.7 4.4 %copy-start.1 = (f32[2,8192]{1,0:T(2,128)S(1)}, f32[2,8192]{1,0:T(2,128)}, u32[]{:S(2)}) copy-start(f32[2,8192]{1,0:T(2,128)} %prec.1) | copy-start | bytes 196612
  11.7 4.4 %copy-start.2 = (f32[32,64]{1,0:T(8,128)S(1)}, f32[32,64]{1,0:T(8,128)}, u32[]{:S(2)}) copy-start(f32[32,64]{1,0:T(8,128)} %w.1) | copy-start | bytes 24580
  11.7 4.4 %copy-start.4 = (s32[64,2]{0,1:T(2,128)S(1)}, s32[64,2]{0,1:T(2,128)}, u32[]{:S(2)}) copy-start(s32[64,2]{0,1:T(2,128)} %param.8) | copy-start | bytes 1540
  11.7 6.7 %collective-permute-start.3 = (bf16[32,4096]{1,0:T(8,128)(2,1)S(1)}, bf16[32,4096]{1,0:T(8,128)(2,1)S(1)}, u32[]{:S(2)}, u32[]{:S(2)}) collective-permute-start(bf16[32,4096]{1,0:T(8,128)(2,1)S(1)} %get-tuple-element.62), channel_id=1, source_target_pairs={{0,4},{4,0},{8,12},{12,8},{16,20},{20,16},{24,28},{28,24},{1,5},{5... | collective-permute-start | bytes 786440 | tf_op jit(solution)/shard_map/ppermute | solution.py:533
  13.3 5.8 %collective-permute-start.2 = (bf16[32,128]{1,0:T(8,128)(2,1)S(1)}, bf16[32,128]{1,0:T(8,128)(2,1)S(1)}, u32[]{:S(2)}, u32[]{:S(2)}) collective-permute-start(bf16[32,128]{1,0:T(8,128)(2,1)S(1)} %get-tuple-element.58), channel_id=1, source_target_pairs={{4,8},{8,4},{12,16},{16,12},{20,24},{24,20},{5,9},{9,5},{13,17},{1... | collective-permute-start | bytes 24584 | tf_op jit(solution)/shard_map/ppermute | solution.py:536
  19.8 5.0 %collective-permute-start.6 = (bf16[128,128]{1,0:T(8,128)(2,1)S(1)}, bf16[128,128]{1,0:T(8,128)(2,1)S(1)}, u32[]{:S(2)}, u32[]{:S(2)}) collective-permute-start(bf16[128,128]{1,0:T(8,128)(2,1)S(1)} %get-tuple-element.71), channel_id=1, source_target_pairs={{0,3},{1,2},{2,1},{3,0},{4,7},{5,6},{6,5},{7,4},{8,11},{9,10},{10,... | collective-permute-start | bytes 98312 | tf_op jit(solution)/shard_map/ppermute | solution.py:605
  23.5 3.7 %collective-permute-start.5 = (bf16[128,128]{1,0:T(8,128)(2,1)S(1)}, bf16[128,128]{1,0:T(8,128)(2,1)S(1)}, u32[]{:S(2)}, u32[]{:S(2)}) collective-permute-start(bf16[128,128]{1,0:T(8,128)(2,1)S(1)} %get-tuple-element.71), channel_id=1, source_target_pairs={{0,2},{1,3},{2,0},{3,1},{4,6},{5,7},{6,4},{7,5},{8,10},{9,11},{10,... | collective-permute-start | bytes 98312 | tf_op jit(solution)/shard_map/ppermute | solution.py:605
  23.5 3.7 %collective-permute-start.4 = (bf16[128,128]{1,0:T(8,128)(2,1)S(1)}, bf16[128,128]{1,0:T(8,128)(2,1)S(1)}, u32[]{:S(2)}, u32[]{:S(2)}) collective-permute-start(bf16[128,128]{1,0:T(8,128)(2,1)S(1)} %get-tuple-element.71), channel_id=1, source_target_pairs={{0,1},{1,0},{2,3},{3,2},{4,5},{5,4},{6,7},{7,6},{8,9},{9,8},{10,11... | collective-permute-start | bytes 98312 | tf_op jit(solution)/shard_map/ppermute | solution.py:605
  27.9 7.0 %collective-permute-start.8 = (f32[64,128]{1,0:T(8,128)S(1)}, f32[64,128]{1,0:T(8,128)S(1)}, u32[]{:S(2)}, u32[]{:S(2)}) collective-permute-start(f32[64,128]{1,0:T(8,128)S(1)} %get-tuple-element.74.own_mate), channel_id=1, source_target_pairs={{0,4},{4,0},{8,12},{12,8},{16,20},{20,16},{24,28},{28,24},{1,5},{5... | collective-permute-start | bytes 98312 | tf_op jit(solution)/shard_map/ppermute | solution.py:533
  28.0 7.0 %collective-permute-start.7 = (bf16[80,128]{1,0:T(8,128)(2,1)S(1)}, bf16[80,128]{1,0:T(8,128)(2,1)S(1)}, u32[]{:S(2)}, u32[]{:S(2)}) collective-permute-start(bf16[80,128]{1,0:T(8,128)(2,1)S(1)} %get-tuple-element.75), channel_id=1, source_target_pairs={{4,8},{8,4},{12,16},{16,12},{20,24},{24,20},{5,9},{9,5},{13,17},{1... | collective-permute-start | bytes 61448 | tf_op jit(solution)/shard_map/ppermute | solution.py:536
  36.5 8.6 %collective-permute-start.9 = (bf16[192,128]{1,0:T(8,128)(2,1)S(1)}, bf16[192,128]{1,0:T(8,128)(2,1)S(1)}, u32[]{:S(2)}, u32[]{:S(2)}) collective-permute-start(bf16[192,128]{1,0:T(8,128)(2,1)S(1)} %get-tuple-element.84), channel_id=1, source_target_pairs={{4,8},{8,4},{12,16},{16,12},{20,24},{24,20},{5,9},{9,5},{13,17},{1... | collective-permute-start | bytes 147464 | tf_op jit(solution)/shard_map/ppermute | solution.py:536
  40.1 4.9 %collective-permute-start.10 = (f32[32,128]{1,0:T(8,128)S(1)}, f32[32,128]{1,0:T(8,128)S(1)}, u32[]{:S(2)}, u32[]{:S(2)}) collective-permute-start(f32[32,128]{1,0:T(8,128)S(1)} %get-tuple-element.85), channel_id=1, source_target_pairs={{0,8},{4,12},{8,0},{12,4},{16,24},{20,28},{24,16},{28,20},{1,9},{5... | collective-permute-start | bytes 49160 | tf_op jit(solution)/shard_map/ppermute | solution.py:539
  45.6 5.2 %collective-permute-start.11 = (bf16[32,32,128]{2,1,0:T(8,128)(2,1)S(1)}, bf16[32,32,128]{2,1,0:T(8,128)(2,1)S(1)}, u32[]{:S(2)}, u32[]{:S(2)}) collective-permute-start(bf16[32,32,128]{2,1,0:T(8,128)(2,1)S(1)} %get-tuple-element.89), channel_id=1, source_target_pairs={{0,4},{4,0},{8,12},{12,8},{16,20},{20,16},{24,28},{28,24},{1,5},{5... | collective-permute-start | bytes 786440 | tf_op jit(solution)/shard_map/ppermute | solution.py:533
  45.6 2.7 %collective-permute-start.12 = (f32[32,128]{1,0:T(8,128)S(1)}, f32[32,128]{1,0:T(8,128)S(1)}, u32[]{:S(2)}, u32[]{:S(2)}) collective-permute-start(f32[32,128]{1,0:T(8,128)S(1)} %add.6), channel_id=1, source_target_pairs={{0,16},{4,20},{8,24},{12,28},{16,0},{20,4},{24,8},{28,12},{1,17},{... | collective-permute-start | bytes 49160 | tf_op jit(solution)/shard_map/ppermute | solution.py:539
  48.3 2.4 %collective-permute-start.13 = (f32[32,128]{1,0:T(8,128)S(1)}, f32[32,128]{1,0:T(8,128)S(1)}, u32[]{:S(2)}, u32[]{:S(2)}) collective-permute-start(f32[32,128]{1,0:T(8,128)S(1)} %add.7.total), channel_id=1, source_target_pairs={{0,4},{4,0},{8,12},{12,8},{16,20},{20,16},{24,28},{28,24},{1,5},{5... | collective-permute-start | bytes 49160 | tf_op jit(solution)/shard_map/ppermute | solution.py:533

commit v9 on v7

--- a/solution.py
+++ b/solution.py
@@ -414,18 +414,38 @@
         chunks(REACH, some)
 
 
-def finish(own, off, mate, gw, total, mate_total, out, direction, *, count):
+def write_side(own, q, halo, row, out, half, sems):
     size = own.shape[2]
+    groups = sems.shape[0]
+    step = REACH // groups
+    copies = []
+    for g in range(groups):
+        for i in range(g * step, (g + 1) * step):
+            half[:, i * size : (i + 1) * size] = own[q + i] + halo[i].astype(F32)
+        part = half.at[:, g * step * size : (g + 1) * step * size]
+        place = out.at[:, pl.ds(pl.multiple_of((row + g * step) * size, size), step * size)]
+        copies.append(pltpu.make_async_copy(part, place, sems.at[g]))
+        copies[-1].start()
+    return copies
+
+
+def finish_mate(own, mate, out, half, sems):
     sides = Sides(own.shape[0])
+    for copy in write_side(own, REACH, mate, sides.mate_row, out, half, sems):
+        copy.wait()
+
+
+def finish_off(own, off, gw, total, mate_total, out_in, out, direction, half, sems, *, count):
+    sides = Sides(own.shape[0])
+    copies = write_side(own, 0, off, sides.off_row, out, half, sems)
     drawn = off[REACH].astype(F32)
     drawn = drawn[:, :REACH] + drawn[:, REACH : 2 * REACH]
     grown = gw[...]
     grown = jnp.concatenate([grown[:, :REACH] + drawn, grown[:, REACH:]], 1)
     mean = (total[:, :1] + mate_total[:, :1]) / count
     direction[...] = turned(sides, grown / jnp.sqrt(mean + 1e-06))
-    for row, q, halo in ((sides.off_row, 0, off), (sides.mate_row, REACH, mate)):
-        for i in range(REACH):
-            lanes(out, row + i, size)[...] = own[q + i] + halo[i].astype(F32)
+    for copy in copies:
+        copy.wait()
 
 
 SMEM = pl.BlockSpec(memory_space=pltpu.SMEM)
@@ -433,10 +453,10 @@
 FAR = pl.BlockSpec(memory_space=pltpu.HBM)
 
 
-def run(body, outs, args, scalars=0, scratch=(), far=0, alias=None, near=True, table=None, **fixed):
+def run(body, outs, args, scalars=0, scratch=(), far=0, alias=None, near=True, far_outs=0, table=None, **fixed):
     kind_of = pltpu.VMEM if near else jax.ShapeDtypeStruct
     shapes = [kind_of(shape, kind) for shape, kind in outs]
-    places = [VMEM] * len(outs)
+    places = [FAR] * far_outs + [VMEM] * (len(outs) - far_outs)
     if table is not None:
         shapes.append(pltpu.SMEM(table, I32))
         places.append(SMEM)
@@ -574,11 +594,19 @@
     (own,) = run(adjoint_inner, [acc_kind], (table, mid_off, mid_mate, sums_off, sums_mate, ops), 1)
     total, own = lax.optimization_barrier((total, own))
     mate_total = to_mate(total)
+    half = pltpu.VMEM((members, halo), F32)
+    grad_kind = ((members, length), F32)
+    (grad_ens,) = run(finish_mate, [grad_kind], (own, from_mate), 0, [half, sem((4,))], near=False, far_outs=1)
     grad_ens, direction = run(
-        finish,
-        [((members, length), F32), ((members, rows), F32)],
-        (own, from_off, from_mate, grad_weights, total, mate_total),
+        finish_off,
+        [grad_kind, ((members, rows), F32)],
+        (own, from_off, grad_weights, total, mate_total, grad_ens),
+        0,
+        [half, sem((4,))],
+        far=1,
+        alias={5: 0},
         near=False,
+        far_outs=1,
         count=rows * tiles,
     )
     return (grad_ens, direction)

time: 49.7 us -> 50.1 us (level)
  Pallas kernels: 15 us -> 16.2 us
  waiting for transfers between devices: 7.01 us -> 6.14 us
    pallas_call x13 -> x14, Pallas kernels: 15 us -> 16.2 us  [run(): pl.pallas_call(functools.partial(body, **fixed) if fixed else body, out_s...]
    ppermute x5, waiting for transfers between devices: 0.85 us -> 0.01 us  [to_mate(): return lax.ppermute(value, 'space', mates)]
  transfers between devices with their start and end apart: 14 -> 14, of which waited for: 7 -> 6; matrix products, arithmetic and copies ran while one was open for 0% -> 0% of each run, Pallas kernels for 21% -> 23%
where the time goes in v9:
time: 50.1 us; the launch traced here: 49.8 us
  starting transfers between devices  25.9 us (52%)
  Pallas kernels  16.2 us (32%)
  waiting for transfers between devices  6.14 us (12%)
  between operations  0.86 us (2%)
  local copies, waits for them, and re-layouts  0.7 us (1%)
    pallas_call x14, Pallas kernels, run(): pl.pallas_call(functools.partial(body, **fixed) if fixed else body, out_s...  16.2 us
    ppermute x4, starting transfers between devices, to_off(): return lax.ppermute(value, 'space', offs)  14.6 us
    ppermute x2, starting transfers between devices, partner(): return lax.ppermute(value, 'space', [(i, i ^ stride) for i in range(tiles)])  5.59 us
    ppermute x3, starting transfers between devices, on_device(): lax.ppermute(send, 'members', [(i, i ^ step) for i in range(groups)])  4.06 us
    ppermute x3, waiting for transfers between devices, on_device(): lax.ppermute(send, 'members', [(i, i ^ step) for i in range(groups)])  3.31 us
    ppermute x4, waiting for transfers between devices, to_off(): return lax.ppermute(value, 'space', offs)  2.58 us
    ppermute x5, starting transfers between devices, to_mate(): return lax.ppermute(value, 'space', mates)  1.61 us
  transfers between devices with their start and end apart: 14, of which 6 were waited for; matrix products, arithmetic and copies ran while one was open for 0% of the time, Pallas kernels for 23%

profile of v9, /device:TPU:1, one launch (start us, length us, event | category | flops | bytes accessed | tf_op | source)
XLA Modules:
  0.0 49.8 jit_solution(11890093686944739061)
XLA Ops:
  0.6 1.2 %load.1 = (bf16[32,4224]{1,0:T(8,128)(2,1)S(1)}, bf16[32,4096]{1,0:T(8,128)(2,1)S(1)}) custom-call(bf16[32,8192]{1,0:T(8,128)(2,1)} %ens.1, f32[32,64]{1,0:T(8,128)} %w.1, s32[2,64]{1,0:T(2,128)} %bitcast.1), custom_call_target="tpu_custom_call" | custom-call | tf_op jit(solution)/shard_map/load/pallas_call | solution.py:463
  1.8 0.1 collective-permute-start
  1.9 4.5 %collective-permute-start.1 = (bf16[32,4224]{1,0:T(8,128)(2,1)S(1)}, bf16[32,4224]{1,0:T(8,128)(2,1)S(1)}, u32[]{:S(2)}, u32[]{:S(2)}) collective-permute-start(bf16[32,4224]{1,0:T(8,128)(2,1)S(1)} %get-tuple-element.47.off), channel_id=1, source_target_pairs={{4,8},{8,4},{12,16},{16,12},{20,24},{24,20},{5,9},{9,5},{13,17},{1... | collective-permute-start | bytes 811016 | tf_op jit(solution)/shard_map/ppermute | solution.py:496
  6.4 0.0 copy-start.3
  6.4 0.7 %copy-done.3 = s32[64,2]{0,1:T(2,128)S(1)} copy-done((s32[64,2]{0,1:T(2,128)S(1)}, s32[64,2]{0,1:T(2,128)}, u32[]{:S(2)}) %copy-start.3) | copy-done | bytes 536
  7.1 3.9 %first_inner.1 = (f32[64,32,128]{2,1,0:T(8,128)S(1)}, bf16[32,16384]{1,0:T(8,128)(2,1)S(1)}, bf16[64,3,128,128]{3,2,1,0:T(8,128)(2,1)S(1)}, s32[2,64]{1,0:T(2,128)S(4)}) custom-call(s32[2,64]{1,0:T(2,128)S(1)} %bitcast.2, bf16[32,4224]{1,0:T(8,128)(2,1)S(1)} %get-tuple-element.47.off, bf16[32,4096]{1,0:T(8,128)(2,1)S(1)} %get-tuple-element.48.mate, ...), custom_call_target="tpu_custom_call" | custom-call | tf_op jit(solution)/shard_map/first_inner/pallas_call | solution.py:463
  11.0 0.0 collective-permute-done.halo
  11.0 0.7 %first_mate.1 = (bf16[32,16384]{1,0:T(8,128)(2,1)S(1)}, bf16[32,16384]{1,0:T(8,128)(2,1)S(1)}, bf16[32,4096]{1,0:T(8,128)(2,1)S(1)}) custom-call(s32[2,64]{1,0:T(2,128)S(4)} %get-tuple-element.49.cols, f32[64,32,128]{2,1,0:T(8,128)S(1)} %get-tuple-element.50.acc, bf16[32,16384]{1,0:T(8,128)(2,1)S(1)} %get-tuple-element.51.wide_in, ...), custom_call_target="tpu_custom_call", output_to_operand_aliasing={{0}: (2, {})} | custom-call | tf_op jit(solution)/shard_map/first_mate/pallas_call | solution.py:463
  11.7 0.0 copy-start.1
  11.7 0.0 copy-start.2
  11.7 0.1 collective-permute-start.3
  11.8 0.7 %collective-permute-done.1.halo = bf16[32,4224]{1,0:T(8,128)(2,1)S(1)} collective-permute-done((bf16[32,4224]{1,0:T(8,128)(2,1)S(1)}, bf16[32,4224]{1,0:T(8,128)(2,1)S(1)}, u32[]{:S(2)}, u32[]{:S(2)}) %collective-permute-start.1) | collective-permute-done | bytes 270368 | tf_op jit(solution)/shard_map/ppermute | solution.py:496
  12.5 0.8 %first_off.1 = (bf16[32,16384]{1,0:T(8,128)(2,1)S(1)}, bf16[32,16384]{1,0:T(8,128)(2,1)S(1)}, bf16[32,128]{1,0:T(8,128)(2,1)S(1)}, s32[32,128]{1,0:T(8,128)S(1)}...) custom-call(s32[2,64]{1,0:T(2,128)S(4)} %get-tuple-element.49.cols, ...), custom_call_target="tpu_custom_call", output_to_operand_aliasing={{0}: (2, {}), {1}: (3, {})} | custom-call | tf_op jit(solution)/shard_map/first_off/pallas_call | solution.py:463
  13.3 2.8 %collective-permute-start.2 = (bf16[32,128]{1,0:T(8,128)(2,1)S(1)}, bf16[32,128]{1,0:T(8,128)(2,1)S(1)}, u32[]{:S(2)}, u32[]{:S(2)}) collective-permute-start(bf16[32,128]{1,0:T(8,128)(2,1)S(1)} %get-tuple-element.57), channel_id=1, source_target_pairs={{4,8},{8,4},{12,16},{16,12},{20,24},{24,20},{5,9},{9,5},{13,17},{1... | collective-permute-start | bytes 24584 | tf_op jit(solution)/shard_map/ppermute | solution.py:496
  16.1 0.0 copy-done
  16.1 2.2 %second_inner.1 = (f32[64,32,128]{2,1,0:T(8,128)S(1)}, f32[64,128]{1,0:T(8,128)S(1)}, f32[128,128]{1,0:T(8,128)S(1)}, f32[128,128]{1,0:T(8,128)S(1)}, f32[32,64]...) custom-call(s32[2,64]{1,0:T(2,128)S(4)} %get-tuple-element.49.cols, ...), custom_call_target="tpu_custom_call" | custom-call | tf_op jit(solution)/shard_map/second_inner/pallas_call | solution.py:463
  18.3 0.0 collective-permute-done.3.halo
  18.3 0.0 copy-start.4
  18.4 0.7 %second_mate.1 = (bf16[32,16384]{1,0:T(8,128)(2,1)S(1)}, bf16[32,4096]{1,0:T(8,128)(2,1)S(1)}, f32[32,128]{1,0:T(8,128)S(1)}) custom-call(s32[2,64]{1,0:T(2,128)S(4)} %get-tuple-element.49.cols, f32[64,32,128]{2,1,0:T(8,128)S(1)} %get-tuple-element.60.acc, bf16[32,16384]{1,0:T(8,128)(2,1)S(1)} %get-tuple-element.55.wide.wide_in, ...), custom_call_target="tpu_custom_call", output_to_operand_aliasing={{0}: (2, {})} | custom-call | tf_op jit(solution)/shard_map/second_mate/pallas_call | solution.py:463
  19.1 0.0 collective-permute-done.2.halo
  19.1 0.7 %second_off.1 = (f32[128,128]{1,0:T(8,128)S(1)}, bf16[128,128]{1,0:T(8,128)(2,1)S(1)}) custom-call(bf16[32,128]{1,0:T(8,128)(2,1)S(1)} %collective-permute-done.2.halo, bf16[64,3,128,128]{3,2,1,0:T(8,128)(2,1)S(1)} %get-tuple-element.52.ops, f32[64,128]{1,0:T(8,128)S(1)} %get-tuple-element.58.inc_one, f32[32,128]{1,0:T(8,128)S(1)} %get-tuple-element.59.inc_off, ...), custom_call_target="tpu_custom_call" | custom-call | tf_op jit(solution)/shard_map/second_off/pallas_call | solution.py:463
  19.8 3.7 %collective-permute-start.6 = (bf16[128,128]{1,0:T(8,128)(2,1)S(1)}, bf16[128,128]{1,0:T(8,128)(2,1)S(1)}, u32[]{:S(2)}, u32[]{:S(2)}) collective-permute-start(bf16[128,128]{1,0:T(8,128)(2,1)S(1)} %get-tuple-element.69), channel_id=1, source_target_pairs={{0,3},{1,2},{2,1},{3,0},{4,7},{5,6},{6,5},{7,4},{8,11},{9,10},{10,... | collective-permute-start | bytes 98312 | tf_op jit(solution)/shard_map/ppermute | solution.py:556
  23.5 0.0 collective-permute-start.5
  23.5 0.3 collective-permute-start.4
  23.9 0.9 %collective-permute-done.6.rest_2_ = bf16[128,128]{1,0:T(8,128)(2,1)S(1)} collective-permute-done((bf16[128,128]{1,0:T(8,128)(2,1)S(1)}, bf16[128,128]{1,0:T(8,128)(2,1)S(1)}, u32[]{:S(2)}, u32[]{:S(2)}) %collective-permute-start.6) | collective-permute-done | bytes 32800 | tf_op jit(solution)/shard_map/ppermute | solution.py:556
  24.8 2.4 %collective-permute-done.5.rest_1_ = bf16[128,128]{1,0:T(8,128)(2,1)S(1)} collective-permute-done((bf16[128,128]{1,0:T(8,128)(2,1)S(1)}, bf16[128,128]{1,0:T(8,128)(2,1)S(1)}, u32[]{:S(2)}, u32[]{:S(2)}) %collective-permute-start.5) | collective-permute-done | bytes 32800 | tf_op jit(solution)/shard_map/ppermute | solution.py:556
  27.2 0.0 collective-permute-done.4.rest_0_
  27.2 0.7 %residual_rim.1 = (f32[128,128]{1,0:T(8,128)S(1)}, f32[32,128]{1,0:T(8,128)S(1)}, bf16[64,128]{1,0:T(8,128)(2,1)S(1)}, f32[64,128]{1,0:T(8,128)S(1)}, f32[32,64]{1,0:T(8,128)S(1)}) custom-call(s32[2,64]{1,0:T(2,128)S(1)} %bitcast.3, f32[128,128]{1,0:T(8,128)S(1)} %get-tuple-element.63.inc, f32[128,128]{1,0:T(8,128)S(1)} %get-tuple-element.64.innov, ...), custom_call_target="tpu_custom_call" | custom-call | tf_op jit(solution)/shard_map/residual_rim/pallas_call | solution.py:463
  27.9 0.0 collective-permute-start.8
  27.9 5.5 %collective-permute-start.7 = (bf16[64,128]{1,0:T(8,128)(2,1)S(1)}, bf16[64,128]{1,0:T(8,128)(2,1)S(1)}, u32[]{:S(2)}, u32[]{:S(2)}) collective-permute-start(bf16[64,128]{1,0:T(8,128)(2,1)S(1)} %get-tuple-element.73), channel_id=1, source_target_pairs={{4,8},{8,4},{12,16},{16,12},{20,24},{24,20},{5,9},{9,5},{13,17},{1... | collective-permute-start | bytes 49160 | tf_op jit(solution)/shard_map/ppermute | solution.py:496
  33.4 0.7 %residual_inner.1.y = f32[128,128]{1,0:T(8,128)S(1)} custom-call(f32[128,128]{1,0:T(8,128)S(1)} %get-tuple-element.70.res, bf16[64,3,128,128]{3,2,1,0:T(8,128)(2,1)S(1)} %get-tuple-element.52.ops), custom_call_target="tpu_custom_call" | custom-call | tf_op jit(solution)/shard_map/residual_inner/pallas_call | solution.py:463
  34.1 0.7 %collective-permute-done.7.off = bf16[64,128]{1,0:T(8,128)(2,1)S(1)} collective-permute-done((bf16[64,128]{1,0:T(8,128)(2,1)S(1)}, bf16[64,128]{1,0:T(8,128)(2,1)S(1)}, u32[]{:S(2)}, u32[]{:S(2)}) %collective-permute-start.7) | collective-permute-done | bytes 16416 | tf_op jit(solution)/shard_map/ppermute | solution.py:496
  34.8 0.0 collective-permute-done.8.mate
  34.8 0.8 %adjoint_off.1 = (bf16[1024,128]{1,0:T(8,128)(2,1)S(1)}, f32[64,32,128]{2,1,0:T(8,128)S(1)}, bf16[33,32,128]{2,1,0:T(8,128)(2,1)S(1)}, bf16[256,128]{1,0:T(8,128...) custom-call(s32[2,64]{1,0:T(2,128)S(4)} %get-tuple-element.49.cols, ...), custom_call_target="tpu_custom_call" | custom-call | tf_op jit(solution)/shard_map/adjoint_off/pallas_call | solution.py:463
  35.6 2.4 %collective-permute-start.9 = (f32[32,128]{1,0:T(8,128)S(1)}, f32[32,128]{1,0:T(8,128)S(1)}, u32[]{:S(2)}, u32[]{:S(2)}) collective-permute-start(f32[32,128]{1,0:T(8,128)S(1)} %get-tuple-element.82), channel_id=1, source_target_pairs={{0,8},{4,12},{8,0},{12,4},{16,24},{20,28},{24,16},{28,20},{1,9},{5... | collective-permute-start | bytes 49160 | tf_op jit(solution)/shard_map/ppermute | solution.py:499
  38.1 1.9 %collective-permute-start.11 = (bf16[33,32,128]{2,1,0:T(8,128)(2,1)S(1)}, bf16[33,32,128]{2,1,0:T(8,128)(2,1)S(1)}, u32[]{:S(2)}, u32[]{:S(2)}) collective-permute-start(bf16[33,32,128]{2,1,0:T(8,128)(2,1)S(1)} %get-tuple-element.89), channel_id=1, source_target_pairs={{4,8},{8,4},{12,16},{16,12},{20,24},{24,20},{5,9},{9,5},{13,17},{1... | collective-permute-start | bytes 811016 | tf_op jit(solution)/shard_map/ppermute | solution.py:496
  40.0 0.6 %adjoint_mate.1 = (bf16[1024,128]{1,0:T(8,128)(2,1)S(1)}, f32[64,32,128]{2,1,0:T(8,128)S(1)}, bf16[32,32,128]{2,1,0:T(8,128)(2,1)S(1)}) custom-call(s32[2,64]{1,0:T(2,128)S(4)} %get-tuple-element.49.cols, f32[32,256]{1,0:T(8,128)S(1)} %get-tuple-element.78.wp, s32[1,256]{1,0:T(1,128)S(1)} %get-tuple-element.79.tgt, ...), custom_call_target="tpu_custom_call" | custom-call | tf_op jit(solution)/shard_map/adjoint_mate/pallas_call | solution.py:463
  40.7 0.0 collective-permute-done.9
  40.7 0.1 collective-permute-start.13
  40.8 3.1 %collective-permute-start.10 = (f32[32,128]{1,0:T(8,128)S(1)}, f32[32,128]{1,0:T(8,128)S(1)}, u32[]{:S(2)}, u32[]{:S(2)}) collective-permute-start(f32[32,128]{1,0:T(8,128)S(1)} %add.6), channel_id=1, source_target_pairs={{0,16},{4,20},{8,24},{12,28},{16,0},{20,4},{24,8},{28,12},{1,17},{... | collective-permute-start | bytes 49160 | tf_op jit(solution)/shard_map/ppermute | solution.py:499
  43.9 0.9 %adjoint_inner.1.own = f32[64,32,128]{2,1,0:T(8,128)S(1)} custom-call(s32[2,64]{1,0:T(2,128)S(4)} %get-tuple-element.49.cols, bf16[1024,128]{1,0:T(8,128)(2,1)S(1)} %get-tuple-element.84.mid_off, bf16[1024,128]{1,0:T(8,128)(2,1)S(1)} %get-tuple-element.85.mid_mate, f32[64,32,128]{2,1,0:T(8,128)S(1)} %get-tuple-element.86.sums_off, ...), custom_call_target="tpu_custom_call" | custom-call | tf_op jit(solution)/shard_map/adjoint_inner/pallas_call | solution.py:463
  44.8 0.2 collective-permute-done.10
  45.0 1.3 %collective-permute-start.12 = (f32[32,128]{1,0:T(8,128)S(1)}, f32[32,128]{1,0:T(8,128)S(1)}, u32[]{:S(2)}, u32[]{:S(2)}) collective-permute-start(f32[32,128]{1,0:T(8,128)S(1)} %add.7.total), channel_id=1, source_target_pairs={{0,4},{4,0},{8,12},{12,8},{16,20},{20,16},{24,28},{28,24},{1,5},{5... | collective-permute-start | bytes 49160 | tf_op jit(solution)/shard_map/ppermute | solution.py:493
  46.3 0.0 collective-permute-done.13.mate
  46.3 0.8 %finish_mate.1.out_in = f32[32,8192]{1,0:T(8,128)} custom-call(f32[64,32,128]{2,1,0:T(8,128)S(1)} %adjoint_inner.1.own, bf16[32,32,128]{2,1,0:T(8,128)(2,1)S(1)} %collective-permute-done.13.mate), custom_call_target="tpu_custom_call" | custom-call | tf_op jit(solution)/shard_map/finish_mate/pallas_call | solution.py:463
  47.2 0.0 collective-permute-done.12.mate_total
  47.2 1.1 %collective-permute-done.11.off = bf16[33,32,128]{2,1,0:T(8,128)(2,1)S(1)} collective-permute-done((bf16[33,32,128]{2,1,0:T(8,128)(2,1)S(1)}, bf16[33,32,128]{2,1,0:T(8,128)(2,1)S(1)}, u32[]{:S(2)}, u32[]{:S(2)}) %collective-permute-start.11) | collective-permute-done | bytes 270368 | tf_op jit(solution)/shard_map/ppermute | solution.py:496
  48.3 1.5 %finish_off.1 = (f32[32,8192]{1,0:T(8,128)}, f32[32,64]{1,0:T(8,128)}) custom-call(f32[64,32,128]{2,1,0:T(8,128)S(1)} %adjoint_inner.1.own, bf16[33,32,128]{2,1,0:T(8,128)(2,1)S(1)} %collective-permute-done.11.off, f32[32,64]{1,0:T(8,128)S(1)} %get-tuple-element.76.gw, f32[32,128]{1,0:T(8,128)S(1)} %add.7.total, ...), custom_call_target="tpu_custom_call", output_to_operand_aliasing={{0}: (5, {})} | custom-call | tf_op jit(solution)/shard_map/finish_off/pallas_call | solution.py:463
  (6 shorter events, 0.0 us)
Async XLA Ops:
  1.8 9.2 %collective-permute-start = (bf16[32,4096]{1,0:T(8,128)(2,1)S(1)}, bf16[32,4096]{1,0:T(8,128)(2,1)S(1)}, u32[]{:S(2)}, u32[]{:S(2)}) collective-permute-start(bf16[32,4096]{1,0:T(8,128)(2,1)S(1)} %get-tuple-element.48.mate), channel_id=1, source_target_pairs={{0,4},{4,0},{8,12},{12,8},{16,20},{20,16},{24,28},{28,24},{1,5},{5... | collective-permute-start | bytes 786440 | tf_op jit(solution)/shard_map/ppermute | solution.py:493
  1.9 10.6 %collective-permute-start.1 = (bf16[32,4224]{1,0:T(8,128)(2,1)S(1)}, bf16[32,4224]{1,0:T(8,128)(2,1)S(1)}, u32[]{:S(2)}, u32[]{:S(2)}) collective-permute-start(bf16[32,4224]{1,0:T(8,128)(2,1)S(1)} %get-tuple-element.47.off), channel_id=1, source_target_pairs={{4,8},{8,4},{12,16},{16,12},{20,24},{24,20},{5,9},{9,5},{13,17},{1... | collective-permute-start | bytes 811016 | tf_op jit(solution)/shard_map/ppermute | solution.py:496
  6.4 0.7 %copy-start.3 = (s32[64,2]{0,1:T(2,128)S(1)}, s32[64,2]{0,1:T(2,128)}, u32[]{:S(2)}) copy-start(s32[64,2]{0,1:T(2,128)} %param.8) | copy-start | bytes 1540
  11.7 4.4 %copy-start = (f32[2,8192]{1,0:T(2,128)S(1)}, f32[2,8192]{1,0:T(2,128)}, u32[]{:S(2)}) copy-start(f32[2,8192]{1,0:T(2,128)} %innov.1) | copy-start | bytes 196612
  11.7 4.4 %copy-start.1 = (f32[2,8192]{1,0:T(2,128)S(1)}, f32[2,8192]{1,0:T(2,128)}, u32[]{:S(2)}) copy-start(f32[2,8192]{1,0:T(2,128)} %prec.1) | copy-start | bytes 196612
  11.7 4.4 %copy-start.2 = (f32[32,64]{1,0:T(8,128)S(1)}, f32[32,64]{1,0:T(8,128)}, u32[]{:S(2)}) copy-start(f32[32,64]{1,0:T(8,128)} %w.1) | copy-start | bytes 24580
  11.7 6.6 %collective-permute-start.3 = (bf16[32,4096]{1,0:T(8,128)(2,1)S(1)}, bf16[32,4096]{1,0:T(8,128)(2,1)S(1)}, u32[]{:S(2)}, u32[]{:S(2)}) collective-permute-start(bf16[32,4096]{1,0:T(8,128)(2,1)S(1)} %get-tuple-element.61), channel_id=1, source_target_pairs={{0,4},{4,0},{8,12},{12,8},{16,20},{20,16},{24,28},{28,24},{1,5},{5... | collective-permute-start | bytes 786440 | tf_op jit(solution)/shard_map/ppermute | solution.py:493
  13.3 5.8 %collective-permute-start.2 = (bf16[32,128]{1,0:T(8,128)(2,1)S(1)}, bf16[32,128]{1,0:T(8,128)(2,1)S(1)}, u32[]{:S(2)}, u32[]{:S(2)}) collective-permute-start(bf16[32,128]{1,0:T(8,128)(2,1)S(1)} %get-tuple-element.57), channel_id=1, source_target_pairs={{4,8},{8,4},{12,16},{16,12},{20,24},{24,20},{5,9},{9,5},{13,17},{1... | collective-permute-start | bytes 24584 | tf_op jit(solution)/shard_map/ppermute | solution.py:496
  18.3 8.8 %copy-start.4 = (s32[64,2]{0,1:T(2,128)S(1)}, s32[64,2]{0,1:T(2,128)}, u32[]{:S(2)}) copy-start(s32[64,2]{0,1:T(2,128)} %param.8) | copy-start | bytes 1540
  19.8 5.0 %collective-permute-start.6 = (bf16[128,128]{1,0:T(8,128)(2,1)S(1)}, bf16[128,128]{1,0:T(8,128)(2,1)S(1)}, u32[]{:S(2)}, u32[]{:S(2)}) collective-permute-start(bf16[128,128]{1,0:T(8,128)(2,1)S(1)} %get-tuple-element.69), channel_id=1, source_target_pairs={{0,3},{1,2},{2,1},{3,0},{4,7},{5,6},{6,5},{7,4},{8,11},{9,10},{10,... | collective-permute-start | bytes 98312 | tf_op jit(solution)/shard_map/ppermute | solution.py:556
  23.5 3.7 %collective-permute-start.5 = (bf16[128,128]{1,0:T(8,128)(2,1)S(1)}, bf16[128,128]{1,0:T(8,128)(2,1)S(1)}, u32[]{:S(2)}, u32[]{:S(2)}) collective-permute-start(bf16[128,128]{1,0:T(8,128)(2,1)S(1)} %get-tuple-element.69), channel_id=1, source_target_pairs={{0,2},{1,3},{2,0},{3,1},{4,6},{5,7},{6,4},{7,5},{8,10},{9,11},{10,... | collective-permute-start | bytes 98312 | tf_op jit(solution)/shard_map/ppermute | solution.py:556
  23.5 3.7 %collective-permute-start.4 = (bf16[128,128]{1,0:T(8,128)(2,1)S(1)}, bf16[128,128]{1,0:T(8,128)(2,1)S(1)}, u32[]{:S(2)}, u32[]{:S(2)}) collective-permute-start(bf16[128,128]{1,0:T(8,128)(2,1)S(1)} %get-tuple-element.69), channel_id=1, source_target_pairs={{0,1},{1,0},{2,3},{3,2},{4,5},{5,4},{6,7},{7,6},{8,9},{9,8},{10,11... | collective-permute-start | bytes 98312 | tf_op jit(solution)/shard_map/ppermute | solution.py:556
  27.9 7.0 %collective-permute-start.8 = (f32[64,128]{1,0:T(8,128)S(1)}, f32[64,128]{1,0:T(8,128)S(1)}, u32[]{:S(2)}, u32[]{:S(2)}) collective-permute-start(f32[64,128]{1,0:T(8,128)S(1)} %get-tuple-element.72.own_mate), channel_id=1, source_target_pairs={{0,4},{4,0},{8,12},{12,8},{16,20},{20,16},{24,28},{28,24},{1,5},{5... | collective-permute-start | bytes 98312 | tf_op jit(solution)/shard_map/ppermute | solution.py:493
  27.9 6.9 %collective-permute-start.7 = (bf16[64,128]{1,0:T(8,128)(2,1)S(1)}, bf16[64,128]{1,0:T(8,128)(2,1)S(1)}, u32[]{:S(2)}, u32[]{:S(2)}) collective-permute-start(bf16[64,128]{1,0:T(8,128)(2,1)S(1)} %get-tuple-element.73), channel_id=1, source_target_pairs={{4,8},{8,4},{12,16},{16,12},{20,24},{24,20},{5,9},{9,5},{13,17},{1... | collective-permute-start | bytes 49160 | tf_op jit(solution)/shard_map/ppermute | solution.py:496
  35.6 5.0 %collective-permute-start.9 = (f32[32,128]{1,0:T(8,128)S(1)}, f32[32,128]{1,0:T(8,128)S(1)}, u32[]{:S(2)}, u32[]{:S(2)}) collective-permute-start(f32[32,128]{1,0:T(8,128)S(1)} %get-tuple-element.82), channel_id=1, source_target_pairs={{0,8},{4,12},{8,0},{12,4},{16,24},{20,28},{24,16},{28,20},{1,9},{5... | collective-permute-start | bytes 49160 | tf_op jit(solution)/shard_map/ppermute | solution.py:499
  38.1 10.2 %collective-permute-start.11 = (bf16[33,32,128]{2,1,0:T(8,128)(2,1)S(1)}, bf16[33,32,128]{2,1,0:T(8,128)(2,1)S(1)}, u32[]{:S(2)}, u32[]{:S(2)}) collective-permute-start(bf16[33,32,128]{2,1,0:T(8,128)(2,1)S(1)} %get-tuple-element.89), channel_id=1, source_target_pairs={{4,8},{8,4},{12,16},{16,12},{20,24},{24,20},{5,9},{9,5},{13,17},{1... | collective-permute-start | bytes 811016 | tf_op jit(solution)/shard_map/ppermute | solution.py:496
  40.7 5.7 %collective-permute-start.13 = (bf16[32,32,128]{2,1,0:T(8,128)(2,1)S(1)}, bf16[32,32,128]{2,1,0:T(8,128)(2,1)S(1)}, u32[]{:S(2)}, u32[]{:S(2)}) collective-permute-start(bf16[32,32,128]{2,1,0:T(8,128)(2,1)S(1)} %get-tuple-element.91), channel_id=1, source_target_pairs={{0,4},{4,0},{8,12},{12,8},{16,20},{20,16},{24,28},{28,24},{1,5},{5... | collective-permute-start | bytes 786440 | tf_op jit(solution)/shard_map/ppermute | solution.py:493
  40.8 4.3 %collective-permute-start.10 = (f32[32,128]{1,0:T(8,128)S(1)}, f32[32,128]{1,0:T(8,128)S(1)}, u32[]{:S(2)}, u32[]{:S(2)}) collective-permute-start(f32[32,128]{1,0:T(8,128)S(1)} %add.6), channel_id=1, source_target_pairs={{0,16},{4,20},{8,24},{12,28},{16,0},{20,4},{24,8},{28,12},{1,17},{... | collective-permute-start | bytes 49160 | tf_op jit(solution)/shard_map/ppermute | solution.py:499
  45.0 2.2 %collective-permute-start.12 = (f32[32,128]{1,0:T(8,128)S(1)}, f32[32,128]{1,0:T(8,128)S(1)}, u32[]{:S(2)}, u32[]{:S(2)}) collective-permute-start(f32[32,128]{1,0:T(8,128)S(1)} %add.7.total), channel_id=1, source_target_pairs={{0,4},{4,0},{8,12},{12,8},{16,20},{20,16},{24,28},{28,24},{1,5},{5... | collective-permute-start | bytes 49160 | tf_op jit(solution)/shard_map/ppermute | solution.py:493

commit v10 on v9

--- a/solution.py
+++ b/solution.py
@@ -75,22 +75,23 @@
     size = ens.shape[1] // (2 * REACH)
     sides = Sides(2 * REACH)
     width = REACH * size
-    copies = []
-    for n, (row, out) in enumerate(((sides.off_row, off.at[:, :width]), (sides.mate_row, mate))):
-        source = ens.at[:, pl.ds(pl.multiple_of(row * size, size), width)]
-        copies.append(pltpu.make_async_copy(source, out, sems.at[n]))
-    copies.append(pltpu.make_async_copy(w_far, w, sems.at[2]))
-    copies.append(pltpu.make_async_copy(cols_far, cols, sems.at[3]))
-    for copy in copies:
+    small = [pltpu.make_async_copy(w_far, w, sems.at[0]), pltpu.make_async_copy(cols_far, cols, sems.at[1])]
+    large = []
+    step = 16
+    for row, out in ((sides.off_row, off), (sides.mate_row, mate)):
+        for m in range(0, ens.shape[0], step):
+            source = ens.at[m : m + step, pl.ds(pl.multiple_of(row * size, size), width)]
+            large.append(pltpu.make_async_copy(source, out.at[m : m + step, :width], sems.at[2 + len(large)]))
+    for copy in small + large:
         copy.start()
-    copies[3].wait()
-    copies[2].wait()
+    for copy in small:
+        copy.wait()
     high, low = split_terms(sides.pick(w[:, :REACH], w[:, REACH:])[0])
     col = sides.pick(cols[:1, :REACH], cols[1:, REACH:])[0]
     spread = [jnp.broadcast_to(part.astype(F32), high.shape).astype(BF16) for part in (col >> 8, col & 255)]
     off[:, width:] = jnp.concatenate([high, low] + spread, 1)
-    copies[1].wait()
-    copies[0].wait()
+    for copy in large:
+        copy.wait()
 
 
 def inner(cols, wide, ops, acc, sides, ready=None):
@@ -246,8 +247,9 @@
     inc[:rows, :] = inc_one[...]
     inc[rows + REACH :, :] = inc_mate[...]
     parts = []
+    sums = halo[...].astype(F32)
     for i in range(REACH):
-        row = jnp.broadcast_to(halo[i : i + 1, :].astype(F32), (8, size)).astype(BF16)
+        row = jnp.broadcast_to(sums[i : i + 1, :], (8, size)).astype(BF16)
         parts.append(dot_t(row, ops[sides.off_row + i, sides.off_k]))
     for i, part in enumerate(parts):
         inc[rows + i : rows + i + 1, :] = inc_off[i : i + 1, :] + part[:1]
@@ -298,7 +300,7 @@
     send_off[REACH:, :] = jnp.concatenate([high, low, jnp.zeros((members, size - 2 * REACH), BF16)], 1)
 
 
-def residual_inner(res, ops, y):
+def residual_inner(res, ops, w, cols, rim_off, own_mate, near_w, near_at, vals, wp, tgt, y):
     rows, _, size, _ = ops.shape
     sides = Sides(rows)
     for row, k, q in ((sides.off_row, sides.mate_k, 0), (sides.mate_row, sides.off_k, REACH)):
@@ -314,6 +316,20 @@
                 y[pl.ds(rows + place, 1), :] = o[:1, size:]
 
         chunks(REACH, some)
+    vals[:rows, :] = y[:rows, :].astype(BF16)
+    vals[2 * rows : 3 * rows, :] = y[rows:, :].astype(BF16)
+    for n, part in enumerate((rim_off, own_mate)):
+        vals[rows + n * REACH : rows + (n + 1) * REACH, :] = part[:REACH, :].astype(BF16)
+    for k in range(3):
+        wp[:, k * rows : (k + 1) * rows] = w[...] * SCALE
+    col = cols[...]
+    rims = sides.pick(col[:1, :REACH], col[1:, REACH:])
+    inners = sides.pick(col[1:, :REACH], col[:1, REACH:])
+    tgt[:, :rows] = lax.broadcasted_iota(I32, (1, rows), 1) + REACH
+    for n, part in enumerate(rims + inners):
+        tgt[:, rows + n * REACH : rows + (n + 1) * REACH] = sides.place(part)
+    wp[:, 3 * rows : 3 * rows + REACH] = near_w[...] * SCALE
+    tgt[:, 3 * rows : 3 * rows + REACH] = near_at[...]
 
 
 def middle(weights, target, vals, q, mid):
@@ -341,26 +357,13 @@
     chunks(REACH, some)
 
 
-def adjoint_off(cols, col_rows, w, y, own_off, own_mate, off, mate, near_w, near_at, ops, one, gw, slot, mid, sums, send, vals, wp, tgt, squares):
+def adjoint_off(
+    cols, vals_in, wp_in, tgt_in, off, mate, ops, one, gw, slot, mid, sums, send, vals, wp, tgt, squares
+):
     rows, _, size, _ = ops.shape
-    members = w.shape[0]
+    members = gw.shape[0]
     sides = Sides(rows)
-    vals[:rows, :] = y[:rows, :].astype(BF16)
-    vals[2 * rows : 3 * rows, :] = y[rows:, :].astype(BF16)
-    for n, part in enumerate((own_off, own_mate)):
-        vals[rows + n * REACH : rows + (n + 1) * REACH, :] = part[:REACH, :].astype(BF16)
-    for k in range(3):
-        wp[:, k * rows : (k + 1) * rows] = w[...] * SCALE
-    col = col_rows[...]
-    rim_off, rim_mate = sides.pick(col[:1, :REACH], col[1:, REACH:])
-    inner_off, inner_mate = sides.pick(col[1:, :REACH], col[:1, REACH:])
-    tgt[:, :rows] = lax.broadcasted_iota(I32, (1, rows), 1) + REACH
-    for n, part in enumerate((rim_off, rim_mate, inner_off, inner_mate)):
-        tgt[:, rows + n * REACH : rows + (n + 1) * REACH] = sides.place(part)
-    where = slice(3 * rows, 3 * rows + REACH)
-    vals[where, :] = off[:REACH, :]
-    wp[:, where] = near_w[...] * SCALE
-    tgt[:, where] = near_at[...]
+    vals[3 * rows : 3 * rows + REACH, :] = off[:REACH, :]
     where = slice(3 * rows + REACH, 3 * rows + 2 * REACH)
     vals[where, :] = mate[:REACH, :].astype(BF16)
     wp[:, where] = mate[REACH:, :REACH] * SCALE
@@ -414,14 +417,17 @@
         chunks(REACH, some)
 
 
-def write_side(own, q, halo, row, out, half, sems):
+def write_side(own, q, halos, row, out, half, sems):
     size = own.shape[2]
     groups = sems.shape[0]
     step = REACH // groups
     copies = []
     for g in range(groups):
         for i in range(g * step, (g + 1) * step):
-            half[:, i * size : (i + 1) * size] = own[q + i] + halo[i].astype(F32)
+            value = own[q + i]
+            for halo in halos:
+                value = value + halo[i].astype(F32)
+            half[:, i * size : (i + 1) * size] = value
         part = half.at[:, g * step * size : (g + 1) * step * size]
         place = out.at[:, pl.ds(pl.multiple_of((row + g * step) * size, size), step * size)]
         copies.append(pltpu.make_async_copy(part, place, sems.at[g]))
@@ -431,19 +437,21 @@
 
 def finish_mate(own, mate, out, half, sems):
     sides = Sides(own.shape[0])
-    for copy in write_side(own, REACH, mate, sides.mate_row, out, half, sems):
+    for copy in write_side(own, REACH, [mate], sides.mate_row, out, half, sems):
         copy.wait()
 
 
-def finish_off(own, off, gw, total, mate_total, out_in, out, direction, half, sems, *, count):
+def finish_off(own, far, near, gw, total, mate_total, out_in, out, direction, half, normal, sems, sem, *, count):
     sides = Sides(own.shape[0])
-    copies = write_side(own, 0, off, sides.off_row, out, half, sems)
-    drawn = off[REACH].astype(F32)
+    copies = write_side(own, 0, [far, near], sides.off_row, out, half, sems)
+    drawn = far[REACH].astype(F32) + near[REACH].astype(F32)
     drawn = drawn[:, :REACH] + drawn[:, REACH : 2 * REACH]
     grown = gw[...]
     grown = jnp.concatenate([grown[:, :REACH] + drawn, grown[:, REACH:]], 1)
     mean = (total[:, :1] + mate_total[:, :1]) / count
-    direction[...] = turned(sides, grown / jnp.sqrt(mean + 1e-06))
+    normal[...] = turned(sides, grown / jnp.sqrt(mean + 1e-06))
+    copies.append(pltpu.make_async_copy(normal, direction, sem))
+    copies[-1].start()
     for copy in copies:
         copy.wait()
 
@@ -481,9 +489,10 @@
     tiles = lax.axis_size("space")
     groups = lax.axis_size("members")
     mates = [(i, i ^ 1) for i in range(tiles)]
-    offs = []
+    far_edges, near_edges = [], []
     for i in range(1, tiles - 1, 2):
-        offs += [(i, i + 1), (i + 1, i)]
+        edges = near_edges if i % 4 == 1 else far_edges
+        edges += [(i, i + 1), (i + 1, i)]
     sem = pltpu.SemaphoreType.DMA
 
     def far(value):
@@ -493,7 +502,13 @@
         return lax.ppermute(value, "space", mates)
 
     def to_off(value):
-        return lax.ppermute(value, "space", offs)
+        return lax.ppermute(value, "space", far_edges + near_edges)
+
+    def to_far(value):
+        return lax.ppermute(value, "space", far_edges)
+
+    def to_near(value):
+        return lax.ppermute(value, "space", near_edges)
 
     def partner(value, stride):
         return lax.ppermute(value, "space", [(i, i ^ stride) for i in range(tiles)])
@@ -510,7 +525,7 @@
         [((members, halo + 4 * REACH), BF16), side_kind],
         (far(ensemble), far(weights), far(cols)),
         0,
-        [pltpu.VMEM((members, rows), F32), pltpu.VMEM(cols.shape, I32), sem((4,))],
+        [pltpu.VMEM((members, rows), F32), pltpu.VMEM(cols.shape, I32), sem((2 + members // 8,))],
         far=3,
     )
     from_off, from_mate = to_off(off), to_mate(mate)
@@ -561,26 +576,26 @@
         (cols, inc, innov, prec, ops, w, one, two_off, two_mate, *received),
     )
     from_off, from_mate = to_off(own_off), to_mate(own_mate)
-    (y,) = run(residual_inner, [row_kind], (res, ops))
     pairs = 3 * rows + 2 * REACH
+    pair_kinds = [((pairs, size), BF16), ((members, pairs), F32), ((1, pairs), I32)]
+    vals, wp, tgt = run(
+        residual_inner,
+        pair_kinds,
+        (res, ops, w, cols, rim_off, own_mate, near_w, near_at),
+        0,
+        [pltpu.VMEM(*row_kind)],
+    )
     mid_kind = ((REACH * members, size), BF16)
     sums_kind = ((2 * REACH, members, size), F32)
     send_kind = ((REACH, members, size), BF16)
     mid_off, sums_off, send, vals, wp, tgt, total = run(
         adjoint_off,
-        [
-            mid_kind,
-            sums_kind,
-            ((REACH + 1, members, size), BF16),
-            ((pairs, size), BF16),
-            ((members, pairs), F32),
-            ((1, pairs), I32),
-            ((members, size), F32),
-        ],
-        (table, cols, w, y, rim_off, own_mate, from_off, from_mate, near_w, near_at, ops, one, grad_weights, slot),
+        [mid_kind, sums_kind, ((REACH + 1, members, size), BF16), *pair_kinds, ((members, size), F32)],
+        (table, vals, wp, tgt, from_off, from_mate, ops, one, grad_weights, slot),
         1,
-    )
-    from_off = to_off(send)
+        alias={1: 3, 2: 4, 3: 5},
+    )
+    from_near, from_far = to_near(send), to_far(send)
     total = total + partner(total, 2)
     mid_mate, sums_mate, send = run(
         adjoint_mate, [mid_kind, sums_kind, send_kind], (table, wp, tgt, vals, ops), 1
@@ -596,17 +611,17 @@
     mate_total = to_mate(total)
     half = pltpu.VMEM((members, halo), F32)
     grad_kind = ((members, length), F32)
-    (grad_ens,) = run(finish_mate, [grad_kind], (own, from_mate), 0, [half, sem((4,))], near=False, far_outs=1)
+    (grad_ens,) = run(finish_mate, [grad_kind], (own, from_mate), 0, [half, sem((2,))], near=False, far_outs=1)
     grad_ens, direction = run(
         finish_off,
         [grad_kind, ((members, rows), F32)],
-        (own, from_off, grad_weights, total, mate_total, grad_ens),
+        (own, from_far, from_near, grad_weights, total, mate_total, grad_ens),
         0,
-        [half, sem((4,))],
+        [half, pltpu.VMEM((members, rows), F32), sem((2,)), sem(())],
         far=1,
-        alias={5: 0},
+        alias={6: 0},
         near=False,
-        far_outs=1,
+        far_outs=2,
         count=rows * tiles,
     )
     return (grad_ens, direction)

time: 50.1 us -> 49.4 us (0.986)
  waiting for transfers between devices: 6.14 us -> 5.03 us
  starting transfers between devices: 25.9 us -> 26.6 us
  Pallas kernels: 16.2 us -> 15.6 us
    ppermute x4 -> x5, waiting for transfers between devices: 2.58 us -> 1.47 us  [the longest x3 1.46 us: to_off(): return lax.ppermute(value, 'space', far_edges + near_edges)]
    ppermute x4 -> x5, starting transfers between devices: 14.6 us -> 15.3 us  [the longest x3 12.7 us: to_off(): return lax.ppermute(value, 'space', far_edges + near_edges)]
    pallas_call x14, Pallas kernels: 16.2 us -> 15.6 us  [run(): pl.pallas_call(functools.partial(body, **fixed) if fixed else body, out_s...]
  transfers between devices with their start and end apart: 14 -> 15, of which waited for: 6 -> 5; matrix products, arithmetic and copies ran while one was open for 0% -> 0% of each run, Pallas kernels for 23% -> 23%
where the time goes in v10:
time: 49.4 us; the launch traced here: 48.8 us
  starting transfers between devices  26.6 us (54%)
  Pallas kernels  15.6 us (32%)
  waiting for transfers between devices  5.03 us (10%)
  between operations  0.89 us (2%)
  local copies, waits for them, and re-layouts  0.7 us (1%)
    pallas_call x14, Pallas kernels, run(): pl.pallas_call(functools.partial(body, **fixed) if fixed else body, out_s...  15.6 us
    ppermute x3, starting transfers between devices, to_off(): return lax.ppermute(value, 'space', far_edges + near_edges)  12.7 us
    ppermute x2, starting transfers between devices, partner(): return lax.ppermute(value, 'space', [(i, i ^ stride) for i in range(tiles)])  5.59 us
    ppermute x3, starting transfers between devices, on_device(): lax.ppermute(send, 'members', [(i, i ^ step) for i in range(groups)])  4.07 us
    ppermute x3, waiting for transfers between devices, on_device(): lax.ppermute(send, 'members', [(i, i ^ step) for i in range(groups)])  3.31 us
    ppermute x1, starting transfers between devices, to_near(): return lax.ppermute(value, 'space', near_edges)  1.91 us
    ppermute x5, starting transfers between devices, to_mate(): return lax.ppermute(value, 'space', mates)  1.61 us
    ppermute x3, waiting for transfers between devices, to_off(): return lax.ppermute(value, 'space', far_edges + near_edges)  1.46 us
  transfers between devices with their start and end apart: 15, of which 5 were waited for; matrix products, arithmetic and copies ran while one was open for 0% of the time, Pallas kernels for 23%

profile of v10, /device:TPU:1, one launch (start us, length us, event | category | flops | bytes accessed | tf_op | source)
XLA Modules:
  0.0 48.8 jit_solution(10540548567397685600)
XLA Ops:
  0.6 1.2 %load.1 = (bf16[32,4224]{1,0:T(8,128)(2,1)S(1)}, bf16[32,4096]{1,0:T(8,128)(2,1)S(1)}) custom-call(bf16[32,8192]{1,0:T(8,128)(2,1)} %ens.1, f32[32,64]{1,0:T(8,128)} %w.1, s32[2,64]{1,0:T(2,128)} %bitcast.1), custom_call_target="tpu_custom_call" | custom-call | tf_op jit(solution)/shard_map/load/pallas_call | solution.py:471
  1.8 0.1 collective-permute-start
  1.9 4.5 %collective-permute-start.1 = (bf16[32,4224]{1,0:T(8,128)(2,1)S(1)}, bf16[32,4224]{1,0:T(8,128)(2,1)S(1)}, u32[]{:S(2)}, u32[]{:S(2)}) collective-permute-start(bf16[32,4224]{1,0:T(8,128)(2,1)S(1)} %get-tuple-element.50.off), channel_id=1, source_target_pairs={{12,16},{16,12},{4,8},{8,4},{20,24},{24,20},{13,17},{17,13},{5,9},... | collective-permute-start | bytes 811016 | tf_op jit(solution)/shard_map/ppermute | solution.py:505
  6.4 0.0 copy-start.3
  6.4 0.7 %copy-done.3 = s32[64,2]{0,1:T(2,128)S(1)} copy-done((s32[64,2]{0,1:T(2,128)S(1)}, s32[64,2]{0,1:T(2,128)}, u32[]{:S(2)}) %copy-start.3) | copy-done | bytes 536
  7.1 3.9 %first_inner.1 = (f32[64,32,128]{2,1,0:T(8,128)S(1)}, bf16[32,16384]{1,0:T(8,128)(2,1)S(1)}, bf16[64,3,128,128]{3,2,1,0:T(8,128)(2,1)S(1)}, s32[2,64]{1,0:T(2,128)S(4)}) custom-call(s32[2,64]{1,0:T(2,128)S(1)} %bitcast.2, bf16[32,4224]{1,0:T(8,128)(2,1)S(1)} %get-tuple-element.50.off, bf16[32,4096]{1,0:T(8,128)(2,1)S(1)} %get-tuple-element.51.mate, ...), custom_call_target="tpu_custom_call" | custom-call | tf_op jit(solution)/shard_map/first_inner/pallas_call | solution.py:471
  11.0 0.0 collective-permute-done.halo
  11.0 0.7 %first_mate.1 = (bf16[32,16384]{1,0:T(8,128)(2,1)S(1)}, bf16[32,16384]{1,0:T(8,128)(2,1)S(1)}, bf16[32,4096]{1,0:T(8,128)(2,1)S(1)}) custom-call(s32[2,64]{1,0:T(2,128)S(4)} %get-tuple-element.52.cols, f32[64,32,128]{2,1,0:T(8,128)S(1)} %get-tuple-element.53.acc, bf16[32,16384]{1,0:T(8,128)(2,1)S(1)} %get-tuple-element.54.wide_in, ...), custom_call_target="tpu_custom_call", output_to_operand_aliasing={{0}: (2, {})} | custom-call | tf_op jit(solution)/shard_map/first_mate/pallas_call | solution.py:471
  11.7 0.0 copy-start.1
  11.7 0.0 copy-start.2
  11.7 0.1 collective-permute-start.3
  11.8 0.7 %collective-permute-done.1.halo = bf16[32,4224]{1,0:T(8,128)(2,1)S(1)} collective-permute-done((bf16[32,4224]{1,0:T(8,128)(2,1)S(1)}, bf16[32,4224]{1,0:T(8,128)(2,1)S(1)}, u32[]{:S(2)}, u32[]{:S(2)}) %collective-permute-start.1) | collective-permute-done | bytes 270368 | tf_op jit(solution)/shard_map/ppermute | solution.py:505
  12.6 0.8 %first_off.1 = (bf16[32,16384]{1,0:T(8,128)(2,1)S(1)}, bf16[32,16384]{1,0:T(8,128)(2,1)S(1)}, bf16[32,128]{1,0:T(8,128)(2,1)S(1)}, s32[32,128]{1,0:T(8,128)S(1)}...) custom-call(s32[2,64]{1,0:T(2,128)S(4)} %get-tuple-element.52.cols, ...), custom_call_target="tpu_custom_call", output_to_operand_aliasing={{0}: (2, {}), {1}: (3, {})} | custom-call | tf_op jit(solution)/shard_map/first_off/pallas_call | solution.py:471
  13.3 2.8 %collective-permute-start.2 = (bf16[32,128]{1,0:T(8,128)(2,1)S(1)}, bf16[32,128]{1,0:T(8,128)(2,1)S(1)}, u32[]{:S(2)}, u32[]{:S(2)}) collective-permute-start(bf16[32,128]{1,0:T(8,128)(2,1)S(1)} %get-tuple-element.58), channel_id=1, source_target_pairs={{12,16},{16,12},{4,8},{8,4},{20,24},{24,20},{13,17},{17,13},{5,9},... | collective-permute-start | bytes 24584 | tf_op jit(solution)/shard_map/ppermute | solution.py:505
  16.1 2.2 %second_inner.1 = (f32[64,32,128]{2,1,0:T(8,128)S(1)}, f32[64,128]{1,0:T(8,128)S(1)}, f32[128,128]{1,0:T(8,128)S(1)}, f32[128,128]{1,0:T(8,128)S(1)}, f32[32,64]...) custom-call(s32[2,64]{1,0:T(2,128)S(4)} %get-tuple-element.52.cols, ...), custom_call_target="tpu_custom_call" | custom-call | tf_op jit(solution)/shard_map/second_inner/pallas_call | solution.py:471
  18.3 0.0 collective-permute-done.3.halo
  18.4 0.0 copy-start.4
  18.4 0.7 %second_mate.1 = (bf16[32,16384]{1,0:T(8,128)(2,1)S(1)}, bf16[32,4096]{1,0:T(8,128)(2,1)S(1)}, f32[32,128]{1,0:T(8,128)S(1)}) custom-call(s32[2,64]{1,0:T(2,128)S(4)} %get-tuple-element.52.cols, f32[64,32,128]{2,1,0:T(8,128)S(1)} %get-tuple-element.62.acc, bf16[32,16384]{1,0:T(8,128)(2,1)S(1)} %get-tuple-element.59.wide.wide_in, ...), custom_call_target="tpu_custom_call", output_to_operand_aliasing={{0}: (2, {})} | custom-call | tf_op jit(solution)/shard_map/second_mate/pallas_call | solution.py:471
  19.1 0.0 collective-permute-done.2.halo
  19.1 0.7 %second_off.1 = (f32[128,128]{1,0:T(8,128)S(1)}, bf16[128,128]{1,0:T(8,128)(2,1)S(1)}) custom-call(bf16[32,128]{1,0:T(8,128)(2,1)S(1)} %collective-permute-done.2.halo, bf16[64,3,128,128]{3,2,1,0:T(8,128)(2,1)S(1)} %get-tuple-element.55.ops, f32[64,128]{1,0:T(8,128)S(1)} %get-tuple-element.60.inc_one, f32[32,128]{1,0:T(8,128)S(1)} %get-tuple-element.61.inc_off, ...), custom_call_target="tpu_custom_call" | custom-call | tf_op jit(solution)/shard_map/second_off/pallas_call | solution.py:471
  19.8 3.7 %collective-permute-start.6 = (bf16[128,128]{1,0:T(8,128)(2,1)S(1)}, bf16[128,128]{1,0:T(8,128)(2,1)S(1)}, u32[]{:S(2)}, u32[]{:S(2)}) collective-permute-start(bf16[128,128]{1,0:T(8,128)(2,1)S(1)} %get-tuple-element.72), channel_id=1, source_target_pairs={{0,3},{1,2},{2,1},{3,0},{4,7},{5,6},{6,5},{7,4},{8,11},{9,10},{10,... | collective-permute-start | bytes 98312 | tf_op jit(solution)/shard_map/ppermute | solution.py:571
  23.5 0.0 collective-permute-start.5
  23.5 0.3 collective-permute-start.4
  23.9 0.9 %collective-permute-done.6.rest_2_ = bf16[128,128]{1,0:T(8,128)(2,1)S(1)} collective-permute-done((bf16[128,128]{1,0:T(8,128)(2,1)S(1)}, bf16[128,128]{1,0:T(8,128)(2,1)S(1)}, u32[]{:S(2)}, u32[]{:S(2)}) %collective-permute-start.6) | collective-permute-done | bytes 32800 | tf_op jit(solution)/shard_map/ppermute | solution.py:571
  24.8 2.4 %collective-permute-done.5.rest_1_ = bf16[128,128]{1,0:T(8,128)(2,1)S(1)} collective-permute-done((bf16[128,128]{1,0:T(8,128)(2,1)S(1)}, bf16[128,128]{1,0:T(8,128)(2,1)S(1)}, u32[]{:S(2)}, u32[]{:S(2)}) %collective-permute-start.5) | collective-permute-done | bytes 32800 | tf_op jit(solution)/shard_map/ppermute | solution.py:571
  27.2 0.0 collective-permute-done.4.rest_0_
  27.2 0.7 %residual_rim.1 = (f32[128,128]{1,0:T(8,128)S(1)}, f32[32,128]{1,0:T(8,128)S(1)}, bf16[64,128]{1,0:T(8,128)(2,1)S(1)}, f32[64,128]{1,0:T(8,128)S(1)}, f32[32,64]{1,0:T(8,128)S(1)}) custom-call(s32[2,64]{1,0:T(2,128)S(1)} %bitcast.3, f32[128,128]{1,0:T(8,128)S(1)} %get-tuple-element.66.inc, f32[128,128]{1,0:T(8,128)S(1)} %get-tuple-element.67.innov, ...), custom_call_target="tpu_custom_call" | custom-call | tf_op jit(solution)/shard_map/residual_rim/pallas_call | solution.py:471
  27.9 0.0 collective-permute-start.8
  27.9 5.5 %collective-permute-start.7 = (bf16[64,128]{1,0:T(8,128)(2,1)S(1)}, bf16[64,128]{1,0:T(8,128)(2,1)S(1)}, u32[]{:S(2)}, u32[]{:S(2)}) collective-permute-start(bf16[64,128]{1,0:T(8,128)(2,1)S(1)} %get-tuple-element.81), channel_id=1, source_target_pairs={{12,16},{16,12},{4,8},{8,4},{20,24},{24,20},{13,17},{17,13},{5,9},... | collective-permute-start | bytes 49160 | tf_op jit(solution)/shard_map/ppermute | solution.py:505
  33.4 0.7 %residual_inner.1 = (bf16[256,128]{1,0:T(8,128)(2,1)S(1)}, f32[32,256]{1,0:T(8,128)S(1)}, s32[1,256]{1,0:T(1,128)S(1)}) custom-call(f32[128,128]{1,0:T(8,128)S(1)} %get-tuple-element.73.res, bf16[64,3,128,128]{3,2,1,0:T(8,128)(2,1)S(1)} %get-tuple-element.55.ops, f32[32,64]{1,0:T(8,128)S(1)} %get-tuple-element.64.w, s32[2,64]{1,0:T(2,128)S(1)} %bitcast.4, ...), custom_call_target="tpu_custom_call" | custom-call | tf_op jit(solution)/shard_map/residual_inner/pallas_call | solution.py:471
  34.1 0.7 %collective-permute-done.7.off = bf16[64,128]{1,0:T(8,128)(2,1)S(1)} collective-permute-done((bf16[64,128]{1,0:T(8,128)(2,1)S(1)}, bf16[64,128]{1,0:T(8,128)(2,1)S(1)}, u32[]{:S(2)}, u32[]{:S(2)}) %collective-permute-start.7) | collective-permute-done | bytes 16416 | tf_op jit(solution)/shard_map/ppermute | solution.py:505
  34.9 0.0 collective-permute-done.8.mate
  34.9 0.7 %adjoint_off.1 = (bf16[1024,128]{1,0:T(8,128)(2,1)S(1)}, f32[64,32,128]{2,1,0:T(8,128)S(1)}, bf16[33,32,128]{2,1,0:T(8,128)(2,1)S(1)}, bf16[256,128]{1,0:T(8,128...) custom-call(s32[2,64]{1,0:T(2,128)S(4)} %get-tuple-element.52.cols, ...), custom_call_target="tpu_custom_call", output_to_operand_aliasing={{3}: (1, {}), {4}: (2, {}), {5}: (3, {})} | custom-call | tf_op jit(solution)/shard_map/adjoint_off/pallas_call | solution.py:471
  35.6 2.4 %collective-permute-start.9 = (f32[32,128]{1,0:T(8,128)S(1)}, f32[32,128]{1,0:T(8,128)S(1)}, u32[]{:S(2)}, u32[]{:S(2)}) collective-permute-start(f32[32,128]{1,0:T(8,128)S(1)} %get-tuple-element.88), channel_id=1, source_target_pairs={{0,8},{4,12},{8,0},{12,4},{16,24},{20,28},{24,16},{28,20},{1,9},{5... | collective-permute-start | bytes 49160 | tf_op jit(solution)/shard_map/ppermute | solution.py:514
  38.0 1.9 %collective-permute-start.12 = (bf16[33,32,128]{2,1,0:T(8,128)(2,1)S(1)}, bf16[33,32,128]{2,1,0:T(8,128)(2,1)S(1)}, u32[]{:S(2)}, u32[]{:S(2)}) collective-permute-start(bf16[33,32,128]{2,1,0:T(8,128)(2,1)S(1)} %get-tuple-element.95), channel_id=1, source_target_pairs={{4,8},{8,4},{20,24},{24,20},{5,9},{9,5},{21,25},{25,21},{6,10},{10... | collective-permute-start | bytes 811016 | tf_op jit(solution)/shard_map/ppermute | solution.py:511
  39.9 0.7 %collective-permute-start.11 = (bf16[33,32,128]{2,1,0:T(8,128)(2,1)S(1)}, bf16[33,32,128]{2,1,0:T(8,128)(2,1)S(1)}, u32[]{:S(2)}, u32[]{:S(2)}) collective-permute-start(bf16[33,32,128]{2,1,0:T(8,128)(2,1)S(1)} %get-tuple-element.95), channel_id=1, source_target_pairs={{12,16},{16,12},{13,17},{17,13},{14,18},{18,14},{15,19},{19,15}} | collective-permute-start | bytes 811016 | tf_op jit(solution)/shard_map/ppermute | solution.py:508
  40.6 0.6 %adjoint_mate.1 = (bf16[1024,128]{1,0:T(8,128)(2,1)S(1)}, f32[64,32,128]{2,1,0:T(8,128)S(1)}, bf16[32,32,128]{2,1,0:T(8,128)(2,1)S(1)}) custom-call(s32[2,64]{1,0:T(2,128)S(4)} %get-tuple-element.52.cols, f32[32,256]{1,0:T(8,128)S(1)} %get-tuple-element.84.wp, s32[1,256]{1,0:T(1,128)S(1)} %get-tuple-element.85.tgt, ...), custom_call_target="tpu_custom_call" | custom-call | tf_op jit(solution)/shard_map/adjoint_mate/pallas_call | solution.py:471
  41.3 0.0 collective-permute-done.9
  41.3 0.1 collective-permute-start.14
  41.4 3.1 %collective-permute-start.10 = (f32[32,128]{1,0:T(8,128)S(1)}, f32[32,128]{1,0:T(8,128)S(1)}, u32[]{:S(2)}, u32[]{:S(2)}) collective-permute-start(f32[32,128]{1,0:T(8,128)S(1)} %add.6), channel_id=1, source_target_pairs={{0,16},{4,20},{8,24},{12,28},{16,0},{20,4},{24,8},{28,12},{1,17},{... | collective-permute-start | bytes 49160 | tf_op jit(solution)/shard_map/ppermute | solution.py:514
  44.5 0.9 %adjoint_inner.1.own = f32[64,32,128]{2,1,0:T(8,128)S(1)} custom-call(s32[2,64]{1,0:T(2,128)S(4)} %get-tuple-element.52.cols, bf16[1024,128]{1,0:T(8,128)(2,1)S(1)} %get-tuple-element.90.mid_off, bf16[1024,128]{1,0:T(8,128)(2,1)S(1)} %get-tuple-element.91.mid_mate, f32[64,32,128]{2,1,0:T(8,128)S(1)} %get-tuple-element.92.sums_off, ...), custom_call_target="tpu_custom_call" | custom-call | tf_op jit(solution)/shard_map/adjoint_inner/pallas_call | solution.py:471
  45.4 0.2 collective-permute-done.10
  45.7 1.3 %collective-permute-start.13 = (f32[32,128]{1,0:T(8,128)S(1)}, f32[32,128]{1,0:T(8,128)S(1)}, u32[]{:S(2)}, u32[]{:S(2)}) collective-permute-start(f32[32,128]{1,0:T(8,128)S(1)} %add.7.total), channel_id=1, source_target_pairs={{0,4},{4,0},{8,12},{12,8},{16,20},{20,16},{24,28},{28,24},{1,5},{5... | collective-permute-start | bytes 49160 | tf_op jit(solution)/shard_map/ppermute | solution.py:502
  47.0 0.0 collective-permute-done.14.mate
  47.0 0.8 %finish_mate.1.out_in = f32[32,8192]{1,0:T(8,128)} custom-call(f32[64,32,128]{2,1,0:T(8,128)S(1)} %adjoint_inner.1.own, bf16[32,32,128]{2,1,0:T(8,128)(2,1)S(1)} %collective-permute-done.14.mate), custom_call_target="tpu_custom_call" | custom-call | tf_op jit(solution)/shard_map/finish_mate/pallas_call | solution.py:471
  47.8 0.0 collective-permute-done.13.mate_total
  47.8 0.0 collective-permute-done.12.near
  47.8 1.0 %finish_off.1 = (f32[32,8192]{1,0:T(8,128)}, f32[32,64]{1,0:T(8,128)}) custom-call(f32[64,32,128]{2,1,0:T(8,128)S(1)} %adjoint_inner.1.own, bf16[33,32,128]{2,1,0:T(8,128)(2,1)S(1)} %collective-permute-done.11.far, bf16[33,32,128]{2,1,0:T(8,128)(2,1)S(1)} %collective-permute-done.12.near, ...), custom_call_target="tpu_custom_call", output_to_operand_aliasing={{0}: (6, {})} | custom-call | tf_op jit(solution)/shard_map/finish_off/pallas_call | solution.py:471
  (8 shorter events, 0.0 us)
Async XLA Ops:
  1.8 9.2 %collective-permute-start = (bf16[32,4096]{1,0:T(8,128)(2,1)S(1)}, bf16[32,4096]{1,0:T(8,128)(2,1)S(1)}, u32[]{:S(2)}, u32[]{:S(2)}) collective-permute-start(bf16[32,4096]{1,0:T(8,128)(2,1)S(1)} %get-tuple-element.51.mate), channel_id=1, source_target_pairs={{0,4},{4,0},{8,12},{12,8},{16,20},{20,16},{24,28},{28,24},{1,5},{5... | collective-permute-start | bytes 786440 | tf_op jit(solution)/shard_map/ppermute | solution.py:502
  1.9 10.6 %collective-permute-start.1 = (bf16[32,4224]{1,0:T(8,128)(2,1)S(1)}, bf16[32,4224]{1,0:T(8,128)(2,1)S(1)}, u32[]{:S(2)}, u32[]{:S(2)}) collective-permute-start(bf16[32,4224]{1,0:T(8,128)(2,1)S(1)} %get-tuple-element.50.off), channel_id=1, source_target_pairs={{12,16},{16,12},{4,8},{8,4},{20,24},{24,20},{13,17},{17,13},{5,9},... | collective-permute-start | bytes 811016 | tf_op jit(solution)/shard_map/ppermute | solution.py:505
  6.4 0.7 %copy-start.3 = (s32[64,2]{0,1:T(2,128)S(1)}, s32[64,2]{0,1:T(2,128)}, u32[]{:S(2)}) copy-start(s32[64,2]{0,1:T(2,128)} %param.8) | copy-start | bytes 1540
  11.7 4.4 %copy-start = (f32[2,8192]{1,0:T(2,128)S(1)}, f32[2,8192]{1,0:T(2,128)}, u32[]{:S(2)}) copy-start(f32[2,8192]{1,0:T(2,128)} %innov.1) | copy-start | bytes 196612
  11.7 4.4 %copy-start.1 = (f32[2,8192]{1,0:T(2,128)S(1)}, f32[2,8192]{1,0:T(2,128)}, u32[]{:S(2)}) copy-start(f32[2,8192]{1,0:T(2,128)} %prec.1) | copy-start | bytes 196612
  11.7 4.4 %copy-start.2 = (f32[32,64]{1,0:T(8,128)S(1)}, f32[32,64]{1,0:T(8,128)}, u32[]{:S(2)}) copy-start(f32[32,64]{1,0:T(8,128)} %w.1) | copy-start | bytes 24580
  11.7 6.6 %collective-permute-start.3 = (bf16[32,4096]{1,0:T(8,128)(2,1)S(1)}, bf16[32,4096]{1,0:T(8,128)(2,1)S(1)}, u32[]{:S(2)}, u32[]{:S(2)}) collective-permute-start(bf16[32,4096]{1,0:T(8,128)(2,1)S(1)} %get-tuple-element.63), channel_id=1, source_target_pairs={{0,4},{4,0},{8,12},{12,8},{16,20},{20,16},{24,28},{28,24},{1,5},{5... | collective-permute-start | bytes 786440 | tf_op jit(solution)/shard_map/ppermute | solution.py:502
  13.3 5.8 %collective-permute-start.2 = (bf16[32,128]{1,0:T(8,128)(2,1)S(1)}, bf16[32,128]{1,0:T(8,128)(2,1)S(1)}, u32[]{:S(2)}, u32[]{:S(2)}) collective-permute-start(bf16[32,128]{1,0:T(8,128)(2,1)S(1)} %get-tuple-element.58), channel_id=1, source_target_pairs={{12,16},{16,12},{4,8},{8,4},{20,24},{24,20},{13,17},{17,13},{5,9},... | collective-permute-start | bytes 24584 | tf_op jit(solution)/shard_map/ppermute | solution.py:505
  18.4 8.8 %copy-start.4 = (s32[64,2]{0,1:T(2,128)S(1)}, s32[64,2]{0,1:T(2,128)}, u32[]{:S(2)}) copy-start(s32[64,2]{0,1:T(2,128)} %param.8) | copy-start | bytes 1540
  19.8 5.0 %collective-permute-start.6 = (bf16[128,128]{1,0:T(8,128)(2,1)S(1)}, bf16[128,128]{1,0:T(8,128)(2,1)S(1)}, u32[]{:S(2)}, u32[]{:S(2)}) collective-permute-start(bf16[128,128]{1,0:T(8,128)(2,1)S(1)} %get-tuple-element.72), channel_id=1, source_target_pairs={{0,3},{1,2},{2,1},{3,0},{4,7},{5,6},{6,5},{7,4},{8,11},{9,10},{10,... | collective-permute-start | bytes 98312 | tf_op jit(solution)/shard_map/ppermute | solution.py:571
  23.5 3.7 %collective-permute-start.5 = (bf16[128,128]{1,0:T(8,128)(2,1)S(1)}, bf16[128,128]{1,0:T(8,128)(2,1)S(1)}, u32[]{:S(2)}, u32[]{:S(2)}) collective-permute-start(bf16[128,128]{1,0:T(8,128)(2,1)S(1)} %get-tuple-element.72), channel_id=1, source_target_pairs={{0,2},{1,3},{2,0},{3,1},{4,6},{5,7},{6,4},{7,5},{8,10},{9,11},{10,... | collective-permute-start | bytes 98312 | tf_op jit(solution)/shard_map/ppermute | solution.py:571
  23.5 3.7 %collective-permute-start.4 = (bf16[128,128]{1,0:T(8,128)(2,1)S(1)}, bf16[128,128]{1,0:T(8,128)(2,1)S(1)}, u32[]{:S(2)}, u32[]{:S(2)}) collective-permute-start(bf16[128,128]{1,0:T(8,128)(2,1)S(1)} %get-tuple-element.72), channel_id=1, source_target_pairs={{0,1},{1,0},{2,3},{3,2},{4,5},{5,4},{6,7},{7,6},{8,9},{9,8},{10,11... | collective-permute-start | bytes 98312 | tf_op jit(solution)/shard_map/ppermute | solution.py:571
  27.9 7.0 %collective-permute-start.8 = (f32[64,128]{1,0:T(8,128)S(1)}, f32[64,128]{1,0:T(8,128)S(1)}, u32[]{:S(2)}, u32[]{:S(2)}) collective-permute-start(f32[64,128]{1,0:T(8,128)S(1)} %get-tuple-element.75.own_mate), channel_id=1, source_target_pairs={{0,4},{4,0},{8,12},{12,8},{16,20},{20,16},{24,28},{28,24},{1,5},{5... | collective-permute-start | bytes 98312 | tf_op jit(solution)/shard_map/ppermute | solution.py:502
  27.9 6.9 %collective-permute-start.7 = (bf16[64,128]{1,0:T(8,128)(2,1)S(1)}, bf16[64,128]{1,0:T(8,128)(2,1)S(1)}, u32[]{:S(2)}, u32[]{:S(2)}) collective-permute-start(bf16[64,128]{1,0:T(8,128)(2,1)S(1)} %get-tuple-element.81), channel_id=1, source_target_pairs={{12,16},{16,12},{4,8},{8,4},{20,24},{24,20},{13,17},{17,13},{5,9},... | collective-permute-start | bytes 49160 | tf_op jit(solution)/shard_map/ppermute | solution.py:505
  35.6 5.7 %collective-permute-start.9 = (f32[32,128]{1,0:T(8,128)S(1)}, f32[32,128]{1,0:T(8,128)S(1)}, u32[]{:S(2)}, u32[]{:S(2)}) collective-permute-start(f32[32,128]{1,0:T(8,128)S(1)} %get-tuple-element.88), channel_id=1, source_target_pairs={{0,8},{4,12},{8,0},{12,4},{16,24},{20,28},{24,16},{28,20},{1,9},{5... | collective-permute-start | bytes 49160 | tf_op jit(solution)/shard_map/ppermute | solution.py:514
  38.0 9.8 %collective-permute-start.12 = (bf16[33,32,128]{2,1,0:T(8,128)(2,1)S(1)}, bf16[33,32,128]{2,1,0:T(8,128)(2,1)S(1)}, u32[]{:S(2)}, u32[]{:S(2)}) collective-permute-start(bf16[33,32,128]{2,1,0:T(8,128)(2,1)S(1)} %get-tuple-element.95), channel_id=1, source_target_pairs={{4,8},{8,4},{20,24},{24,20},{5,9},{9,5},{21,25},{25,21},{6,10},{10... | collective-permute-start | bytes 811016 | tf_op jit(solution)/shard_map/ppermute | solution.py:511
  39.9 7.9 %collective-permute-start.11 = (bf16[33,32,128]{2,1,0:T(8,128)(2,1)S(1)}, bf16[33,32,128]{2,1,0:T(8,128)(2,1)S(1)}, u32[]{:S(2)}, u32[]{:S(2)}) collective-permute-start(bf16[33,32,128]{2,1,0:T(8,128)(2,1)S(1)} %get-tuple-element.95), channel_id=1, source_target_pairs={{12,16},{16,12},{13,17},{17,13},{14,18},{18,14},{15,19},{19,15}} | collective-permute-start | bytes 811016 | tf_op jit(solution)/shard_map/ppermute | solution.py:508
  41.3 5.7 %collective-permute-start.14 = (bf16[32,32,128]{2,1,0:T(8,128)(2,1)S(1)}, bf16[32,32,128]{2,1,0:T(8,128)(2,1)S(1)}, u32[]{:S(2)}, u32[]{:S(2)}) collective-permute-start(bf16[32,32,128]{2,1,0:T(8,128)(2,1)S(1)} %get-tuple-element.97), channel_id=1, source_target_pairs={{0,4},{4,0},{8,12},{12,8},{16,20},{20,16},{24,28},{28,24},{1,5},{5... | collective-permute-start | bytes 786440 | tf_op jit(solution)/shard_map/ppermute | solution.py:502
  41.4 4.3 %collective-permute-start.10 = (f32[32,128]{1,0:T(8,128)S(1)}, f32[32,128]{1,0:T(8,128)S(1)}, u32[]{:S(2)}, u32[]{:S(2)}) collective-permute-start(f32[32,128]{1,0:T(8,128)S(1)} %add.6), channel_id=1, source_target_pairs={{0,16},{4,20},{8,24},{12,28},{16,0},{20,4},{24,8},{28,12},{1,17},{... | collective-permute-start | bytes 49160 | tf_op jit(solution)/shard_map/ppermute | solution.py:514
  45.7 2.1 %collective-permute-start.13 = (f32[32,128]{1,0:T(8,128)S(1)}, f32[32,128]{1,0:T(8,128)S(1)}, u32[]{:S(2)}, u32[]{:S(2)}) collective-permute-start(f32[32,128]{1,0:T(8,128)S(1)} %add.7.total), channel_id=1, source_target_pairs={{0,4},{4,0},{8,12},{12,8},{16,20},{20,16},{24,28},{28,24},{1,5},{5... | collective-permute-start | bytes 49160 | tf_op jit(solution)/shard_map/ppermute | solution.py:502
